TPU v7x, 256 devices: a whole 4x4x8 slice. The times are simulated.
256 devices in a mesh: shot: 4 (over x_hi, core), dom: 64 (over x_lo, z, y).
Axes of the slice: x: 4 (x_hi: 2, x_lo: 2; x = x_hi * 2 + x_lo), y: 4, z: 8, core: 2. Of those that a mesh axis runs over, the one named last changes fastest.
Arguments:
- parked: bfloat16 [4, 4096, 4096], P('shot', 'dom'), may hold values from -6 to 6
- parked_slot: int32 [4, 64, 64], P('shot', 'dom'), may hold values from 0 to 63, as said below
- holder_list: int32 [4, 64, 64], P('shot', 'dom'), may hold values from 0 to 63, as said below
- speed_sq: float32 [512, 128, 128], P('dom'), may hold values from 0.04 to 0.18
- adjoint_next: float32 [4, 512, 128, 128], P('shot', 'dom'), may hold values from -6 to 6
- adjoint_now: float32 [4, 512, 128, 128], P('shot', 'dom'), may hold values from -6 to 6
- wavelet: float32 [4, 3], P('shot'), may hold values from -9 to 9
- src_depth: int32 [4], P('shot'), may hold values from 0 to 511
- src_row: int32 [4], P('shot'), may hold values from 0 to 16383
- rec_depth: int32 [1024], replicated, may hold values from 0 to 511
- rec_row: int32 [1024], replicated, may hold values from 0 to 16383
- residuals: float32 [4, 4, 1024], P('shot'), may hold values from -6 to 6
Outputs:
- gradient: float32 [512, 128, 128], P('dom', 'shot')
- adjoint_late: float32 [4, 512, 128, 128], P('shot', 'dom')
- adjoint_early: float32 [4, 512, 128, 128], P('shot', 'dom')
Inputs may be any that keep to these rules, and one draw needn't show every extreme that they name: Each row of parked_slot names every slot of its holder once. Each row of holder_list names every holder slab once.
All inputs are finite; a program needn't handle non-finite values.
Results may differ from a plain program's by a relative error of at most 0.0005.
Values may be sent and summed in bfloat16 or wider, within the bound.
No kernel may reach another device: no remote copies, remote signals or barrier semaphores. Data moves between devices by JAX's collectives and lax.ppermute only.
A program may use at most 64 MiB of HBM per device.

v0:
```python
import jax
import jax.numpy as jnp
from jax import lax
from jax.sharding import PartitionSpec as P

STEPS = 4


stencil_coef = (-205.0 / 72.0, 8.0 / 5.0, -1.0 / 5.0, 8.0 / 315.0, -1.0 / 560.0)
grad_scale = 0.0625


def extended_2(value, sides, width):
    for axis, dim in sides:
        peers, length = (lax.axis_size(axis), value.shape[dim])
        up = [(i, (i + 1) % peers) for i in range(peers - 1)]
        down = [(j, i) for i, j in up]
        last = lax.slice_in_dim(value, length - width, length, axis=dim)
        initial = lax.slice_in_dim(value, 0, width, axis=dim)
        before = lax.ppermute(last, axis, up)
        after = lax.ppermute(initial, axis, down)
        value = jnp.concatenate([before, value, after], axis=dim)
    return value


def lateral(field):
    width_x, width_y = (field.shape[1], field.shape[2])
    padded = jnp.pad(field, ((0, 0), (4, 4), (4, 4)))
    summed = 3.0 * stencil_coef[0] * field
    for offset in range(1, 5):
        neighbours = (
            padded[:, 4 + offset : 4 + offset + width_x, 4 : 4 + width_y]
            + padded[:, 4 - offset : 4 - offset + width_x, 4 : 4 + width_y]
        )
        neighbours = (
            neighbours
            + padded[:, 4 : 4 + width_x, 4 + offset : 4 + offset + width_y]
            + padded[:, 4 : 4 + width_x, 4 - offset : 4 - offset + width_y]
        )
        summed = summed + stencil_coef[offset] * neighbours
    return summed


def vertical(extended, slab_depth):
    summed = stencil_coef[1] * (extended[5 : 5 + slab_depth] + extended[3 : 3 + slab_depth])
    for offset in range(2, 5):
        summed = summed + stencil_coef[offset] * (
            extended[4 + offset : 4 + offset + slab_depth]
            + extended[4 - offset : 4 - offset + slab_depth]
        )
    return summed


def laplace(field, extended):
    return lateral(field) + vertical(extended, field.shape[0])


def inject(field, depth_at, row_at, amount, top_plane):
    slab_depth, width_x, width_y = field.shape
    local_depth = depth_at - top_plane
    inside = (local_depth >= 0) & (local_depth < slab_depth)
    flat_index = jnp.clip(local_depth, 0, slab_depth - 1) * (width_x * width_y) + row_at
    updated = field.reshape(-1).at[flat_index].add(jnp.where(inside, amount, 0.0))
    return updated.reshape(slab_depth, width_x, width_y)


def per_device(
    parked,
    parked_slot,
    holder_list,
    speed_sq,
    adjoint_next,
    adjoint_now,
    wavelet,
    src_depth,
    src_row,
    rec_depth,
    rec_row,
    residuals,
):
    slab_depth, width_x, width_y = speed_sq.shape
    top_plane = lax.axis_index("dom") * slab_depth
    outgoing = jnp.take(parked[0], parked_slot[0, 0], axis=0)
    incoming = lax.all_to_all(outgoing, "dom", split_axis=0, concat_axis=0, tiled=True)
    pieces = jnp.take(incoming, holder_list[0, 0], axis=0)
    stored = pieces.reshape(2, slab_depth, width_x, width_y).astype(jnp.float32)
    previous = stored[0]
    current = stored[1]
    adj_later = adjoint_next[0]
    present = adjoint_now[0]
    forward_laps = []
    adjoint_fields = []
    for step_num in range(STEPS):
        extended = extended_2(current, (("dom", 0),), 4)
        lap_forward = laplace(current, extended)
        forward_laps.append(lap_forward)
        if step_num + 1 < STEPS:
            forward_advanced = 2.0 * current - previous + speed_sq * lap_forward
            previous, current = (
                current,
                inject(
                    forward_advanced,
                    src_depth,
                    src_row,
                    wavelet[0, step_num : step_num + 1],
                    top_plane,
                ),
            )
    for step_num in range(STEPS):
        scaled = speed_sq * present
        extended = extended_2(scaled, (("dom", 0),), 4)
        lap_adjoint = laplace(scaled, extended)
        adjoint_fields.append(present)
        advanced = 2.0 * present - adj_later + lap_adjoint
        adj_later, present = (
            present,
            inject(advanced, rec_depth, rec_row, residuals[0, step_num], top_plane),
        )
    summed = adjoint_fields[0] * forward_laps[STEPS - 1]
    for step_num in range(1, STEPS):
        summed = summed + adjoint_fields[step_num] * forward_laps[STEPS - 1 - step_num]
    gradient = lax.psum_scatter(grad_scale * summed, "shot", scatter_dimension=1, tiled=True)
    return (gradient, adj_later[None], present[None])


def solution(mesh):
    in_specs = (
        P("shot", "dom", None),
        P("shot", "dom", None),
        P("shot", "dom", None),
        P("dom", None, None),
        P("shot", "dom", None, None),
        P("shot", "dom", None, None),
        P("shot", None),
        P("shot"),
        P("shot"),
        P(),
        P(),
        P("shot", None, None),
    )
    out_specs = (P("dom", "shot", None), P("shot", "dom", None, None), P("shot", "dom", None, None))
    return jax.shard_map(
        per_device, mesh=mesh, in_specs=in_specs, out_specs=out_specs, check_vma=False
    )
```

profile of v0, /device:TPU:2, one launch (start us, length us, event | category | flops | bytes accessed | tf_op | source)
XLA Modules:
  0.0 207.3 jit_solution(14877753646206573463)
XLA Ops:
  8.6 0.9 gather_fusion
  10.1 1.0 reduce.6
  11.1 1.2 reshape.240
  12.3 13.2 %all-to-all-start = ((bf16[64,2,2048]{2,1,0:T(2,128)(2,1)}), bf16[64,2,2048]{2,1,0:T(2,128)(2,1)S(1)}, u32[]{:S(2)}, u32[]{:S(2)}) async-start(bf16[64,2,2048]{2,1,0:T(2,128)(2,1)} %reshape.240), calls=%async_computation | async-start | bytes 1048576 | tf_op jit(solution)/shard_map/all_to_all | solution.py:84
  28.1 13.7 %all-to-all-done = bf16[64,2,2048]{2,1,0:T(2,128)(2,1)S(1)} async-done(((bf16[64,2,2048]{2,1,0:T(2,128)(2,1)}), bf16[64,2,2048]{2,1,0:T(2,128)(2,1)S(1)}, u32[]{:S(2)}, u32[]{:S(2)}) %all-to-all-start) | async-done | bytes 524320 | tf_op jit(solution)/shard_map/all_to_all | solution.py:84
  42.9 0.9 gather_fusion.1
  44.1 0.8 slice_bitcast_fusion.1
  44.9 5.9 %collective-permute-start = (f32[4,128,128]{2,1,0:T(8,128)}, f32[4,128,128]{2,1,0:T(8,128)S(1)}, u32[]{:S(2)}, u32[]{:S(2)}) collective-permute-start(f32[4,128,128]{2,1,0:T(8,128)} %get-tuple-element.48), channel_id=1, source_target_pairs={{1,0},{2,1},{3,2},{4,3},{5,4},{6,5},{7,6},{8,7},{9,8},{10,9},{11,1... | collective-permute-start | bytes 786440 | tf_op jit(solution)/shard_map/ppermute | solution.py:21
  50.8 1.9 collective-permute-start.1
  52.9 0.9 squeeze.47
  53.8 9.8 %collective-permute-done.1 = f32[4,128,128]{2,1,0:T(8,128)} collective-permute-done((f32[4,128,128]{2,1,0:T(8,128)}, f32[4,128,128]{2,1,0:T(8,128)}, u32[]{:S(2)}, u32[]{:S(2)}) %collective-permute-start.1) | collective-permute-done | bytes 262176 | tf_op jit(solution)/shard_map/ppermute | solution.py:20
  63.6 1.0 constant_dynamic-update-slice_fusion.3
  64.8 0.9 copy-done.3
  66.0 2.0 multiply_add_fusion.2
  68.0 2.1 collective-permute-start.8
  70.0 3.9 %collective-permute-start.9 = (f32[4,128,128]{2,1,0:T(8,128)S(1)}, f32[4,128,128]{2,1,0:T(8,128)S(1)}, u32[]{:S(2)}, u32[]{:S(2)}) collective-permute-start(f32[4,128,128]{2,1,0:T(8,128)S(1)} %get-tuple-element.63), channel_id=1, source_target_pairs={{0,1},{1,2},{2,3},{3,4},{4,5},{5,6},{6,7},{7,8},{8,9},{9,10},{10,1... | collective-permute-start | bytes 786440 | tf_op jit(solution)/shard_map/ppermute | solution.py:20
  73.9 2.0 fusion.303
  76.7 1.9 collective-permute-start.3
  78.6 8.1 %collective-permute-start.2 = (f32[4,128,128]{2,1,0:T(8,128)}, f32[4,128,128]{2,1,0:T(8,128)}, u32[]{:S(2)}, u32[]{:S(2)}) collective-permute-start(f32[4,128,128]{2,1,0:T(8,128)} %bitcast.12), channel_id=1, source_target_pairs={{1,0},{2,1},{3,2},{4,3},{5,4},{6,5},{7,6},{8,7},{9,8},{10,9},{11,1... | collective-permute-start | bytes 786440 | tf_op jit(solution)/shard_map/ppermute | solution.py:21
  86.8 1.2 fusion.57
  88.0 6.3 %scatter_fusion = f32[131072]{0:T(1024)S(1)} fusion(f32[131072]{0:T(1024)S(1)} %bitcast.71, s32[1024]{0:T(1024)S(1)} %compare_select_fusion, f32[1024]{0:T(1024)S(1)} %get-tuple-element.79), kind=kCustom, calls=%fused_computation.2 | custom fusion | flops 1024 | bytes 16384 | tf_op jit(solution)/shard_map/scatter-add | solution.py:63
  94.3 3.0 %multiply_add_fusion.1 = (f32[8,128,128]{2,1,0:T(8,128)S(1)}, f32[8,128,128]{2,1,0:T(8,128)}, f32[8,128,128]{2,1,0:T(8,128)S(1)}) fusion(f32[8,128,128]{2,1,0:T(8,128)S(1)} %copy-done.4, f32[8,128,128]{2,1,0:T(8,128)S(1)} %squeeze.46, f32[8,128,128]{2,1,0:T(8,128)S(1)} %bitcast.89, f32[4,128,128]{2,1,0:T(8,128)S(1)} %collective-permute-done.3, ...), kind=kLoop, calls=%fused_computation.547 | loop fusion | flops 6029312 | bytes 4194304 | tf_op jit(solution)/shard_map/add | solution.py:98
  97.3 5.2 %collective-permute-start.10 = (f32[4,128,128]{2,1,0:T(8,128)S(1)}, f32[4,128,128]{2,1,0:T(8,128)S(1)}, u32[]{:S(2)}, u32[]{:S(2)}) collective-permute-start(f32[4,128,128]{2,1,0:T(8,128)S(1)} %get-tuple-element.59), channel_id=1, source_target_pairs={{1,0},{2,1},{3,2},{4,3},{5,4},{6,5},{7,6},{8,7},{9,8},{10,9},{11,1... | collective-permute-start | bytes 786440 | tf_op jit(solution)/shard_map/ppermute | solution.py:21
  102.5 1.9 collective-permute-start.11
  104.4 1.9 fusion.304
  106.4 0.9 fusion.316
  107.3 1.9 collective-permute-start.5
  109.2 8.1 %collective-permute-start.4 = (f32[4,128,128]{2,1,0:T(8,128)}, f32[4,128,128]{2,1,0:T(8,128)}, u32[]{:S(2)}, u32[]{:S(2)}) collective-permute-start(f32[4,128,128]{2,1,0:T(8,128)} %bitcast.17), channel_id=1, source_target_pairs={{1,0},{2,1},{3,2},{4,3},{5,4},{6,5},{7,6},{8,7},{9,8},{10,9},{11,1... | collective-permute-start | bytes 786440 | tf_op jit(solution)/shard_map/ppermute | solution.py:21
  117.3 1.2 fusion.40
  118.5 6.5 %scatter_fusion.1 = f32[131072]{0:T(1024)S(1)} fusion(f32[131072]{0:T(1024)S(1)} %bitcast.76, s32[1024]{0:T(1024)S(1)} %compare_select_fusion, f32[1024]{0:T(1024)S(1)} %get-tuple-element.78), kind=kCustom, calls=%fused_computation.3 | custom fusion | flops 1024 | bytes 16384 | tf_op jit(solution)/shard_map/scatter-add | solution.py:63
  125.0 8.9 %multiply_add_fusion = (f32[8,128,128]{2,1,0:T(8,128)S(1)}, f32[8,128,128]{2,1,0:T(8,128)}, f32[8,128,128]{2,1,0:T(8,128)S(1)}) fusion(f32[8,128,128]{2,1,0:T(8,128)S(1)} %copy-done.4, f32[8,128,128]{2,1,0:T(8,128)S(1)} %bitcast.90, f32[8,128,128]{2,1,0:T(8,128)} %bitcast.94, f32[4,128,128]{2,1,0:T(8,128)S(1)} %collective-permute-done.5, ...), kind=kLoop, calls=%fused_computation.546 | loop fusion | flops 6029312 | bytes 4194304 | tf_op jit(solution)/shard_map/add | solution.py:98
  133.9 5.1 %collective-permute-start.12 = (f32[4,128,128]{2,1,0:T(8,128)S(1)}, f32[4,128,128]{2,1,0:T(8,128)S(1)}, u32[]{:S(2)}, u32[]{:S(2)}) collective-permute-start(f32[4,128,128]{2,1,0:T(8,128)S(1)} %get-tuple-element.56), channel_id=1, source_target_pairs={{1,0},{2,1},{3,2},{4,3},{5,4},{6,5},{7,6},{8,7},{9,8},{10,9},{11,1... | collective-permute-start | bytes 786440 | tf_op jit(solution)/shard_map/ppermute | solution.py:21
  139.1 1.9 collective-permute-start.13
  141.0 1.9 fusion.305
  142.9 0.9 fusion.315
  143.8 1.9 collective-permute-start.7
  145.7 8.1 %collective-permute-start.6 = (f32[4,128,128]{2,1,0:T(8,128)}, f32[4,128,128]{2,1,0:T(8,128)}, u32[]{:S(2)}, u32[]{:S(2)}) collective-permute-start(f32[4,128,128]{2,1,0:T(8,128)} %bitcast.22), channel_id=1, source_target_pairs={{1,0},{2,1},{3,2},{4,3},{5,4},{6,5},{7,6},{8,7},{9,8},{10,9},{11,1... | collective-permute-start | bytes 786440 | tf_op jit(solution)/shard_map/ppermute | solution.py:21
  153.9 1.2 fusion.23
  155.0 6.3 %scatter_fusion.2 = f32[131072]{0:T(1024)S(1)} fusion(f32[131072]{0:T(1024)S(1)} %bitcast.81, s32[1024]{0:T(1024)S(1)} %compare_select_fusion, f32[1024]{0:T(1024)S(1)} %get-tuple-element.77), kind=kCustom, calls=%fused_computation.4 | custom fusion | flops 1024 | bytes 16384 | tf_op jit(solution)/shard_map/scatter-add | solution.py:63
  161.3 9.9 %fusion.311 = (f32[8,128,128]{2,1,0:T(8,128)}, f32[8,128,128]{2,1,0:T(8,128)}) fusion(f32[8,128,128]{2,1,0:T(8,128)S(1)} %copy-done.4, f32[8,128,128]{2,1,0:T(8,128)S(1)} %bitcast.82, f32[8,128,128]{2,1,0:T(8,128)} %get-tuple-element.47, f32[8,128,128]{2,1,0:T(8,128)S(1)} %bitcast.79, f32[8,128,128]{2,1,0:T(8,128)} %get-tuple-element.45, ...), kind=kLoop, calls=%fused_computation.581 | loop fusion | flops 6553600 | bytes 6291456 | tf_op jit(solution)/shard_map/mul | solution.py:110
  171.3 1.1 fusion.310
  172.4 5.3 %collective-permute-start.14 = (f32[4,128,128]{2,1,0:T(8,128)S(1)}, f32[4,128,128]{2,1,0:T(8,128)S(1)}, u32[]{:S(2)}, u32[]{:S(2)}) collective-permute-start(f32[4,128,128]{2,1,0:T(8,128)S(1)} %get-tuple-element.52), channel_id=1, source_target_pairs={{1,0},{2,1},{3,2},{4,3},{5,4},{6,5},{7,6},{8,7},{9,8},{10,9},{11,1... | collective-permute-start | bytes 786440 | tf_op jit(solution)/shard_map/ppermute | solution.py:21
  177.7 1.9 collective-permute-start.15
  179.6 1.9 collective-permute-done.14
  181.5 8.6 %collective-permute-done.15 = f32[4,128,128]{2,1,0:T(8,128)S(1)} collective-permute-done((f32[4,128,128]{2,1,0:T(8,128)S(1)}, f32[4,128,128]{2,1,0:T(8,128)S(1)}, u32[]{:S(2)}, u32[]{:S(2)}) %collective-permute-start.15) | collective-permute-done | bytes 262176 | tf_op jit(solution)/shard_map/ppermute | solution.py:20
  190.2 1.1 fusion.6
  191.3 6.3 %scatter_fusion.3 = f32[131072]{0:T(1024)S(1)} fusion(f32[131072]{0:T(1024)S(1)} %bitcast.85, s32[1024]{0:T(1024)S(1)} %compare_select_fusion, f32[1024]{0:T(1024)S(1)} %get-tuple-element.40), kind=kCustom, calls=%fused_computation.5 | custom fusion | flops 1024 | bytes 16384 | tf_op jit(solution)/shard_map/scatter-add | solution.py:63
  197.6 2.8 %reduce-scatter.2.cloned.1.call-done = f32[8,32,128]{2,1,0:T(8,128)} async-done(((f32[8,128,128]{2,1,0:T(8,128)}), f32[8,32,128]{2,1,0:T(8,128)}) %reduce-scatter.2.cloned.1.call-update) | async-done | bytes 131088 | tf_op jit(solution)/shard_map/reduce_scatter | solution.py:122
  (69 shorter events, 5.8 us)
Async XLA Ops:
  7.2 1.4 copy-start
  11.1 14.5 %copy-start.14 = (s32[1,1,64]{2,1,0:T(1,128)S(1)}, s32[1,1,64]{2,1,0:T(1,128)}, u32[]{:S(2)}) copy-start(s32[1,1,64]{2,1,0:T(1,128)} %param.22) | copy-start | bytes 772
  11.1 16.3 %copy-start.12 = (f32[1,3]{1,0:T(1,128)S(1)}, f32[1,3]{1,0:T(1,128)}, u32[]{:S(2)}) copy-start(f32[1,3]{1,0:T(1,128)} %param.26) | copy-start | bytes 40
  11.1 17.0 %copy-start.10 = (s32[1024]{0:T(1024)S(1)}, s32[1024]{0:T(1024)}, u32[]{:S(2)}) copy-start(s32[1024]{0:T(1024)} %param.29) | copy-start | bytes 12292
  11.1 16.9 %copy-start.13 = (s32[1024]{0:T(1024)S(1)}, s32[1024]{0:T(1024)}, u32[]{:S(2)}) copy-start(s32[1024]{0:T(1024)} %param.30) | copy-start | bytes 12292
  11.1 16.9 %copy-start.11 = (f32[1,4,1024]{2,1,0:T(4,128)S(1)}, f32[1,4,1024]{2,1,0:T(4,128)}, u32[]{:S(2)}) copy-start(f32[1,4,1024]{2,1,0:T(4,128)} %param.31) | copy-start | bytes 49156
  12.3 29.5 %all-to-all-start = ((bf16[64,2,2048]{2,1,0:T(2,128)(2,1)}), bf16[64,2,2048]{2,1,0:T(2,128)(2,1)S(1)}, u32[]{:S(2)}, u32[]{:S(2)}) async-start(bf16[64,2,2048]{2,1,0:T(2,128)(2,1)} %reshape.240), calls=%async_computation | async-start | bytes 1048576 | tf_op jit(solution)/shard_map/all_to_all | solution.py:84
  25.5 174.9 %reduce-scatter.2.cloned.1.call-start = ((), (), s32[]{:S(2)}) async-start(), calls=%async_computation.2 | async-start | bytes 655360 | tf_op jit(solution)/shard_map/reduce_scatter | solution.py:122
  44.9 19.8 %collective-permute-start = (f32[4,128,128]{2,1,0:T(8,128)}, f32[4,128,128]{2,1,0:T(8,128)S(1)}, u32[]{:S(2)}, u32[]{:S(2)}) collective-permute-start(f32[4,128,128]{2,1,0:T(8,128)} %get-tuple-element.48), channel_id=1, source_target_pairs={{1,0},{2,1},{3,2},{4,3},{5,4},{6,5},{7,6},{8,7},{9,8},{10,9},{11,1... | collective-permute-start | bytes 786440 | tf_op jit(solution)/shard_map/ppermute | solution.py:21
  50.8 12.8 %collective-permute-start.1 = (f32[4,128,128]{2,1,0:T(8,128)}, f32[4,128,128]{2,1,0:T(8,128)}, u32[]{:S(2)}, u32[]{:S(2)}) collective-permute-start(f32[4,128,128]{2,1,0:T(8,128)} %get-tuple-element.49), channel_id=1, source_target_pairs={{0,1},{1,2},{2,3},{3,4},{4,5},{5,6},{6,7},{7,8},{8,9},{9,10},{10,1... | collective-permute-start | bytes 786440 | tf_op jit(solution)/shard_map/ppermute | solution.py:20
  64.6 1.0 copy-start.3
  64.6 1.2 copy-start.4
  64.6 1.3 copy-start.8
  67.9 18.9 %copy-start.9 = (f32[1,8,128,128]{3,2,1,0:T(8,128)S(1)}, f32[1,8,128,128]{3,2,1,0:T(8,128)}, u32[]{:S(2)}) copy-start(f32[1,8,128,128]{3,2,1,0:T(8,128)} %param.24) | copy-start | bytes 1572868
  68.0 18.8 %collective-permute-start.8 = (f32[4,128,128]{2,1,0:T(8,128)S(1)}, f32[4,128,128]{2,1,0:T(8,128)S(1)}, u32[]{:S(2)}, u32[]{:S(2)}) collective-permute-start(f32[4,128,128]{2,1,0:T(8,128)S(1)} %get-tuple-element.62), channel_id=1, source_target_pairs={{1,0},{2,1},{3,2},{4,3},{5,4},{6,5},{7,6},{8,7},{9,8},{10,9},{11,1... | collective-permute-start | bytes 786440 | tf_op jit(solution)/shard_map/ppermute | solution.py:21
  70.0 16.8 %collective-permute-start.9 = (f32[4,128,128]{2,1,0:T(8,128)S(1)}, f32[4,128,128]{2,1,0:T(8,128)S(1)}, u32[]{:S(2)}, u32[]{:S(2)}) collective-permute-start(f32[4,128,128]{2,1,0:T(8,128)S(1)} %get-tuple-element.63), channel_id=1, source_target_pairs={{0,1},{1,2},{2,3},{3,4},{4,5},{5,6},{6,7},{7,8},{8,9},{9,10},{10,1... | collective-permute-start | bytes 786440 | tf_op jit(solution)/shard_map/ppermute | solution.py:20
  76.7 17.5 %collective-permute-start.3 = (f32[4,128,128]{2,1,0:T(8,128)}, f32[4,128,128]{2,1,0:T(8,128)S(1)}, u32[]{:S(2)}, u32[]{:S(2)}) collective-permute-start(f32[4,128,128]{2,1,0:T(8,128)} %bitcast.13), channel_id=1, source_target_pairs={{0,1},{1,2},{2,3},{3,4},{4,5},{5,6},{6,7},{7,8},{8,9},{9,10},{10,1... | collective-permute-start | bytes 786440 | tf_op jit(solution)/shard_map/ppermute | solution.py:20
  78.6 15.6 %collective-permute-start.2 = (f32[4,128,128]{2,1,0:T(8,128)}, f32[4,128,128]{2,1,0:T(8,128)}, u32[]{:S(2)}, u32[]{:S(2)}) collective-permute-start(f32[4,128,128]{2,1,0:T(8,128)} %bitcast.12), channel_id=1, source_target_pairs={{1,0},{2,1},{3,2},{4,3},{5,4},{6,5},{7,6},{8,7},{9,8},{10,9},{11,1... | collective-permute-start | bytes 786440 | tf_op jit(solution)/shard_map/ppermute | solution.py:21
  97.3 20.0 %collective-permute-start.10 = (f32[4,128,128]{2,1,0:T(8,128)S(1)}, f32[4,128,128]{2,1,0:T(8,128)S(1)}, u32[]{:S(2)}, u32[]{:S(2)}) collective-permute-start(f32[4,128,128]{2,1,0:T(8,128)S(1)} %get-tuple-element.59), channel_id=1, source_target_pairs={{1,0},{2,1},{3,2},{4,3},{5,4},{6,5},{7,6},{8,7},{9,8},{10,9},{11,1... | collective-permute-start | bytes 786440 | tf_op jit(solution)/shard_map/ppermute | solution.py:21
  102.5 14.8 %collective-permute-start.11 = (f32[4,128,128]{2,1,0:T(8,128)S(1)}, f32[4,128,128]{2,1,0:T(8,128)S(1)}, u32[]{:S(2)}, u32[]{:S(2)}) collective-permute-start(f32[4,128,128]{2,1,0:T(8,128)S(1)} %get-tuple-element.60), channel_id=1, source_target_pairs={{0,1},{1,2},{2,3},{3,4},{4,5},{5,6},{6,7},{7,8},{8,9},{9,10},{10,1... | collective-permute-start | bytes 786440 | tf_op jit(solution)/shard_map/ppermute | solution.py:20
  106.4 12.1 %copy-start.6 = (f32[131072]{0:T(1024)}, f32[131072]{0:T(1024)S(1)}, u32[]{:S(2)}) copy-start(f32[131072]{0:T(1024)S(1)} %fusion.304) | copy-start | bytes 1572868
  107.3 17.7 %collective-permute-start.5 = (f32[4,128,128]{2,1,0:T(8,128)}, f32[4,128,128]{2,1,0:T(8,128)S(1)}, u32[]{:S(2)}, u32[]{:S(2)}) collective-permute-start(f32[4,128,128]{2,1,0:T(8,128)} %bitcast.18), channel_id=1, source_target_pairs={{0,1},{1,2},{2,3},{3,4},{4,5},{5,6},{6,7},{7,8},{8,9},{9,10},{10,1... | collective-permute-start | bytes 786440 | tf_op jit(solution)/shard_map/ppermute | solution.py:20
  109.2 15.8 %collective-permute-start.4 = (f32[4,128,128]{2,1,0:T(8,128)}, f32[4,128,128]{2,1,0:T(8,128)}, u32[]{:S(2)}, u32[]{:S(2)}) collective-permute-start(f32[4,128,128]{2,1,0:T(8,128)} %bitcast.17), channel_id=1, source_target_pairs={{1,0},{2,1},{3,2},{4,3},{5,4},{6,5},{7,6},{8,7},{9,8},{10,9},{11,1... | collective-permute-start | bytes 786440 | tf_op jit(solution)/shard_map/ppermute | solution.py:21
  133.9 19.9 %collective-permute-start.12 = (f32[4,128,128]{2,1,0:T(8,128)S(1)}, f32[4,128,128]{2,1,0:T(8,128)S(1)}, u32[]{:S(2)}, u32[]{:S(2)}) collective-permute-start(f32[4,128,128]{2,1,0:T(8,128)S(1)} %get-tuple-element.56), channel_id=1, source_target_pairs={{1,0},{2,1},{3,2},{4,3},{5,4},{6,5},{7,6},{8,7},{9,8},{10,9},{11,1... | collective-permute-start | bytes 786440 | tf_op jit(solution)/shard_map/ppermute | solution.py:21
  139.1 14.8 %collective-permute-start.13 = (f32[4,128,128]{2,1,0:T(8,128)S(1)}, f32[4,128,128]{2,1,0:T(8,128)S(1)}, u32[]{:S(2)}, u32[]{:S(2)}) collective-permute-start(f32[4,128,128]{2,1,0:T(8,128)S(1)} %get-tuple-element.57), channel_id=1, source_target_pairs={{0,1},{1,2},{2,3},{3,4},{4,5},{5,6},{6,7},{7,8},{8,9},{9,10},{10,1... | collective-permute-start | bytes 786440 | tf_op jit(solution)/shard_map/ppermute | solution.py:20
  142.9 12.1 %copy-start.5 = (f32[131072]{0:T(1024)}, f32[131072]{0:T(1024)S(1)}, u32[]{:S(2)}) copy-start(f32[131072]{0:T(1024)S(1)} %fusion.305) | copy-start | bytes 1572868
  143.8 17.6 %collective-permute-start.7 = (f32[4,128,128]{2,1,0:T(8,128)}, f32[4,128,128]{2,1,0:T(8,128)S(1)}, u32[]{:S(2)}, u32[]{:S(2)}) collective-permute-start(f32[4,128,128]{2,1,0:T(8,128)} %bitcast.23), channel_id=1, source_target_pairs={{0,1},{1,2},{2,3},{3,4},{4,5},{5,6},{6,7},{7,8},{8,9},{9,10},{10,1... | collective-permute-start | bytes 786440 | tf_op jit(solution)/shard_map/ppermute | solution.py:20
  145.7 15.7 %collective-permute-start.6 = (f32[4,128,128]{2,1,0:T(8,128)}, f32[4,128,128]{2,1,0:T(8,128)}, u32[]{:S(2)}, u32[]{:S(2)}) collective-permute-start(f32[4,128,128]{2,1,0:T(8,128)} %bitcast.22), channel_id=1, source_target_pairs={{1,0},{2,1},{3,2},{4,3},{5,4},{6,5},{7,6},{8,7},{9,8},{10,9},{11,1... | collective-permute-start | bytes 786440 | tf_op jit(solution)/shard_map/ppermute | solution.py:21
  161.3 28.8 %copy-start.1 = (f32[131072]{0:T(1024)}, f32[131072]{0:T(1024)S(1)}, u32[]{:S(2)}) copy-start(f32[131072]{0:T(1024)S(1)} %scatter_fusion.2) | copy-start | bytes 1572868
  171.2 18.9 %copy-start.7 = (f32[8,128,128]{2,1,0:T(8,128)S(1)}, f32[8,128,128]{2,1,0:T(8,128)}, u32[]{:S(2)}) copy-start(f32[8,128,128]{2,1,0:T(8,128)} %get-tuple-element.54) | copy-start | bytes 1572868
  172.4 9.2 %collective-permute-start.14 = (f32[4,128,128]{2,1,0:T(8,128)S(1)}, f32[4,128,128]{2,1,0:T(8,128)S(1)}, u32[]{:S(2)}, u32[]{:S(2)}) collective-permute-start(f32[4,128,128]{2,1,0:T(8,128)S(1)} %get-tuple-element.52), channel_id=1, source_target_pairs={{1,0},{2,1},{3,2},{4,3},{5,4},{6,5},{7,6},{8,7},{9,8},{10,9},{11,1... | collective-permute-start | bytes 786440 | tf_op jit(solution)/shard_map/ppermute | solution.py:21
  177.7 12.5 %collective-permute-start.15 = (f32[4,128,128]{2,1,0:T(8,128)S(1)}, f32[4,128,128]{2,1,0:T(8,128)S(1)}, u32[]{:S(2)}, u32[]{:S(2)}) collective-permute-start(f32[4,128,128]{2,1,0:T(8,128)S(1)} %get-tuple-element.53), channel_id=1, source_target_pairs={{0,1},{1,2},{2,3},{3,4},{4,5},{5,6},{6,7},{7,8},{8,9},{9,10},{10,1... | collective-permute-start | bytes 786440 | tf_op jit(solution)/shard_map/ppermute | solution.py:20
  197.6 2.8 %copy-start.2 = (f32[131072]{0:T(1024)}, f32[131072]{0:T(1024)S(1)}, u32[]{:S(2)}) copy-start(f32[131072]{0:T(1024)S(1)} %scatter_fusion.3) | copy-start | bytes 1572868
Sparse Core Ops, SparseCore 0:
  171.4 28.9 reduce-scatter.1
where the time goes:
time: 210 us; the launch traced here: 207 us
  starting transfers between devices  78.6 us (37%)
  other arithmetic  62 us (30%)
  waiting for transfers between devices  36.9 us (18%)
  between operations  16.4 us (8%)
  local copies, waits for them, and re-layouts  13.4 us (6%)
    ppermute x8, starting transfers between devices, extended_2(): after = lax.ppermute(initial, axis, down)  48 us
    scatter-add x7, other arithmetic, inject(): field.reshape(-1).at[flat_index].add(jnp.where(inside, amount, 0.0))  31 us
    ppermute x8, waiting for transfers between devices, extended_2(): before = lax.ppermute(last, axis, up)  18.5 us
    ppermute x8, starting transfers between devices, extended_2(): before = lax.ppermute(last, axis, up)  17.3 us
    add x3, other arithmetic, per_device(): forward_advanced = 2.0 * current - previous + speed_sq * lap_forward  13.8 us
    all_to_all x1, waiting for transfers between devices, per_device(): lax.all_to_all(outgoing, 'dom', split_axis=0, concat_axis=0, tiled=True)  13.7 us
    all_to_all x1, starting transfers between devices, per_device(): lax.all_to_all(outgoing, 'dom', split_axis=0, concat_axis=0, tiled=True)  13.2 us
    mul x1, other arithmetic, per_device(): scaled = speed_sq * present  9.87 us
  transfers between devices with their start and end apart: 18, of which 5 were waited for; matrix products, arithmetic and copies ran while one was open for 20% of the time, Pallas kernels for 0%

commit v1 on v0

v1 whole, which is shorter than its diff:
```python
import functools

import jax
import jax.numpy as jnp
from jax import lax
from jax.experimental import pallas as pl
from jax.experimental.pallas import tpu as pltpu
from jax.sharding import PartitionSpec as P

stencil_coef = (-205.0 / 72.0, 8.0 / 5.0, -1.0 / 5.0, 8.0 / 315.0, -1.0 / 560.0)
grad_scale = 0.0625

DEPTH = 8
HALF = 4
EXT = DEPTH + 2 * HALF
WIDE = DEPTH + 4 * HALF
NX = 128
NY = 128
PAD = 8
CHUNK = 32
bf16 = jnp.bfloat16
f32 = jnp.float32

VM = pl.BlockSpec(memory_space=pltpu.VMEM)
SM = pl.BlockSpec(memory_space=pltpu.SMEM)


def call(kernel, name, ins, outs, scratch, args, flops=0, nbytes=0, limit=40 << 20):
    return pl.pallas_call(
        kernel,
        name=name,
        out_shape=[jax.ShapeDtypeStruct(s, d) for s, d in outs],
        in_specs=ins,
        out_specs=[VM] * len(outs),
        scratch_shapes=scratch,
        compiler_params=pltpu.CompilerParams(vmem_limit_bytes=limit),
        cost_estimate=pl.CostEstimate(flops=flops, bytes_accessed=nbytes, transcendentals=0),
    )(*args)


def buffer():
    return pltpu.VMEM((WIDE, NX + 2 * PAD, NY), f32)


def edge_weights():
    lane = lax.broadcasted_iota(jnp.int32, (CHUNK, NY), 1)
    left = [jnp.where(lane >= k, stencil_coef[k], 0.0) for k in range(1, HALF + 1)]
    right = [jnp.where(lane < NY - k, stencil_coef[k], 0.0) for k in range(1, HALF + 1)]
    return left, right


def zero_pads(buf):
    zeros = jnp.zeros((WIDE, PAD, NY), f32)
    buf[:, 0:PAD, :] = zeros
    buf[:, PAD + NX : PAD + NX + PAD, :] = zeros


def zero_far(buf):
    zeros = jnp.zeros((HALF, NX, NY), f32)
    buf[0:HALF, PAD : PAD + NX, :] = zeros
    buf[WIDE - HALF : WIDE, PAD : PAD + NX, :] = zeros


def lap_chunk(buf, plane, row, weights):
    left, right = weights
    base = PAD + row
    centre = buf[plane, base : base + CHUNK, :]
    total = (3.0 * stencil_coef[0]) * centre
    for k in range(1, HALF + 1):
        near = buf[plane + k, base : base + CHUNK, :] + buf[plane - k, base : base + CHUNK, :]
        near = near + buf[plane, base + k : base + k + CHUNK, :]
        near = near + buf[plane, base - k : base - k + CHUNK, :]
        total = total + stencil_coef[k] * near
        total = total + pltpu.roll(centre, k, 1) * left[k - 1]
        total = total + pltpu.roll(centre, NY - k, 1) * right[k - 1]
    return total


def sweep(buf, first, count, body):
    weights = edge_weights()

    @pl.loop(first, first + count)
    def _(e):
        for row in range(0, NX, CHUNK):
            body(e, row, lap_chunk(buf, e + HALF, row, weights))


def rows(row):
    return slice(row, row + CHUNK)


def padded(row):
    return slice(PAD + row, PAD + row + CHUNK)


def add_cell(ref, plane, row, column, amount):
    lane = lax.broadcasted_iota(jnp.int32, (1, NY), 1)
    old = ref[plane, pl.ds(row, 1), :]
    ref[plane, pl.ds(row, 1), :] = old + jnp.where(lane == column, amount, 0.0)


def parity():
    return lax.rem(lax.axis_index("dom"), 2)


def by_side(par, first, second, body):
    @pl.when(par == 0)
    def _():
        body(second, first)

    @pl.when(par == 1)
    def _():
        body(first, second)


def gather_kernel(slot_ref, parked_ref, out_ref, held):
    pieces = parked_ref.shape[0]
    row = lax.broadcasted_iota(jnp.int32, (pieces, pieces), 0)
    pick = jnp.where(row == slot_ref[...], 1.0, 0.0).astype(bf16)
    for col in range(32):
        part = lax.dot_general(
            pick,
            parked_ref[:, col * NY : (col + 1) * NY],
            (((0,), (0,)), ((), ())),
            preferred_element_type=f32,
        )
        held[pl.ds(col, pieces, stride=32), :] = part
    out_ref[...] = held[...].reshape(pieces, 32, NY).astype(bf16)


def split(value):
    head = value.astype(bf16)
    return head, (value - head.astype(f32)).astype(bf16)


def adjoint_pack_kernel(now_ref, next_ref, speed_ref, first_ref, second_ref):
    par = parity()
    for out_ref, near in ((first_ref, HALF * (1 - par)), (second_ref, HALF * par)):
        far = HALF - near
        close = near + near // 2
        for n, ref in enumerate((now_ref, next_ref, speed_ref)):
            out_ref[pl.ds(HALF * n, HALF)] = ref[pl.ds(near, HALF)].astype(bf16)
            out_ref[pl.ds(4 * HALF + 2 * n, 2)] = split(ref[pl.ds(close, 2)])[1]
        out_ref[pl.ds(3 * HALF, HALF)] = (now_ref[pl.ds(far, HALF)] * speed_ref[pl.ds(far, HALF)]).astype(bf16)


def inject_kernel(depth_ref, row_ref, amount_ref, out_ref, table):
    top = lax.axis_index("dom") * DEPTH - HALF
    count = depth_ref.shape[1]
    steps = amount_ref.shape[0]
    local = depth_ref[...] - top
    place = row_ref[...]
    across = lax.rem(place, NY)
    key = jnp.where((local >= 0) & (local < EXT), local * NX + place // NY, -1)
    lane_id = lax.broadcasted_iota(jnp.int32, (NY, count), 0)
    hit = lane_id == across
    for k in range(steps):
        amount = amount_ref[k : k + 1, :]
        head = amount.astype(bf16).astype(f32)
        table[0, k * NY : (k + 1) * NY, :] = jnp.where(hit, head, 0.0).astype(bf16)
        table[1, k * NY : (k + 1) * NY, :] = jnp.where(hit, amount - head, 0.0).astype(bf16)
    planes = 2
    cell = lax.broadcasted_iota(jnp.int32, (planes * NX, count), 0)

    @pl.loop(0, EXT // planes)
    def _(group):
        pick = jnp.where(cell + group * (planes * NX) == key, 1.0, 0.0).astype(bf16)
        field = lax.dot_general(
            pick, table[0], (((1,), (1,)), ((), ())), preferred_element_type=f32
        ) + lax.dot_general(pick, table[1], (((1,), (1,)), ((), ())), preferred_element_type=f32)
        for k in range(steps):
            for j in range(planes):
                out_ref[k, group * planes + j] = field[j * NX : (j + 1) * NX, k * NY : (k + 1) * NY]


def correction(buf, near_up, scale):
    for p in range(DEPTH):
        for row in range(0, NX, CHUNK):
            total = None
            for k in range(1, HALF + 1):
                q = p - k if p >= HALF else p + k
                if (p >= HALF) == (q >= HALF):
                    continue
                term = stencil_coef[k] * buf[q + 2 * HALF, padded(row), :]
                total = term if total is None else total + term
            if scale is not None:
                total = total * scale[p + HALF, rows(row), :]
            near_up[p, rows(row), :] = total.astype(bf16)


def send_second(par, near, far, first_ref, second_ref):
    for out_ref, at in ((first_ref, HALF * (1 - par)), (second_ref, HALF * par)):
        out_ref[pl.ds(0, HALF)] = near[pl.ds(at, HALF)]
        out_ref[pl.ds(HALF, HALF)] = far[pl.ds(HALF - at, HALF)]


def adjoint_first_kernel(
    now_ref, next_ref, speed_ref, got_a, got_b, inject_ref,
    first_ref, second_ref, lam3_ref, lam2_ref, speed_ext,
    buf4, buf3, now_ext, next_ext, near, far,
):
    par = parity()
    zero_pads(buf4)
    zero_pads(buf3)
    zero_far(buf3)
    own = slice(HALF, HALF + DEPTH)
    now_ext[own] = now_ref[...]
    next_ext[own] = next_ref[...]
    speed_ext[own] = speed_ref[...]
    buf4[2 * HALF : 2 * HALF + DEPTH, PAD : PAD + NX, :] = now_ref[...] * speed_ref[...]

    def halo(lower, upper):
        for ref, at, close, far_at in (
            (lower, 0, 2, 0),
            (upper, HALF + DEPTH, 0, WIDE - HALF),
        ):
            for n, ext in enumerate((now_ext, next_ext, speed_ext)):
                ext[at : at + HALF] = ref[HALF * n : HALF * n + HALF].astype(f32)
                ext[at + close : at + close + 2] = ext[at + close : at + close + 2] + ref[
                    4 * HALF + 2 * n : 4 * HALF + 2 * n + 2
                ].astype(f32)
            buf4[far_at : far_at + HALF, PAD : PAD + NX, :] = ref[3 * HALF : 4 * HALF].astype(f32)
            buf4[at + HALF : at + 2 * HALF, PAD : PAD + NX, :] = (
                now_ext[at : at + HALF] * speed_ext[at : at + HALF]
            )

    by_side(par, got_a, got_b, halo)

    def to_lam3(e, row, lap):
        lam = 2.0 * now_ext[e, rows(row), :] - next_ext[e, rows(row), :] + lap
        lam = lam + inject_ref[0, e, rows(row), :]
        lam3_ref[e, rows(row), :] = lam
        buf3[e + HALF, padded(row), :] = lam * speed_ext[e, rows(row), :]

    sweep(buf4, 0, EXT, to_lam3)

    def to_lam2(e, row, lap):
        lam = 2.0 * lam3_ref[e, rows(row), :] - now_ext[e, rows(row), :] + lap
        lam2_ref[e, rows(row), :] = lam + inject_ref[1, e, rows(row), :]

    sweep(buf3, 0, EXT, to_lam2)
    correction(buf3, near, None)
    far[...] = (lam2_ref[own] * speed_ext[own]).astype(bf16)
    send_second(par, near, far, first_ref, second_ref)


def second_halo(par, got_a, got_b, field, buf, scale):
    def halo(lower, upper):
        for ref, at, far_at in ((lower, 0, 0), (upper, HALF + DEPTH, WIDE - HALF)):
            field[at : at + HALF] = field[at : at + HALF] + ref[0:HALF].astype(f32)
            buf[far_at : far_at + HALF, PAD : PAD + NX, :] = ref[HALF : 2 * HALF].astype(f32)

    by_side(par, got_a, got_b, halo)
    for e in range(EXT):
        value = field[e]
        buf[e + HALF, PAD : PAD + NX, :] = value if scale is None else value * scale[e]


def adjoint_second_kernel(
    lam3_ref, lam2_ref, speed_ext, got_a, got_b, inject_ref, late_ref, early_ref, buf2, buf1, lam2, lam1
):
    par = parity()
    zero_pads(buf2)
    zero_pads(buf1)
    lam2[...] = lam2_ref[...]
    second_halo(par, got_a, got_b, lam2, buf2, speed_ext)

    def to_lam1(e, row, lap):
        lam = 2.0 * lam2[e, rows(row), :] - lam3_ref[e, rows(row), :] + lap
        lam = lam + inject_ref[2, e, rows(row), :]
        lam1[e, rows(row), :] = lam
        buf1[e + HALF, padded(row), :] = lam * speed_ext[e, rows(row), :]

    sweep(buf2, 0, EXT, to_lam1)
    late_ref[...] = lam1[HALF : HALF + DEPTH]

    def to_lam0(e, row, lap):
        lam = 2.0 * lam1[e, rows(row), :] - lam2[e, rows(row), :] + lap
        early_ref[e - HALF, rows(row), :] = lam + inject_ref[3, e, rows(row), :]

    sweep(buf1, HALF, DEPTH, to_lam0)


def forward_pack_kernel(holder_ref, pieces_ref, first_ref, second_ref):
    par = parity()
    per_plane = NX // 32
    for p in range(DEPTH):
        for j in range(per_plane):
            piece = pieces_ref[holder_ref[0, 0, (DEPTH + p) * per_plane + j]]
            first_ref[HALF + p, 32 * j : 32 * j + 32, :] = piece
            second_ref[HALF + p, 32 * j : 32 * j + 32, :] = piece
    at = HALF * (1 - par)
    for p in range(HALF):
        for j in range(per_plane):
            first_ref[p, 32 * j : 32 * j + 32, :] = pieces_ref[holder_ref[0, 0, (at + p) * per_plane + j]]
            second_ref[p, 32 * j : 32 * j + 32, :] = pieces_ref[
                holder_ref[0, 0, (HALF - at + p) * per_plane + j]
            ]


def source_place(depth_ref, row_ref):
    local = depth_ref[0] - (lax.axis_index("dom") * DEPTH - HALF)
    return local, row_ref[0] // NY, lax.rem(row_ref[0], NY)


def forward_first_kernel(
    depth_ref, row_ref, wave_ref, mine_a, mine_b, got_a, got_b, speed_ext, late_ref, lam2_ref,
    first_ref, second_ref, u1_ref, u2_ref, grad_ref,
    buf0, buf1, prev_ext, near, far,
):
    par = parity()
    zero_pads(buf0)
    zero_pads(buf1)
    zero_far(buf1)
    low = HALF + HALF * (1 - par)
    prev_ext[pl.ds(low, HALF)] = mine_a[0:HALF].astype(f32)
    prev_ext[pl.ds(HALF + HALF * par, HALF)] = mine_b[0:HALF].astype(f32)
    buf0[2 * HALF : 2 * HALF + DEPTH, PAD : PAD + NX, :] = mine_a[HALF : HALF + DEPTH].astype(f32)

    def halo(lower, upper):
        for ref, at, wide_at in ((lower, 0, 0), (upper, HALF + DEPTH, 2 * HALF + DEPTH)):
            prev_ext[at : at + HALF] = ref[0:HALF].astype(f32)
            buf0[wide_at : wide_at + DEPTH, PAD : PAD + NX, :] = ref[HALF : HALF + DEPTH].astype(f32)

    by_side(par, got_a, got_b, halo)

    def to_u1(e, row, lap):
        value = 2.0 * buf0[e + HALF, padded(row), :] - prev_ext[e, rows(row), :]
        value = value + speed_ext[e, rows(row), :] * lap
        u1_ref[e, rows(row), :] = value
        buf1[e + HALF, padded(row), :] = value

        @pl.when((e >= HALF) & (e < HALF + DEPTH))
        def _():
            grad_ref[e - HALF, rows(row), :] = lap * late_ref[e - HALF, rows(row), :]

    sweep(buf0, 0, EXT, to_u1)
    local, across, along = source_place(depth_ref, row_ref)
    inside = (local >= 0) & (local < EXT)

    @pl.when(inside)
    def _():
        add_cell(u1_ref, local, across, along, wave_ref[0, 0])
        add_cell(buf1, local + HALF, across + PAD, along, wave_ref[0, 0])

    def to_u2(e, row, lap):
        value = 2.0 * u1_ref[e, rows(row), :] - buf0[e + HALF, padded(row), :]
        u2_ref[e, rows(row), :] = value + speed_ext[e, rows(row), :] * lap

        @pl.when((e >= HALF) & (e < HALF + DEPTH))
        def _():
            grad_ref[e - HALF, rows(row), :] = (
                grad_ref[e - HALF, rows(row), :] + lap * lam2_ref[e, rows(row), :]
            )

    sweep(buf1, 0, EXT, to_u2)

    @pl.when(inside)
    def _():
        add_cell(u2_ref, local, across, along, wave_ref[0, 1])

    correction(buf1, near, speed_ext)
    far[...] = u2_ref[HALF : HALF + DEPTH].astype(bf16)
    send_second(par, near, far, first_ref, second_ref)


def forward_second_kernel(
    depth_ref, row_ref, wave_ref, got_a, got_b, u1_ref, u2_ref, speed_ext, lam3_ref, lam4_ref, grad_ref,
    keep_ref, send_ref, buf2, buf3, u2, total,
):
    par = parity()
    zero_pads(buf2)
    zero_pads(buf3)
    u2[...] = u2_ref[...]
    second_halo(par, got_a, got_b, u2, buf2, None)

    def to_u3(e, row, lap):
        value = 2.0 * u2[e, rows(row), :] - u1_ref[e, rows(row), :]
        buf3[e + HALF, padded(row), :] = value + speed_ext[e, rows(row), :] * lap

        @pl.when((e >= HALF) & (e < HALF + DEPTH))
        def _():
            total[e - HALF, rows(row), :] = (
                grad_ref[e - HALF, rows(row), :] + lap * lam3_ref[e, rows(row), :]
            )

    sweep(buf2, 0, EXT, to_u3)
    local, across, along = source_place(depth_ref, row_ref)

    @pl.when((local >= 0) & (local < EXT))
    def _():
        add_cell(buf3, local + HALF, across + PAD, along, wave_ref[0, 2])

    def to_gradient(e, row, lap):
        value = total[e - HALF, rows(row), :] + lap * lam4_ref[e - HALF, rows(row), :]
        total[e - HALF, rows(row), :] = grad_scale * value

    sweep(buf3, HALF, DEPTH, to_gradient)
    shot = lax.axis_index("shot")
    pair, core = shot // 2, lax.rem(shot, 2)
    for n, half in enumerate((pair, 1 - pair)):
        keep_at = pl.multiple_of((half * 2 + core) * 32, 32)
        send_at = pl.multiple_of((half * 2 + 1 - core) * 32, 32)
        keep_ref[n] = total[:, pl.ds(keep_at, 32), :]
        send_ref[n] = total[:, pl.ds(send_at, 32), :]


def per_device(
    parked, parked_slot, holder_list, speed_sq, adjoint_next, adjoint_now,
    wavelet, src_depth, src_row, rec_depth, rec_row, residuals,
):
    peers = lax.axis_size("dom")
    even = [(i, i ^ 1) for i in range(peers)]
    odd = [(i, ((i + 1) ^ 1) - 1) for i in range(1, peers - 1)]
    swap = lambda a, b: (lax.ppermute(a, "dom", even), lax.ppermute(b, "dom", odd))
    lam4, lam5 = adjoint_now[0], adjoint_next[0]
    ext = ((EXT, NX, NY), f32)
    slab = ((DEPTH, NX, NY), f32)

    def planes(count):
        return ((count, NX, NY), bf16)

    lap_flops = 60 * EXT * NX * NY

    send_a, send_b = call(
        adjoint_pack_kernel, "adjoint_pack", [VM] * 3, [planes(22)] * 2, [], (lam4, lam5, speed_sq),
        nbytes=3 << 20,
    )
    got_a, got_b = swap(send_a, send_b)
    (outgoing,) = call(
        gather_kernel, "gather", [VM, VM], [((64, 32, NY), bf16)], [pltpu.VMEM((64 * 32, NY), f32)],
        (parked_slot[0], parked[0]), nbytes=1 << 20,
    )
    incoming = lax.all_to_all(outgoing, "dom", split_axis=0, concat_axis=0, tiled=True)
    count = rec_depth.shape[0]
    (inject,) = call(
        inject_kernel, "inject", [VM] * 3, [((4, EXT, NX, NY), f32)],
        [pltpu.VMEM((2, 4 * NY, count), bf16)],
        (rec_depth.reshape(1, count), rec_row.reshape(1, count), residuals[0]),
        flops=4 * EXT * NX * count * 4 * NY, nbytes=4 << 20,
    )
    send_a, send_b, lam3, lam2, speed_ext = call(
        adjoint_first_kernel, "adjoint_first", [VM] * 6, [planes(8)] * 2 + [ext] * 3,
        [buffer(), buffer(), pltpu.VMEM(*ext), pltpu.VMEM(*ext), pltpu.VMEM(*planes(8)), pltpu.VMEM(*planes(8))],
        (lam4, lam5, speed_sq, got_a, got_b, inject), flops=2 * lap_flops, nbytes=10 << 20,
    )
    got_a, got_b = swap(send_a, send_b)
    late, early = call(
        adjoint_second_kernel, "adjoint_second", [VM] * 6, [slab] * 2,
        [buffer(), buffer(), pltpu.VMEM(*ext), pltpu.VMEM(*ext)],
        (lam3, lam2, speed_ext, got_a, got_b, inject), flops=2 * lap_flops, nbytes=10 << 20,
    )

    mine_a, mine_b = call(
        forward_pack_kernel, "forward_pack", [SM, VM], [planes(12)] * 2, [], (holder_list, incoming), nbytes=1 << 20
    )
    got_a, got_b = swap(mine_a, mine_b)
    send_a, send_b, u1, u2, grad = call(
        forward_first_kernel, "forward_first", [SM] * 3 + [VM] * 7, [planes(8)] * 2 + [ext] * 2 + [slab],
        [buffer(), buffer(), pltpu.VMEM(*ext), pltpu.VMEM(*planes(8)), pltpu.VMEM(*planes(8))],
        (src_depth, src_row, wavelet, mine_a, mine_b, got_a, got_b, speed_ext, late, lam2),
        flops=2 * lap_flops, nbytes=8 << 20,
    )
    got_a, got_b = swap(send_a, send_b)
    quarter = ((2, DEPTH, NX // 4, NY), f32)
    keep, send = call(
        forward_second_kernel, "forward_second", [SM] * 3 + [VM] * 8, [quarter] * 2,
        [buffer(), buffer(), pltpu.VMEM(*ext), pltpu.VMEM(*slab)],
        (src_depth, src_row, wavelet, got_a, got_b, u1, u2, speed_ext, lam3, lam4, grad),
        flops=2 * lap_flops, nbytes=6 << 20,
    )
    got = lax.ppermute(send, "shot", [(0, 1), (1, 0), (2, 3), (3, 2)])
    other = lax.ppermute(keep[1] + got[1], "shot", [(0, 2), (2, 0), (1, 3), (3, 1)])
    gradient = keep[0] + got[0] + other
    return (gradient, late[None], early[None])


def solution(mesh):
    in_specs = (
        P("shot", "dom", None),
        P("shot", "dom", None),
        P("shot", "dom", None),
        P("dom", None, None),
        P("shot", "dom", None, None),
        P("shot", "dom", None, None),
        P("shot", None),
        P("shot"),
        P("shot"),
        P(),
        P(),
        P("shot", None, None),
    )
    out_specs = (P("dom", "shot", None), P("shot", "dom", None, None), P("shot", "dom", None, None))
    return jax.shard_map(
        per_device, mesh=mesh, in_specs=in_specs, out_specs=out_specs, check_vma=False
    )
```

time: 210 us -> 123 us (0.59); the launches traced: 207 us -> 123 us
  other arithmetic: 62 us -> 0.7 us
  Pallas kernels: 0 us -> 46 us
  starting transfers between devices: 78.6 us -> 39.1 us
  between operations: 16.4 us -> 2.15 us
  waiting for transfers between devices: 36.9 us -> 28.2 us
  local copies, waits for them, and re-layouts: 13.4 us -> 6.54 us
    pallas_call x0 -> x8, Pallas kernels: none -> 46 us  [call(): pl.pallas_call(kernel, name=name, out_shape=[jax.ShapeDtypeStruct(s, d) f...]
    ppermute x16 -> x10, starting transfers between devices: 65.3 us -> 25.9 us  [the longest x4 20.2 us: per_device(): lax.ppermute(b, 'dom', odd)]
    scatter-add x7 -> x0, other arithmetic: 31 us -> none  [inject(): field.reshape(-1).at[flat_index].add(jnp.where(inside, amount, 0.0))]
    add x7 -> x2, other arithmetic: 18.4 us -> 0.7 us  [the longest x1 0.68 us: per_device(): gradient = keep[0] + got[0] + other]
    mul x1 -> x0, other arithmetic: 9.87 us -> none  [per_device(): scaled = speed_sq * present]
    all_to_all x1, waiting for transfers between devices: 13.7 us -> 5.71 us  [per_device(): lax.all_to_all(outgoing, 'dom', split_axis=0, concat_axis=0, tiled=True)]
    slice x11 -> x0, local copies, waits for them, and re-layouts: 5.37 us -> none  [the longest x8 4.64 us: extended_2(): initial = lax.slice_in_dim(value, 0, width, axis=dim)]
    reduce_scatter x1 -> x0, waiting for transfers between devices: 2.82 us -> none  [per_device(): lax.psum_scatter(grad_scale * summed, 'shot', scatter_dimension=1, tiled=...]
  transfers between devices with their start and end apart: 18 -> 11, of which waited for: 5 -> 8; matrix products, arithmetic and copies ran while one was open for 20% -> 0% of each run, Pallas kernels for 0% -> 17%
where the time goes in v1:
time: 123 us
  Pallas kernels  46 us (37%)
  starting transfers between devices  39.1 us (32%)
  waiting for transfers between devices  28.2 us (23%)
  local copies, waits for them, and re-layouts  6.54 us (5%)
  between operations  2.15 us (2%)
    pallas_call x8, Pallas kernels, call(): pl.pallas_call(kernel, name=name, out_shape=[jax.ShapeDtypeStruct(s, d) f...  46 us
    ppermute x4, starting transfers between devices, per_device(): lax.ppermute(b, 'dom', odd)  20.2 us
    all_to_all x1, starting transfers between devices, per_device(): lax.all_to_all(outgoing, 'dom', split_axis=0, concat_axis=0, tiled=True)  13.2 us
    ppermute x4, waiting for transfers between devices, per_device(): lax.ppermute(b, 'dom', odd)  12.4 us
    unnamed x28, local copies, waits for them, and re-layouts  6.54 us
    all_to_all x1, waiting for transfers between devices, per_device(): lax.all_to_all(outgoing, 'dom', split_axis=0, concat_axis=0, tiled=True)  5.71 us
    ppermute x1, waiting for transfers between devices, per_device(): lax.ppermute(keep[1] + got[1], 'shot', [(0, 2), (2, 0), (1, 3), (3, 1)])  4.9 us
    ppermute x4, waiting for transfers between devices, per_device(): lax.ppermute(a, 'dom', even)  3.67 us
  transfers between devices with their start and end apart: 11, of which 8 were waited for; matrix products, arithmetic and copies ran while one was open for 0% of the time, Pallas kernels for 17%

profile of v1, /device:TPU:2, one launch (start us, length us, event | category | flops | bytes accessed | tf_op | source)
XLA Modules:
  0.0 122.7 jit_solution(17932352193494625442)
XLA Ops:
  0.6 0.0 copy-start.7
  0.6 1.0 copy-done.7
  1.7 0.7 copy-done.9
  2.3 1.8 %gather.1 = bf16[64,32,128]{2,1,0:T(8,128)(2,1)} custom-call(s32[1,64]{1,0:T(1,128)S(1)} %bitcast.22, bf16[64,4096]{1,0:T(8,128)(2,1)S(1)} %bitcast.21), custom_call_target="tpu_custom_call" | custom-call | bytes 1048576 | tf_op jit(solution)/shard_map/gather/pallas_call | solution.py:29
  4.1 13.2 %all-to-all-start = ((bf16[64,32,128]{2,1,0:T(8,128)(2,1)}), bf16[64,32,128]{2,1,0:T(8,128)(2,1)S(1)}, u32[]{:S(2)}, u32[]{:S(2)}) async-start(bf16[64,32,128]{2,1,0:T(8,128)(2,1)} %gather.1), calls=%async_computation | async-start | bytes 1048576 | tf_op jit(solution)/shard_map/all_to_all | solution.py:434
  17.3 0.0 copy-start
  17.4 1.0 copy-done
  18.4 1.0 copy-done.2
  19.4 1.0 copy-done.4
  20.5 0.2 adjoint_pack.1
  20.6 1.6 %collective-permute-start.2 = (bf16[22,128,128]{2,1,0:T(8,128)(2,1)S(1)}, bf16[22,128,128]{2,1,0:T(8,128)(2,1)S(1)}, u32[]{:S(2)}, u32[]{:S(2)}) collective-permute-start(bf16[22,128,128]{2,1,0:T(8,128)(2,1)S(1)} %get-tuple-element.23), channel_id=1, source_target_pairs={{0,1},{1,0},{2,3},{3,2},{4,5},{5,4},{6,7},{7,6},{8,9},{9,8},{10,11... | collective-permute-start | bytes 2162696 | tf_op jit(solution)/shard_map/ppermute | solution.py:415
  22.2 6.1 %collective-permute-start.3 = (bf16[22,128,128]{2,1,0:T(8,128)(2,1)S(1)}, bf16[22,128,128]{2,1,0:T(8,128)(2,1)S(1)}, u32[]{:S(2)}, u32[]{:S(2)}) collective-permute-start(bf16[22,128,128]{2,1,0:T(8,128)(2,1)S(1)} %get-tuple-element.24), channel_id=1, source_target_pairs={{1,2},{2,1},{3,4},{4,3},{5,6},{6,5},{7,8},{8,7},{9,10},{10,9},{11,... | collective-permute-start | bytes 2162696 | tf_op jit(solution)/shard_map/ppermute | solution.py:415
  28.3 5.7 %all-to-all-done.pieces_ref = bf16[64,32,128]{2,1,0:T(8,128)(2,1)S(1)} async-done(((bf16[64,32,128]{2,1,0:T(8,128)(2,1)}), bf16[64,32,128]{2,1,0:T(8,128)(2,1)S(1)}, u32[]{:S(2)}, u32[]{:S(2)}) %all-to-all-start) | async-done | bytes 524320 | tf_op jit(solution)/shard_map/all_to_all | solution.py:434
  34.0 0.7 copy-done.10
  34.6 0.7 forward_pack.1
  35.3 1.6 %collective-permute-start = (bf16[12,128,128]{2,1,0:T(8,128)(2,1)S(1)}, bf16[12,128,128]{2,1,0:T(8,128)(2,1)S(1)}, u32[]{:S(2)}, u32[]{:S(2)}) collective-permute-start(bf16[12,128,128]{2,1,0:T(8,128)(2,1)S(1)} %get-tuple-element.21.mine_a), channel_id=1, source_target_pairs={{0,1},{1,0},{2,3},{3,2},{4,5},{5,4},{6,7},{7,6},{8,9},{9,8},{10,11... | collective-permute-start | bytes 1179656 | tf_op jit(solution)/shard_map/ppermute | solution.py:415
  36.9 6.1 %collective-permute-start.1 = (bf16[12,128,128]{2,1,0:T(8,128)(2,1)S(1)}, bf16[12,128,128]{2,1,0:T(8,128)(2,1)S(1)}, u32[]{:S(2)}, u32[]{:S(2)}) collective-permute-start(bf16[12,128,128]{2,1,0:T(8,128)(2,1)S(1)} %get-tuple-element.22.mine_b), channel_id=1, source_target_pairs={{1,2},{2,1},{3,4},{4,3},{5,6},{6,5},{7,8},{8,7},{9,10},{10,9},{11,... | collective-permute-start | bytes 1179656 | tf_op jit(solution)/shard_map/ppermute | solution.py:415
  43.0 0.0 copy-done.11
  43.0 0.0 copy-start.1
  43.0 0.0 copy-start.3
  43.0 0.0 copy-start.5
  43.1 6.3 %inject.1.inject_ref = f32[4,16,128,128]{3,2,1,0:T(8,128)S(1)} custom-call(s32[1,1024]{1,0:T(1,128)S(1)} %bitcast.24, s32[1,1024]{1,0:T(1,128)S(1)} %bitcast.25, f32[4,1024]{1,0:T(4,128)S(1)} %bitcast.23), custom_call_target="tpu_custom_call" | custom-call | flops 4294967296 | bytes 4194304 | tf_op jit(solution)/shard_map/inject/pallas_call | solution.py:29
  49.4 0.0 collective-permute-done.2.got_a
  49.4 0.2 collective-permute-done.3.got_b
  49.6 0.0 copy-done.3
  49.6 7.3 %adjoint_first.1 = (bf16[8,128,128]{2,1,0:T(8,128)(2,1)S(1)}, bf16[8,128,128]{2,1,0:T(8,128)(2,1)S(1)}, f32[16,128,128]{2,1,0:T(8,128)S(1)}, f32[16,128,128]{2,1,0:T(8,128)S(1)}, f32[16,128,128]{2,1,0:T(8,128)S(1)}) custom-call(f32[8,128,128]{2,1,0:T(8,128)S(1)} %bitcast.16, f32[8,128,128]{2,1,0:T(8,128)S(1)} %bitcast.19, f32[8,128,128]{2,1,0:T(8,128)S(1)} %copy-done.5, ...), custom_call_target="tpu_custom_call" | custom-call | flops 31457280 | bytes 10485760 | tf_op jit(solution)/shard_map/adjoint_first/pallas_call | solution.py:29
  56.9 0.0 copy-start.8
  56.9 0.1 collective-permute-start.4
  57.0 4.2 %collective-permute-start.5 = (bf16[8,128,128]{2,1,0:T(8,128)(2,1)S(1)}, bf16[8,128,128]{2,1,0:T(8,128)(2,1)S(1)}, u32[]{:S(2)}, u32[]{:S(2)}) collective-permute-start(bf16[8,128,128]{2,1,0:T(8,128)(2,1)S(1)} %get-tuple-element.29), channel_id=1, source_target_pairs={{1,2},{2,1},{3,4},{4,3},{5,6},{6,5},{7,8},{8,7},{9,10},{10,9},{11,... | collective-permute-start | bytes 786440 | tf_op jit(solution)/shard_map/ppermute | solution.py:415
  62.5 1.2 collective-permute-done.4.got_a
  63.7 6.1 %collective-permute-done.5.got_b = bf16[8,128,128]{2,1,0:T(8,128)(2,1)S(1)} collective-permute-done((bf16[8,128,128]{2,1,0:T(8,128)(2,1)S(1)}, bf16[8,128,128]{2,1,0:T(8,128)(2,1)S(1)}, u32[]{:S(2)}, u32[]{:S(2)}) %collective-permute-start.5) | collective-permute-done | bytes 262176 | tf_op jit(solution)/shard_map/ppermute | solution.py:415
  69.8 6.1 %adjoint_second.1 = (f32[8,128,128]{2,1,0:T(8,128)}, f32[8,128,128]{2,1,0:T(8,128)}) custom-call(f32[16,128,128]{2,1,0:T(8,128)S(1)} %get-tuple-element.26.lam3_ref, f32[16,128,128]{2,1,0:T(8,128)S(1)} %get-tuple-element.27.lam2_ref, f32[16,128,128]{2,1,0:T(8,128)S(1)} %get-tuple-element.25.speed_ext, bf16[8,128,128]{2,1,0:T(8,128)(2,1)S(1)} %collective-permute-done.4.got_a, ...), custom_call_target="tpu_custom_call" | custom-call | flops 31457280 | bytes 10485760 | tf_op jit(solution)/shard_map/adjoint_second/pallas_call | solution.py:29
  75.9 0.0 collective-permute-done.got_a
  75.9 0.0 collective-permute-done.1.got_b
  75.9 0.0 copy-done.8
  75.9 0.0 copy-start.6
  75.9 1.0 copy-done.6
  77.0 14.4 %forward_first.1 = (bf16[8,128,128]{2,1,0:T(8,128)(2,1)S(1)}, bf16[8,128,128]{2,1,0:T(8,128)(2,1)S(1)}, f32[16,128,128]{2,1,0:T(8,128)S(1)}, f32[16,128,128]{2,1,0:T(8,128)S(1)}, f32[8,128,128]{2,1,0:T(8,128)S(1)}) custom-call(s32[1]{0:T(128)S(6)} %copy.15.depth_ref, s32[1]{0:T(128)S(6)} %copy.16.row_ref, f32[1,3]{1,0:T(1,128)S(1)} %copy-done.8, ...), custom_call_target="tpu_custom_call" | custom-call | flops 31457280 | bytes 8388608 | tf_op jit(solution)/shard_map/forward_first/pallas_call | solution.py:29
  91.4 0.1 collective-permute-start.6
  91.5 3.9 %collective-permute-start.7 = (bf16[8,128,128]{2,1,0:T(8,128)(2,1)S(1)}, bf16[8,128,128]{2,1,0:T(8,128)(2,1)S(1)}, u32[]{:S(2)}, u32[]{:S(2)}) collective-permute-start(bf16[8,128,128]{2,1,0:T(8,128)(2,1)S(1)} %get-tuple-element.32), channel_id=1, source_target_pairs={{1,2},{2,1},{3,4},{4,3},{5,6},{6,5},{7,8},{8,7},{9,10},{10,9},{11,... | collective-permute-start | bytes 786440 | tf_op jit(solution)/shard_map/ppermute | solution.py:415
  95.4 2.5 %collective-permute-done.6.got_a = bf16[8,128,128]{2,1,0:T(8,128)(2,1)S(1)} collective-permute-done((bf16[8,128,128]{2,1,0:T(8,128)(2,1)S(1)}, bf16[8,128,128]{2,1,0:T(8,128)(2,1)S(1)}, u32[]{:S(2)}, u32[]{:S(2)}) %collective-permute-start.6) | collective-permute-done | bytes 262176 | tf_op jit(solution)/shard_map/ppermute | solution.py:415
  97.9 6.1 %collective-permute-done.7.got_b = bf16[8,128,128]{2,1,0:T(8,128)(2,1)S(1)} collective-permute-done((bf16[8,128,128]{2,1,0:T(8,128)(2,1)S(1)}, bf16[8,128,128]{2,1,0:T(8,128)(2,1)S(1)}, u32[]{:S(2)}, u32[]{:S(2)}) %collective-permute-start.7) | collective-permute-done | bytes 262176 | tf_op jit(solution)/shard_map/ppermute | solution.py:415
  104.0 9.2 %forward_second.1 = (f32[2,8,32,128]{3,2,1,0:T(8,128)S(1)}, f32[2,8,32,128]{3,2,1,0:T(8,128)S(1)}) custom-call(s32[1]{0:T(128)S(6)} %copy.15.depth_ref, s32[1]{0:T(128)S(6)} %copy.16.row_ref, f32[1,3]{1,0:T(1,128)S(1)} %copy-done.8, bf16[8,128,128]{2,1,0:T(8,128)(2,1)S(1)} %collective-permute-done.6.got_a, ...), custom_call_target="tpu_custom_call" | custom-call | flops 31457280 | bytes 6291456 | tf_op jit(solution)/shard_map/forward_second/pallas_call | solution.py:29
  113.2 0.1 collective-permute-start.8
  113.3 1.5 %collective-permute-done.8 = f32[2,8,32,128]{3,2,1,0:T(8,128)S(1)} collective-permute-done((f32[2,8,32,128]{3,2,1,0:T(8,128)S(1)}, f32[2,8,32,128]{3,2,1,0:T(8,128)S(1)}, u32[]{:S(2)}, u32[]{:S(2)}) %collective-permute-start.8) | collective-permute-done | bytes 262176 | tf_op jit(solution)/shard_map/ppermute | solution.py:472
  114.9 2.2 %collective-permute-start.9 = (f32[8,32,128]{2,1,0:T(8,128)S(1)}, f32[8,32,128]{2,1,0:T(8,128)S(1)}, u32[]{:S(2)}, u32[]{:S(2)}) collective-permute-start(f32[8,32,128]{2,1,0:T(8,128)S(1)} %fusion), channel_id=1, source_target_pairs={{0,128},{128,0},{64,192},{192,64},{1,129},{129,1},{65,193},{193,65... | collective-permute-start | bytes 393224 | tf_op jit(solution)/shard_map/ppermute | solution.py:473
  117.1 4.9 %collective-permute-done.9 = f32[8,32,128]{2,1,0:T(8,128)S(1)} collective-permute-done((f32[8,32,128]{2,1,0:T(8,128)S(1)}, f32[8,32,128]{2,1,0:T(8,128)S(1)}, u32[]{:S(2)}, u32[]{:S(2)}) %collective-permute-start.9) | collective-permute-done | bytes 131104 | tf_op jit(solution)/shard_map/ppermute | solution.py:473
  122.0 0.7 fusion.2
  (12 shorter events, 0.0 us)
Async XLA Ops:
  0.6 1.0 copy-start.7
  1.7 0.7 copy-start.9
  2.3 40.7 %copy-start.11 = (f32[1,4,1024]{2,1,0:T(4,128)S(1)}, f32[1,4,1024]{2,1,0:T(4,128)}, u32[]{:S(2)}) copy-start(f32[1,4,1024]{2,1,0:T(4,128)} %param.23) | copy-start | bytes 49156
  2.3 40.7 %copy-start.12 = (s32[1024]{0:T(1024)S(1)}, s32[1024]{0:T(1024)}, u32[]{:S(2)}) copy-start(s32[1024]{0:T(1024)} %param.21) | copy-start | bytes 12292
  2.3 40.7 %copy-start.13 = (s32[1024]{0:T(1024)S(1)}, s32[1024]{0:T(1024)}, u32[]{:S(2)}) copy-start(s32[1024]{0:T(1024)} %param.22) | copy-start | bytes 12292
  4.1 29.9 %all-to-all-start = ((bf16[64,32,128]{2,1,0:T(8,128)(2,1)}), bf16[64,32,128]{2,1,0:T(8,128)(2,1)S(1)}, u32[]{:S(2)}, u32[]{:S(2)}) async-start(bf16[64,32,128]{2,1,0:T(8,128)(2,1)} %gather.1), calls=%async_computation | async-start | bytes 1048576 | tf_op jit(solution)/shard_map/all_to_all | solution.py:434
  17.3 1.0 copy-start
  18.4 1.0 copy-start.2
  19.4 1.0 copy-start.4
  20.6 28.7 %collective-permute-start.2 = (bf16[22,128,128]{2,1,0:T(8,128)(2,1)S(1)}, bf16[22,128,128]{2,1,0:T(8,128)(2,1)S(1)}, u32[]{:S(2)}, u32[]{:S(2)}) collective-permute-start(bf16[22,128,128]{2,1,0:T(8,128)(2,1)S(1)} %get-tuple-element.23), channel_id=1, source_target_pairs={{0,1},{1,0},{2,3},{3,2},{4,5},{5,4},{6,7},{7,6},{8,9},{9,8},{10,11... | collective-permute-start | bytes 2162696 | tf_op jit(solution)/shard_map/ppermute | solution.py:415
  22.2 27.4 %collective-permute-start.3 = (bf16[22,128,128]{2,1,0:T(8,128)(2,1)S(1)}, bf16[22,128,128]{2,1,0:T(8,128)(2,1)S(1)}, u32[]{:S(2)}, u32[]{:S(2)}) collective-permute-start(bf16[22,128,128]{2,1,0:T(8,128)(2,1)S(1)} %get-tuple-element.24), channel_id=1, source_target_pairs={{1,2},{2,1},{3,4},{4,3},{5,6},{6,5},{7,8},{8,7},{9,10},{10,9},{11,... | collective-permute-start | bytes 2162696 | tf_op jit(solution)/shard_map/ppermute | solution.py:415
  34.0 0.7 copy-start.10
  35.3 40.6 %collective-permute-start = (bf16[12,128,128]{2,1,0:T(8,128)(2,1)S(1)}, bf16[12,128,128]{2,1,0:T(8,128)(2,1)S(1)}, u32[]{:S(2)}, u32[]{:S(2)}) collective-permute-start(bf16[12,128,128]{2,1,0:T(8,128)(2,1)S(1)} %get-tuple-element.21.mine_a), channel_id=1, source_target_pairs={{0,1},{1,0},{2,3},{3,2},{4,5},{5,4},{6,7},{7,6},{8,9},{9,8},{10,11... | collective-permute-start | bytes 1179656 | tf_op jit(solution)/shard_map/ppermute | solution.py:415
  36.9 39.0 %collective-permute-start.1 = (bf16[12,128,128]{2,1,0:T(8,128)(2,1)S(1)}, bf16[12,128,128]{2,1,0:T(8,128)(2,1)S(1)}, u32[]{:S(2)}, u32[]{:S(2)}) collective-permute-start(bf16[12,128,128]{2,1,0:T(8,128)(2,1)S(1)} %get-tuple-element.22.mine_b), channel_id=1, source_target_pairs={{1,2},{2,1},{3,4},{4,3},{5,6},{6,5},{7,8},{8,7},{9,10},{10,9},{11,... | collective-permute-start | bytes 1179656 | tf_op jit(solution)/shard_map/ppermute | solution.py:415
  43.0 6.5 %copy-start.1 = (f32[1,8,128,128]{3,2,1,0:T(8,128)S(1)}, f32[1,8,128,128]{3,2,1,0:T(8,128)}, u32[]{:S(2)}) copy-start(f32[1,8,128,128]{3,2,1,0:T(8,128)} %param.17) | copy-start | bytes 1572868
  43.0 6.5 %copy-start.3 = (f32[1,8,128,128]{3,2,1,0:T(8,128)S(1)}, f32[1,8,128,128]{3,2,1,0:T(8,128)}, u32[]{:S(2)}) copy-start(f32[1,8,128,128]{3,2,1,0:T(8,128)} %param.16) | copy-start | bytes 1572868
  43.0 6.5 %copy-start.5 = (f32[8,128,128]{2,1,0:T(8,128)S(1)}, f32[8,128,128]{2,1,0:T(8,128)}, u32[]{:S(2)}) copy-start(f32[8,128,128]{2,1,0:T(8,128)} %speed_ref.3) | copy-start | bytes 1572868
  56.9 19.1 %copy-start.8 = (f32[1,3]{1,0:T(1,128)S(1)}, f32[1,3]{1,0:T(1,128)}, u32[]{:S(2)}) copy-start(f32[1,3]{1,0:T(1,128)} %wave_ref.3) | copy-start | bytes 40
  56.9 6.8 %collective-permute-start.4 = (bf16[8,128,128]{2,1,0:T(8,128)(2,1)S(1)}, bf16[8,128,128]{2,1,0:T(8,128)(2,1)S(1)}, u32[]{:S(2)}, u32[]{:S(2)}) collective-permute-start(bf16[8,128,128]{2,1,0:T(8,128)(2,1)S(1)} %get-tuple-element.28), channel_id=1, source_target_pairs={{0,1},{1,0},{2,3},{3,2},{4,5},{5,4},{6,7},{7,6},{8,9},{9,8},{10,11... | collective-permute-start | bytes 786440 | tf_op jit(solution)/shard_map/ppermute | solution.py:415
  57.0 12.8 %collective-permute-start.5 = (bf16[8,128,128]{2,1,0:T(8,128)(2,1)S(1)}, bf16[8,128,128]{2,1,0:T(8,128)(2,1)S(1)}, u32[]{:S(2)}, u32[]{:S(2)}) collective-permute-start(bf16[8,128,128]{2,1,0:T(8,128)(2,1)S(1)} %get-tuple-element.29), channel_id=1, source_target_pairs={{1,2},{2,1},{3,4},{4,3},{5,6},{6,5},{7,8},{8,7},{9,10},{10,9},{11,... | collective-permute-start | bytes 786440 | tf_op jit(solution)/shard_map/ppermute | solution.py:415
  75.9 1.0 copy-start.6
  91.4 6.5 %collective-permute-start.6 = (bf16[8,128,128]{2,1,0:T(8,128)(2,1)S(1)}, bf16[8,128,128]{2,1,0:T(8,128)(2,1)S(1)}, u32[]{:S(2)}, u32[]{:S(2)}) collective-permute-start(bf16[8,128,128]{2,1,0:T(8,128)(2,1)S(1)} %get-tuple-element.31), channel_id=1, source_target_pairs={{0,1},{1,0},{2,3},{3,2},{4,5},{5,4},{6,7},{7,6},{8,9},{9,8},{10,11... | collective-permute-start | bytes 786440 | tf_op jit(solution)/shard_map/ppermute | solution.py:415
  91.5 12.5 %collective-permute-start.7 = (bf16[8,128,128]{2,1,0:T(8,128)(2,1)S(1)}, bf16[8,128,128]{2,1,0:T(8,128)(2,1)S(1)}, u32[]{:S(2)}, u32[]{:S(2)}) collective-permute-start(bf16[8,128,128]{2,1,0:T(8,128)(2,1)S(1)} %get-tuple-element.32), channel_id=1, source_target_pairs={{1,2},{2,1},{3,4},{4,3},{5,6},{6,5},{7,8},{8,7},{9,10},{10,9},{11,... | collective-permute-start | bytes 786440 | tf_op jit(solution)/shard_map/ppermute | solution.py:415
  113.2 1.6 %collective-permute-start.8 = (f32[2,8,32,128]{3,2,1,0:T(8,128)S(1)}, f32[2,8,32,128]{3,2,1,0:T(8,128)S(1)}, u32[]{:S(2)}, u32[]{:S(2)}) collective-permute-start(f32[2,8,32,128]{3,2,1,0:T(8,128)S(1)} %get-tuple-element.37), channel_id=1, source_target_pairs={{0,64},{64,0},{128,192},{192,128},{1,65},{65,1},{129,193},{193,129... | collective-permute-start | bytes 786440 | tf_op jit(solution)/shard_map/ppermute | solution.py:472
  114.9 7.1 %collective-permute-start.9 = (f32[8,32,128]{2,1,0:T(8,128)S(1)}, f32[8,32,128]{2,1,0:T(8,128)S(1)}, u32[]{:S(2)}, u32[]{:S(2)}) collective-permute-start(f32[8,32,128]{2,1,0:T(8,128)S(1)} %fusion), channel_id=1, source_target_pairs={{0,128},{128,0},{64,192},{192,64},{1,129},{129,1},{65,193},{193,65... | collective-permute-start | bytes 393224 | tf_op jit(solution)/shard_map/ppermute | solution.py:473

commit v2 on v1

v2 whole, which is shorter than its diff:
```python
import functools

import jax
import jax.numpy as jnp
from jax import lax
from jax.experimental import pallas as pl
from jax.experimental.pallas import tpu as pltpu
from jax.sharding import PartitionSpec as P

stencil_coef = (-205.0 / 72.0, 8.0 / 5.0, -1.0 / 5.0, 8.0 / 315.0, -1.0 / 560.0)
grad_scale = 0.0625

DEPTH = 8
HALF = 4
EXT = DEPTH + 2 * HALF
WIDE = DEPTH + 4 * HALF
NX = 128
NY = 128
PAD = 8
ROWS = NX + 2 * PAD
CHUNK = 32
GROUP = 4
bf16 = jnp.bfloat16
f32 = jnp.float32

VM = pl.BlockSpec(memory_space=pltpu.VMEM)
HB = pl.BlockSpec(memory_space=pltpu.HBM)
SM = pl.BlockSpec(memory_space=pltpu.SMEM)


def call(kernel, name, ins, outs, scratch, args, flops=0, nbytes=0, limit=40 << 20):
    return pl.pallas_call(
        kernel,
        name=name,
        out_shape=[jax.ShapeDtypeStruct(s, d) for s, d in outs],
        in_specs=ins,
        out_specs=[VM] * len(outs),
        scratch_shapes=scratch,
        compiler_params=pltpu.CompilerParams(vmem_limit_bytes=limit),
        cost_estimate=pl.CostEstimate(flops=flops, bytes_accessed=nbytes, transcendentals=0),
    )(*args)


def buffer(planes):
    return pltpu.VMEM((planes, ROWS, NY), f32)


def zero_pads(buf):
    zeros = jnp.zeros((buf.shape[0], PAD, NY), f32)
    buf[:, 0:PAD, :] = zeros
    buf[:, PAD + NX : ROWS, :] = zeros


def band():
    apart = jnp.abs(
        lax.broadcasted_iota(jnp.int32, (NY, NY), 0) - lax.broadcasted_iota(jnp.int32, (NY, NY), 1)
    )
    weights = jnp.zeros((NY, NY), f32)
    for k in range(1, HALF + 1):
        weights = jnp.where(apart == k, 5.0 * stencil_coef[k], weights)
    head = weights.astype(bf16)
    rest = (weights - head.astype(f32)).astype(bf16)
    both = jnp.concatenate([head, rest], axis=1)
    return jnp.concatenate([both, both], axis=0), head


def along(plane, weights):
    both, head = weights
    first = plane.astype(bf16)
    left = plane - first.astype(f32)
    second = left.astype(bf16)
    third = (left - second.astype(f32)).astype(bf16)
    pair = jnp.dot(jnp.concatenate([first, second], axis=1), both, preferred_element_type=f32)
    return 0.2 * (pair[:, :NY] + pair[:, NY:] + jnp.dot(third, head, preferred_element_type=f32))


def rows(row):
    return slice(row, row + CHUNK)


def padded(row):
    return slice(PAD + row, PAD + row + CHUNK)


def group_laps(buf, first, weights, body):
    static = isinstance(first, int)
    parts = [along(buf[first + j, PAD : PAD + NX, :], weights) for j in range(GROUP)]
    for j in range(GROUP):
        at = first + j
        for row in range(0, NX, CHUNK):
            base = PAD + row
            lap = (3.0 * stencil_coef[0]) * buf[at, padded(row), :] + parts[j][row : row + CHUNK]
            for k in range(1, HALF + 1):
                near = buf[at, base + k : base + k + CHUNK, :] + buf[at, base - k : base - k + CHUNK, :]
                for q in (at + k, at - k):
                    if not static or 0 <= q < buf.shape[0]:
                        near = near + buf[q, padded(row), :]
                lap = lap + stencil_coef[k] * near
            body(j, row, lap)


def sweep_own(buf, shift, weights, body):
    @pl.loop(0, DEPTH // GROUP)
    def _(g):
        group_laps(buf, g * GROUP + shift, weights, lambda j, row, lap: body(g * GROUP + j, row, lap))


def sweep_halo(buf, weights, body):
    @pl.loop(0, 2)
    def _(g):
        group_laps(
            buf, HALF + g * (HALF + DEPTH), weights, lambda j, row, lap: body(g * GROUP + j, row, lap)
        )


def sweep_halo_alone(buf, weights, body):
    for g in range(2):
        group_laps(
            buf, g * (HALF + DEPTH), weights, lambda j, row, lap, g=g: body(g * GROUP + j, row, lap)
        )


def ext_of_halo(h):
    return h + DEPTH * (h // HALF) if isinstance(h, int) else jnp.where(h < HALF, h, h + DEPTH)


def add_cell(ref, plane, row, column, amount):
    lane = lax.broadcasted_iota(jnp.int32, (1, NY), 1)
    old = ref[plane, pl.ds(row, 1), :]
    ref[plane, pl.ds(row, 1), :] = old + jnp.where(lane == column, amount, 0.0)


def parity():
    return lax.rem(lax.axis_index("dom"), 2)


def by_side(par, first, second, body):
    @pl.when(par == 0)
    def _():
        body(second, first)

    @pl.when(par == 1)
    def _():
        body(first, second)


def gather_kernel(slot_hbm, parked_hbm, out_ref, held, slot_ref, parked_ref, sems):
    copies = [
        pltpu.make_async_copy(slot_hbm, slot_ref, sems.at[0]),
        pltpu.make_async_copy(parked_hbm, parked_ref, sems.at[1]),
    ]
    for copy in copies:
        copy.start()
    for copy in copies:
        copy.wait()
    pieces = parked_ref.shape[0]
    row = lax.broadcasted_iota(jnp.int32, (pieces, pieces), 0)
    pick = jnp.where(row == slot_ref[...], 1.0, 0.0).astype(bf16)
    for col in range(32):
        part = lax.dot_general(
            pick,
            parked_ref[:, col * NY : (col + 1) * NY],
            (((0,), (0,)), ((), ())),
            preferred_element_type=f32,
        )
        held[pl.ds(col, pieces, stride=32), :] = part
    out_ref[...] = held[...].reshape(pieces, 32, NY).astype(bf16)


def adjoint_pack_kernel(now_hbm, next_hbm, speed_hbm, first_ref, second_ref, now_ref, next_ref, speed_ref, sems):
    fields = (now_ref, next_ref, speed_ref)
    copies = [
        pltpu.make_async_copy(src, dst, sems.at[n])
        for n, (src, dst) in enumerate(zip((now_hbm, next_hbm, speed_hbm), fields))
    ]
    for copy in copies:
        copy.start()
    for copy in copies:
        copy.wait()
    par = parity()
    for out_ref, near in ((first_ref, HALF * (1 - par)), (second_ref, HALF * par)):
        far = HALF - near
        close = near + near // 2
        for n, ref in enumerate(fields):
            out_ref[pl.ds(HALF * n, HALF)] = ref[pl.ds(near, HALF)].astype(bf16)
            value = ref[pl.ds(close, 2)]
            out_ref[pl.ds(4 * HALF + 2 * n, 2)] = (value - value.astype(bf16).astype(f32)).astype(bf16)
        out_ref[pl.ds(3 * HALF, HALF)] = (now_ref[pl.ds(far, HALF)] * speed_ref[pl.ds(far, HALF)]).astype(bf16)


def inject_kernel(depth_ref, row_ref, amount_ref, out_ref, table):
    top = lax.axis_index("dom") * DEPTH - HALF
    count = depth_ref.shape[1]
    steps = amount_ref.shape[0]
    local = depth_ref[...] - top
    place = row_ref[...]
    across = lax.rem(place, NY)
    key = jnp.where((local >= 0) & (local < EXT), local * NX + place // NY, -1)
    lane_id = lax.broadcasted_iota(jnp.int32, (NY, count), 0)
    hit = lane_id == across
    for k in range(steps):
        amount = amount_ref[k : k + 1, :]
        head = amount.astype(bf16).astype(f32)
        table[0, k * NY : (k + 1) * NY, :] = jnp.where(hit, head, 0.0).astype(bf16)
        table[1, k * NY : (k + 1) * NY, :] = jnp.where(hit, amount - head, 0.0).astype(bf16)
    planes = 2
    cell = lax.broadcasted_iota(jnp.int32, (planes * NX, count), 0)

    @pl.loop(0, EXT // planes)
    def _(group):
        pick = jnp.where(cell + group * (planes * NX) == key, 1.0, 0.0).astype(bf16)
        field = lax.dot_general(
            pick, table[0], (((1,), (1,)), ((), ())), preferred_element_type=f32
        ) + lax.dot_general(pick, table[1], (((1,), (1,)), ((), ())), preferred_element_type=f32)
        for k in range(steps):
            for j in range(planes):
                out_ref[k, group * planes + j] = field[j * NX : (j + 1) * NX, k * NY : (k + 1) * NY]


def ordered(kernel):
    def with_mark(depth_ref, row_ref, amount_ref, out_ref, mark_ref, table):
        kernel(depth_ref, row_ref, amount_ref, out_ref, table)
        mark_ref[...] = jnp.zeros(mark_ref.shape, f32)

    return with_mark


def send_second(par, buf, far_ref, speed_ext, scale_far, first_ref, second_ref):
    for p in range(DEPTH):
        out_at = p % HALF
        for row in range(0, NX, CHUNK):
            total = None
            for k in range(1, HALF + 1):
                q = p - k if p >= HALF else p + k
                if (p >= HALF) == (q >= HALF):
                    continue
                term = stencil_coef[k] * buf[q + HALF, padded(row), :]
                total = term if total is None else total + term
            if not scale_far:
                total = total * speed_ext[p + HALF, rows(row), :]
            fresh = far_ref[p, rows(row), :]
            if scale_far:
                fresh = fresh * speed_ext[p + HALF, rows(row), :]
            total = total.astype(bf16)
            fresh = fresh.astype(bf16)
            near_first = par == (0 if p >= HALF else 1)

            @pl.when(near_first)
            def _():
                first_ref[out_at, rows(row), :] = total
                second_ref[HALF + out_at, rows(row), :] = fresh

            @pl.when(jnp.logical_not(near_first))
            def _():
                second_ref[out_at, rows(row), :] = total
                first_ref[HALF + out_at, rows(row), :] = fresh


def adjoint_first_kernel(
    now_ref, next_ref, speed_ref, got_a, got_b, inject_ref,
    first_ref, second_ref, lam3_ref, q3_ref, lam2_ref, base_ref, speed_ext,
    buf4, now_halo, next_halo,
):
    par = parity()
    zero_pads(buf4)
    zero_pads(q3_ref)
    weights = band()
    own = slice(HALF, HALF + DEPTH)
    inner = slice(PAD, PAD + NX)
    speed_ext[own] = speed_ref[...]
    buf4[2 * HALF : 2 * HALF + DEPTH, inner, :] = now_ref[...] * speed_ref[...]

    def halo(lower, upper):
        for ref, at, close, far_at in ((lower, 0, 2, 0), (upper, HALF, 0, WIDE - HALF)):
            ext_at = ext_of_halo(at)
            for n, (held, to) in enumerate(((now_halo, at), (next_halo, at), (speed_ext, ext_at))):
                held[to : to + HALF] = ref[HALF * n : HALF * n + HALF].astype(f32)
                held[to + close : to + close + 2] = held[to + close : to + close + 2] + ref[
                    4 * HALF + 2 * n : 4 * HALF + 2 * n + 2
                ].astype(f32)
            buf4[far_at : far_at + HALF, inner, :] = ref[3 * HALF : 4 * HALF].astype(f32)
            buf4[ext_at + HALF : ext_at + 2 * HALF, inner, :] = (
                now_halo[at : at + HALF] * speed_ext[ext_at : ext_at + HALF]
            )

    by_side(par, got_a, got_b, halo)

    def halo_lam3(h, row, lap):
        e = ext_of_halo(h)
        now = now_halo[h, rows(row), :]
        lam = 2.0 * now - next_halo[h, rows(row), :] + lap + inject_ref[0, e, rows(row), :]
        lam3_ref[e, rows(row), :] = lam
        base_ref[h, rows(row), :] = 2.0 * lam - now + inject_ref[1, e, rows(row), :]
        q3_ref[e, padded(row), :] = lam * speed_ext[e, rows(row), :]

    sweep_halo(buf4, weights, halo_lam3)

    def own_lam3(p, row, lap):
        lam = 2.0 * now_ref[p, rows(row), :] - next_ref[p, rows(row), :] + lap
        lam = lam + inject_ref[0, p + HALF, rows(row), :]
        lam3_ref[p + HALF, rows(row), :] = lam
        q3_ref[p + HALF, padded(row), :] = lam * speed_ext[p + HALF, rows(row), :]

    sweep_own(buf4, 2 * HALF, weights, own_lam3)

    def own_lam2(p, row, lap):
        lam = 2.0 * lam3_ref[p + HALF, rows(row), :] - now_ref[p, rows(row), :] + lap
        lam2_ref[p, rows(row), :] = lam + inject_ref[1, p + HALF, rows(row), :]

    sweep_own(q3_ref, HALF, weights, own_lam2)
    send_second(par, q3_ref, lam2_ref, speed_ext, True, first_ref, second_ref)


def forward_pack_kernel(holder_ref, pieces_ref, order_ref, first_ref, second_ref):
    par = parity()
    per_plane = NX // 32
    for p in range(DEPTH):
        for j in range(per_plane):
            piece = pieces_ref[holder_ref[(DEPTH + p) * per_plane + j]]
            first_ref[HALF + p, 32 * j : 32 * j + 32, :] = piece
            second_ref[HALF + p, 32 * j : 32 * j + 32, :] = piece
    at = HALF * (1 - par)
    for p in range(HALF):
        for j in range(per_plane):
            first_ref[p, 32 * j : 32 * j + 32, :] = pieces_ref[holder_ref[(at + p) * per_plane + j]]
            second_ref[p, 32 * j : 32 * j + 32, :] = pieces_ref[holder_ref[(HALF - at + p) * per_plane + j]]


def source_place(depth_ref, row_ref):
    local = depth_ref[0] - (lax.axis_index("dom") * DEPTH - HALF)
    return local, row_ref[0] // NY, lax.rem(row_ref[0], NY)


def forward_first_kernel(
    depth_ref, row_ref, wave_ref, mine_a, mine_b, got_a, got_b, speed_ext,
    first_ref, second_ref, u1_ref, u2_ref, base_ref, lap0_ref, lap1_ref,
    buf0, prev_ext,
):
    par = parity()
    zero_pads(buf0)
    zero_pads(u1_ref)
    weights = band()
    inner = slice(PAD, PAD + NX)
    prev_ext[pl.ds(HALF + HALF * (1 - par), HALF)] = mine_a[0:HALF].astype(f32)
    prev_ext[pl.ds(HALF + HALF * par, HALF)] = mine_b[0:HALF].astype(f32)
    buf0[2 * HALF : 2 * HALF + DEPTH, inner, :] = mine_a[HALF : HALF + DEPTH].astype(f32)

    def halo(lower, upper):
        for ref, at, wide_at in ((lower, 0, 0), (upper, HALF + DEPTH, 2 * HALF + DEPTH)):
            prev_ext[at : at + HALF] = ref[0:HALF].astype(f32)
            buf0[wide_at : wide_at + DEPTH, inner, :] = ref[HALF : HALF + DEPTH].astype(f32)

    by_side(par, got_a, got_b, halo)

    def step(e, row, lap):
        now = buf0[e + HALF, padded(row), :]
        value = 2.0 * now - prev_ext[e, rows(row), :] + speed_ext[e, rows(row), :] * lap
        u1_ref[e, padded(row), :] = value
        return now

    sweep_halo(buf0, weights, lambda h, row, lap: step(ext_of_halo(h), row, lap))

    def own_u1(p, row, lap):
        step(p + HALF, row, lap)
        lap0_ref[p, rows(row), :] = lap

    sweep_own(buf0, 2 * HALF, weights, own_u1)
    local, across, along_y = source_place(depth_ref, row_ref)

    @pl.when((local >= 0) & (local < EXT))
    def _():
        add_cell(u1_ref, local, across + PAD, along_y, wave_ref[0, 0])

    def own_u2(p, row, lap):
        value = 2.0 * u1_ref[p + HALF, padded(row), :] - buf0[p + 2 * HALF, padded(row), :]
        u2_ref[p, rows(row), :] = value + speed_ext[p + HALF, rows(row), :] * lap
        lap1_ref[p, rows(row), :] = lap

    sweep_own(u1_ref, HALF, weights, own_u2)

    @pl.when((local >= HALF) & (local < HALF + DEPTH))
    def _():
        add_cell(u2_ref, local - HALF, across, along_y, wave_ref[0, 1])

    send_second(par, u1_ref, u2_ref, speed_ext, False, first_ref, second_ref)
    for h in range(2 * HALF):
        e = ext_of_halo(h)
        base_ref[h] = 2.0 * u1_ref[e, inner, :] - buf0[e + HALF, inner, :]


def middle_kernel(
    depth_ref, row_ref, wave_ref, got_a, got_b, inject_ref, lam3_ref, q3_ref, lam2_ref, base_lam_ref, speed_ext,
    u1_ref, base_u_ref, lap0_ref, lap1_ref,
    late_ref, early_ref, u2_ref, grad_ref,
    lam2_halo, lam1, buf2, buf1,
):
    par = parity()
    zero_pads(buf2)
    zero_pads(buf1)
    weights = band()
    inner = slice(PAD, PAD + NX)

    def alone(h, row, lap):
        lam2_halo[h, rows(row), :] = base_lam_ref[h, rows(row), :] + lap

    sweep_halo_alone(q3_ref, weights, alone)

    def halo(lower, upper):
        for ref, at, far_at in ((lower, 0, 0), (upper, HALF, WIDE - HALF)):
            ext_at = ext_of_halo(at)
            value = lam2_halo[at : at + HALF] + ref[0:HALF].astype(f32)
            lam2_halo[at : at + HALF] = value
            buf2[ext_at + HALF : ext_at + 2 * HALF, inner, :] = value * speed_ext[ext_at : ext_at + HALF]
            buf2[far_at : far_at + HALF, inner, :] = ref[HALF : 2 * HALF].astype(f32)

    by_side(par, got_a, got_b, halo)
    buf2[2 * HALF : 2 * HALF + DEPTH, inner, :] = lam2_ref[...] * speed_ext[HALF : HALF + DEPTH]

    def halo_lam1(h, row, lap):
        e = ext_of_halo(h)
        lam = 2.0 * lam2_halo[h, rows(row), :] - lam3_ref[e, rows(row), :] + lap
        lam = lam + inject_ref[2, e, rows(row), :]
        buf1[e, padded(row), :] = lam * speed_ext[e, rows(row), :]

    sweep_halo(buf2, weights, halo_lam1)

    def own_lam1(p, row, lap):
        lam2 = lam2_ref[p, rows(row), :]
        lam = 2.0 * lam2 - lam3_ref[p + HALF, rows(row), :] + lap
        lam = lam + inject_ref[2, p + HALF, rows(row), :]
        late_ref[p, rows(row), :] = lam
        buf1[p + HALF, padded(row), :] = lam * speed_ext[p + HALF, rows(row), :]
        grad_ref[p, rows(row), :] = lam * lap0_ref[p, rows(row), :] + lam2 * lap1_ref[p, rows(row), :]

    sweep_own(buf2, 2 * HALF, weights, own_lam1)

    def own_lam0(p, row, lap):
        lam = 2.0 * late_ref[p, rows(row), :] - lam2_ref[p, rows(row), :] + lap
        early_ref[p, rows(row), :] = lam + inject_ref[3, p + HALF, rows(row), :]

    sweep_own(buf1, HALF, weights, own_lam0)

    def halo_u2(h, row, lap):
        e = ext_of_halo(h)
        u2_ref[h, rows(row), :] = base_u_ref[h, rows(row), :] + speed_ext[e, rows(row), :] * lap

    sweep_halo_alone(u1_ref, weights, halo_u2)
    local, across, along_y = source_place(depth_ref, row_ref)

    @pl.when(((local >= 0) & (local < HALF)) | ((local >= HALF + DEPTH) & (local < EXT)))
    def _():
        add_cell(u2_ref, jnp.where(local < HALF, local, local - DEPTH), across, along_y, wave_ref[0, 1])


def forward_second_kernel(
    depth_ref, row_ref, wave_ref, got_a, got_b, u1_ref, u2_ref, u2_halo_ref, speed_ext, lam3_ref, lam4_ref, grad_ref,
    keep_ref, send_ref, buf2, buf3, total,
):
    par = parity()
    zero_pads(buf2)
    zero_pads(buf3)
    weights = band()
    inner = slice(PAD, PAD + NX)

    def halo(lower, upper):
        for ref, at, far_at in ((lower, 0, 0), (upper, HALF, WIDE - HALF)):
            ext_at = ext_of_halo(at)
            buf2[ext_at + HALF : ext_at + 2 * HALF, inner, :] = u2_halo_ref[at : at + HALF] + ref[0:HALF].astype(f32)
            buf2[far_at : far_at + HALF, inner, :] = ref[HALF : 2 * HALF].astype(f32)

    by_side(par, got_a, got_b, halo)
    buf2[2 * HALF : 2 * HALF + DEPTH, inner, :] = u2_ref[...]

    def step(e, row, lap):
        value = 2.0 * buf2[e + HALF, padded(row), :] - u1_ref[e, padded(row), :]
        buf3[e, padded(row), :] = value + speed_ext[e, rows(row), :] * lap

    sweep_halo(buf2, weights, lambda h, row, lap: step(ext_of_halo(h), row, lap))

    def own_u3(p, row, lap):
        step(p + HALF, row, lap)
        total[p, rows(row), :] = grad_ref[p, rows(row), :] + lap * lam3_ref[p + HALF, rows(row), :]

    sweep_own(buf2, 2 * HALF, weights, own_u3)
    local, across, along_y = source_place(depth_ref, row_ref)

    @pl.when((local >= 0) & (local < EXT))
    def _():
        add_cell(buf3, local, across + PAD, along_y, wave_ref[0, 2])

    def to_gradient(p, row, lap):
        value = total[p, rows(row), :] + lap * lam4_ref[p, rows(row), :]
        total[p, rows(row), :] = grad_scale * value

    sweep_own(buf3, HALF, weights, to_gradient)
    shot = lax.axis_index("shot")
    pair, core = shot // 2, lax.rem(shot, 2)
    for n, half in enumerate((pair, 1 - pair)):
        keep_at = pl.multiple_of((half * 2 + core) * 32, 32)
        send_at = pl.multiple_of((half * 2 + 1 - core) * 32, 32)
        keep_ref[n] = total[:, pl.ds(keep_at, 32), :]
        send_ref[n] = total[:, pl.ds(send_at, 32), :]


def per_device(
    parked, parked_slot, holder_list, speed_sq, adjoint_next, adjoint_now,
    wavelet, src_depth, src_row, rec_depth, rec_row, residuals,
):
    peers = lax.axis_size("dom")
    even = [(i, i ^ 1) for i in range(peers)]
    odd = [(i, ((i + 1) ^ 1) - 1) for i in range(1, peers - 1)]
    swap = lambda a, b: (lax.ppermute(a, "dom", even), lax.ppermute(b, "dom", odd))
    lam4, lam5 = adjoint_now[0], adjoint_next[0]
    ext = ((EXT, NX, NY), f32)
    slab = ((DEPTH, NX, NY), f32)
    wide = ((EXT, ROWS, NY), f32)

    def planes(count):
        return ((count, NX, NY), bf16)

    lap_flops = 60 * EXT * NX * NY

    (outgoing,) = call(
        gather_kernel, "gather", [HB, HB], [((64, 32, NY), bf16)],
        [
            pltpu.VMEM((64 * 32, NY), f32), pltpu.VMEM((1, 64), jnp.int32), pltpu.VMEM((64, 4096), bf16),
            pltpu.SemaphoreType.DMA((2,)),
        ],
        (parked_slot[0], parked[0]), nbytes=1 << 20,
    )
    incoming = lax.all_to_all(outgoing, "dom", split_axis=0, concat_axis=0, tiled=True)
    send_a, send_b = call(
        adjoint_pack_kernel, "adjoint_pack", [HB] * 3, [planes(22)] * 2,
        [pltpu.VMEM(*slab)] * 3 + [pltpu.SemaphoreType.DMA((3,))], (lam4, lam5, speed_sq), nbytes=3 << 20,
    )
    got_a, got_b = swap(send_a, send_b)
    count = rec_depth.shape[0]
    inject, order = call(
        ordered(inject_kernel), "inject", [VM] * 3, [((4, EXT, NX, NY), f32), ((8, NY), f32)],
        [pltpu.VMEM((2, 4 * NY, count), bf16)],
        (rec_depth.reshape(1, count), rec_row.reshape(1, count), residuals[0]),
        flops=4 * EXT * NX * count * 4 * NY, nbytes=4 << 20,
    )
    send_a, send_b, lam3, q3, lam2, base_lam, speed_ext = call(
        adjoint_first_kernel, "adjoint_first", [VM] * 6, [planes(8)] * 2 + [ext, wide, slab, slab, ext],
        [buffer(WIDE), pltpu.VMEM(*slab), pltpu.VMEM(*slab)],
        (lam4, lam5, speed_sq, got_a, got_b, inject), flops=2 * lap_flops, nbytes=10 << 20,
    )
    back_a, back_b = swap(send_a, send_b)

    mine_a, mine_b = call(
        forward_pack_kernel, "forward_pack", [SM, VM, VM], [planes(12)] * 2, [],
        (holder_list.reshape(64), incoming, order), nbytes=1 << 20,
    )
    got_a, got_b = swap(mine_a, mine_b)
    send_a, send_b, u1, u2, base_u, lap0, lap1 = call(
        forward_first_kernel, "forward_first", [SM] * 3 + [VM] * 5,
        [planes(8)] * 2 + [wide, slab, slab, slab, slab],
        [buffer(WIDE), pltpu.VMEM(*ext)],
        (src_depth, src_row, wavelet, mine_a, mine_b, got_a, got_b, speed_ext),
        flops=2 * lap_flops, nbytes=8 << 20,
    )
    got_a, got_b = swap(send_a, send_b)
    late, early, u2_halo, grad = call(
        middle_kernel, "middle", [SM] * 3 + [VM] * 12, [slab] * 4,
        [pltpu.VMEM(*slab), pltpu.VMEM(*slab), buffer(WIDE), buffer(EXT)],
        (
            src_depth, src_row, wavelet, back_a, back_b, inject, lam3, q3, lam2, base_lam, speed_ext,
            u1, base_u, lap0, lap1,
        ),
        flops=3 * lap_flops, nbytes=10 << 20,
    )
    quarter = ((2, DEPTH, NX // 4, NY), f32)
    keep, send = call(
        forward_second_kernel, "forward_second", [SM] * 3 + [VM] * 9, [quarter] * 2,
        [buffer(WIDE), buffer(EXT), pltpu.VMEM(*slab)],
        (src_depth, src_row, wavelet, got_a, got_b, u1, u2, u2_halo, speed_ext, lam3, lam4, grad),
        flops=2 * lap_flops, nbytes=6 << 20,
    )
    got = lax.ppermute(send, "shot", [(0, 1), (1, 0), (2, 3), (3, 2)])
    other = lax.ppermute(keep[1] + got[1], "shot", [(0, 2), (2, 0), (1, 3), (3, 1)])
    gradient = keep[0] + got[0] + other
    return (gradient, late[None], early[None])


def solution(mesh):
    in_specs = (
        P("shot", "dom", None),
        P("shot", "dom", None),
        P("shot", "dom", None),
        P("dom", None, None),
        P("shot", "dom", None, None),
        P("shot", "dom", None, None),
        P("shot", None),
        P("shot"),
        P("shot"),
        P(),
        P(),
        P("shot", None, None),
    )
    out_specs = (P("dom", "shot", None), P("shot", "dom", None, None), P("shot", "dom", None, None))
    return jax.shard_map(
        per_device, mesh=mesh, in_specs=in_specs, out_specs=out_specs, check_vma=False
    )
```

time: 123 us -> 91.1 us (0.74)
  Pallas kernels: 46 us -> 27.6 us
  waiting for transfers between devices: 28.2 us -> 14.1 us
    pallas_call x8, Pallas kernels: 46 us -> 27.6 us  [call(): pl.pallas_call(kernel, name=name, out_shape=[jax.ShapeDtypeStruct(s, d) f...]
    all_to_all x1, waiting for transfers between devices: 5.71 us -> 0.01 us  [per_device(): lax.all_to_all(outgoing, 'dom', split_axis=0, concat_axis=0, tiled=True)]
    ppermute x4, waiting for transfers between devices: 12.4 us -> 7.59 us  [per_device(): lax.ppermute(b, 'dom', odd)]
    ppermute x4, waiting for transfers between devices: 3.67 us -> 0.02 us  [per_device(): lax.ppermute(a, 'dom', even)]
    unnamed x28 -> x26, local copies, waits for them, and re-layouts: 6.54 us -> 6 us
  transfers between devices with their start and end apart: 11 -> 11, of which waited for: 8 -> 3; matrix products, arithmetic and copies ran while one was open for 0% -> 0% of each run, Pallas kernels for 17% -> 24%
where the time goes in v2:
time: 91.1 us; the launch traced here: 90.8 us
  starting transfers between devices  40.2 us (44%)
  Pallas kernels  27.6 us (30%)
  waiting for transfers between devices  14.1 us (15%)
  local copies, waits for them, and re-layouts  6 us (7%)
  between operations  2.21 us (2%)
    pallas_call x8, Pallas kernels, call(): pl.pallas_call(kernel, name=name, out_shape=[jax.ShapeDtypeStruct(s, d) f...  27.6 us
    ppermute x4, starting transfers between devices, per_device(): lax.ppermute(b, 'dom', odd)  21.2 us
    all_to_all x1, starting transfers between devices, per_device(): lax.all_to_all(outgoing, 'dom', split_axis=0, concat_axis=0, tiled=True)  13.2 us
    ppermute x4, waiting for transfers between devices, per_device(): lax.ppermute(b, 'dom', odd)  7.59 us
    unnamed x26, local copies, waits for them, and re-layouts  6 us
    ppermute x1, waiting for transfers between devices, per_device(): lax.ppermute(keep[1] + got[1], 'shot', [(0, 2), (2, 0), (1, 3), (3, 1)])  4.92 us
    ppermute x4, starting transfers between devices, per_device(): lax.ppermute(a, 'dom', even)  3.51 us
    ppermute x1, starting transfers between devices, per_device(): lax.ppermute(keep[1] + got[1], 'shot', [(0, 2), (2, 0), (1, 3), (3, 1)])  2.21 us
  transfers between devices with their start and end apart: 11, of which 3 were waited for; matrix products, arithmetic and copies ran while one was open for 0% of the time, Pallas kernels for 24%

profile of v2, /device:TPU:2, one launch (start us, length us, event | category | flops | bytes accessed | tf_op | source)
XLA Modules:
  0.0 90.8 jit_solution(11438971243582830816)
XLA Ops:
  0.6 0.0 copy-start.3
  0.6 0.0 copy-start.4
  0.7 0.0 copy-start.5
  0.7 0.0 copy-start.6
  0.7 1.1 %copy-done.6 = bf16[1,64,4096]{2,1,0:T(8,128)(2,1)S(1)} copy-done((bf16[1,64,4096]{2,1,0:T(8,128)(2,1)S(1)}, bf16[1,64,4096]{2,1,0:T(8,128)(2,1)}, u32[]{:S(2)}) %copy-start.6) | copy-done | bytes 524312
  1.8 0.7 copy-done.8
  2.5 1.8 %gather.1 = bf16[64,32,128]{2,1,0:T(8,128)(2,1)} custom-call(s32[1,64]{1,0:T(1,128)S(1)} %bitcast.22, bf16[64,4096]{1,0:T(8,128)(2,1)S(1)} %bitcast.21), custom_call_target="tpu_custom_call" | custom-call | bytes 1048576 | tf_op jit(solution)/shard_map/gather/pallas_call | solution.py:32
  4.3 0.0 copy-start.11
  4.3 0.0 copy-start.12
  4.3 13.2 %all-to-all-start = ((bf16[64,32,128]{2,1,0:T(8,128)(2,1)}), bf16[64,32,128]{2,1,0:T(8,128)(2,1)S(1)}, u32[]{:S(2)}, u32[]{:S(2)}) async-start(bf16[64,32,128]{2,1,0:T(8,128)(2,1)} %gather.1), calls=%async_computation | async-start | bytes 1048576 | tf_op jit(solution)/shard_map/all_to_all | solution.py:531
  17.6 0.0 copy-start.10
  17.6 0.0 copy-done.3
  17.6 0.0 copy-done.4
  17.6 0.0 copy-done.5
  17.6 1.4 %adjoint_pack.1 = (bf16[22,128,128]{2,1,0:T(8,128)(2,1)}, bf16[22,128,128]{2,1,0:T(8,128)(2,1)}) custom-call(f32[8,128,128]{2,1,0:T(8,128)S(1)} %bitcast.16, f32[8,128,128]{2,1,0:T(8,128)S(1)} %bitcast.19, f32[8,128,128]{2,1,0:T(8,128)S(1)} %copy-done.5), custom_call_target="tpu_custom_call" | custom-call | bytes 3145728 | tf_op jit(solution)/shard_map/adjoint_pack/pallas_call | solution.py:32
  19.0 1.6 %collective-permute-start.2 = (bf16[22,128,128]{2,1,0:T(8,128)(2,1)}, bf16[22,128,128]{2,1,0:T(8,128)(2,1)S(1)}, u32[]{:S(2)}, u32[]{:S(2)}) collective-permute-start(bf16[22,128,128]{2,1,0:T(8,128)(2,1)} %get-tuple-element.32), channel_id=1, source_target_pairs={{0,1},{1,0},{2,3},{3,2},{4,5},{5,4},{6,7},{7,6},{8,9},{9,8},{10,11... | collective-permute-start | bytes 2162696 | tf_op jit(solution)/shard_map/ppermute | solution.py:512
  20.6 6.1 %collective-permute-start.3 = (bf16[22,128,128]{2,1,0:T(8,128)(2,1)}, bf16[22,128,128]{2,1,0:T(8,128)(2,1)S(1)}, u32[]{:S(2)}, u32[]{:S(2)}) collective-permute-start(bf16[22,128,128]{2,1,0:T(8,128)(2,1)} %get-tuple-element.33), channel_id=1, source_target_pairs={{1,2},{2,1},{3,4},{4,3},{5,6},{6,5},{7,8},{8,7},{9,10},{10,9},{11,... | collective-permute-start | bytes 2162696 | tf_op jit(solution)/shard_map/ppermute | solution.py:512
  26.6 0.0 copy-done.11
  26.7 0.0 copy-start.9
  26.7 6.3 %inject.1 = (f32[4,16,128,128]{3,2,1,0:T(8,128)S(1)}, f32[8,128]{1,0:T(8,128)S(1)}) custom-call(s32[1,1024]{1,0:T(1,128)S(1)} %bitcast.25, s32[1,1024]{1,0:T(1,128)S(1)} %bitcast.26, f32[4,1024]{1,0:T(4,128)S(1)} %bitcast.24), custom_call_target="tpu_custom_call" | custom-call | flops 4294967296 | bytes 4194304 | tf_op jit(solution)/shard_map/inject/pallas_call | solution.py:32
  33.0 2.0 %copy-done = f32[4,16,128,128]{3,2,1,0:T(8,128)} copy-done((f32[4,16,128,128]{3,2,1,0:T(8,128)}, f32[4,16,128,128]{3,2,1,0:T(8,128)S(1)}, u32[]{:S(2)}) %copy-start) | copy-done | bytes 4194328
  35.0 0.0 all-to-all-done.pieces_ref
  35.0 0.0 copy-done.9
  35.0 0.7 forward_pack.1
  35.7 0.8 collective-permute-start
  36.5 6.0 %collective-permute-start.1 = (bf16[12,128,128]{2,1,0:T(8,128)(2,1)S(1)}, bf16[12,128,128]{2,1,0:T(8,128)(2,1)S(1)}, u32[]{:S(2)}, u32[]{:S(2)}) collective-permute-start(bf16[12,128,128]{2,1,0:T(8,128)(2,1)S(1)} %get-tuple-element.31.mine_b), channel_id=1, source_target_pairs={{1,2},{2,1},{3,4},{4,3},{5,6},{6,5},{7,8},{8,7},{9,10},{10,9},{11,... | collective-permute-start | bytes 1179656 | tf_op jit(solution)/shard_map/ppermute | solution.py:512
  42.5 0.0 collective-permute-done.2.got_a
  42.5 7.6 %collective-permute-done.3.got_b = bf16[22,128,128]{2,1,0:T(8,128)(2,1)S(1)} collective-permute-done((bf16[22,128,128]{2,1,0:T(8,128)(2,1)}, bf16[22,128,128]{2,1,0:T(8,128)(2,1)S(1)}, u32[]{:S(2)}, u32[]{:S(2)}) %collective-permute-start.3) | collective-permute-done | bytes 720928 | tf_op jit(solution)/shard_map/ppermute | solution.py:512
  50.1 2.2 %copy-done.1 = f32[4,16,128,128]{3,2,1,0:T(8,128)S(1)} copy-done((f32[4,16,128,128]{3,2,1,0:T(8,128)S(1)}, f32[4,16,128,128]{3,2,1,0:T(8,128)}, u32[]{:S(2)}) %copy-start.1) | copy-done | bytes 4194328
  52.3 3.4 %adjoint_first.1 = (bf16[8,128,128]{2,1,0:T(8,128)(2,1)S(1)}, bf16[8,128,128]{2,1,0:T(8,128)(2,1)S(1)}, f32[16,128,128]{2,1,0:T(8,128)S(1)}, f32[16,144,128]{2,1...) custom-call(f32[8,128,128]{2,1,0:T(8,128)S(1)} %bitcast.17, ...), custom_call_target="tpu_custom_call" | custom-call | flops 31457280 | bytes 10485760 | tf_op jit(solution)/shard_map/adjoint_first/pallas_call | solution.py:32
  55.7 0.1 collective-permute-start.6
  55.8 3.0 %collective-permute-start.7 = (bf16[8,128,128]{2,1,0:T(8,128)(2,1)S(1)}, bf16[8,128,128]{2,1,0:T(8,128)(2,1)S(1)}, u32[]{:S(2)}, u32[]{:S(2)}) collective-permute-start(bf16[8,128,128]{2,1,0:T(8,128)(2,1)S(1)} %get-tuple-element.41), channel_id=1, source_target_pairs={{1,2},{2,1},{3,4},{4,3},{5,6},{6,5},{7,8},{8,7},{9,10},{10,9},{11,... | collective-permute-start | bytes 786440 | tf_op jit(solution)/shard_map/ppermute | solution.py:512
  60.1 0.0 collective-permute-done.got_a
  60.1 0.0 collective-permute-done.1.got_b
  60.2 3.9 %forward_first.1 = (bf16[8,128,128]{2,1,0:T(8,128)(2,1)S(1)}, bf16[8,128,128]{2,1,0:T(8,128)(2,1)S(1)}, f32[16,144,128]{2,1,0:T(8,128)S(1)}, f32[8,128,128]{2,1,...) custom-call(s32[1]{0:T(128)S(6)} %copy.15.depth_ref, ...), custom_call_target="tpu_custom_call" | custom-call | flops 31457280 | bytes 8388608 | tf_op jit(solution)/shard_map/forward_first/pallas_call | solution.py:32
  64.1 1.0 %collective-permute-start.4 = (bf16[8,128,128]{2,1,0:T(8,128)(2,1)S(1)}, bf16[8,128,128]{2,1,0:T(8,128)(2,1)S(1)}, u32[]{:S(2)}, u32[]{:S(2)}) collective-permute-start(bf16[8,128,128]{2,1,0:T(8,128)(2,1)S(1)} %get-tuple-element.36), channel_id=1, source_target_pairs={{0,1},{1,0},{2,3},{3,2},{4,5},{5,4},{6,7},{7,6},{8,9},{9,8},{10,11... | collective-permute-start | bytes 786440 | tf_op jit(solution)/shard_map/ppermute | solution.py:512
  65.1 6.1 %collective-permute-start.5 = (bf16[8,128,128]{2,1,0:T(8,128)(2,1)S(1)}, bf16[8,128,128]{2,1,0:T(8,128)(2,1)S(1)}, u32[]{:S(2)}, u32[]{:S(2)}) collective-permute-start(bf16[8,128,128]{2,1,0:T(8,128)(2,1)S(1)} %get-tuple-element.37), channel_id=1, source_target_pairs={{1,2},{2,1},{3,4},{4,3},{5,6},{6,5},{7,8},{8,7},{9,10},{10,9},{11,... | collective-permute-start | bytes 786440 | tf_op jit(solution)/shard_map/ppermute | solution.py:512
  71.2 0.0 collective-permute-done.6.got_a
  71.2 0.0 collective-permute-done.7.got_b
  71.3 6.5 %middle.1 = (f32[8,128,128]{2,1,0:T(8,128)}, f32[8,128,128]{2,1,0:T(8,128)}, f32[8,128,128]{2,1,0:T(8,128)S(1)}, f32[8,128,128]{2,1,0:T(8,128)S(1)}) custom-call(s32[1]{0:T(128)S(6)} %copy.15.depth_ref, s32[1]{0:T(128)S(6)} %copy.16.row_ref, f32[1,3]{1,0:T(1,128)S(1)} %copy-done.7, bf16[8,128,128]{2,1,0:T(8,128)(2,1)S(1)} %collective-permute-done.6.got_a, ...), custom_call_target="tpu_custom_call" | custom-call | flops 47185920 | bytes 10485760 | tf_op jit(solution)/shard_map/middle/pallas_call | solution.py:32
  77.8 0.0 collective-permute-done.4.got_a
  77.8 0.0 collective-permute-done.5.got_b
  77.8 3.5 %forward_second.1 = (f32[2,8,32,128]{3,2,1,0:T(8,128)S(1)}, f32[2,8,32,128]{3,2,1,0:T(8,128)S(1)}) custom-call(s32[1]{0:T(128)S(6)} %copy.15.depth_ref, s32[1]{0:T(128)S(6)} %copy.16.row_ref, f32[1,3]{1,0:T(1,128)S(1)} %copy-done.7, bf16[8,128,128]{2,1,0:T(8,128)(2,1)S(1)} %collective-permute-done.4.got_a, ...), custom_call_target="tpu_custom_call" | custom-call | flops 31457280 | bytes 6291456 | tf_op jit(solution)/shard_map/forward_second/pallas_call | solution.py:32
  81.3 0.1 collective-permute-start.8
  81.4 1.5 %collective-permute-done.8 = f32[2,8,32,128]{3,2,1,0:T(8,128)S(1)} collective-permute-done((f32[2,8,32,128]{3,2,1,0:T(8,128)S(1)}, f32[2,8,32,128]{3,2,1,0:T(8,128)S(1)}, u32[]{:S(2)}, u32[]{:S(2)}) %collective-permute-start.8) | collective-permute-done | bytes 262176 | tf_op jit(solution)/shard_map/ppermute | solution.py:580
  83.0 2.2 %collective-permute-start.9 = (f32[8,32,128]{2,1,0:T(8,128)S(1)}, f32[8,32,128]{2,1,0:T(8,128)S(1)}, u32[]{:S(2)}, u32[]{:S(2)}) collective-permute-start(f32[8,32,128]{2,1,0:T(8,128)S(1)} %fusion), channel_id=1, source_target_pairs={{0,128},{128,0},{64,192},{192,64},{1,129},{129,1},{65,193},{193,65... | collective-permute-start | bytes 393224 | tf_op jit(solution)/shard_map/ppermute | solution.py:581
  85.2 4.9 %collective-permute-done.9 = f32[8,32,128]{2,1,0:T(8,128)S(1)} collective-permute-done((f32[8,32,128]{2,1,0:T(8,128)S(1)}, f32[8,32,128]{2,1,0:T(8,128)S(1)}, u32[]{:S(2)}, u32[]{:S(2)}) %collective-permute-start.9) | collective-permute-done | bytes 131104 | tf_op jit(solution)/shard_map/ppermute | solution.py:581
  90.1 0.7 fusion.2
  (10 shorter events, 0.0 us)
Async XLA Ops:
  0.6 17.0 %copy-start.3 = (f32[1,8,128,128]{3,2,1,0:T(8,128)S(1)}, f32[1,8,128,128]{3,2,1,0:T(8,128)}, u32[]{:S(2)}) copy-start(f32[1,8,128,128]{3,2,1,0:T(8,128)} %param.17) | copy-start | bytes 1572868
  0.6 17.0 %copy-start.4 = (f32[1,8,128,128]{3,2,1,0:T(8,128)S(1)}, f32[1,8,128,128]{3,2,1,0:T(8,128)}, u32[]{:S(2)}) copy-start(f32[1,8,128,128]{3,2,1,0:T(8,128)} %param.16) | copy-start | bytes 1572868
  0.7 17.0 %copy-start.5 = (f32[8,128,128]{2,1,0:T(8,128)S(1)}, f32[8,128,128]{2,1,0:T(8,128)}, u32[]{:S(2)}) copy-start(f32[8,128,128]{2,1,0:T(8,128)} %speed_ref.1) | copy-start | bytes 1572868
  0.7 1.2 %copy-start.6 = (bf16[1,64,4096]{2,1,0:T(8,128)(2,1)S(1)}, bf16[1,64,4096]{2,1,0:T(8,128)(2,1)}, u32[]{:S(2)}) copy-start(bf16[1,64,4096]{2,1,0:T(8,128)(2,1)} %param.12) | copy-start | bytes 1572868
  1.8 0.7 copy-start.8
  4.3 22.3 %copy-start.11 = (s32[1024]{0:T(1024)S(1)}, s32[1024]{0:T(1024)}, u32[]{:S(2)}) copy-start(s32[1024]{0:T(1024)} %param.21) | copy-start | bytes 12292
  4.3 22.3 %copy-start.12 = (s32[1024]{0:T(1024)S(1)}, s32[1024]{0:T(1024)}, u32[]{:S(2)}) copy-start(s32[1024]{0:T(1024)} %param.22) | copy-start | bytes 12292
  4.3 30.6 %all-to-all-start = ((bf16[64,32,128]{2,1,0:T(8,128)(2,1)}), bf16[64,32,128]{2,1,0:T(8,128)(2,1)S(1)}, u32[]{:S(2)}, u32[]{:S(2)}) async-start(bf16[64,32,128]{2,1,0:T(8,128)(2,1)} %gather.1), calls=%async_computation | async-start | bytes 1048576 | tf_op jit(solution)/shard_map/all_to_all | solution.py:531
  17.6 9.1 %copy-start.10 = (f32[1,4,1024]{2,1,0:T(4,128)S(1)}, f32[1,4,1024]{2,1,0:T(4,128)}, u32[]{:S(2)}) copy-start(f32[1,4,1024]{2,1,0:T(4,128)} %param.23) | copy-start | bytes 49156
  19.0 23.5 %collective-permute-start.2 = (bf16[22,128,128]{2,1,0:T(8,128)(2,1)}, bf16[22,128,128]{2,1,0:T(8,128)(2,1)S(1)}, u32[]{:S(2)}, u32[]{:S(2)}) collective-permute-start(bf16[22,128,128]{2,1,0:T(8,128)(2,1)} %get-tuple-element.32), channel_id=1, source_target_pairs={{0,1},{1,0},{2,3},{3,2},{4,5},{5,4},{6,7},{7,6},{8,9},{9,8},{10,11... | collective-permute-start | bytes 2162696 | tf_op jit(solution)/shard_map/ppermute | solution.py:512
  20.6 29.5 %collective-permute-start.3 = (bf16[22,128,128]{2,1,0:T(8,128)(2,1)}, bf16[22,128,128]{2,1,0:T(8,128)(2,1)S(1)}, u32[]{:S(2)}, u32[]{:S(2)}) collective-permute-start(bf16[22,128,128]{2,1,0:T(8,128)(2,1)} %get-tuple-element.33), channel_id=1, source_target_pairs={{1,2},{2,1},{3,4},{4,3},{5,6},{6,5},{7,8},{8,7},{9,10},{10,9},{11,... | collective-permute-start | bytes 2162696 | tf_op jit(solution)/shard_map/ppermute | solution.py:512
  26.7 8.3 %copy-start.9 = (s32[1,1,64]{2,1,0:T(1,128)S(1)}, s32[1,1,64]{2,1,0:T(1,128)}, u32[]{:S(2)}) copy-start(s32[1,1,64]{2,1,0:T(1,128)} %param.14) | copy-start | bytes 772
  33.0 2.0 %copy-start = (f32[4,16,128,128]{3,2,1,0:T(8,128)}, f32[4,16,128,128]{3,2,1,0:T(8,128)S(1)}, u32[]{:S(2)}) copy-start(f32[4,16,128,128]{3,2,1,0:T(8,128)S(1)} %get-tuple-element.34.inject_ref) | copy-start | bytes 12582916
  35.7 24.5 %collective-permute-start = (bf16[12,128,128]{2,1,0:T(8,128)(2,1)S(1)}, bf16[12,128,128]{2,1,0:T(8,128)(2,1)S(1)}, u32[]{:S(2)}, u32[]{:S(2)}) collective-permute-start(bf16[12,128,128]{2,1,0:T(8,128)(2,1)S(1)} %get-tuple-element.30.mine_a), channel_id=1, source_target_pairs={{0,1},{1,0},{2,3},{3,2},{4,5},{5,4},{6,7},{7,6},{8,9},{9,8},{10,11... | collective-permute-start | bytes 1179656 | tf_op jit(solution)/shard_map/ppermute | solution.py:512
  36.5 23.6 %collective-permute-start.1 = (bf16[12,128,128]{2,1,0:T(8,128)(2,1)S(1)}, bf16[12,128,128]{2,1,0:T(8,128)(2,1)S(1)}, u32[]{:S(2)}, u32[]{:S(2)}) collective-permute-start(bf16[12,128,128]{2,1,0:T(8,128)(2,1)S(1)} %get-tuple-element.31.mine_b), channel_id=1, source_target_pairs={{1,2},{2,1},{3,4},{4,3},{5,6},{6,5},{7,8},{8,7},{9,10},{10,9},{11,... | collective-permute-start | bytes 1179656 | tf_op jit(solution)/shard_map/ppermute | solution.py:512
  50.1 2.2 %copy-start.1 = (f32[4,16,128,128]{3,2,1,0:T(8,128)S(1)}, f32[4,16,128,128]{3,2,1,0:T(8,128)}, u32[]{:S(2)}) copy-start(f32[4,16,128,128]{3,2,1,0:T(8,128)} %copy-done) | copy-start | bytes 12582916
  52.3 7.9 %copy-start.7 = (f32[1,3]{1,0:T(1,128)S(1)}, f32[1,3]{1,0:T(1,128)}, u32[]{:S(2)}) copy-start(f32[1,3]{1,0:T(1,128)} %wave_ref.5) | copy-start | bytes 40
  52.3 19.0 %copy-start.2 = (f32[4,16,128,128]{3,2,1,0:T(8,128)S(1)}, f32[4,16,128,128]{3,2,1,0:T(8,128)}, u32[]{:S(2)}) copy-start(f32[4,16,128,128]{3,2,1,0:T(8,128)} %copy-done) | copy-start | bytes 12582916
  55.7 15.5 %collective-permute-start.6 = (bf16[8,128,128]{2,1,0:T(8,128)(2,1)S(1)}, bf16[8,128,128]{2,1,0:T(8,128)(2,1)S(1)}, u32[]{:S(2)}, u32[]{:S(2)}) collective-permute-start(bf16[8,128,128]{2,1,0:T(8,128)(2,1)S(1)} %get-tuple-element.40), channel_id=1, source_target_pairs={{0,1},{1,0},{2,3},{3,2},{4,5},{5,4},{6,7},{7,6},{8,9},{9,8},{10,11... | collective-permute-start | bytes 786440 | tf_op jit(solution)/shard_map/ppermute | solution.py:512
  55.8 15.4 %collective-permute-start.7 = (bf16[8,128,128]{2,1,0:T(8,128)(2,1)S(1)}, bf16[8,128,128]{2,1,0:T(8,128)(2,1)S(1)}, u32[]{:S(2)}, u32[]{:S(2)}) collective-permute-start(bf16[8,128,128]{2,1,0:T(8,128)(2,1)S(1)} %get-tuple-element.41), channel_id=1, source_target_pairs={{1,2},{2,1},{3,4},{4,3},{5,6},{6,5},{7,8},{8,7},{9,10},{10,9},{11,... | collective-permute-start | bytes 786440 | tf_op jit(solution)/shard_map/ppermute | solution.py:512
  64.1 13.7 %collective-permute-start.4 = (bf16[8,128,128]{2,1,0:T(8,128)(2,1)S(1)}, bf16[8,128,128]{2,1,0:T(8,128)(2,1)S(1)}, u32[]{:S(2)}, u32[]{:S(2)}) collective-permute-start(bf16[8,128,128]{2,1,0:T(8,128)(2,1)S(1)} %get-tuple-element.36), channel_id=1, source_target_pairs={{0,1},{1,0},{2,3},{3,2},{4,5},{5,4},{6,7},{7,6},{8,9},{9,8},{10,11... | collective-permute-start | bytes 786440 | tf_op jit(solution)/shard_map/ppermute | solution.py:512
  65.1 12.7 %collective-permute-start.5 = (bf16[8,128,128]{2,1,0:T(8,128)(2,1)S(1)}, bf16[8,128,128]{2,1,0:T(8,128)(2,1)S(1)}, u32[]{:S(2)}, u32[]{:S(2)}) collective-permute-start(bf16[8,128,128]{2,1,0:T(8,128)(2,1)S(1)} %get-tuple-element.37), channel_id=1, source_target_pairs={{1,2},{2,1},{3,4},{4,3},{5,6},{6,5},{7,8},{8,7},{9,10},{10,9},{11,... | collective-permute-start | bytes 786440 | tf_op jit(solution)/shard_map/ppermute | solution.py:512
  81.3 1.6 %collective-permute-start.8 = (f32[2,8,32,128]{3,2,1,0:T(8,128)S(1)}, f32[2,8,32,128]{3,2,1,0:T(8,128)S(1)}, u32[]{:S(2)}, u32[]{:S(2)}) collective-permute-start(f32[2,8,32,128]{3,2,1,0:T(8,128)S(1)} %get-tuple-element.52), channel_id=1, source_target_pairs={{0,64},{64,0},{128,192},{192,128},{1,65},{65,1},{129,193},{193,129... | collective-permute-start | bytes 786440 | tf_op jit(solution)/shard_map/ppermute | solution.py:580
  83.0 7.1 %collective-permute-start.9 = (f32[8,32,128]{2,1,0:T(8,128)S(1)}, f32[8,32,128]{2,1,0:T(8,128)S(1)}, u32[]{:S(2)}, u32[]{:S(2)}) collective-permute-start(f32[8,32,128]{2,1,0:T(8,128)S(1)} %fusion), channel_id=1, source_target_pairs={{0,128},{128,0},{64,192},{192,64},{1,129},{129,1},{65,193},{193,65... | collective-permute-start | bytes 393224 | tf_op jit(solution)/shard_map/ppermute | solution.py:581

commit v3 on v2

--- a/solution.py
+++ b/solution.py
@@ -24,11 +24,22 @@
 f32 = jnp.float32
 
 VM = pl.BlockSpec(memory_space=pltpu.VMEM)
+SM = pl.BlockSpec(memory_space=pltpu.SMEM)
 HB = pl.BlockSpec(memory_space=pltpu.HBM)
-SM = pl.BlockSpec(memory_space=pltpu.SMEM)
-
-
-def call(kernel, name, ins, outs, scratch, args, flops=0, nbytes=0, limit=40 << 20):
+
+
+def in_hbm(*arrays):
+    return tuple(pltpu.with_memory_space_constraint(a, pltpu.HBM) for a in arrays)
+
+
+def fetch(sources, targets, sems):
+    copies = [pltpu.make_async_copy(src, dst, sems.at[n]) for n, (src, dst) in enumerate(zip(sources, targets))]
+    for copy in copies:
+        copy.start()
+    return copies
+
+
+def call(kernel, name, ins, outs, scratch, args, us=0, limit=20 << 20):
     return pl.pallas_call(
         kernel,
         name=name,
@@ -37,7 +48,7 @@
         out_specs=[VM] * len(outs),
         scratch_shapes=scratch,
         compiler_params=pltpu.CompilerParams(vmem_limit_bytes=limit),
-        cost_estimate=pl.CostEstimate(flops=flops, bytes_accessed=nbytes, transcendentals=0),
+        cost_estimate=pl.CostEstimate(flops=us * 10**9, bytes_accessed=us * 3_600_000, transcendentals=0),
     )(*args)
 
 
@@ -144,15 +155,7 @@
         body(first, second)
 
 
-def gather_kernel(slot_hbm, parked_hbm, out_ref, held, slot_ref, parked_ref, sems):
-    copies = [
-        pltpu.make_async_copy(slot_hbm, slot_ref, sems.at[0]),
-        pltpu.make_async_copy(parked_hbm, parked_ref, sems.at[1]),
-    ]
-    for copy in copies:
-        copy.start()
-    for copy in copies:
-        copy.wait()
+def gather_kernel(slot_ref, parked_ref, order_ref, out_ref, held):
     pieces = parked_ref.shape[0]
     row = lax.broadcasted_iota(jnp.int32, (pieces, pieces), 0)
     pick = jnp.where(row == slot_ref[...], 1.0, 0.0).astype(bf16)
@@ -167,16 +170,11 @@
     out_ref[...] = held[...].reshape(pieces, 32, NY).astype(bf16)
 
 
-def adjoint_pack_kernel(now_hbm, next_hbm, speed_hbm, first_ref, second_ref, now_ref, next_ref, speed_ref, sems):
+def adjoint_pack_kernel(now_hbm, next_hbm, speed_hbm, first_ref, second_ref, mark_ref, now_ref, next_ref, speed_ref, sems):
     fields = (now_ref, next_ref, speed_ref)
-    copies = [
-        pltpu.make_async_copy(src, dst, sems.at[n])
-        for n, (src, dst) in enumerate(zip((now_hbm, next_hbm, speed_hbm), fields))
-    ]
-    for copy in copies:
-        copy.start()
-    for copy in copies:
+    for copy in fetch((now_hbm, next_hbm, speed_hbm), fields, sems):
         copy.wait()
+    mark_ref[...] = jnp.zeros(mark_ref.shape, f32)
     par = parity()
     for out_ref, near in ((first_ref, HALF * (1 - par)), (second_ref, HALF * par)):
         far = HALF - near
@@ -188,87 +186,90 @@
         out_ref[pl.ds(3 * HALF, HALF)] = (now_ref[pl.ds(far, HALF)] * speed_ref[pl.ds(far, HALF)]).astype(bf16)
 
 
-def inject_kernel(depth_ref, row_ref, amount_ref, out_ref, table):
+def inject_fields(depth_ref, row_ref, amount_ref, first_step, out_ref, table, last_on_halo):
     top = lax.axis_index("dom") * DEPTH - HALF
     count = depth_ref.shape[1]
-    steps = amount_ref.shape[0]
+    steps = out_ref.shape[0]
     local = depth_ref[...] - top
     place = row_ref[...]
-    across = lax.rem(place, NY)
     key = jnp.where((local >= 0) & (local < EXT), local * NX + place // NY, -1)
-    lane_id = lax.broadcasted_iota(jnp.int32, (NY, count), 0)
-    hit = lane_id == across
+    hit = lax.broadcasted_iota(jnp.int32, (NY, count), 0) == lax.rem(place, NY)
     for k in range(steps):
-        amount = amount_ref[k : k + 1, :]
+        amount = amount_ref[first_step + k : first_step + k + 1, :]
         head = amount.astype(bf16).astype(f32)
         table[0, k * NY : (k + 1) * NY, :] = jnp.where(hit, head, 0.0).astype(bf16)
         table[1, k * NY : (k + 1) * NY, :] = jnp.where(hit, amount - head, 0.0).astype(bf16)
     planes = 2
     cell = lax.broadcasted_iota(jnp.int32, (planes * NX, count), 0)
 
-    @pl.loop(0, EXT // planes)
-    def _(group):
-        pick = jnp.where(cell + group * (planes * NX) == key, 1.0, 0.0).astype(bf16)
-        field = lax.dot_general(
-            pick, table[0], (((1,), (1,)), ((), ())), preferred_element_type=f32
-        ) + lax.dot_general(pick, table[1], (((1,), (1,)), ((), ())), preferred_element_type=f32)
-        for k in range(steps):
+    def group(g, used):
+        pick = jnp.where(cell + g * (planes * NX) == key, 1.0, 0.0).astype(bf16)
+        field = jnp.zeros((planes * NX, used * NY), f32)
+        for n in range(2):
+            field = field + lax.dot_general(
+                pick, table[n, : used * NY], (((1,), (1,)), ((), ())), preferred_element_type=f32
+            )
+        for k in range(used):
             for j in range(planes):
-                out_ref[k, group * planes + j] = field[j * NX : (j + 1) * NX, k * NY : (k + 1) * NY]
-
-
-def ordered(kernel):
-    def with_mark(depth_ref, row_ref, amount_ref, out_ref, mark_ref, table):
-        kernel(depth_ref, row_ref, amount_ref, out_ref, table)
-        mark_ref[...] = jnp.zeros(mark_ref.shape, f32)
-
-    return with_mark
+                out_ref[k, g * planes + j] = field[j * NX : (j + 1) * NX, k * NY : (k + 1) * NY]
+
+    if last_on_halo:
+
+        @pl.loop(0, EXT // planes)
+        def _(g):
+            group(g, steps)
+    else:
+
+        @pl.loop(0, DEPTH // planes)
+        def _(g):
+            group(g + HALF // planes, steps)
+
+        @pl.loop(0, DEPTH // planes)
+        def _(h):
+            group(jnp.where(h < HALF // planes, h, h + DEPTH // planes), steps - 1)
 
 
 def send_second(par, buf, far_ref, speed_ext, scale_far, first_ref, second_ref):
-    for p in range(DEPTH):
-        out_at = p % HALF
-        for row in range(0, NX, CHUNK):
-            total = None
-            for k in range(1, HALF + 1):
-                q = p - k if p >= HALF else p + k
-                if (p >= HALF) == (q >= HALF):
-                    continue
-                term = stencil_coef[k] * buf[q + HALF, padded(row), :]
-                total = term if total is None else total + term
-            if not scale_far:
-                total = total * speed_ext[p + HALF, rows(row), :]
-            fresh = far_ref[p, rows(row), :]
-            if scale_far:
-                fresh = fresh * speed_ext[p + HALF, rows(row), :]
-            total = total.astype(bf16)
-            fresh = fresh.astype(bf16)
-            near_first = par == (0 if p >= HALF else 1)
-
-            @pl.when(near_first)
-            def _():
-                first_ref[out_at, rows(row), :] = total
-                second_ref[HALF + out_at, rows(row), :] = fresh
-
-            @pl.when(jnp.logical_not(near_first))
-            def _():
-                second_ref[out_at, rows(row), :] = total
-                first_ref[HALF + out_at, rows(row), :] = fresh
+    def emit(lower, upper):
+        for p in range(DEPTH):
+            near_ref, other_ref = (upper, lower) if p >= HALF else (lower, upper)
+            for row in range(0, NX, CHUNK):
+                total = None
+                for k in range(1, HALF + 1):
+                    q = p - k if p >= HALF else p + k
+                    if (p >= HALF) == (q >= HALF):
+                        continue
+                    term = stencil_coef[k] * buf[q + HALF, padded(row), :]
+                    total = term if total is None else total + term
+                fresh = far_ref[p, rows(row), :]
+                if scale_far:
+                    fresh = fresh * speed_ext[p + HALF, rows(row), :]
+                else:
+                    total = total * speed_ext[p + HALF, rows(row), :]
+                near_ref[p % HALF, rows(row), :] = total.astype(bf16)
+                other_ref[HALF + p % HALF, rows(row), :] = fresh.astype(bf16)
+
+    by_side(par, first_ref, second_ref, emit)
 
 
 def adjoint_first_kernel(
-    now_ref, next_ref, speed_ref, got_a, got_b, inject_ref,
-    first_ref, second_ref, lam3_ref, q3_ref, lam2_ref, base_ref, speed_ext,
-    buf4, now_halo, next_halo,
+    depth_ref, row_ref, amount_ref, now_hbm, next_hbm, speed_hbm, got_a_hbm, got_b_hbm,
+    first_ref, second_ref, lam_ref, speed_ext, mark_ref,
+    buf4, q3_ref, now_halo, next_halo, now_ref, next_ref, got_a, got_b, sems, inject_ref, table,
 ):
     par = parity()
+    own = slice(HALF, HALF + DEPTH)
+    copies = fetch(
+        (now_hbm, next_hbm, speed_hbm, got_a_hbm, got_b_hbm), (now_ref, next_ref, speed_ext.at[own], got_a, got_b), sems
+    )
+    inject_fields(depth_ref, row_ref, amount_ref, 0, inject_ref, table, True)
     zero_pads(buf4)
     zero_pads(q3_ref)
     weights = band()
-    own = slice(HALF, HALF + DEPTH)
     inner = slice(PAD, PAD + NX)
-    speed_ext[own] = speed_ref[...]
-    buf4[2 * HALF : 2 * HALF + DEPTH, inner, :] = now_ref[...] * speed_ref[...]
+    for copy in copies:
+        copy.wait()
+    buf4[2 * HALF : 2 * HALF + DEPTH, inner, :] = now_ref[...] * speed_ext[own]
 
     def halo(lower, upper):
         for ref, at, close, far_at in ((lower, 0, 2, 0), (upper, HALF, 0, WIDE - HALF)):
@@ -289,8 +290,8 @@
         e = ext_of_halo(h)
         now = now_halo[h, rows(row), :]
         lam = 2.0 * now - next_halo[h, rows(row), :] + lap + inject_ref[0, e, rows(row), :]
-        lam3_ref[e, rows(row), :] = lam
-        base_ref[h, rows(row), :] = 2.0 * lam - now + inject_ref[1, e, rows(row), :]
+        lam_ref[e, rows(row), :] = lam
+        lam_ref[EXT + DEPTH + h, rows(row), :] = 2.0 * lam - now + inject_ref[1, e, rows(row), :]
         q3_ref[e, padded(row), :] = lam * speed_ext[e, rows(row), :]
 
     sweep_halo(buf4, weights, halo_lam3)
@@ -298,21 +299,23 @@
     def own_lam3(p, row, lap):
         lam = 2.0 * now_ref[p, rows(row), :] - next_ref[p, rows(row), :] + lap
         lam = lam + inject_ref[0, p + HALF, rows(row), :]
-        lam3_ref[p + HALF, rows(row), :] = lam
+        lam_ref[p + HALF, rows(row), :] = lam
         q3_ref[p + HALF, padded(row), :] = lam * speed_ext[p + HALF, rows(row), :]
 
     sweep_own(buf4, 2 * HALF, weights, own_lam3)
 
     def own_lam2(p, row, lap):
-        lam = 2.0 * lam3_ref[p + HALF, rows(row), :] - now_ref[p, rows(row), :] + lap
-        lam2_ref[p, rows(row), :] = lam + inject_ref[1, p + HALF, rows(row), :]
+        lam = 2.0 * lam_ref[p + HALF, rows(row), :] - now_ref[p, rows(row), :] + lap
+        lam_ref[EXT + p, rows(row), :] = lam + inject_ref[1, p + HALF, rows(row), :]
 
     sweep_own(q3_ref, HALF, weights, own_lam2)
-    send_second(par, q3_ref, lam2_ref, speed_ext, True, first_ref, second_ref)
-
-
-def forward_pack_kernel(holder_ref, pieces_ref, order_ref, first_ref, second_ref):
+    send_second(par, q3_ref, lam_ref.at[EXT : EXT + DEPTH], speed_ext, True, first_ref, second_ref)
+    mark_ref[...] = jnp.zeros(mark_ref.shape, f32)
+
+
+def forward_pack_kernel(holder_ref, pieces_ref, order_ref, first_ref, second_ref, mark_ref):
     par = parity()
+    mark_ref[...] = jnp.zeros(mark_ref.shape, f32)
     per_plane = NX // 32
     for p in range(DEPTH):
         for j in range(per_plane):
@@ -332,7 +335,7 @@
 
 
 def forward_first_kernel(
-    depth_ref, row_ref, wave_ref, mine_a, mine_b, got_a, got_b, speed_ext,
+    depth_ref, row_ref, wave_ref, mine_a, mine_b, got_a, got_b, speed_ext, order_ref,
     first_ref, second_ref, u1_ref, u2_ref, base_ref, lap0_ref, lap1_ref,
     buf0, prev_ext,
 ):
@@ -388,22 +391,24 @@
         base_ref[h] = 2.0 * u1_ref[e, inner, :] - buf0[e + HALF, inner, :]
 
 
-def middle_kernel(
-    depth_ref, row_ref, wave_ref, got_a, got_b, inject_ref, lam3_ref, q3_ref, lam2_ref, base_lam_ref, speed_ext,
-    u1_ref, base_u_ref, lap0_ref, lap1_ref,
-    late_ref, early_ref, u2_ref, grad_ref,
-    lam2_halo, lam1, buf2, buf1,
+def adjoint_second_kernel(
+    depth_ref, row_ref, amount_ref, got_a, got_b, lam_ref, speed_ext, order_ref,
+    late_ref, early_ref, mark_ref,
+    lam2_halo, buf2, buf1, inject_ref, table,
 ):
     par = parity()
+    mark_ref[...] = jnp.zeros(mark_ref.shape, f32)
+    inject_fields(depth_ref, row_ref, amount_ref, 2, inject_ref, table, False)
     zero_pads(buf2)
     zero_pads(buf1)
     weights = band()
     inner = slice(PAD, PAD + NX)
+    buf1[:, inner, :] = lam_ref[0:EXT] * speed_ext[...]
 
     def alone(h, row, lap):
-        lam2_halo[h, rows(row), :] = base_lam_ref[h, rows(row), :] + lap
-
-    sweep_halo_alone(q3_ref, weights, alone)
+        lam2_halo[h, rows(row), :] = lam_ref[EXT + DEPTH + h, rows(row), :] + lap
+
+    sweep_halo_alone(buf1, weights, alone)
 
     def halo(lower, upper):
         for ref, at, far_at in ((lower, 0, 0), (upper, HALF, WIDE - HALF)):
@@ -414,35 +419,41 @@
             buf2[far_at : far_at + HALF, inner, :] = ref[HALF : 2 * HALF].astype(f32)
 
     by_side(par, got_a, got_b, halo)
-    buf2[2 * HALF : 2 * HALF + DEPTH, inner, :] = lam2_ref[...] * speed_ext[HALF : HALF + DEPTH]
+    buf2[2 * HALF : 2 * HALF + DEPTH, inner, :] = lam_ref[EXT : EXT + DEPTH] * speed_ext[HALF : HALF + DEPTH]
 
     def halo_lam1(h, row, lap):
         e = ext_of_halo(h)
-        lam = 2.0 * lam2_halo[h, rows(row), :] - lam3_ref[e, rows(row), :] + lap
-        lam = lam + inject_ref[2, e, rows(row), :]
+        lam = 2.0 * lam2_halo[h, rows(row), :] - lam_ref[e, rows(row), :] + lap
+        lam = lam + inject_ref[0, e, rows(row), :]
         buf1[e, padded(row), :] = lam * speed_ext[e, rows(row), :]
 
     sweep_halo(buf2, weights, halo_lam1)
 
     def own_lam1(p, row, lap):
-        lam2 = lam2_ref[p, rows(row), :]
-        lam = 2.0 * lam2 - lam3_ref[p + HALF, rows(row), :] + lap
-        lam = lam + inject_ref[2, p + HALF, rows(row), :]
+        lam = 2.0 * lam_ref[EXT + p, rows(row), :] - lam_ref[p + HALF, rows(row), :] + lap
+        lam = lam + inject_ref[0, p + HALF, rows(row), :]
         late_ref[p, rows(row), :] = lam
         buf1[p + HALF, padded(row), :] = lam * speed_ext[p + HALF, rows(row), :]
-        grad_ref[p, rows(row), :] = lam * lap0_ref[p, rows(row), :] + lam2 * lap1_ref[p, rows(row), :]
 
     sweep_own(buf2, 2 * HALF, weights, own_lam1)
 
     def own_lam0(p, row, lap):
-        lam = 2.0 * late_ref[p, rows(row), :] - lam2_ref[p, rows(row), :] + lap
-        early_ref[p, rows(row), :] = lam + inject_ref[3, p + HALF, rows(row), :]
+        lam = 2.0 * late_ref[p, rows(row), :] - lam_ref[EXT + p, rows(row), :] + lap
+        early_ref[p, rows(row), :] = lam + inject_ref[1, p + HALF, rows(row), :]
 
     sweep_own(buf1, HALF, weights, own_lam0)
+
+
+def middle_kernel(
+    depth_ref, row_ref, wave_ref, lam_ref, late_ref, speed_ext, u1_ref, base_ref, lap0_ref, lap1_ref,
+    u2_ref, grad_ref,
+):
+    weights = band()
+    grad_ref[...] = late_ref[...] * lap0_ref[...] + lam_ref[EXT : EXT + DEPTH] * lap1_ref[...]
 
     def halo_u2(h, row, lap):
         e = ext_of_halo(h)
-        u2_ref[h, rows(row), :] = base_u_ref[h, rows(row), :] + speed_ext[e, rows(row), :] * lap
+        u2_ref[h, rows(row), :] = base_ref[h, rows(row), :] + speed_ext[e, rows(row), :] * lap
 
     sweep_halo_alone(u1_ref, weights, halo_u2)
     local, across, along_y = source_place(depth_ref, row_ref)
@@ -518,64 +529,58 @@
     def planes(count):
         return ((count, NX, NY), bf16)
 
-    lap_flops = 60 * EXT * NX * NY
-
+    mark = ((8, NY), f32)
+    lam23_shape = (EXT + 2 * DEPTH, NX, NY)
+    send_a, send_b, order = call(
+        adjoint_pack_kernel, "adjoint_pack", [HB] * 3, [planes(22)] * 2 + [mark],
+        [pltpu.VMEM(*slab)] * 3 + [pltpu.SemaphoreType.DMA((3,))], in_hbm(lam4, lam5, speed_sq),
+    )
+    got_a, got_b = swap(send_a, send_b)
     (outgoing,) = call(
-        gather_kernel, "gather", [HB, HB], [((64, 32, NY), bf16)],
-        [
-            pltpu.VMEM((64 * 32, NY), f32), pltpu.VMEM((1, 64), jnp.int32), pltpu.VMEM((64, 4096), bf16),
-            pltpu.SemaphoreType.DMA((2,)),
-        ],
-        (parked_slot[0], parked[0]), nbytes=1 << 20,
+        gather_kernel, "gather", [VM] * 3, [((64, 32, NY), bf16)], [pltpu.VMEM((64 * 32, NY), f32)],
+        (parked_slot[0], parked[0], order),
     )
     incoming = lax.all_to_all(outgoing, "dom", split_axis=0, concat_axis=0, tiled=True)
-    send_a, send_b = call(
-        adjoint_pack_kernel, "adjoint_pack", [HB] * 3, [planes(22)] * 2,
-        [pltpu.VMEM(*slab)] * 3 + [pltpu.SemaphoreType.DMA((3,))], (lam4, lam5, speed_sq), nbytes=3 << 20,
-    )
-    got_a, got_b = swap(send_a, send_b)
     count = rec_depth.shape[0]
-    inject, order = call(
-        ordered(inject_kernel), "inject", [VM] * 3, [((4, EXT, NX, NY), f32), ((8, NY), f32)],
-        [pltpu.VMEM((2, 4 * NY, count), bf16)],
-        (rec_depth.reshape(1, count), rec_row.reshape(1, count), residuals[0]),
-        flops=4 * EXT * NX * count * 4 * NY, nbytes=4 << 20,
-    )
-    send_a, send_b, lam3, q3, lam2, base_lam, speed_ext = call(
-        adjoint_first_kernel, "adjoint_first", [VM] * 6, [planes(8)] * 2 + [ext, wide, slab, slab, ext],
-        [buffer(WIDE), pltpu.VMEM(*slab), pltpu.VMEM(*slab)],
-        (lam4, lam5, speed_sq, got_a, got_b, inject), flops=2 * lap_flops, nbytes=10 << 20,
+    receivers = (rec_depth.reshape(1, count), rec_row.reshape(1, count), residuals[0])
+    fields = [pltpu.VMEM((2, EXT, NX, NY), f32), pltpu.VMEM((2, 2 * NY, count), bf16)]
+    send_a, send_b, lam23, speed_ext, order = call(
+        adjoint_first_kernel, "adjoint_first", [VM] * 3 + [HB] * 5, [planes(8)] * 2 + [(lam23_shape, f32), ext, mark],
+        [buffer(WIDE), buffer(EXT)] + [pltpu.VMEM(*slab)] * 4 + [pltpu.VMEM(*planes(22))] * 2
+        + [pltpu.SemaphoreType.DMA((5,))] + fields,
+        receivers + in_hbm(lam4, lam5, speed_sq, got_a, got_b), us=4,
     )
     back_a, back_b = swap(send_a, send_b)
 
-    mine_a, mine_b = call(
-        forward_pack_kernel, "forward_pack", [SM, VM, VM], [planes(12)] * 2, [],
-        (holder_list.reshape(64), incoming, order), nbytes=1 << 20,
+    mine_a, mine_b, order = call(
+        forward_pack_kernel, "forward_pack", [SM, VM, VM], [planes(12)] * 2 + [mark], [],
+        (holder_list.reshape(64), incoming, order), us=4,
     )
     got_a, got_b = swap(mine_a, mine_b)
+    late, early, order = call(
+        adjoint_second_kernel, "adjoint_second", [VM] * 8, [slab] * 2 + [mark],
+        [pltpu.VMEM(*slab), buffer(WIDE), buffer(EXT)] + fields,
+        receivers + (back_a, back_b, lam23, speed_ext, order), us=4,
+    )
     send_a, send_b, u1, u2, base_u, lap0, lap1 = call(
-        forward_first_kernel, "forward_first", [SM] * 3 + [VM] * 5,
+        forward_first_kernel, "forward_first", [SM] * 3 + [VM] * 6,
         [planes(8)] * 2 + [wide, slab, slab, slab, slab],
         [buffer(WIDE), pltpu.VMEM(*ext)],
-        (src_depth, src_row, wavelet, mine_a, mine_b, got_a, got_b, speed_ext),
-        flops=2 * lap_flops, nbytes=8 << 20,
+        (src_depth, src_row, wavelet, mine_a, mine_b, got_a, got_b, speed_ext, order),
+        us=4,
     )
     got_a, got_b = swap(send_a, send_b)
-    late, early, u2_halo, grad = call(
-        middle_kernel, "middle", [SM] * 3 + [VM] * 12, [slab] * 4,
-        [pltpu.VMEM(*slab), pltpu.VMEM(*slab), buffer(WIDE), buffer(EXT)],
-        (
-            src_depth, src_row, wavelet, back_a, back_b, inject, lam3, q3, lam2, base_lam, speed_ext,
-            u1, base_u, lap0, lap1,
-        ),
-        flops=3 * lap_flops, nbytes=10 << 20,
+    u2_halo, grad = call(
+        middle_kernel, "middle", [SM] * 3 + [VM] * 7, [slab] * 2, [],
+        (src_depth, src_row, wavelet, lam23, late, speed_ext, u1, base_u, lap0, lap1),
+        us=0,
     )
     quarter = ((2, DEPTH, NX // 4, NY), f32)
     keep, send = call(
         forward_second_kernel, "forward_second", [SM] * 3 + [VM] * 9, [quarter] * 2,
         [buffer(WIDE), buffer(EXT), pltpu.VMEM(*slab)],
-        (src_depth, src_row, wavelet, got_a, got_b, u1, u2, u2_halo, speed_ext, lam3, lam4, grad),
-        flops=2 * lap_flops, nbytes=6 << 20,
+        (src_depth, src_row, wavelet, got_a, got_b, u1, u2, u2_halo, speed_ext, lam23, lam4, grad),
+        us=0,
     )
     got = lax.ppermute(send, "shot", [(0, 1), (1, 0), (2, 3), (3, 2)])
     other = lax.ppermute(keep[1] + got[1], "shot", [(0, 2), (2, 0), (1, 3), (3, 1)])

time: 91.1 us -> 101 us (1.11)
  waiting for transfers between devices: 14.1 us -> 22.2 us
  local copies, waits for them, and re-layouts: 6 us -> 2.62 us
  Pallas kernels: 27.6 us -> 30.3 us
  starting transfers between devices: 40.2 us -> 42 us
    ppermute x4, starting transfers between devices: 21.2 us -> 30.6 us  [per_device(): lax.ppermute(b, 'dom', odd)]
    ppermute x4, waiting for transfers between devices: 7.59 us -> 16.5 us  [per_device(): lax.ppermute(b, 'dom', odd)]
    all_to_all x1, starting transfers between devices: 13.2 us -> 6.45 us  [per_device(): lax.all_to_all(outgoing, 'dom', split_axis=0, concat_axis=0, tiled=True)]
    unnamed x26 -> x22, local copies, waits for them, and re-layouts: 6 us -> 2.62 us
    pallas_call x8, Pallas kernels: 27.6 us -> 30.3 us  [call(): pl.pallas_call(kernel, name=name, out_shape=[jax.ShapeDtypeStruct(s, d) f...]
    ppermute x4, starting transfers between devices: 3.51 us -> 1.94 us  [per_device(): lax.ppermute(a, 'dom', even)]
  transfers between devices with their start and end apart: 11 -> 11, of which waited for: 3 -> 5; matrix products, arithmetic and copies ran while one was open for 0% -> 0% of each run, Pallas kernels for 24% -> 21%
where the time goes in v3:
time: 101 us; the launch traced here: 100 us
  starting transfers between devices  42 us (42%)
  Pallas kernels  30.3 us (30%)
  waiting for transfers between devices  22.2 us (22%)
  local copies, waits for them, and re-layouts  2.62 us (3%)
  between operations  2.17 us (2%)
    ppermute x4, starting transfers between devices, per_device(): lax.ppermute(b, 'dom', odd)  30.6 us
    pallas_call x8, Pallas kernels, call(): pl.pallas_call(kernel, name=name, out_shape=[jax.ShapeDtypeStruct(s, d) f...  30.3 us
    ppermute x4, waiting for transfers between devices, per_device(): lax.ppermute(b, 'dom', odd)  16.5 us
    all_to_all x1, starting transfers between devices, per_device(): lax.all_to_all(outgoing, 'dom', split_axis=0, concat_axis=0, tiled=True)  6.45 us
    ppermute x1, waiting for transfers between devices, per_device(): lax.ppermute(keep[1] + got[1], 'shot', [(0, 2), (2, 0), (1, 3), (3, 1)])  4.22 us
    ppermute x1, starting transfers between devices, per_device(): lax.ppermute(keep[1] + got[1], 'shot', [(0, 2), (2, 0), (1, 3), (3, 1)])  2.9 us
    unnamed x22, local copies, waits for them, and re-layouts  2.62 us
  transfers between devices with their start and end apart: 11, of which 5 were waited for; matrix products, arithmetic and copies ran while one was open for 0% of the time, Pallas kernels for 21%

profile of v3, /device:TPU:2, one launch (start us, length us, event | category | flops | bytes accessed | tf_op | source)
XLA Modules:
  0.0 100.0 jit_solution(5438053186373405175)
XLA Ops:
  0.6 0.0 copy-start.5
  0.6 0.0 copy-start.7
  0.7 0.0 copy-start.6
  0.7 1.6 %adjoint_pack.1 = (bf16[22,128,128]{2,1,0:T(8,128)(2,1)S(1)}, bf16[22,128,128]{2,1,0:T(8,128)(2,1)S(1)}, f32[8,128]{1,0:T(8,128)S(1)}) custom-call(f32[8,128,128]{2,1,0:T(8,128)} %bitcast.16, f32[8,128,128]{2,1,0:T(8,128)} %bitcast.29, f32[8,128,128]{2,1,0:T(8,128)} %speed_hbm.3), custom_call_target="tpu_custom_call" | custom-call | tf_op jit(solution)/shard_map/adjoint_pack/pallas_call | solution.py:43
  2.2 1.7 %collective-permute-start = (bf16[22,128,128]{2,1,0:T(8,128)(2,1)S(1)}, bf16[22,128,128]{2,1,0:T(8,128)(2,1)S(1)}, u32[]{:S(2)}, u32[]{:S(2)}) collective-permute-start(bf16[22,128,128]{2,1,0:T(8,128)(2,1)S(1)} %get-tuple-element.29), channel_id=1, source_target_pairs={{0,1},{1,0},{2,3},{3,2},{4,5},{5,4},{6,7},{7,6},{8,9},{9,8},{10,11... | collective-permute-start | bytes 2162696 | tf_op jit(solution)/shard_map/ppermute | solution.py:523
  3.9 9.3 %collective-permute-start.1 = (bf16[22,128,128]{2,1,0:T(8,128)(2,1)S(1)}, bf16[22,128,128]{2,1,0:T(8,128)(2,1)S(1)}, u32[]{:S(2)}, u32[]{:S(2)}) collective-permute-start(bf16[22,128,128]{2,1,0:T(8,128)(2,1)S(1)} %get-tuple-element.30), channel_id=1, source_target_pairs={{1,2},{2,1},{3,4},{4,3},{5,6},{6,5},{7,8},{8,7},{9,10},{10,9},{11,... | collective-permute-start | bytes 2162696 | tf_op jit(solution)/shard_map/ppermute | solution.py:523
  13.3 0.0 copy-start.1
  13.3 1.0 %copy-done.1 = bf16[1,64,4096]{2,1,0:T(8,128)(2,1)S(1)} copy-done((bf16[1,64,4096]{2,1,0:T(8,128)(2,1)S(1)}, bf16[1,64,4096]{2,1,0:T(8,128)(2,1)}, u32[]{:S(2)}) %copy-start.1) | copy-done | bytes 524312
  14.3 0.7 copy-done.4
  15.0 1.8 %gather.1 = bf16[64,32,128]{2,1,0:T(8,128)(2,1)} custom-call(s32[1,64]{1,0:T(1,128)S(1)} %bitcast.21, bf16[64,4096]{1,0:T(8,128)(2,1)S(1)} %bitcast.19, f32[8,128]{1,0:T(8,128)S(1)} %get-tuple-element.28.order_ref), custom_call_target="tpu_custom_call" | custom-call | tf_op jit(solution)/shard_map/gather/pallas_call | solution.py:43
  16.7 6.5 %all-to-all-start = ((bf16[64,32,128]{2,1,0:T(8,128)(2,1)}), bf16[64,32,128]{2,1,0:T(8,128)(2,1)}, u32[]{:S(2)}, u32[]{:S(2)}) async-start(bf16[64,32,128]{2,1,0:T(8,128)(2,1)} %gather.1), calls=%async_computation | async-start | bytes 1048576 | tf_op jit(solution)/shard_map/all_to_all | solution.py:543
  23.2 0.0 collective-permute-done.got_a_hbm
  23.2 0.0 copy-start.9
  23.2 13.5 %collective-permute-done.1.got_b_hbm = bf16[22,128,128]{2,1,0:T(8,128)(2,1)S(1)} collective-permute-done((bf16[22,128,128]{2,1,0:T(8,128)(2,1)S(1)}, bf16[22,128,128]{2,1,0:T(8,128)(2,1)S(1)}, u32[]{:S(2)}, u32[]{:S(2)}) %collective-permute-start.1) | collective-permute-done | bytes 720928 | tf_op jit(solution)/shard_map/ppermute | solution.py:523
  36.7 0.0 copy-done.9
  36.7 0.9 copy-done.10
  37.6 0.0 copy-done.5
  37.6 0.0 copy-done.7
  37.6 0.0 copy-done.6
  37.6 7.9 %adjoint_first.1 = (bf16[8,128,128]{2,1,0:T(8,128)(2,1)}, bf16[8,128,128]{2,1,0:T(8,128)(2,1)}, f32[32,128,128]{2,1,0:T(8,128)S(1)}, f32[16,128,128]{2,1,0:T(8,128)S(1)}, f32[8,128]{1,0:T(8,128)S(1)}) custom-call(s32[1,1024]{1,0:T(1,128)S(1)} %bitcast.24, s32[1,1024]{1,0:T(1,128)S(1)} %bitcast.26, f32[4,1024]{1,0:T(4,128)S(1)} %bitcast.22, ...), custom_call_target="tpu_custom_call" | custom-call | flops 4000000000 | bytes 14400000 | tf_op jit(solution)/shard_map/adjoint_first/pallas_call | solution.py:43
  45.5 0.1 collective-permute-start.4
  45.6 8.7 %collective-permute-start.5 = (bf16[8,128,128]{2,1,0:T(8,128)(2,1)}, bf16[8,128,128]{2,1,0:T(8,128)(2,1)}, u32[]{:S(2)}, u32[]{:S(2)}) collective-permute-start(bf16[8,128,128]{2,1,0:T(8,128)(2,1)} %get-tuple-element.36), channel_id=1, source_target_pairs={{1,2},{2,1},{3,4},{4,3},{5,6},{6,5},{7,8},{8,7},{9,10},{10,9},{11,... | collective-permute-start | bytes 786440 | tf_op jit(solution)/shard_map/ppermute | solution.py:523
  54.4 0.0 all-to-all-done.pieces_ref
  54.4 0.0 copy-done.8
  54.4 1.2 %forward_pack.1 = (bf16[12,128,128]{2,1,0:T(8,128)(2,1)S(1)}, bf16[12,128,128]{2,1,0:T(8,128)(2,1)S(1)}, f32[8,128]{1,0:T(8,128)S(1)}) custom-call(s32[64]{0:T(128)S(1)} %bitcast.28, bf16[64,32,128]{2,1,0:T(8,128)(2,1)} %all-to-all-done.pieces_ref, f32[8,128]{1,0:T(8,128)S(1)} %get-tuple-element.31.order_ref), custom_call_target="tpu_custom_call" | custom-call | flops 4000000000 | bytes 14400000 | tf_op jit(solution)/shard_map/forward_pack/pallas_call | solution.py:43
  55.6 0.1 collective-permute-start.2
  55.7 3.9 %collective-permute-start.3 = (bf16[12,128,128]{2,1,0:T(8,128)(2,1)S(1)}, bf16[12,128,128]{2,1,0:T(8,128)(2,1)S(1)}, u32[]{:S(2)}, u32[]{:S(2)}) collective-permute-start(bf16[12,128,128]{2,1,0:T(8,128)(2,1)S(1)} %get-tuple-element.33.mine_b), channel_id=1, source_target_pairs={{1,2},{2,1},{3,4},{4,3},{5,6},{6,5},{7,8},{8,7},{9,10},{10,9},{11,... | collective-permute-start | bytes 1179656 | tf_op jit(solution)/shard_map/ppermute | solution.py:523
  60.9 0.0 collective-permute-done.4.got_a
  60.9 0.1 collective-permute-done.5.got_b
  61.0 9.1 %adjoint_second.1 = (f32[8,128,128]{2,1,0:T(8,128)}, f32[8,128,128]{2,1,0:T(8,128)}, f32[8,128]{1,0:T(8,128)S(1)}) custom-call(s32[1,1024]{1,0:T(1,128)S(1)} %bitcast.25, s32[1,1024]{1,0:T(1,128)S(1)} %bitcast.27, f32[4,1024]{1,0:T(4,128)S(1)} %bitcast.23, bf16[8,128,128]{2,1,0:T(8,128)(2,1)S(1)} %collective-permute-done.4.got_a, ...), custom_call_target="tpu_custom_call" | custom-call | flops 4000000000 | bytes 14400000 | tf_op jit(solution)/shard_map/adjoint_second/pallas_call | solution.py:43
  70.1 0.0 collective-permute-done.2.got_a
  70.1 0.0 collective-permute-done.3.got_b
  70.1 0.0 copy-done.3
  70.1 0.0 copy-start.2
  70.1 3.8 %forward_first.1 = (bf16[8,128,128]{2,1,0:T(8,128)(2,1)S(1)}, bf16[8,128,128]{2,1,0:T(8,128)(2,1)S(1)}, f32[16,144,128]{2,1,0:T(8,128)S(1)}, f32[8,128,128]{2,1,...) custom-call(s32[1]{0:T(128)S(6)} %copy.15.depth_ref, ...), custom_call_target="tpu_custom_call" | custom-call | flops 4000000000 | bytes 14400000 | tf_op jit(solution)/shard_map/forward_first/pallas_call | solution.py:43
  73.9 0.1 collective-permute-start.6
  74.0 8.6 %collective-permute-start.7 = (bf16[8,128,128]{2,1,0:T(8,128)(2,1)S(1)}, bf16[8,128,128]{2,1,0:T(8,128)(2,1)S(1)}, u32[]{:S(2)}, u32[]{:S(2)}) collective-permute-start(bf16[8,128,128]{2,1,0:T(8,128)(2,1)S(1)} %get-tuple-element.41), channel_id=1, source_target_pairs={{1,2},{2,1},{3,4},{4,3},{5,6},{6,5},{7,8},{8,7},{9,10},{10,9},{11,... | collective-permute-start | bytes 786440 | tf_op jit(solution)/shard_map/ppermute | solution.py:523
  82.6 0.0 copy-done.2
  82.6 0.0 copy-start
  82.6 1.5 %middle.1 = (f32[8,128,128]{2,1,0:T(8,128)S(1)}, f32[8,128,128]{2,1,0:T(8,128)S(1)}) custom-call(s32[1]{0:T(128)S(6)} %copy.15.depth_ref, s32[1]{0:T(128)S(6)} %copy.16.row_ref, f32[1,3]{1,0:T(1,128)S(1)} %copy-done.3, f32[32,128,128]{2,1,0:T(8,128)S(1)} %get-tuple-element.37.lam_ref.lam3_ref, f32[8,128,128]{2,1,0:T(8,128)S(1)} %copy-done.2, ...), custom_call_target="tpu_custom_call" | custom-call | tf_op jit(solution)/shard_map/middle/pallas_call | solution.py:43
  84.1 0.0 collective-permute-done.6.got_a
  84.1 2.9 %collective-permute-done.7.got_b = bf16[8,128,128]{2,1,0:T(8,128)(2,1)S(1)} collective-permute-done((bf16[8,128,128]{2,1,0:T(8,128)(2,1)S(1)}, bf16[8,128,128]{2,1,0:T(8,128)(2,1)S(1)}, u32[]{:S(2)}, u32[]{:S(2)}) %collective-permute-start.7) | collective-permute-done | bytes 262176 | tf_op jit(solution)/shard_map/ppermute | solution.py:523
  87.0 3.5 %forward_second.1 = (f32[2,8,32,128]{3,2,1,0:T(8,128)S(1)}, f32[2,8,32,128]{3,2,1,0:T(8,128)S(1)}) custom-call(s32[1]{0:T(128)S(6)} %copy.15.depth_ref, s32[1]{0:T(128)S(6)} %copy.16.row_ref, f32[1,3]{1,0:T(1,128)S(1)} %copy-done.3, bf16[8,128,128]{2,1,0:T(8,128)(2,1)S(1)} %collective-permute-done.6.got_a, ...), custom_call_target="tpu_custom_call" | custom-call | tf_op jit(solution)/shard_map/forward_second/pallas_call | solution.py:43
  90.5 0.1 collective-permute-start.8
  90.6 1.5 %collective-permute-done.8 = f32[2,8,32,128]{3,2,1,0:T(8,128)S(1)} collective-permute-done((f32[2,8,32,128]{3,2,1,0:T(8,128)S(1)}, f32[2,8,32,128]{3,2,1,0:T(8,128)S(1)}, u32[]{:S(2)}, u32[]{:S(2)}) %collective-permute-start.8) | collective-permute-done | bytes 262176 | tf_op jit(solution)/shard_map/ppermute | solution.py:585
  92.2 2.9 %collective-permute-start.9 = (f32[8,32,128]{2,1,0:T(8,128)S(1)}, f32[8,32,128]{2,1,0:T(8,128)S(1)}, u32[]{:S(2)}, u32[]{:S(2)}) collective-permute-start(f32[8,32,128]{2,1,0:T(8,128)S(1)} %fusion), channel_id=1, source_target_pairs={{0,128},{128,0},{64,192},{192,64},{1,129},{129,1},{65,193},{193,65... | collective-permute-start | bytes 393224 | tf_op jit(solution)/shard_map/ppermute | solution.py:586
  95.1 4.2 %collective-permute-done.9 = f32[8,32,128]{2,1,0:T(8,128)S(1)} collective-permute-done((f32[8,32,128]{2,1,0:T(8,128)S(1)}, f32[8,32,128]{2,1,0:T(8,128)S(1)}, u32[]{:S(2)}, u32[]{:S(2)}) %collective-permute-start.9) | collective-permute-done | bytes 131104 | tf_op jit(solution)/shard_map/ppermute | solution.py:586
  99.3 0.7 fusion.2
  (6 shorter events, 0.0 us)
Async XLA Ops:
  0.6 37.0 %copy-start.5 = (f32[1,4,1024]{2,1,0:T(4,128)S(1)}, f32[1,4,1024]{2,1,0:T(4,128)}, u32[]{:S(2)}) copy-start(f32[1,4,1024]{2,1,0:T(4,128)} %param.23) | copy-start | bytes 49156
  0.6 37.0 %copy-start.7 = (s32[1024]{0:T(1024)S(1)}, s32[1024]{0:T(1024)}, u32[]{:S(2)}) copy-start(s32[1024]{0:T(1024)} %param.22) | copy-start | bytes 12292
  0.7 36.9 %copy-start.6 = (s32[1024]{0:T(1024)S(1)}, s32[1024]{0:T(1024)}, u32[]{:S(2)}) copy-start(s32[1024]{0:T(1024)} %param.21) | copy-start | bytes 12292
  2.2 21.0 %collective-permute-start = (bf16[22,128,128]{2,1,0:T(8,128)(2,1)S(1)}, bf16[22,128,128]{2,1,0:T(8,128)(2,1)S(1)}, u32[]{:S(2)}, u32[]{:S(2)}) collective-permute-start(bf16[22,128,128]{2,1,0:T(8,128)(2,1)S(1)} %get-tuple-element.29), channel_id=1, source_target_pairs={{0,1},{1,0},{2,3},{3,2},{4,5},{5,4},{6,7},{7,6},{8,9},{9,8},{10,11... | collective-permute-start | bytes 2162696 | tf_op jit(solution)/shard_map/ppermute | solution.py:523
  3.9 32.8 %collective-permute-start.1 = (bf16[22,128,128]{2,1,0:T(8,128)(2,1)S(1)}, bf16[22,128,128]{2,1,0:T(8,128)(2,1)S(1)}, u32[]{:S(2)}, u32[]{:S(2)}) collective-permute-start(bf16[22,128,128]{2,1,0:T(8,128)(2,1)S(1)} %get-tuple-element.30), channel_id=1, source_target_pairs={{1,2},{2,1},{3,4},{4,3},{5,6},{6,5},{7,8},{8,7},{9,10},{10,9},{11,... | collective-permute-start | bytes 2162696 | tf_op jit(solution)/shard_map/ppermute | solution.py:523
  13.3 1.0 %copy-start.1 = (bf16[1,64,4096]{2,1,0:T(8,128)(2,1)S(1)}, bf16[1,64,4096]{2,1,0:T(8,128)(2,1)}, u32[]{:S(2)}) copy-start(bf16[1,64,4096]{2,1,0:T(8,128)(2,1)} %param.12) | copy-start | bytes 1572868
  14.3 0.7 copy-start.4
  16.7 37.6 %all-to-all-start = ((bf16[64,32,128]{2,1,0:T(8,128)(2,1)}), bf16[64,32,128]{2,1,0:T(8,128)(2,1)}, u32[]{:S(2)}, u32[]{:S(2)}) async-start(bf16[64,32,128]{2,1,0:T(8,128)(2,1)} %gather.1), calls=%async_computation | async-start | bytes 1048576 | tf_op jit(solution)/shard_map/all_to_all | solution.py:543
  23.2 13.5 %copy-start.9 = (bf16[22,128,128]{2,1,0:T(8,128)(2,1)}, bf16[22,128,128]{2,1,0:T(8,128)(2,1)S(1)}, u32[]{:S(2)}) copy-start(bf16[22,128,128]{2,1,0:T(8,128)(2,1)S(1)} %collective-permute-done.got_a_hbm) | copy-start | bytes 2162692
  36.7 0.9 copy-start.10
  37.6 16.8 %copy-start.8 = (s32[1,1,64]{2,1,0:T(1,128)S(1)}, s32[1,1,64]{2,1,0:T(1,128)}, u32[]{:S(2)}) copy-start(s32[1,1,64]{2,1,0:T(1,128)} %param.14) | copy-start | bytes 772
  45.5 15.4 %collective-permute-start.4 = (bf16[8,128,128]{2,1,0:T(8,128)(2,1)}, bf16[8,128,128]{2,1,0:T(8,128)(2,1)S(1)}, u32[]{:S(2)}, u32[]{:S(2)}) collective-permute-start(bf16[8,128,128]{2,1,0:T(8,128)(2,1)} %get-tuple-element.35), channel_id=1, source_target_pairs={{0,1},{1,0},{2,3},{3,2},{4,5},{5,4},{6,7},{7,6},{8,9},{9,8},{10,11... | collective-permute-start | bytes 786440 | tf_op jit(solution)/shard_map/ppermute | solution.py:523
  45.6 15.4 %collective-permute-start.5 = (bf16[8,128,128]{2,1,0:T(8,128)(2,1)}, bf16[8,128,128]{2,1,0:T(8,128)(2,1)}, u32[]{:S(2)}, u32[]{:S(2)}) collective-permute-start(bf16[8,128,128]{2,1,0:T(8,128)(2,1)} %get-tuple-element.36), channel_id=1, source_target_pairs={{1,2},{2,1},{3,4},{4,3},{5,6},{6,5},{7,8},{8,7},{9,10},{10,9},{11,... | collective-permute-start | bytes 786440 | tf_op jit(solution)/shard_map/ppermute | solution.py:523
  55.6 14.5 %collective-permute-start.2 = (bf16[12,128,128]{2,1,0:T(8,128)(2,1)S(1)}, bf16[12,128,128]{2,1,0:T(8,128)(2,1)S(1)}, u32[]{:S(2)}, u32[]{:S(2)}) collective-permute-start(bf16[12,128,128]{2,1,0:T(8,128)(2,1)S(1)} %get-tuple-element.32.mine_a), channel_id=1, source_target_pairs={{0,1},{1,0},{2,3},{3,2},{4,5},{5,4},{6,7},{7,6},{8,9},{9,8},{10,11... | collective-permute-start | bytes 1179656 | tf_op jit(solution)/shard_map/ppermute | solution.py:523
  55.7 14.4 %collective-permute-start.3 = (bf16[12,128,128]{2,1,0:T(8,128)(2,1)S(1)}, bf16[12,128,128]{2,1,0:T(8,128)(2,1)S(1)}, u32[]{:S(2)}, u32[]{:S(2)}) collective-permute-start(bf16[12,128,128]{2,1,0:T(8,128)(2,1)S(1)} %get-tuple-element.33.mine_b), channel_id=1, source_target_pairs={{1,2},{2,1},{3,4},{4,3},{5,6},{6,5},{7,8},{8,7},{9,10},{10,9},{11,... | collective-permute-start | bytes 1179656 | tf_op jit(solution)/shard_map/ppermute | solution.py:523
  61.0 9.1 %copy-start.3 = (f32[1,3]{1,0:T(1,128)S(1)}, f32[1,3]{1,0:T(1,128)}, u32[]{:S(2)}) copy-start(f32[1,3]{1,0:T(1,128)} %wave_ref.5) | copy-start | bytes 40
  70.1 12.5 %copy-start.2 = (f32[8,128,128]{2,1,0:T(8,128)S(1)}, f32[8,128,128]{2,1,0:T(8,128)}, u32[]{:S(2)}) copy-start(f32[8,128,128]{2,1,0:T(8,128)} %get-tuple-element.44.late_ref) | copy-start | bytes 1572868
  73.9 10.2 %collective-permute-start.6 = (bf16[8,128,128]{2,1,0:T(8,128)(2,1)S(1)}, bf16[8,128,128]{2,1,0:T(8,128)(2,1)S(1)}, u32[]{:S(2)}, u32[]{:S(2)}) collective-permute-start(bf16[8,128,128]{2,1,0:T(8,128)(2,1)S(1)} %get-tuple-element.40), channel_id=1, source_target_pairs={{0,1},{1,0},{2,3},{3,2},{4,5},{5,4},{6,7},{7,6},{8,9},{9,8},{10,11... | collective-permute-start | bytes 786440 | tf_op jit(solution)/shard_map/ppermute | solution.py:523
  74.0 13.0 %collective-permute-start.7 = (bf16[8,128,128]{2,1,0:T(8,128)(2,1)S(1)}, bf16[8,128,128]{2,1,0:T(8,128)(2,1)S(1)}, u32[]{:S(2)}, u32[]{:S(2)}) collective-permute-start(bf16[8,128,128]{2,1,0:T(8,128)(2,1)S(1)} %get-tuple-element.41), channel_id=1, source_target_pairs={{1,2},{2,1},{3,4},{4,3},{5,6},{6,5},{7,8},{8,7},{9,10},{10,9},{11,... | collective-permute-start | bytes 786440 | tf_op jit(solution)/shard_map/ppermute | solution.py:523
  82.6 4.4 %copy-start = (f32[1,8,128,128]{3,2,1,0:T(8,128)S(1)}, f32[1,8,128,128]{3,2,1,0:T(8,128)}, u32[]{:S(2)}) copy-start(f32[1,8,128,128]{3,2,1,0:T(8,128)} %param.17) | copy-start | bytes 1572868
  90.5 1.6 %collective-permute-start.8 = (f32[2,8,32,128]{3,2,1,0:T(8,128)S(1)}, f32[2,8,32,128]{3,2,1,0:T(8,128)S(1)}, u32[]{:S(2)}, u32[]{:S(2)}) collective-permute-start(f32[2,8,32,128]{3,2,1,0:T(8,128)S(1)} %get-tuple-element.51), channel_id=1, source_target_pairs={{0,64},{64,0},{128,192},{192,128},{1,65},{65,1},{129,193},{193,129... | collective-permute-start | bytes 786440 | tf_op jit(solution)/shard_map/ppermute | solution.py:585
  92.2 7.1 %collective-permute-start.9 = (f32[8,32,128]{2,1,0:T(8,128)S(1)}, f32[8,32,128]{2,1,0:T(8,128)S(1)}, u32[]{:S(2)}, u32[]{:S(2)}) collective-permute-start(f32[8,32,128]{2,1,0:T(8,128)S(1)} %fusion), channel_id=1, source_target_pairs={{0,128},{128,0},{64,192},{192,64},{1,129},{129,1},{65,193},{193,65... | collective-permute-start | bytes 393224 | tf_op jit(solution)/shard_map/ppermute | solution.py:586

commit v4 on v3

--- a/solution.py
+++ b/solution.py
@@ -39,13 +39,13 @@
     return copies
 
 
-def call(kernel, name, ins, outs, scratch, args, us=0, limit=20 << 20):
+def call(kernel, name, ins, outs, scratch, args, us=2, limit=20 << 20):
     return pl.pallas_call(
         kernel,
         name=name,
-        out_shape=[jax.ShapeDtypeStruct(s, d) for s, d in outs],
+        out_shape=[pltpu.HBM(*o) if name == "inject" else jax.ShapeDtypeStruct(*o) for o in outs],
         in_specs=ins,
-        out_specs=[VM] * len(outs),
+        out_specs=[HB if name == "inject" else VM] * len(outs),
         scratch_shapes=scratch,
         compiler_params=pltpu.CompilerParams(vmem_limit_bytes=limit),
         cost_estimate=pl.CostEstimate(flops=us * 10**9, bytes_accessed=us * 3_600_000, transcendentals=0),
@@ -155,7 +155,9 @@
         body(first, second)
 
 
-def gather_kernel(slot_ref, parked_ref, order_ref, out_ref, held):
+def gather_kernel(slot_hbm, parked_hbm, out_ref, held, slot_ref, parked_ref, sems):
+    for copy in fetch((slot_hbm, parked_hbm), (slot_ref, parked_ref), sems):
+        copy.wait()
     pieces = parked_ref.shape[0]
     row = lax.broadcasted_iota(jnp.int32, (pieces, pieces), 0)
     pick = jnp.where(row == slot_ref[...], 1.0, 0.0).astype(bf16)
@@ -170,63 +172,57 @@
     out_ref[...] = held[...].reshape(pieces, 32, NY).astype(bf16)
 
 
-def adjoint_pack_kernel(now_hbm, next_hbm, speed_hbm, first_ref, second_ref, mark_ref, now_ref, next_ref, speed_ref, sems):
+def adjoint_pack_kernel(now_hbm, next_hbm, speed_hbm, first_ref, second_ref, now_ref, next_ref, speed_ref, sems):
     fields = (now_ref, next_ref, speed_ref)
     for copy in fetch((now_hbm, next_hbm, speed_hbm), fields, sems):
         copy.wait()
-    mark_ref[...] = jnp.zeros(mark_ref.shape, f32)
     par = parity()
     for out_ref, near in ((first_ref, HALF * (1 - par)), (second_ref, HALF * par)):
         far = HALF - near
-        close = near + near // 2
+        close = near + 3 * (near // HALF)
         for n, ref in enumerate(fields):
             out_ref[pl.ds(HALF * n, HALF)] = ref[pl.ds(near, HALF)].astype(bf16)
-            value = ref[pl.ds(close, 2)]
-            out_ref[pl.ds(4 * HALF + 2 * n, 2)] = (value - value.astype(bf16).astype(f32)).astype(bf16)
+            value = ref[pl.ds(close, 1)]
+            out_ref[pl.ds(4 * HALF + n, 1)] = (value - value.astype(bf16).astype(f32)).astype(bf16)
         out_ref[pl.ds(3 * HALF, HALF)] = (now_ref[pl.ds(far, HALF)] * speed_ref[pl.ds(far, HALF)]).astype(bf16)
 
 
-def inject_fields(depth_ref, row_ref, amount_ref, first_step, out_ref, table, last_on_halo):
+def inject_kernel(depth_ref, row_ref, amount_ref, out_hbm, mark_hbm, table, fields, sems):
     top = lax.axis_index("dom") * DEPTH - HALF
     count = depth_ref.shape[1]
-    steps = out_ref.shape[0]
+    steps = amount_ref.shape[0]
     local = depth_ref[...] - top
     place = row_ref[...]
     key = jnp.where((local >= 0) & (local < EXT), local * NX + place // NY, -1)
     hit = lax.broadcasted_iota(jnp.int32, (NY, count), 0) == lax.rem(place, NY)
     for k in range(steps):
-        amount = amount_ref[first_step + k : first_step + k + 1, :]
+        amount = amount_ref[k : k + 1, :]
         head = amount.astype(bf16).astype(f32)
         table[0, k * NY : (k + 1) * NY, :] = jnp.where(hit, head, 0.0).astype(bf16)
         table[1, k * NY : (k + 1) * NY, :] = jnp.where(hit, amount - head, 0.0).astype(bf16)
     planes = 2
     cell = lax.broadcasted_iota(jnp.int32, (planes * NX, count), 0)
 
-    def group(g, used):
+    def store(g):
+        at = pl.ds(g * planes, planes)
+        return pltpu.make_async_copy(fields.at[at], out_hbm.at[at], sems.at[g])
+
+    @pl.loop(0, EXT // planes)
+    def _(g):
         pick = jnp.where(cell + g * (planes * NX) == key, 1.0, 0.0).astype(bf16)
-        field = jnp.zeros((planes * NX, used * NY), f32)
-        for n in range(2):
-            field = field + lax.dot_general(
-                pick, table[n, : used * NY], (((1,), (1,)), ((), ())), preferred_element_type=f32
-            )
-        for k in range(used):
+        field = lax.dot_general(
+            pick, table[0], (((1,), (1,)), ((), ())), preferred_element_type=f32
+        ) + lax.dot_general(pick, table[1], (((1,), (1,)), ((), ())), preferred_element_type=f32)
+        for k in range(steps):
             for j in range(planes):
-                out_ref[k, g * planes + j] = field[j * NX : (j + 1) * NX, k * NY : (k + 1) * NY]
-
-    if last_on_halo:
-
-        @pl.loop(0, EXT // planes)
-        def _(g):
-            group(g, steps)
-    else:
-
-        @pl.loop(0, DEPTH // planes)
-        def _(g):
-            group(g + HALF // planes, steps)
-
-        @pl.loop(0, DEPTH // planes)
-        def _(h):
-            group(jnp.where(h < HALF // planes, h, h + DEPTH // planes), steps - 1)
+                fields[g * planes + j, k] = field[j * NX : (j + 1) * NX, k * NY : (k + 1) * NY]
+        store(g).start()
+
+    mark = pltpu.make_async_copy(fields.at[0, 0, 0:8], mark_hbm, sems.at[EXT // planes])
+    mark.start()
+    for g in range(EXT // planes):
+        store(g).wait()
+    mark.wait()
 
 
 def send_second(par, buf, far_ref, speed_ext, scale_far, first_ref, second_ref):
@@ -253,52 +249,51 @@
 
 
 def adjoint_first_kernel(
-    depth_ref, row_ref, amount_ref, now_hbm, next_hbm, speed_hbm, got_a_hbm, got_b_hbm,
-    first_ref, second_ref, lam_ref, speed_ext, mark_ref,
-    buf4, q3_ref, now_halo, next_halo, now_ref, next_ref, got_a, got_b, sems, inject_ref, table,
+    now_hbm, next_hbm, speed_hbm, inject_hbm, got_a, got_b,
+    first_ref, second_ref, lam_ref, speed_ext,
+    buf4, q3_ref, now_halo, next_halo, now_ref, next_ref, inject_ref, sems,
 ):
     par = parity()
     own = slice(HALF, HALF + DEPTH)
     copies = fetch(
-        (now_hbm, next_hbm, speed_hbm, got_a_hbm, got_b_hbm), (now_ref, next_ref, speed_ext.at[own], got_a, got_b), sems
-    )
-    inject_fields(depth_ref, row_ref, amount_ref, 0, inject_ref, table, True)
+        (speed_hbm, now_hbm, next_hbm, inject_hbm.at[:, 0:2]), (speed_ext.at[own], now_ref, next_ref, inject_ref), sems
+    )
     zero_pads(buf4)
     zero_pads(q3_ref)
     weights = band()
     inner = slice(PAD, PAD + NX)
-    for copy in copies:
+    for copy in copies[:2]:
         copy.wait()
     buf4[2 * HALF : 2 * HALF + DEPTH, inner, :] = now_ref[...] * speed_ext[own]
 
     def halo(lower, upper):
-        for ref, at, close, far_at in ((lower, 0, 2, 0), (upper, HALF, 0, WIDE - HALF)):
+        for ref, at, close, far_at in ((lower, 0, 3, 0), (upper, HALF, 0, WIDE - HALF)):
             ext_at = ext_of_halo(at)
             for n, (held, to) in enumerate(((now_halo, at), (next_halo, at), (speed_ext, ext_at))):
                 held[to : to + HALF] = ref[HALF * n : HALF * n + HALF].astype(f32)
-                held[to + close : to + close + 2] = held[to + close : to + close + 2] + ref[
-                    4 * HALF + 2 * n : 4 * HALF + 2 * n + 2
-                ].astype(f32)
+                held[to + close] = held[to + close] + ref[4 * HALF + n].astype(f32)
             buf4[far_at : far_at + HALF, inner, :] = ref[3 * HALF : 4 * HALF].astype(f32)
             buf4[ext_at + HALF : ext_at + 2 * HALF, inner, :] = (
                 now_halo[at : at + HALF] * speed_ext[ext_at : ext_at + HALF]
             )
 
     by_side(par, got_a, got_b, halo)
+    for copy in copies[2:]:
+        copy.wait()
 
     def halo_lam3(h, row, lap):
         e = ext_of_halo(h)
         now = now_halo[h, rows(row), :]
-        lam = 2.0 * now - next_halo[h, rows(row), :] + lap + inject_ref[0, e, rows(row), :]
+        lam = 2.0 * now - next_halo[h, rows(row), :] + lap + inject_ref[e, 0, rows(row), :]
         lam_ref[e, rows(row), :] = lam
-        lam_ref[EXT + DEPTH + h, rows(row), :] = 2.0 * lam - now + inject_ref[1, e, rows(row), :]
+        lam_ref[EXT + DEPTH + h, rows(row), :] = 2.0 * lam - now + inject_ref[e, 1, rows(row), :]
         q3_ref[e, padded(row), :] = lam * speed_ext[e, rows(row), :]
 
     sweep_halo(buf4, weights, halo_lam3)
 
     def own_lam3(p, row, lap):
         lam = 2.0 * now_ref[p, rows(row), :] - next_ref[p, rows(row), :] + lap
-        lam = lam + inject_ref[0, p + HALF, rows(row), :]
+        lam = lam + inject_ref[p + HALF, 0, rows(row), :]
         lam_ref[p + HALF, rows(row), :] = lam
         q3_ref[p + HALF, padded(row), :] = lam * speed_ext[p + HALF, rows(row), :]
 
@@ -306,16 +301,14 @@
 
     def own_lam2(p, row, lap):
         lam = 2.0 * lam_ref[p + HALF, rows(row), :] - now_ref[p, rows(row), :] + lap
-        lam_ref[EXT + p, rows(row), :] = lam + inject_ref[1, p + HALF, rows(row), :]
+        lam_ref[EXT + p, rows(row), :] = lam + inject_ref[p + HALF, 1, rows(row), :]
 
     sweep_own(q3_ref, HALF, weights, own_lam2)
     send_second(par, q3_ref, lam_ref.at[EXT : EXT + DEPTH], speed_ext, True, first_ref, second_ref)
-    mark_ref[...] = jnp.zeros(mark_ref.shape, f32)
-
-
-def forward_pack_kernel(holder_ref, pieces_ref, order_ref, first_ref, second_ref, mark_ref):
+
+
+def forward_pack_kernel(holder_ref, pieces_ref, order_ref, first_ref, second_ref):
     par = parity()
-    mark_ref[...] = jnp.zeros(mark_ref.shape, f32)
     per_plane = NX // 32
     for p in range(DEPTH):
         for j in range(per_plane):
@@ -335,7 +328,7 @@
 
 
 def forward_first_kernel(
-    depth_ref, row_ref, wave_ref, mine_a, mine_b, got_a, got_b, speed_ext, order_ref,
+    depth_ref, row_ref, wave_ref, mine_a, mine_b, got_a, got_b, speed_ext,
     first_ref, second_ref, u1_ref, u2_ref, base_ref, lap0_ref, lap1_ref,
     buf0, prev_ext,
 ):
@@ -391,14 +384,13 @@
         base_ref[h] = 2.0 * u1_ref[e, inner, :] - buf0[e + HALF, inner, :]
 
 
-def adjoint_second_kernel(
-    depth_ref, row_ref, amount_ref, got_a, got_b, lam_ref, speed_ext, order_ref,
-    late_ref, early_ref, mark_ref,
-    lam2_halo, buf2, buf1, inject_ref, table,
+def middle_kernel(
+    depth_ref, row_ref, wave_ref, inject_hbm, got_a, got_b, lam_ref, speed_ext, u1_ref, base_ref, lap0_ref, lap1_ref,
+    late_ref, early_ref, u2_ref, grad_ref,
+    lam2_halo, buf2, buf1, inject_ref, sems,
 ):
     par = parity()
-    mark_ref[...] = jnp.zeros(mark_ref.shape, f32)
-    inject_fields(depth_ref, row_ref, amount_ref, 2, inject_ref, table, False)
+    (copy,) = fetch((inject_hbm.at[:, 2:4],), (inject_ref,), sems)
     zero_pads(buf2)
     zero_pads(buf1)
     weights = band()
@@ -409,6 +401,7 @@
         lam2_halo[h, rows(row), :] = lam_ref[EXT + DEPTH + h, rows(row), :] + lap
 
     sweep_halo_alone(buf1, weights, alone)
+    copy.wait()
 
     def halo(lower, upper):
         for ref, at, far_at in ((lower, 0, 0), (upper, HALF, WIDE - HALF)):
@@ -424,32 +417,27 @@
     def halo_lam1(h, row, lap):
         e = ext_of_halo(h)
         lam = 2.0 * lam2_halo[h, rows(row), :] - lam_ref[e, rows(row), :] + lap
-        lam = lam + inject_ref[0, e, rows(row), :]
+        lam = lam + inject_ref[e, 0, rows(row), :]
         buf1[e, padded(row), :] = lam * speed_ext[e, rows(row), :]
 
     sweep_halo(buf2, weights, halo_lam1)
 
     def own_lam1(p, row, lap):
         lam = 2.0 * lam_ref[EXT + p, rows(row), :] - lam_ref[p + HALF, rows(row), :] + lap
-        lam = lam + inject_ref[0, p + HALF, rows(row), :]
+        lam = lam + inject_ref[p + HALF, 0, rows(row), :]
         late_ref[p, rows(row), :] = lam
+        grad_ref[p, rows(row), :] = (
+            lam * lap0_ref[p, rows(row), :] + lam_ref[EXT + p, rows(row), :] * lap1_ref[p, rows(row), :]
+        )
         buf1[p + HALF, padded(row), :] = lam * speed_ext[p + HALF, rows(row), :]
 
     sweep_own(buf2, 2 * HALF, weights, own_lam1)
 
     def own_lam0(p, row, lap):
         lam = 2.0 * late_ref[p, rows(row), :] - lam_ref[EXT + p, rows(row), :] + lap
-        early_ref[p, rows(row), :] = lam + inject_ref[1, p + HALF, rows(row), :]
+        early_ref[p, rows(row), :] = lam + inject_ref[p + HALF, 1, rows(row), :]
 
     sweep_own(buf1, HALF, weights, own_lam0)
-
-
-def middle_kernel(
-    depth_ref, row_ref, wave_ref, lam_ref, late_ref, speed_ext, u1_ref, base_ref, lap0_ref, lap1_ref,
-    u2_ref, grad_ref,
-):
-    weights = band()
-    grad_ref[...] = late_ref[...] * lap0_ref[...] + lam_ref[EXT : EXT + DEPTH] * lap1_ref[...]
 
     def halo_u2(h, row, lap):
         e = ext_of_halo(h)
@@ -530,57 +518,62 @@
         return ((count, NX, NY), bf16)
 
     mark = ((8, NY), f32)
-    lam23_shape = (EXT + 2 * DEPTH, NX, NY)
-    send_a, send_b, order = call(
-        adjoint_pack_kernel, "adjoint_pack", [HB] * 3, [planes(22)] * 2 + [mark],
+    (outgoing,) = call(
+        gather_kernel, "gather", [HB] * 2, [((64, 32, NY), bf16)],
+        [
+            pltpu.VMEM((64 * 32, NY), f32), pltpu.VMEM((1, 64), jnp.int32), pltpu.VMEM((64, 4096), bf16),
+            pltpu.SemaphoreType.DMA((2,)),
+        ],
+        in_hbm(parked_slot[0], parked[0]),
+    )
+    incoming = lax.all_to_all(outgoing, "dom", split_axis=0, concat_axis=0, tiled=True)
+    send_a, send_b = call(
+        adjoint_pack_kernel, "adjoint_pack", [HB] * 3, [planes(19)] * 2,
         [pltpu.VMEM(*slab)] * 3 + [pltpu.SemaphoreType.DMA((3,))], in_hbm(lam4, lam5, speed_sq),
     )
     got_a, got_b = swap(send_a, send_b)
-    (outgoing,) = call(
-        gather_kernel, "gather", [VM] * 3, [((64, 32, NY), bf16)], [pltpu.VMEM((64 * 32, NY), f32)],
-        (parked_slot[0], parked[0], order),
-    )
-    incoming = lax.all_to_all(outgoing, "dom", split_axis=0, concat_axis=0, tiled=True)
     count = rec_depth.shape[0]
-    receivers = (rec_depth.reshape(1, count), rec_row.reshape(1, count), residuals[0])
-    fields = [pltpu.VMEM((2, EXT, NX, NY), f32), pltpu.VMEM((2, 2 * NY, count), bf16)]
-    send_a, send_b, lam23, speed_ext, order = call(
-        adjoint_first_kernel, "adjoint_first", [VM] * 3 + [HB] * 5, [planes(8)] * 2 + [(lam23_shape, f32), ext, mark],
-        [buffer(WIDE), buffer(EXT)] + [pltpu.VMEM(*slab)] * 4 + [pltpu.VMEM(*planes(22))] * 2
-        + [pltpu.SemaphoreType.DMA((5,))] + fields,
-        receivers + in_hbm(lam4, lam5, speed_sq, got_a, got_b), us=4,
+    steps = residuals.shape[1]
+    inject, order = call(
+        inject_kernel, "inject", [VM] * 3, [((EXT, steps, NX, NY), f32), mark],
+        [
+            pltpu.VMEM((2, steps * NY, count), bf16), pltpu.VMEM((EXT, steps, NX, NY), f32),
+            pltpu.SemaphoreType.DMA((EXT // 2 + 1,)),
+        ],
+        (rec_depth.reshape(1, count), rec_row.reshape(1, count), residuals[0]), us=4,
+    )
+    fields = pltpu.VMEM((EXT, 2, NX, NY), f32)
+    send_a, send_b, lam23, speed_ext = call(
+        adjoint_first_kernel, "adjoint_first", [HB] * 4 + [VM] * 2,
+        [planes(8)] * 2 + [((EXT + 2 * DEPTH, NX, NY), f32), ext],
+        [buffer(WIDE), buffer(EXT)] + [pltpu.VMEM(*slab)] * 4 + [fields, pltpu.SemaphoreType.DMA((4,))],
+        in_hbm(lam4, lam5, speed_sq, inject) + (got_a, got_b),
     )
     back_a, back_b = swap(send_a, send_b)
 
-    mine_a, mine_b, order = call(
-        forward_pack_kernel, "forward_pack", [SM, VM, VM], [planes(12)] * 2 + [mark], [],
-        (holder_list.reshape(64), incoming, order), us=4,
+    mine_a, mine_b = call(
+        forward_pack_kernel, "forward_pack", [SM, VM, HB], [planes(12)] * 2, [],
+        (holder_list.reshape(64), incoming) + in_hbm(order),
     )
     got_a, got_b = swap(mine_a, mine_b)
-    late, early, order = call(
-        adjoint_second_kernel, "adjoint_second", [VM] * 8, [slab] * 2 + [mark],
-        [pltpu.VMEM(*slab), buffer(WIDE), buffer(EXT)] + fields,
-        receivers + (back_a, back_b, lam23, speed_ext, order), us=4,
-    )
     send_a, send_b, u1, u2, base_u, lap0, lap1 = call(
-        forward_first_kernel, "forward_first", [SM] * 3 + [VM] * 6,
+        forward_first_kernel, "forward_first", [SM] * 3 + [VM] * 5,
         [planes(8)] * 2 + [wide, slab, slab, slab, slab],
         [buffer(WIDE), pltpu.VMEM(*ext)],
-        (src_depth, src_row, wavelet, mine_a, mine_b, got_a, got_b, speed_ext, order),
-        us=4,
+        (src_depth, src_row, wavelet, mine_a, mine_b, got_a, got_b, speed_ext),
     )
     got_a, got_b = swap(send_a, send_b)
-    u2_halo, grad = call(
-        middle_kernel, "middle", [SM] * 3 + [VM] * 7, [slab] * 2, [],
-        (src_depth, src_row, wavelet, lam23, late, speed_ext, u1, base_u, lap0, lap1),
-        us=0,
+    late, early, u2_halo, grad = call(
+        middle_kernel, "middle", [SM] * 3 + [HB] + [VM] * 8, [slab] * 4,
+        [pltpu.VMEM(*slab), buffer(WIDE), buffer(EXT), fields, pltpu.SemaphoreType.DMA((1,))],
+        (src_depth, src_row, wavelet) + in_hbm(inject)
+        + (back_a, back_b, lam23, speed_ext, u1, base_u, lap0, lap1),
     )
     quarter = ((2, DEPTH, NX // 4, NY), f32)
     keep, send = call(
         forward_second_kernel, "forward_second", [SM] * 3 + [VM] * 9, [quarter] * 2,
         [buffer(WIDE), buffer(EXT), pltpu.VMEM(*slab)],
         (src_depth, src_row, wavelet, got_a, got_b, u1, u2, u2_halo, speed_ext, lam23, lam4, grad),
-        us=0,
     )
     got = lax.ppermute(send, "shot", [(0, 1), (1, 0), (2, 3), (3, 2)])
     other = lax.ppermute(keep[1] + got[1], "shot", [(0, 2), (2, 0), (1, 3), (3, 1)])

time: 101 us -> 86.8 us (0.86)
  waiting for transfers between devices: 22.2 us -> 11 us
  local copies, waits for them, and re-layouts: 2.62 us -> 0.04 us
  Pallas kernels: 30.3 us -> 31.7 us
  starting transfers between devices: 42 us -> 40.8 us
    ppermute x4, waiting for transfers between devices: 16.5 us -> 4.19 us  [per_device(): lax.ppermute(b, 'dom', odd)]
    ppermute x4, starting transfers between devices: 30.6 us -> 21.1 us  [per_device(): lax.ppermute(b, 'dom', odd)]
    all_to_all x1, starting transfers between devices: 6.45 us -> 13.2 us  [per_device(): lax.all_to_all(outgoing, 'dom', split_axis=0, concat_axis=0, tiled=True)]
    unnamed x22 -> x12, local copies, waits for them, and re-layouts: 2.62 us -> 0.04 us
    ppermute x4, starting transfers between devices: 1.94 us -> 4.17 us  [per_device(): lax.ppermute(a, 'dom', even)]
    pallas_call x8, Pallas kernels: 30.3 us -> 31.7 us  [call(): pl.pallas_call(kernel, name=name, out_shape=[pltpu.HBM(*o) if name == 'in...]
  transfers between devices with their start and end apart: 11 -> 11, of which waited for: 5 -> 4; matrix products, arithmetic and copies ran while one was open for 0% -> 0% of each run, Pallas kernels for 21% -> 29%
where the time goes in v4:
time: 86.8 us; the launch traced here: 86.4 us
  starting transfers between devices  40.8 us (47%)
  Pallas kernels  31.7 us (37%)
  waiting for transfers between devices  11 us (13%)
  between operations  2.18 us (3%)
    pallas_call x8, Pallas kernels, call(): pl.pallas_call(kernel, name=name, out_shape=[pltpu.HBM(*o) if name == 'in...  31.7 us
    ppermute x4, starting transfers between devices, per_device(): lax.ppermute(b, 'dom', odd)  21.1 us
    all_to_all x1, starting transfers between devices, per_device(): lax.all_to_all(outgoing, 'dom', split_axis=0, concat_axis=0, tiled=True)  13.2 us
    ppermute x1, waiting for transfers between devices, per_device(): lax.ppermute(keep[1] + got[1], 'shot', [(0, 2), (2, 0), (1, 3), (3, 1)])  4.92 us
    ppermute x4, waiting for transfers between devices, per_device(): lax.ppermute(b, 'dom', odd)  4.19 us
    ppermute x4, starting transfers between devices, per_device(): lax.ppermute(a, 'dom', even)  4.17 us
    ppermute x1, starting transfers between devices, per_device(): lax.ppermute(keep[1] + got[1], 'shot', [(0, 2), (2, 0), (1, 3), (3, 1)])  2.21 us
  transfers between devices with their start and end apart: 11, of which 4 were waited for; matrix products, arithmetic and copies ran while one was open for 0% of the time, Pallas kernels for 29%

profile of v4, /device:TPU:2, one launch (start us, length us, event | category | flops | bytes accessed | tf_op | source)
XLA Modules:
  0.0 86.4 jit_solution(822164197714131077)
XLA Ops:
  0.6 2.9 %gather.1 = bf16[64,32,128]{2,1,0:T(8,128)(2,1)} custom-call(s32[1,64]{1,0:T(1,128)} %bitcast.28, bf16[64,4096]{1,0:T(8,128)(2,1)} %bitcast.23), custom_call_target="tpu_custom_call" | custom-call | flops 2000000000 | bytes 7200000 | tf_op jit(solution)/shard_map/gather/pallas_call | solution.py:43
  3.5 13.2 %all-to-all-start = ((bf16[64,32,128]{2,1,0:T(8,128)(2,1)}), bf16[64,32,128]{2,1,0:T(8,128)(2,1)S(1)}, u32[]{:S(2)}, u32[]{:S(2)}) async-start(bf16[64,32,128]{2,1,0:T(8,128)(2,1)} %gather.1), calls=%async_computation | async-start | bytes 1048576 | tf_op jit(solution)/shard_map/all_to_all | solution.py:529
  16.7 0.0 copy-start.2
  16.7 0.0 copy-start.3
  16.7 0.0 copy-start.4
  16.8 1.5 %adjoint_pack.1 = (bf16[19,128,128]{2,1,0:T(8,128)(2,1)S(1)}, bf16[19,128,128]{2,1,0:T(8,128)(2,1)S(1)}) custom-call(f32[8,128,128]{2,1,0:T(8,128)} %bitcast.16, f32[8,128,128]{2,1,0:T(8,128)} %bitcast.24, f32[8,128,128]{2,1,0:T(8,128)} %speed_hbm.3), custom_call_target="tpu_custom_call" | custom-call | flops 2000000000 | bytes 7200000 | tf_op jit(solution)/shard_map/adjoint_pack/pallas_call | solution.py:43
  18.3 1.6 %collective-permute-start.2 = (bf16[19,128,128]{2,1,0:T(8,128)(2,1)S(1)}, bf16[19,128,128]{2,1,0:T(8,128)(2,1)S(1)}, u32[]{:S(2)}, u32[]{:S(2)}) collective-permute-start(bf16[19,128,128]{2,1,0:T(8,128)(2,1)S(1)} %get-tuple-element.30), channel_id=1, source_target_pairs={{0,1},{1,0},{2,3},{3,2},{4,5},{5,4},{6,7},{7,6},{8,9},{9,8},{10,11... | collective-permute-start | bytes 1867784 | tf_op jit(solution)/shard_map/ppermute | solution.py:511
  19.9 6.1 %collective-permute-start.3 = (bf16[19,128,128]{2,1,0:T(8,128)(2,1)S(1)}, bf16[19,128,128]{2,1,0:T(8,128)(2,1)S(1)}, u32[]{:S(2)}, u32[]{:S(2)}) collective-permute-start(bf16[19,128,128]{2,1,0:T(8,128)(2,1)S(1)} %get-tuple-element.31), channel_id=1, source_target_pairs={{1,2},{2,1},{3,4},{4,3},{5,6},{6,5},{7,8},{8,7},{9,10},{10,9},{11,... | collective-permute-start | bytes 1867784 | tf_op jit(solution)/shard_map/ppermute | solution.py:511
  25.9 0.0 copy-done.2
  25.9 0.0 copy-done.3
  25.9 0.0 copy-done.4
  26.0 0.0 copy-start.5
  26.0 7.2 %inject.1 = (f32[16,4,128,128]{3,2,1,0:T(8,128)}, f32[8,128]{1,0:T(8,128)}) custom-call(s32[1,1024]{1,0:T(1,128)S(1)} %bitcast.20, s32[1,1024]{1,0:T(1,128)S(1)} %bitcast.21, f32[4,1024]{1,0:T(4,128)S(1)} %bitcast.19), custom_call_target="tpu_custom_call" | custom-call | flops 4000000000 | bytes 14400000 | tf_op jit(solution)/shard_map/inject/pallas_call | solution.py:43
  33.2 0.4 all-to-all-done.pieces_ref
  33.6 0.0 copy-done.5
  33.6 0.7 forward_pack.1
  34.2 1.4 %collective-permute-start = (bf16[12,128,128]{2,1,0:T(8,128)(2,1)S(1)}, bf16[12,128,128]{2,1,0:T(8,128)(2,1)S(1)}, u32[]{:S(2)}, u32[]{:S(2)}) collective-permute-start(bf16[12,128,128]{2,1,0:T(8,128)(2,1)S(1)} %get-tuple-element.27.mine_a), channel_id=1, source_target_pairs={{0,1},{1,0},{2,3},{3,2},{4,5},{5,4},{6,7},{7,6},{8,9},{9,8},{10,11... | collective-permute-start | bytes 1179656 | tf_op jit(solution)/shard_map/ppermute | solution.py:511
  35.7 6.0 %collective-permute-start.1 = (bf16[12,128,128]{2,1,0:T(8,128)(2,1)S(1)}, bf16[12,128,128]{2,1,0:T(8,128)(2,1)S(1)}, u32[]{:S(2)}, u32[]{:S(2)}) collective-permute-start(bf16[12,128,128]{2,1,0:T(8,128)(2,1)S(1)} %get-tuple-element.28.mine_b), channel_id=1, source_target_pairs={{1,2},{2,1},{3,4},{4,3},{5,6},{6,5},{7,8},{8,7},{9,10},{10,9},{11,... | collective-permute-start | bytes 1179656 | tf_op jit(solution)/shard_map/ppermute | solution.py:511
  42.9 0.0 collective-permute-done.2.got_a
  42.9 4.2 %collective-permute-done.3.got_b = bf16[19,128,128]{2,1,0:T(8,128)(2,1)S(1)} collective-permute-done((bf16[19,128,128]{2,1,0:T(8,128)(2,1)S(1)}, bf16[19,128,128]{2,1,0:T(8,128)(2,1)S(1)}, u32[]{:S(2)}, u32[]{:S(2)}) %collective-permute-start.3) | collective-permute-done | bytes 622624 | tf_op jit(solution)/shard_map/ppermute | solution.py:511
  47.1 0.0 copy-start
  47.1 5.0 %adjoint_first.1 = (bf16[8,128,128]{2,1,0:T(8,128)(2,1)S(1)}, bf16[8,128,128]{2,1,0:T(8,128)(2,1)S(1)}, f32[32,128,128]{2,1,0:T(8,128)S(1)}, f32[16,128,128]{2,1,0:T(8,128)S(1)}) custom-call(f32[8,128,128]{2,1,0:T(8,128)} %bitcast.17, f32[8,128,128]{2,1,0:T(8,128)} %bitcast.25, f32[8,128,128]{2,1,0:T(8,128)} %speed_hbm.3, ...), custom_call_target="tpu_custom_call" | custom-call | flops 2000000000 | bytes 7200000 | tf_op jit(solution)/shard_map/adjoint_first/pallas_call | solution.py:43
  52.1 0.1 collective-permute-start.6
  52.2 2.9 %collective-permute-start.7 = (bf16[8,128,128]{2,1,0:T(8,128)(2,1)S(1)}, bf16[8,128,128]{2,1,0:T(8,128)(2,1)S(1)}, u32[]{:S(2)}, u32[]{:S(2)}) collective-permute-start(bf16[8,128,128]{2,1,0:T(8,128)(2,1)S(1)} %get-tuple-element.38), channel_id=1, source_target_pairs={{1,2},{2,1},{3,4},{4,3},{5,6},{6,5},{7,8},{8,7},{9,10},{10,9},{11,... | collective-permute-start | bytes 786440 | tf_op jit(solution)/shard_map/ppermute | solution.py:511
  55.1 0.0 collective-permute-done.got_a
  55.1 0.0 collective-permute-done.1.got_b
  55.2 0.0 copy-done
  55.2 3.7 %forward_first.1 = (bf16[8,128,128]{2,1,0:T(8,128)(2,1)S(1)}, bf16[8,128,128]{2,1,0:T(8,128)(2,1)S(1)}, f32[16,144,128]{2,1,0:T(8,128)S(1)}, f32[8,128,128]{2,1,...) custom-call(s32[1]{0:T(128)S(6)} %copy.15.depth_ref, ...), custom_call_target="tpu_custom_call" | custom-call | flops 2000000000 | bytes 7200000 | tf_op jit(solution)/shard_map/forward_first/pallas_call | solution.py:43
  58.9 1.1 %collective-permute-start.4 = (bf16[8,128,128]{2,1,0:T(8,128)(2,1)S(1)}, bf16[8,128,128]{2,1,0:T(8,128)(2,1)S(1)}, u32[]{:S(2)}, u32[]{:S(2)}) collective-permute-start(bf16[8,128,128]{2,1,0:T(8,128)(2,1)S(1)} %get-tuple-element.33), channel_id=1, source_target_pairs={{0,1},{1,0},{2,3},{3,2},{4,5},{5,4},{6,7},{7,6},{8,9},{9,8},{10,11... | collective-permute-start | bytes 786440 | tf_op jit(solution)/shard_map/ppermute | solution.py:511
  60.0 6.1 %collective-permute-start.5 = (bf16[8,128,128]{2,1,0:T(8,128)(2,1)S(1)}, bf16[8,128,128]{2,1,0:T(8,128)(2,1)S(1)}, u32[]{:S(2)}, u32[]{:S(2)}) collective-permute-start(bf16[8,128,128]{2,1,0:T(8,128)(2,1)S(1)} %get-tuple-element.34), channel_id=1, source_target_pairs={{1,2},{2,1},{3,4},{4,3},{5,6},{6,5},{7,8},{8,7},{9,10},{10,9},{11,... | collective-permute-start | bytes 786440 | tf_op jit(solution)/shard_map/ppermute | solution.py:511
  66.1 0.0 collective-permute-done.6.got_a
  66.1 0.0 collective-permute-done.7.got_b
  66.1 0.0 copy-start.1
  66.1 7.2 %middle.1 = (f32[8,128,128]{2,1,0:T(8,128)}, f32[8,128,128]{2,1,0:T(8,128)}, f32[8,128,128]{2,1,0:T(8,128)S(1)}, f32[8,128,128]{2,1,0:T(8,128)S(1)}) custom-call(s32[1]{0:T(128)S(6)} %copy.15.depth_ref, s32[1]{0:T(128)S(6)} %copy.16.row_ref, f32[1,3]{1,0:T(1,128)S(1)} %copy-done, f32[16,4,128,128]{3,2,1,0:T(8,128)} %get-tuple-element.29.inject_hbm, ...), custom_call_target="tpu_custom_call" | custom-call | flops 2000000000 | bytes 7200000 | tf_op jit(solution)/shard_map/middle/pallas_call | solution.py:43
  73.4 0.0 collective-permute-done.4.got_a
  73.4 0.0 collective-permute-done.5.got_b
  73.4 0.0 copy-done.1
  73.4 3.6 %forward_second.1 = (f32[2,8,32,128]{3,2,1,0:T(8,128)S(1)}, f32[2,8,32,128]{3,2,1,0:T(8,128)S(1)}) custom-call(s32[1]{0:T(128)S(6)} %copy.15.depth_ref, s32[1]{0:T(128)S(6)} %copy.16.row_ref, f32[1,3]{1,0:T(1,128)S(1)} %copy-done, bf16[8,128,128]{2,1,0:T(8,128)(2,1)S(1)} %collective-permute-done.4.got_a, ...), custom_call_target="tpu_custom_call" | custom-call | flops 2000000000 | bytes 7200000 | tf_op jit(solution)/shard_map/forward_second/pallas_call | solution.py:43
  77.0 0.1 collective-permute-start.8
  77.1 1.5 %collective-permute-done.8 = f32[2,8,32,128]{3,2,1,0:T(8,128)S(1)} collective-permute-done((f32[2,8,32,128]{3,2,1,0:T(8,128)S(1)}, f32[2,8,32,128]{3,2,1,0:T(8,128)S(1)}, u32[]{:S(2)}, u32[]{:S(2)}) %collective-permute-start.8) | collective-permute-done | bytes 262176 | tf_op jit(solution)/shard_map/ppermute | solution.py:578
  78.6 2.2 %collective-permute-start.9 = (f32[8,32,128]{2,1,0:T(8,128)S(1)}, f32[8,32,128]{2,1,0:T(8,128)S(1)}, u32[]{:S(2)}, u32[]{:S(2)}) collective-permute-start(f32[8,32,128]{2,1,0:T(8,128)S(1)} %fusion), channel_id=1, source_target_pairs={{0,128},{128,0},{64,192},{192,64},{1,129},{129,1},{65,193},{193,65... | collective-permute-start | bytes 393224 | tf_op jit(solution)/shard_map/ppermute | solution.py:579
  80.8 4.9 %collective-permute-done.9 = f32[8,32,128]{2,1,0:T(8,128)S(1)} collective-permute-done((f32[8,32,128]{2,1,0:T(8,128)S(1)}, f32[8,32,128]{2,1,0:T(8,128)S(1)}, u32[]{:S(2)}, u32[]{:S(2)}) %collective-permute-start.9) | collective-permute-done | bytes 131104 | tf_op jit(solution)/shard_map/ppermute | solution.py:579
  85.8 0.7 fusion.2
  (1 shorter events, 0.0 us)
Async XLA Ops:
  3.5 30.1 %all-to-all-start = ((bf16[64,32,128]{2,1,0:T(8,128)(2,1)}), bf16[64,32,128]{2,1,0:T(8,128)(2,1)S(1)}, u32[]{:S(2)}, u32[]{:S(2)}) async-start(bf16[64,32,128]{2,1,0:T(8,128)(2,1)} %gather.1), calls=%async_computation | async-start | bytes 1048576 | tf_op jit(solution)/shard_map/all_to_all | solution.py:529
  16.7 9.2 %copy-start.2 = (f32[1,4,1024]{2,1,0:T(4,128)S(1)}, f32[1,4,1024]{2,1,0:T(4,128)}, u32[]{:S(2)}) copy-start(f32[1,4,1024]{2,1,0:T(4,128)} %param.23) | copy-start | bytes 49156
  16.7 9.2 %copy-start.3 = (s32[1024]{0:T(1024)S(1)}, s32[1024]{0:T(1024)}, u32[]{:S(2)}) copy-start(s32[1024]{0:T(1024)} %param.21) | copy-start | bytes 12292
  16.7 9.2 %copy-start.4 = (s32[1024]{0:T(1024)S(1)}, s32[1024]{0:T(1024)}, u32[]{:S(2)}) copy-start(s32[1024]{0:T(1024)} %param.22) | copy-start | bytes 12292
  18.3 24.6 %collective-permute-start.2 = (bf16[19,128,128]{2,1,0:T(8,128)(2,1)S(1)}, bf16[19,128,128]{2,1,0:T(8,128)(2,1)S(1)}, u32[]{:S(2)}, u32[]{:S(2)}) collective-permute-start(bf16[19,128,128]{2,1,0:T(8,128)(2,1)S(1)} %get-tuple-element.30), channel_id=1, source_target_pairs={{0,1},{1,0},{2,3},{3,2},{4,5},{5,4},{6,7},{7,6},{8,9},{9,8},{10,11... | collective-permute-start | bytes 1867784 | tf_op jit(solution)/shard_map/ppermute | solution.py:511
  19.9 27.3 %collective-permute-start.3 = (bf16[19,128,128]{2,1,0:T(8,128)(2,1)S(1)}, bf16[19,128,128]{2,1,0:T(8,128)(2,1)S(1)}, u32[]{:S(2)}, u32[]{:S(2)}) collective-permute-start(bf16[19,128,128]{2,1,0:T(8,128)(2,1)S(1)} %get-tuple-element.31), channel_id=1, source_target_pairs={{1,2},{2,1},{3,4},{4,3},{5,6},{6,5},{7,8},{8,7},{9,10},{10,9},{11,... | collective-permute-start | bytes 1867784 | tf_op jit(solution)/shard_map/ppermute | solution.py:511
  26.0 7.6 %copy-start.5 = (s32[1,1,64]{2,1,0:T(1,128)S(1)}, s32[1,1,64]{2,1,0:T(1,128)}, u32[]{:S(2)}) copy-start(s32[1,1,64]{2,1,0:T(1,128)} %param.14) | copy-start | bytes 772
  34.2 20.9 %collective-permute-start = (bf16[12,128,128]{2,1,0:T(8,128)(2,1)S(1)}, bf16[12,128,128]{2,1,0:T(8,128)(2,1)S(1)}, u32[]{:S(2)}, u32[]{:S(2)}) collective-permute-start(bf16[12,128,128]{2,1,0:T(8,128)(2,1)S(1)} %get-tuple-element.27.mine_a), channel_id=1, source_target_pairs={{0,1},{1,0},{2,3},{3,2},{4,5},{5,4},{6,7},{7,6},{8,9},{9,8},{10,11... | collective-permute-start | bytes 1179656 | tf_op jit(solution)/shard_map/ppermute | solution.py:511
  35.7 19.5 %collective-permute-start.1 = (bf16[12,128,128]{2,1,0:T(8,128)(2,1)S(1)}, bf16[12,128,128]{2,1,0:T(8,128)(2,1)S(1)}, u32[]{:S(2)}, u32[]{:S(2)}) collective-permute-start(bf16[12,128,128]{2,1,0:T(8,128)(2,1)S(1)} %get-tuple-element.28.mine_b), channel_id=1, source_target_pairs={{1,2},{2,1},{3,4},{4,3},{5,6},{6,5},{7,8},{8,7},{9,10},{10,9},{11,... | collective-permute-start | bytes 1179656 | tf_op jit(solution)/shard_map/ppermute | solution.py:511
  47.1 8.0 %copy-start = (f32[1,3]{1,0:T(1,128)S(1)}, f32[1,3]{1,0:T(1,128)}, u32[]{:S(2)}) copy-start(f32[1,3]{1,0:T(1,128)} %wave_ref.5) | copy-start | bytes 40
  52.1 14.0 %collective-permute-start.6 = (bf16[8,128,128]{2,1,0:T(8,128)(2,1)S(1)}, bf16[8,128,128]{2,1,0:T(8,128)(2,1)S(1)}, u32[]{:S(2)}, u32[]{:S(2)}) collective-permute-start(bf16[8,128,128]{2,1,0:T(8,128)(2,1)S(1)} %get-tuple-element.37), channel_id=1, source_target_pairs={{0,1},{1,0},{2,3},{3,2},{4,5},{5,4},{6,7},{7,6},{8,9},{9,8},{10,11... | collective-permute-start | bytes 786440 | tf_op jit(solution)/shard_map/ppermute | solution.py:511
  52.2 13.9 %collective-permute-start.7 = (bf16[8,128,128]{2,1,0:T(8,128)(2,1)S(1)}, bf16[8,128,128]{2,1,0:T(8,128)(2,1)S(1)}, u32[]{:S(2)}, u32[]{:S(2)}) collective-permute-start(bf16[8,128,128]{2,1,0:T(8,128)(2,1)S(1)} %get-tuple-element.38), channel_id=1, source_target_pairs={{1,2},{2,1},{3,4},{4,3},{5,6},{6,5},{7,8},{8,7},{9,10},{10,9},{11,... | collective-permute-start | bytes 786440 | tf_op jit(solution)/shard_map/ppermute | solution.py:511
  58.9 14.5 %collective-permute-start.4 = (bf16[8,128,128]{2,1,0:T(8,128)(2,1)S(1)}, bf16[8,128,128]{2,1,0:T(8,128)(2,1)S(1)}, u32[]{:S(2)}, u32[]{:S(2)}) collective-permute-start(bf16[8,128,128]{2,1,0:T(8,128)(2,1)S(1)} %get-tuple-element.33), channel_id=1, source_target_pairs={{0,1},{1,0},{2,3},{3,2},{4,5},{5,4},{6,7},{7,6},{8,9},{9,8},{10,11... | collective-permute-start | bytes 786440 | tf_op jit(solution)/shard_map/ppermute | solution.py:511
  60.0 13.4 %collective-permute-start.5 = (bf16[8,128,128]{2,1,0:T(8,128)(2,1)S(1)}, bf16[8,128,128]{2,1,0:T(8,128)(2,1)S(1)}, u32[]{:S(2)}, u32[]{:S(2)}) collective-permute-start(bf16[8,128,128]{2,1,0:T(8,128)(2,1)S(1)} %get-tuple-element.34), channel_id=1, source_target_pairs={{1,2},{2,1},{3,4},{4,3},{5,6},{6,5},{7,8},{8,7},{9,10},{10,9},{11,... | collective-permute-start | bytes 786440 | tf_op jit(solution)/shard_map/ppermute | solution.py:511
  66.1 7.3 %copy-start.1 = (f32[1,8,128,128]{3,2,1,0:T(8,128)S(1)}, f32[1,8,128,128]{3,2,1,0:T(8,128)}, u32[]{:S(2)}) copy-start(f32[1,8,128,128]{3,2,1,0:T(8,128)} %param.17) | copy-start | bytes 1572868
  77.0 1.6 %collective-permute-start.8 = (f32[2,8,32,128]{3,2,1,0:T(8,128)S(1)}, f32[2,8,32,128]{3,2,1,0:T(8,128)S(1)}, u32[]{:S(2)}, u32[]{:S(2)}) collective-permute-start(f32[2,8,32,128]{3,2,1,0:T(8,128)S(1)} %get-tuple-element.46), channel_id=1, source_target_pairs={{0,64},{64,0},{128,192},{192,128},{1,65},{65,1},{129,193},{193,129... | collective-permute-start | bytes 786440 | tf_op jit(solution)/shard_map/ppermute | solution.py:578
  78.6 7.1 %collective-permute-start.9 = (f32[8,32,128]{2,1,0:T(8,128)S(1)}, f32[8,32,128]{2,1,0:T(8,128)S(1)}, u32[]{:S(2)}, u32[]{:S(2)}) collective-permute-start(f32[8,32,128]{2,1,0:T(8,128)S(1)} %fusion), channel_id=1, source_target_pairs={{0,128},{128,0},{64,192},{192,64},{1,129},{129,1},{65,193},{193,65... | collective-permute-start | bytes 393224 | tf_op jit(solution)/shard_map/ppermute | solution.py:579

commit v5 on v4

--- a/solution.py
+++ b/solution.py
@@ -156,12 +156,18 @@
 
 
 def gather_kernel(slot_hbm, parked_hbm, out_ref, held, slot_ref, parked_ref, sems):
-    for copy in fetch((slot_hbm, parked_hbm), (slot_ref, parked_ref), sems):
-        copy.wait()
+    width = parked_ref.shape[1] // 4
+    parts = [pl.ds(width * n, width) for n in range(4)]
+    slots, *copies = fetch(
+        [slot_hbm] + [parked_hbm.at[:, part] for part in parts], [slot_ref] + [parked_ref.at[:, part] for part in parts], sems
+    )
+    slots.wait()
     pieces = parked_ref.shape[0]
     row = lax.broadcasted_iota(jnp.int32, (pieces, pieces), 0)
     pick = jnp.where(row == slot_ref[...], 1.0, 0.0).astype(bf16)
     for col in range(32):
+        if col % 8 == 0:
+            copies[col // 8].wait()
         part = lax.dot_general(
             pick,
             parked_ref[:, col * NY : (col + 1) * NY],
@@ -249,21 +255,18 @@
 
 
 def adjoint_first_kernel(
-    now_hbm, next_hbm, speed_hbm, inject_hbm, got_a, got_b,
-    first_ref, second_ref, lam_ref, speed_ext,
-    buf4, q3_ref, now_halo, next_halo, now_ref, next_ref, inject_ref, sems,
+    now_ref, next_ref, speed_ref, inject_hbm, got_a, got_b,
+    first_ref, second_ref, lam_ref, speed_ext, q3_ref,
+    buf4, now_halo, next_halo, inject_ref, sems,
 ):
     par = parity()
     own = slice(HALF, HALF + DEPTH)
-    copies = fetch(
-        (speed_hbm, now_hbm, next_hbm, inject_hbm.at[:, 0:2]), (speed_ext.at[own], now_ref, next_ref, inject_ref), sems
-    )
+    (copy,) = fetch((inject_hbm.at[:, 0:2],), (inject_ref,), sems)
     zero_pads(buf4)
     zero_pads(q3_ref)
     weights = band()
     inner = slice(PAD, PAD + NX)
-    for copy in copies[:2]:
-        copy.wait()
+    speed_ext[own] = speed_ref[...]
     buf4[2 * HALF : 2 * HALF + DEPTH, inner, :] = now_ref[...] * speed_ext[own]
 
     def halo(lower, upper):
@@ -278,8 +281,7 @@
             )
 
     by_side(par, got_a, got_b, halo)
-    for copy in copies[2:]:
-        copy.wait()
+    copy.wait()
 
     def halo_lam3(h, row, lap):
         e = ext_of_halo(h)
@@ -385,22 +387,20 @@
 
 
 def middle_kernel(
-    depth_ref, row_ref, wave_ref, inject_hbm, got_a, got_b, lam_ref, speed_ext, u1_ref, base_ref, lap0_ref, lap1_ref,
-    late_ref, early_ref, u2_ref, grad_ref,
-    lam2_halo, buf2, buf1, inject_ref, sems,
+    depth_ref, row_ref, wave_ref, inject_hbm, got_a, got_b, lam_ref, q3_ref, speed_ext, u1_ref, base_ref, lap0_ref, lap1_ref,
+    late_ref, u2_ref, grad_ref, lam2_halo, buf2,
+    inject_ref, sems,
 ):
     par = parity()
-    (copy,) = fetch((inject_hbm.at[:, 2:4],), (inject_ref,), sems)
+    (copy,) = fetch((inject_hbm.at[HALF : HALF + DEPTH, 2],), (inject_ref,), sems)
     zero_pads(buf2)
-    zero_pads(buf1)
     weights = band()
     inner = slice(PAD, PAD + NX)
-    buf1[:, inner, :] = lam_ref[0:EXT] * speed_ext[...]
 
     def alone(h, row, lap):
         lam2_halo[h, rows(row), :] = lam_ref[EXT + DEPTH + h, rows(row), :] + lap
 
-    sweep_halo_alone(buf1, weights, alone)
+    sweep_halo_alone(q3_ref, weights, alone)
     copy.wait()
 
     def halo(lower, upper):
@@ -414,6 +414,37 @@
     by_side(par, got_a, got_b, halo)
     buf2[2 * HALF : 2 * HALF + DEPTH, inner, :] = lam_ref[EXT : EXT + DEPTH] * speed_ext[HALF : HALF + DEPTH]
 
+    def own_lam1(p, row, lap):
+        lam = 2.0 * lam_ref[EXT + p, rows(row), :] - lam_ref[p + HALF, rows(row), :] + lap
+        lam = lam + inject_ref[p, rows(row), :]
+        late_ref[p, rows(row), :] = lam
+        grad_ref[p, rows(row), :] = (
+            lam * lap0_ref[p, rows(row), :] + lam_ref[EXT + p, rows(row), :] * lap1_ref[p, rows(row), :]
+        )
+
+    sweep_own(buf2, 2 * HALF, weights, own_lam1)
+
+    def halo_u2(h, row, lap):
+        e = ext_of_halo(h)
+        u2_ref[h, rows(row), :] = base_ref[h, rows(row), :] + speed_ext[e, rows(row), :] * lap
+
+    sweep_halo_alone(u1_ref, weights, halo_u2)
+    local, across, along_y = source_place(depth_ref, row_ref)
+
+    @pl.when(((local >= 0) & (local < HALF)) | ((local >= HALF + DEPTH) & (local < EXT)))
+    def _():
+        add_cell(u2_ref, jnp.where(local < HALF, local, local - DEPTH), across, along_y, wave_ref[0, 1])
+
+
+def adjoint_last_kernel(
+    inject_hbm, late_ref, lam_ref, lam2_halo, buf2, speed_ext, order_hbm, early_ref, buf1, inject_ref, sems
+):
+    (copy,) = fetch((inject_hbm.at[:, 2:4],), (inject_ref,), sems)
+    zero_pads(buf1)
+    weights = band()
+    buf1[HALF : HALF + DEPTH, PAD : PAD + NX, :] = late_ref[...] * speed_ext[HALF : HALF + DEPTH]
+    copy.wait()
+
     def halo_lam1(h, row, lap):
         e = ext_of_halo(h)
         lam = 2.0 * lam2_halo[h, rows(row), :] - lam_ref[e, rows(row), :] + lap
@@ -422,33 +453,11 @@
 
     sweep_halo(buf2, weights, halo_lam1)
 
-    def own_lam1(p, row, lap):
-        lam = 2.0 * lam_ref[EXT + p, rows(row), :] - lam_ref[p + HALF, rows(row), :] + lap
-        lam = lam + inject_ref[p + HALF, 0, rows(row), :]
-        late_ref[p, rows(row), :] = lam
-        grad_ref[p, rows(row), :] = (
-            lam * lap0_ref[p, rows(row), :] + lam_ref[EXT + p, rows(row), :] * lap1_ref[p, rows(row), :]
-        )
-        buf1[p + HALF, padded(row), :] = lam * speed_ext[p + HALF, rows(row), :]
-
-    sweep_own(buf2, 2 * HALF, weights, own_lam1)
-
     def own_lam0(p, row, lap):
         lam = 2.0 * late_ref[p, rows(row), :] - lam_ref[EXT + p, rows(row), :] + lap
         early_ref[p, rows(row), :] = lam + inject_ref[p + HALF, 1, rows(row), :]
 
     sweep_own(buf1, HALF, weights, own_lam0)
-
-    def halo_u2(h, row, lap):
-        e = ext_of_halo(h)
-        u2_ref[h, rows(row), :] = base_ref[h, rows(row), :] + speed_ext[e, rows(row), :] * lap
-
-    sweep_halo_alone(u1_ref, weights, halo_u2)
-    local, across, along_y = source_place(depth_ref, row_ref)
-
-    @pl.when(((local >= 0) & (local < HALF)) | ((local >= HALF + DEPTH) & (local < EXT)))
-    def _():
-        add_cell(u2_ref, jnp.where(local < HALF, local, local - DEPTH), across, along_y, wave_ref[0, 1])
 
 
 def forward_second_kernel(
@@ -508,7 +517,11 @@
     peers = lax.axis_size("dom")
     even = [(i, i ^ 1) for i in range(peers)]
     odd = [(i, ((i + 1) ^ 1) - 1) for i in range(1, peers - 1)]
-    swap = lambda a, b: (lax.ppermute(a, "dom", even), lax.ppermute(b, "dom", odd))
+
+    def swap(a, b):
+        far = lax.ppermute(b, "dom", odd)
+        return lax.ppermute(a, "dom", even), far
+
     lam4, lam5 = adjoint_now[0], adjoint_next[0]
     ext = ((EXT, NX, NY), f32)
     slab = ((DEPTH, NX, NY), f32)
@@ -522,7 +535,7 @@
         gather_kernel, "gather", [HB] * 2, [((64, 32, NY), bf16)],
         [
             pltpu.VMEM((64 * 32, NY), f32), pltpu.VMEM((1, 64), jnp.int32), pltpu.VMEM((64, 4096), bf16),
-            pltpu.SemaphoreType.DMA((2,)),
+            pltpu.SemaphoreType.DMA((5,)),
         ],
         in_hbm(parked_slot[0], parked[0]),
     )
@@ -543,11 +556,11 @@
         (rec_depth.reshape(1, count), rec_row.reshape(1, count), residuals[0]), us=4,
     )
     fields = pltpu.VMEM((EXT, 2, NX, NY), f32)
-    send_a, send_b, lam23, speed_ext = call(
-        adjoint_first_kernel, "adjoint_first", [HB] * 4 + [VM] * 2,
-        [planes(8)] * 2 + [((EXT + 2 * DEPTH, NX, NY), f32), ext],
-        [buffer(WIDE), buffer(EXT)] + [pltpu.VMEM(*slab)] * 4 + [fields, pltpu.SemaphoreType.DMA((4,))],
-        in_hbm(lam4, lam5, speed_sq, inject) + (got_a, got_b),
+    send_a, send_b, lam23, speed_ext, q3 = call(
+        adjoint_first_kernel, "adjoint_first", [VM] * 3 + [HB] + [VM] * 2,
+        [planes(8)] * 2 + [((EXT + 2 * DEPTH, NX, NY), f32), ext, wide],
+        [buffer(WIDE), pltpu.VMEM(*slab), pltpu.VMEM(*slab), fields, pltpu.SemaphoreType.DMA((1,))],
+        (lam4, lam5, speed_sq) + in_hbm(inject) + (got_a, got_b),
     )
     back_a, back_b = swap(send_a, send_b)
 
@@ -563,11 +576,11 @@
         (src_depth, src_row, wavelet, mine_a, mine_b, got_a, got_b, speed_ext),
     )
     got_a, got_b = swap(send_a, send_b)
-    late, early, u2_halo, grad = call(
-        middle_kernel, "middle", [SM] * 3 + [HB] + [VM] * 8, [slab] * 4,
-        [pltpu.VMEM(*slab), buffer(WIDE), buffer(EXT), fields, pltpu.SemaphoreType.DMA((1,))],
+    late, u2_halo, grad, lam2_halo, q2 = call(
+        middle_kernel, "middle", [SM] * 3 + [HB] + [VM] * 9, [slab] * 4 + [((WIDE, ROWS, NY), f32)],
+        [pltpu.VMEM(*slab), pltpu.SemaphoreType.DMA((1,))],
         (src_depth, src_row, wavelet) + in_hbm(inject)
-        + (back_a, back_b, lam23, speed_ext, u1, base_u, lap0, lap1),
+        + (back_a, back_b, lam23, q3, speed_ext, u1, base_u, lap0, lap1),
     )
     quarter = ((2, DEPTH, NX // 4, NY), f32)
     keep, send = call(
@@ -576,7 +589,13 @@
         (src_depth, src_row, wavelet, got_a, got_b, u1, u2, u2_halo, speed_ext, lam23, lam4, grad),
     )
     got = lax.ppermute(send, "shot", [(0, 1), (1, 0), (2, 3), (3, 2)])
-    other = lax.ppermute(keep[1] + got[1], "shot", [(0, 2), (2, 0), (1, 3), (3, 1)])
+    part = keep[1] + got[1]
+    other = lax.ppermute(part, "shot", [(0, 2), (2, 0), (1, 3), (3, 1)])
+    (early,) = call(
+        adjoint_last_kernel, "adjoint_last", [HB] + [VM] * 5 + [HB], [slab],
+        [buffer(EXT), fields, pltpu.SemaphoreType.DMA((1,))],
+        in_hbm(inject) + (late, lam23, lam2_halo, q2, speed_ext) + in_hbm(part),
+    )
     gradient = keep[0] + got[0] + other
     return (gradient, late[None], early[None])
 

time: 86.8 us -> 85.7 us (0.987)
  waiting for transfers between devices: 11 us -> 8.41 us
  Pallas kernels: 31.7 us -> 33.1 us
    ppermute x9, waiting for transfers between devices: 9.12 us -> 6.5 us  [the longest x4 5.85 us: swap(): far = lax.ppermute(b, 'dom', odd)]
    pallas_call x8 -> x9, Pallas kernels: 31.7 us -> 33.1 us  [call(): pl.pallas_call(kernel, name=name, out_shape=[pltpu.HBM(*o) if name == 'in...]
  transfers between devices with their start and end apart: 11 -> 11, of which waited for: 4 -> 5; matrix products, arithmetic and copies ran while one was open for 0% -> 0% of each run, Pallas kernels for 29% -> 31%
where the time goes in v5:
time: 85.7 us; the launch traced here: 85.3 us
  starting transfers between devices  40.8 us (48%)
  Pallas kernels  33.1 us (39%)
  waiting for transfers between devices  8.41 us (10%)
  between operations  2.19 us (3%)
    pallas_call x9, Pallas kernels, call(): pl.pallas_call(kernel, name=name, out_shape=[pltpu.HBM(*o) if name == 'in...  33.1 us
    ppermute x4, starting transfers between devices, swap(): far = lax.ppermute(b, 'dom', odd)  21.1 us
    all_to_all x1, starting transfers between devices, per_device(): lax.all_to_all(outgoing, 'dom', split_axis=0, concat_axis=0, tiled=True)  13.2 us
    ppermute x4, waiting for transfers between devices, swap(): far = lax.ppermute(b, 'dom', odd)  5.85 us
    ppermute x4, starting transfers between devices, swap(): return (lax.ppermute(a, 'dom', even), far)  4.17 us
    ppermute x1, starting transfers between devices, per_device(): other = lax.ppermute(part, 'shot', [(0, 2), (2, 0), (1, 3), (3, 1)])  2.22 us
  transfers between devices with their start and end apart: 11, of which 5 were waited for; matrix products, arithmetic and copies ran while one was open for 0% of the time, Pallas kernels for 31%

profile of v5, /device:TPU:2, one launch (start us, length us, event | category | flops | bytes accessed | tf_op | source)
XLA Modules:
  0.0 85.3 jit_solution(4563135795421598197)
XLA Ops:
  0.6 3.1 %gather.1 = bf16[64,32,128]{2,1,0:T(8,128)(2,1)} custom-call(s32[1,64]{1,0:T(1,128)} %bitcast.28, bf16[64,4096]{1,0:T(8,128)(2,1)} %bitcast.27), custom_call_target="tpu_custom_call" | custom-call | flops 2000000000 | bytes 7200000 | tf_op jit(solution)/shard_map/gather/pallas_call | solution.py:43
  3.7 13.2 %all-to-all-start = ((bf16[64,32,128]{2,1,0:T(8,128)(2,1)}), bf16[64,32,128]{2,1,0:T(8,128)(2,1)S(1)}, u32[]{:S(2)}, u32[]{:S(2)}) async-start(bf16[64,32,128]{2,1,0:T(8,128)(2,1)} %gather.1), calls=%async_computation | async-start | bytes 1048576 | tf_op jit(solution)/shard_map/all_to_all | solution.py:542
  16.9 0.0 copy-start.5
  16.9 0.0 copy-start.6
  17.0 0.0 copy-start.7
  17.0 1.5 %adjoint_pack.1 = (bf16[19,128,128]{2,1,0:T(8,128)(2,1)S(1)}, bf16[19,128,128]{2,1,0:T(8,128)(2,1)S(1)}) custom-call(f32[8,128,128]{2,1,0:T(8,128)} %bitcast.19, f32[8,128,128]{2,1,0:T(8,128)} %bitcast.17, f32[8,128,128]{2,1,0:T(8,128)} %speed_ref.1), custom_call_target="tpu_custom_call" | custom-call | flops 2000000000 | bytes 7200000 | tf_op jit(solution)/shard_map/adjoint_pack/pallas_call | solution.py:43
  18.5 1.6 %collective-permute-start.2 = (bf16[19,128,128]{2,1,0:T(8,128)(2,1)S(1)}, bf16[19,128,128]{2,1,0:T(8,128)(2,1)S(1)}, u32[]{:S(2)}, u32[]{:S(2)}) collective-permute-start(bf16[19,128,128]{2,1,0:T(8,128)(2,1)S(1)} %get-tuple-element.32), channel_id=1, source_target_pairs={{0,1},{1,0},{2,3},{3,2},{4,5},{5,4},{6,7},{7,6},{8,9},{9,8},{10,11... | collective-permute-start | bytes 1867784 | tf_op jit(solution)/shard_map/ppermute | solution.py:523
  20.1 6.1 %collective-permute-start.3 = (bf16[19,128,128]{2,1,0:T(8,128)(2,1)S(1)}, bf16[19,128,128]{2,1,0:T(8,128)(2,1)S(1)}, u32[]{:S(2)}, u32[]{:S(2)}) collective-permute-start(bf16[19,128,128]{2,1,0:T(8,128)(2,1)S(1)} %get-tuple-element.33), channel_id=1, source_target_pairs={{1,2},{2,1},{3,4},{4,3},{5,6},{6,5},{7,8},{8,7},{9,10},{10,9},{11,... | collective-permute-start | bytes 1867784 | tf_op jit(solution)/shard_map/ppermute | solution.py:522
  26.1 0.0 copy-done.5
  26.1 0.0 copy-done.6
  26.2 0.0 copy-done.7
  26.2 0.0 copy-start.8
  26.2 7.2 %inject.1 = (f32[16,4,128,128]{3,2,1,0:T(8,128)}, f32[8,128]{1,0:T(8,128)}) custom-call(s32[1,1024]{1,0:T(1,128)S(1)} %bitcast.23, s32[1,1024]{1,0:T(1,128)S(1)} %bitcast.24, f32[4,1024]{1,0:T(4,128)S(1)} %bitcast.22), custom_call_target="tpu_custom_call" | custom-call | flops 4000000000 | bytes 14400000 | tf_op jit(solution)/shard_map/inject/pallas_call | solution.py:43
  33.4 0.4 all-to-all-done.pieces_ref
  33.8 0.0 copy-done.8
  33.8 0.7 forward_pack.1
  34.5 1.4 %collective-permute-start = (bf16[12,128,128]{2,1,0:T(8,128)(2,1)S(1)}, bf16[12,128,128]{2,1,0:T(8,128)(2,1)S(1)}, u32[]{:S(2)}, u32[]{:S(2)}) collective-permute-start(bf16[12,128,128]{2,1,0:T(8,128)(2,1)S(1)} %get-tuple-element.29.mine_a), channel_id=1, source_target_pairs={{0,1},{1,0},{2,3},{3,2},{4,5},{5,4},{6,7},{7,6},{8,9},{9,8},{10,11... | collective-permute-start | bytes 1179656 | tf_op jit(solution)/shard_map/ppermute | solution.py:523
  35.9 6.0 %collective-permute-start.1 = (bf16[12,128,128]{2,1,0:T(8,128)(2,1)S(1)}, bf16[12,128,128]{2,1,0:T(8,128)(2,1)S(1)}, u32[]{:S(2)}, u32[]{:S(2)}) collective-permute-start(bf16[12,128,128]{2,1,0:T(8,128)(2,1)S(1)} %get-tuple-element.30.mine_b), channel_id=1, source_target_pairs={{1,2},{2,1},{3,4},{4,3},{5,6},{6,5},{7,8},{8,7},{9,10},{10,9},{11,... | collective-permute-start | bytes 1179656 | tf_op jit(solution)/shard_map/ppermute | solution.py:522
  43.2 0.0 collective-permute-done.2.got_a
  43.2 4.2 %collective-permute-done.3.got_b = bf16[19,128,128]{2,1,0:T(8,128)(2,1)S(1)} collective-permute-done((bf16[19,128,128]{2,1,0:T(8,128)(2,1)S(1)}, bf16[19,128,128]{2,1,0:T(8,128)(2,1)S(1)}, u32[]{:S(2)}, u32[]{:S(2)}) %collective-permute-start.3) | collective-permute-done | bytes 622624 | tf_op jit(solution)/shard_map/ppermute | solution.py:522
  47.3 0.0 copy-done.2
  47.4 0.0 copy-done.3
  47.4 0.0 copy-done.4
  47.4 0.0 copy-start.1
  47.4 4.6 %adjoint_first.1 = (bf16[8,128,128]{2,1,0:T(8,128)(2,1)S(1)}, bf16[8,128,128]{2,1,0:T(8,128)(2,1)S(1)}, f32[32,128,128]{2,1,0:T(8,128)S(1)}, f32[16,128,128]{2,1,0:T(8,128)S(1)}, f32[16,144,128]{2,1,0:T(8,128)S(1)}) custom-call(f32[8,128,128]{2,1,0:T(8,128)S(1)} %bitcast.20, f32[8,128,128]{2,1,0:T(8,128)S(1)} %bitcast.18, f32[8,128,128]{2,1,0:T(8,128)S(1)} %copy-done.3, ...), custom_call_target="tpu_custom_call" | custom-call | flops 2000000000 | bytes 7200000 | tf_op jit(solution)/shard_map/adjoint_first/pallas_call | solution.py:43
  51.9 0.1 collective-permute-start.6
  52.0 2.9 %collective-permute-start.7 = (bf16[8,128,128]{2,1,0:T(8,128)(2,1)S(1)}, bf16[8,128,128]{2,1,0:T(8,128)(2,1)S(1)}, u32[]{:S(2)}, u32[]{:S(2)}) collective-permute-start(bf16[8,128,128]{2,1,0:T(8,128)(2,1)S(1)} %get-tuple-element.40), channel_id=1, source_target_pairs={{1,2},{2,1},{3,4},{4,3},{5,6},{6,5},{7,8},{8,7},{9,10},{10,9},{11,... | collective-permute-start | bytes 786440 | tf_op jit(solution)/shard_map/ppermute | solution.py:522
  55.0 0.0 collective-permute-done.got_a
  55.0 0.0 collective-permute-done.1.got_b
  55.0 0.0 copy-done.1
  55.0 3.7 %forward_first.1 = (bf16[8,128,128]{2,1,0:T(8,128)(2,1)S(1)}, bf16[8,128,128]{2,1,0:T(8,128)(2,1)S(1)}, f32[16,144,128]{2,1,0:T(8,128)S(1)}, f32[8,128,128]{2,1,...) custom-call(s32[1]{0:T(128)S(6)} %copy.15.depth_ref, ...), custom_call_target="tpu_custom_call" | custom-call | flops 2000000000 | bytes 7200000 | tf_op jit(solution)/shard_map/forward_first/pallas_call | solution.py:43
  58.7 1.1 %collective-permute-start.4 = (bf16[8,128,128]{2,1,0:T(8,128)(2,1)S(1)}, bf16[8,128,128]{2,1,0:T(8,128)(2,1)S(1)}, u32[]{:S(2)}, u32[]{:S(2)}) collective-permute-start(bf16[8,128,128]{2,1,0:T(8,128)(2,1)S(1)} %get-tuple-element.35), channel_id=1, source_target_pairs={{0,1},{1,0},{2,3},{3,2},{4,5},{5,4},{6,7},{7,6},{8,9},{9,8},{10,11... | collective-permute-start | bytes 786440 | tf_op jit(solution)/shard_map/ppermute | solution.py:523
  59.8 6.2 %collective-permute-start.5 = (bf16[8,128,128]{2,1,0:T(8,128)(2,1)S(1)}, bf16[8,128,128]{2,1,0:T(8,128)(2,1)S(1)}, u32[]{:S(2)}, u32[]{:S(2)}) collective-permute-start(bf16[8,128,128]{2,1,0:T(8,128)(2,1)S(1)} %get-tuple-element.36), channel_id=1, source_target_pairs={{1,2},{2,1},{3,4},{4,3},{5,6},{6,5},{7,8},{8,7},{9,10},{10,9},{11,... | collective-permute-start | bytes 786440 | tf_op jit(solution)/shard_map/ppermute | solution.py:522
  65.9 0.0 collective-permute-done.6.got_a
  66.0 0.0 collective-permute-done.7.got_b
  66.0 4.6 %middle.1 = (f32[8,128,128]{2,1,0:T(8,128)}, f32[8,128,128]{2,1,0:T(8,128)S(1)}, f32[8,128,128]{2,1,0:T(8,128)S(1)}, f32[8,128,128]{2,1,0:T(8,128)S(1)}, f32[24,144,128]{2,1,0:T(8,128)S(1)}) custom-call(s32[1]{0:T(128)S(6)} %copy.15.depth_ref, s32[1]{0:T(128)S(6)} %copy.16.row_ref, f32[1,3]{1,0:T(1,128)S(1)} %copy-done.1, ...), custom_call_target="tpu_custom_call" | custom-call | flops 2000000000 | bytes 7200000 | tf_op jit(solution)/shard_map/middle/pallas_call | solution.py:43
  70.6 0.0 collective-permute-done.4.got_a
  70.6 1.7 %collective-permute-done.5.got_b = bf16[8,128,128]{2,1,0:T(8,128)(2,1)S(1)} collective-permute-done((bf16[8,128,128]{2,1,0:T(8,128)(2,1)S(1)}, bf16[8,128,128]{2,1,0:T(8,128)(2,1)S(1)}, u32[]{:S(2)}, u32[]{:S(2)}) %collective-permute-start.5) | collective-permute-done | bytes 262176 | tf_op jit(solution)/shard_map/ppermute | solution.py:522
  72.3 3.6 %forward_second.1 = (f32[2,8,32,128]{3,2,1,0:T(8,128)S(1)}, f32[2,8,32,128]{3,2,1,0:T(8,128)S(1)}) custom-call(s32[1]{0:T(128)S(6)} %copy.15.depth_ref, s32[1]{0:T(128)S(6)} %copy.16.row_ref, f32[1,3]{1,0:T(1,128)S(1)} %copy-done.1, bf16[8,128,128]{2,1,0:T(8,128)(2,1)S(1)} %collective-permute-done.4.got_a, ...), custom_call_target="tpu_custom_call" | custom-call | flops 2000000000 | bytes 7200000 | tf_op jit(solution)/shard_map/forward_second/pallas_call | solution.py:43
  75.8 0.1 collective-permute-start.8
  75.9 1.5 %collective-permute-done.8 = f32[2,8,32,128]{3,2,1,0:T(8,128)S(1)} collective-permute-done((f32[2,8,32,128]{3,2,1,0:T(8,128)S(1)}, f32[2,8,32,128]{3,2,1,0:T(8,128)S(1)}, u32[]{:S(2)}, u32[]{:S(2)}) %collective-permute-start.8) | collective-permute-done | bytes 262176 | tf_op jit(solution)/shard_map/ppermute | solution.py:591
  77.5 0.0 copy-start.9
  77.5 2.2 %collective-permute-start.9 = (f32[8,32,128]{2,1,0:T(8,128)S(1)}, f32[8,32,128]{2,1,0:T(8,128)S(1)}, u32[]{:S(2)}, u32[]{:S(2)}) collective-permute-start(f32[8,32,128]{2,1,0:T(8,128)S(1)} %fusion.order_hbm), channel_id=1, source_target_pairs={{0,128},{128,0},{64,192},{192,64},{1,129},{129,1},{65,193},{193,65... | collective-permute-start | bytes 393224 | tf_op jit(solution)/shard_map/ppermute | solution.py:593
  79.7 0.0 copy-done.9
  79.7 0.0 copy-done
  79.7 4.3 %adjoint_last.1 = f32[8,128,128]{2,1,0:T(8,128)} custom-call(f32[16,4,128,128]{3,2,1,0:T(8,128)} %get-tuple-element.31.inject_hbm, f32[8,128,128]{2,1,0:T(8,128)S(1)} %copy-done, f32[32,128,128]{2,1,0:T(8,128)S(1)} %get-tuple-element.41.lam_ref.lam3_ref, f32[8,128,128]{2,1,0:T(8,128)S(1)} %get-tuple-element.51.lam2_halo, ...), custom_call_target="tpu_custom_call" | custom-call | flops 2000000000 | bytes 7200000 | tf_op jit(solution)/shard_map/adjoint_last/pallas_call | solution.py:43
  84.0 0.6 collective-permute-done.9
  84.6 0.7 fusion.2
  (5 shorter events, 0.0 us)
Async XLA Ops:
  3.7 30.1 %all-to-all-start = ((bf16[64,32,128]{2,1,0:T(8,128)(2,1)}), bf16[64,32,128]{2,1,0:T(8,128)(2,1)S(1)}, u32[]{:S(2)}, u32[]{:S(2)}) async-start(bf16[64,32,128]{2,1,0:T(8,128)(2,1)} %gather.1), calls=%async_computation | async-start | bytes 1048576 | tf_op jit(solution)/shard_map/all_to_all | solution.py:542
  16.9 9.2 %copy-start.5 = (f32[1,4,1024]{2,1,0:T(4,128)S(1)}, f32[1,4,1024]{2,1,0:T(4,128)}, u32[]{:S(2)}) copy-start(f32[1,4,1024]{2,1,0:T(4,128)} %param.23) | copy-start | bytes 49156
  16.9 9.2 %copy-start.6 = (s32[1024]{0:T(1024)S(1)}, s32[1024]{0:T(1024)}, u32[]{:S(2)}) copy-start(s32[1024]{0:T(1024)} %param.21) | copy-start | bytes 12292
  17.0 9.2 %copy-start.7 = (s32[1024]{0:T(1024)S(1)}, s32[1024]{0:T(1024)}, u32[]{:S(2)}) copy-start(s32[1024]{0:T(1024)} %param.22) | copy-start | bytes 12292
  18.5 24.6 %collective-permute-start.2 = (bf16[19,128,128]{2,1,0:T(8,128)(2,1)S(1)}, bf16[19,128,128]{2,1,0:T(8,128)(2,1)S(1)}, u32[]{:S(2)}, u32[]{:S(2)}) collective-permute-start(bf16[19,128,128]{2,1,0:T(8,128)(2,1)S(1)} %get-tuple-element.32), channel_id=1, source_target_pairs={{0,1},{1,0},{2,3},{3,2},{4,5},{5,4},{6,7},{7,6},{8,9},{9,8},{10,11... | collective-permute-start | bytes 1867784 | tf_op jit(solution)/shard_map/ppermute | solution.py:523
  20.1 27.3 %collective-permute-start.3 = (bf16[19,128,128]{2,1,0:T(8,128)(2,1)S(1)}, bf16[19,128,128]{2,1,0:T(8,128)(2,1)S(1)}, u32[]{:S(2)}, u32[]{:S(2)}) collective-permute-start(bf16[19,128,128]{2,1,0:T(8,128)(2,1)S(1)} %get-tuple-element.33), channel_id=1, source_target_pairs={{1,2},{2,1},{3,4},{4,3},{5,6},{6,5},{7,8},{8,7},{9,10},{10,9},{11,... | collective-permute-start | bytes 1867784 | tf_op jit(solution)/shard_map/ppermute | solution.py:522
  26.2 7.6 %copy-start.8 = (s32[1,1,64]{2,1,0:T(1,128)S(1)}, s32[1,1,64]{2,1,0:T(1,128)}, u32[]{:S(2)}) copy-start(s32[1,1,64]{2,1,0:T(1,128)} %param.14) | copy-start | bytes 772
  33.8 13.6 %copy-start.2 = (f32[1,8,128,128]{3,2,1,0:T(8,128)S(1)}, f32[1,8,128,128]{3,2,1,0:T(8,128)}, u32[]{:S(2)}) copy-start(f32[1,8,128,128]{3,2,1,0:T(8,128)} %param.16) | copy-start | bytes 1572868
  33.8 13.6 %copy-start.3 = (f32[8,128,128]{2,1,0:T(8,128)S(1)}, f32[8,128,128]{2,1,0:T(8,128)}, u32[]{:S(2)}) copy-start(f32[8,128,128]{2,1,0:T(8,128)} %speed_ref.1) | copy-start | bytes 1572868
  33.8 13.6 %copy-start.4 = (f32[1,8,128,128]{3,2,1,0:T(8,128)S(1)}, f32[1,8,128,128]{3,2,1,0:T(8,128)}, u32[]{:S(2)}) copy-start(f32[1,8,128,128]{3,2,1,0:T(8,128)} %param.17) | copy-start | bytes 1572868
  34.5 20.5 %collective-permute-start = (bf16[12,128,128]{2,1,0:T(8,128)(2,1)S(1)}, bf16[12,128,128]{2,1,0:T(8,128)(2,1)S(1)}, u32[]{:S(2)}, u32[]{:S(2)}) collective-permute-start(bf16[12,128,128]{2,1,0:T(8,128)(2,1)S(1)} %get-tuple-element.29.mine_a), channel_id=1, source_target_pairs={{0,1},{1,0},{2,3},{3,2},{4,5},{5,4},{6,7},{7,6},{8,9},{9,8},{10,11... | collective-permute-start | bytes 1179656 | tf_op jit(solution)/shard_map/ppermute | solution.py:523
  35.9 19.1 %collective-permute-start.1 = (bf16[12,128,128]{2,1,0:T(8,128)(2,1)S(1)}, bf16[12,128,128]{2,1,0:T(8,128)(2,1)S(1)}, u32[]{:S(2)}, u32[]{:S(2)}) collective-permute-start(bf16[12,128,128]{2,1,0:T(8,128)(2,1)S(1)} %get-tuple-element.30.mine_b), channel_id=1, source_target_pairs={{1,2},{2,1},{3,4},{4,3},{5,6},{6,5},{7,8},{8,7},{9,10},{10,9},{11,... | collective-permute-start | bytes 1179656 | tf_op jit(solution)/shard_map/ppermute | solution.py:522
  47.4 7.6 %copy-start.1 = (f32[1,3]{1,0:T(1,128)S(1)}, f32[1,3]{1,0:T(1,128)}, u32[]{:S(2)}) copy-start(f32[1,3]{1,0:T(1,128)} %wave_ref.5) | copy-start | bytes 40
  51.9 14.0 %collective-permute-start.6 = (bf16[8,128,128]{2,1,0:T(8,128)(2,1)S(1)}, bf16[8,128,128]{2,1,0:T(8,128)(2,1)S(1)}, u32[]{:S(2)}, u32[]{:S(2)}) collective-permute-start(bf16[8,128,128]{2,1,0:T(8,128)(2,1)S(1)} %get-tuple-element.39), channel_id=1, source_target_pairs={{0,1},{1,0},{2,3},{3,2},{4,5},{5,4},{6,7},{7,6},{8,9},{9,8},{10,11... | collective-permute-start | bytes 786440 | tf_op jit(solution)/shard_map/ppermute | solution.py:523
  52.0 13.9 %collective-permute-start.7 = (bf16[8,128,128]{2,1,0:T(8,128)(2,1)S(1)}, bf16[8,128,128]{2,1,0:T(8,128)(2,1)S(1)}, u32[]{:S(2)}, u32[]{:S(2)}) collective-permute-start(bf16[8,128,128]{2,1,0:T(8,128)(2,1)S(1)} %get-tuple-element.40), channel_id=1, source_target_pairs={{1,2},{2,1},{3,4},{4,3},{5,6},{6,5},{7,8},{8,7},{9,10},{10,9},{11,... | collective-permute-start | bytes 786440 | tf_op jit(solution)/shard_map/ppermute | solution.py:522
  58.7 11.9 %collective-permute-start.4 = (bf16[8,128,128]{2,1,0:T(8,128)(2,1)S(1)}, bf16[8,128,128]{2,1,0:T(8,128)(2,1)S(1)}, u32[]{:S(2)}, u32[]{:S(2)}) collective-permute-start(bf16[8,128,128]{2,1,0:T(8,128)(2,1)S(1)} %get-tuple-element.35), channel_id=1, source_target_pairs={{0,1},{1,0},{2,3},{3,2},{4,5},{5,4},{6,7},{7,6},{8,9},{9,8},{10,11... | collective-permute-start | bytes 786440 | tf_op jit(solution)/shard_map/ppermute | solution.py:523
  59.8 12.5 %collective-permute-start.5 = (bf16[8,128,128]{2,1,0:T(8,128)(2,1)S(1)}, bf16[8,128,128]{2,1,0:T(8,128)(2,1)S(1)}, u32[]{:S(2)}, u32[]{:S(2)}) collective-permute-start(bf16[8,128,128]{2,1,0:T(8,128)(2,1)S(1)} %get-tuple-element.36), channel_id=1, source_target_pairs={{1,2},{2,1},{3,4},{4,3},{5,6},{6,5},{7,8},{8,7},{9,10},{10,9},{11,... | collective-permute-start | bytes 786440 | tf_op jit(solution)/shard_map/ppermute | solution.py:522
  72.2 7.5 %copy-start = (f32[8,128,128]{2,1,0:T(8,128)S(1)}, f32[8,128,128]{2,1,0:T(8,128)}, u32[]{:S(2)}) copy-start(f32[8,128,128]{2,1,0:T(8,128)} %get-tuple-element.50.late_ref) | copy-start | bytes 1572868
  75.8 1.6 %collective-permute-start.8 = (f32[2,8,32,128]{3,2,1,0:T(8,128)S(1)}, f32[2,8,32,128]{3,2,1,0:T(8,128)S(1)}, u32[]{:S(2)}, u32[]{:S(2)}) collective-permute-start(f32[2,8,32,128]{3,2,1,0:T(8,128)S(1)} %get-tuple-element.49), channel_id=1, source_target_pairs={{0,64},{64,0},{128,192},{192,128},{1,65},{65,1},{129,193},{193,129... | collective-permute-start | bytes 786440 | tf_op jit(solution)/shard_map/ppermute | solution.py:591
  77.5 2.2 %copy-start.9 = (f32[8,32,128]{2,1,0:T(8,128)}, f32[8,32,128]{2,1,0:T(8,128)S(1)}, u32[]{:S(2)}) copy-start(f32[8,32,128]{2,1,0:T(8,128)S(1)} %fusion.order_hbm) | copy-start | bytes 393220
  77.5 7.1 %collective-permute-start.9 = (f32[8,32,128]{2,1,0:T(8,128)S(1)}, f32[8,32,128]{2,1,0:T(8,128)S(1)}, u32[]{:S(2)}, u32[]{:S(2)}) collective-permute-start(f32[8,32,128]{2,1,0:T(8,128)S(1)} %fusion.order_hbm), channel_id=1, source_target_pairs={{0,128},{128,0},{64,192},{192,64},{1,129},{129,1},{65,193},{193,65... | collective-permute-start | bytes 393224 | tf_op jit(solution)/shard_map/ppermute | solution.py:593

commit v6 on v5

--- a/solution.py
+++ b/solution.py
@@ -39,13 +39,13 @@
     return copies
 
 
-def call(kernel, name, ins, outs, scratch, args, us=2, limit=20 << 20):
+def call(kernel, name, ins, outs, scratch, args, us=2, limit=20 << 20, out=VM):
     return pl.pallas_call(
         kernel,
         name=name,
-        out_shape=[pltpu.HBM(*o) if name == "inject" else jax.ShapeDtypeStruct(*o) for o in outs],
+        out_shape=[pltpu.HBM(*o) if out is HB else jax.ShapeDtypeStruct(*o) for o in outs],
         in_specs=ins,
-        out_specs=[HB if name == "inject" else VM] * len(outs),
+        out_specs=[out] * len(outs),
         scratch_shapes=scratch,
         compiler_params=pltpu.CompilerParams(vmem_limit_bytes=limit),
         cost_estimate=pl.CostEstimate(flops=us * 10**9, bytes_accessed=us * 3_600_000, transcendentals=0),
@@ -131,6 +131,33 @@
         )
 
 
+def sweep_own_alone(buf, weights, body):
+    for g in range(DEPTH // GROUP):
+        group_laps(buf, g * GROUP, weights, lambda j, row, lap, g=g: body(g * GROUP + j, row, lap))
+
+
+def fill_side(buf, upper, near, far, own):
+    inner = slice(PAD, PAD + NX)
+    for j in range(HALF):
+        buf[HALF + j, inner, :] = near(j)
+        buf[2 * HALF + j if upper else j, inner, :] = far(j)
+        buf[j if upper else 2 * HALF + j, inner, :] = own(HALF + j if upper else j)
+
+
+def side_terms(buf, upper, p, row):
+    total = None
+    for k in range(1, HALF + 1):
+        q = p - HALF + k if upper else 2 * HALF + p - k
+        if HALF <= q < 2 * HALF:
+            term = stencil_coef[k] * buf[q, padded(row), :]
+            total = term if total is None else total + term
+    return total
+
+
+def side_planes(upper):
+    return range(HALF, DEPTH) if upper else range(HALF)
+
+
 def ext_of_halo(h):
     return h + DEPTH * (h // HALF) if isinstance(h, int) else jnp.where(h < HALF, h, h + DEPTH)
 
@@ -155,27 +182,29 @@
         body(first, second)
 
 
-def gather_kernel(slot_hbm, parked_hbm, out_ref, held, slot_ref, parked_ref, sems):
-    width = parked_ref.shape[1] // 4
-    parts = [pl.ds(width * n, width) for n in range(4)]
+def gather_kernel(slot_hbm, parked_hbm, out_hbm, held, slot_ref, parked_ref, staged, sems, out_sems):
+    count, parts = parked_ref.shape[0], 4
+    width, lines = parked_ref.shape[1] // parts, 32 // parts
+    columns = [pl.ds(width * n, width) for n in range(parts)]
     slots, *copies = fetch(
-        [slot_hbm] + [parked_hbm.at[:, part] for part in parts], [slot_ref] + [parked_ref.at[:, part] for part in parts], sems
+        [slot_hbm] + [parked_hbm.at[:, c] for c in columns], [slot_ref] + [parked_ref.at[:, c] for c in columns], sems
     )
     slots.wait()
-    pieces = parked_ref.shape[0]
-    row = lax.broadcasted_iota(jnp.int32, (pieces, pieces), 0)
+    row = lax.broadcasted_iota(jnp.int32, (count, count), 0)
     pick = jnp.where(row == slot_ref[...], 1.0, 0.0).astype(bf16)
-    for col in range(32):
-        if col % 8 == 0:
-            copies[col // 8].wait()
-        part = lax.dot_general(
-            pick,
-            parked_ref[:, col * NY : (col + 1) * NY],
-            (((0,), (0,)), ((), ())),
-            preferred_element_type=f32,
-        )
-        held[pl.ds(col, pieces, stride=32), :] = part
-    out_ref[...] = held[...].reshape(pieces, 32, NY).astype(bf16)
+    stores = []
+    for n in range(parts):
+        copies[n].wait()
+        for line in range(lines):
+            at = n * width + line * NY
+            held[n, pl.ds(line, count, stride=lines), :] = lax.dot_general(
+                pick, parked_ref[:, at : at + NY], (((0,), (0,)), ((), ())), preferred_element_type=f32
+            )
+        staged[n] = held[n].reshape(count, lines, NY).astype(bf16)
+        stores.append(pltpu.make_async_copy(staged.at[n], out_hbm.at[:, pl.ds(n * lines, lines)], out_sems.at[n]))
+        stores[-1].start()
+    for store in stores:
+        store.wait()
 
 
 def adjoint_pack_kernel(now_hbm, next_hbm, speed_hbm, first_ref, second_ref, now_ref, next_ref, speed_ref, sems):
@@ -254,52 +283,114 @@
     by_side(par, first_ref, second_ref, emit)
 
 
-def adjoint_first_kernel(
-    now_ref, next_ref, speed_ref, inject_hbm, got_a, got_b,
-    first_ref, second_ref, lam_ref, speed_ext, q3_ref,
-    buf4, now_halo, next_halo, inject_ref, sems,
+def adjoint_side(ref, upper, now_ref, speed_ref, inject_ref, side, buf, weights, store):
+    now, after, speed = side
+    close = 0 if upper else HALF - 1
+    for n, held in enumerate(side):
+        held[...] = ref[HALF * n : HALF * n + HALF].astype(f32)
+        held[close] = held[close] + ref[4 * HALF + n].astype(f32)
+    fill_side(
+        buf,
+        upper,
+        lambda j: now[j] * speed[j],
+        lambda j: ref[3 * HALF + j].astype(f32),
+        lambda p: now_ref[p] * speed_ref[p],
+    )
+    first = HALF + DEPTH if upper else 0
+
+    def body(j, row, lap):
+        here = now[j, rows(row), :]
+        lam = 2.0 * here - after[j, rows(row), :] + lap + inject_ref[first + j, 0, rows(row), :]
+        base = 2.0 * lam - here + inject_ref[first + j, 1, rows(row), :]
+        store(j, row, lam, base, speed[j, rows(row), :])
+
+    group_laps(buf, HALF, weights, body)
+
+
+def adjoint_side_kernel(
+    now_ref, next_ref, speed_ref, inject_hbm, got_a, out_ref, part_ref, mark_ref,
+    own, buf, now_side, next_side, speed_side, inject_ref, sems,
 ):
     par = parity()
-    own = slice(HALF, HALF + DEPTH)
     (copy,) = fetch((inject_hbm.at[:, 0:2],), (inject_ref,), sems)
-    zero_pads(buf4)
+    mark_ref[...] = jnp.zeros(mark_ref.shape, f32)
+    zero_pads(own)
+    zero_pads(buf)
+    weights = band()
+    own[:, PAD : PAD + NX, :] = now_ref[...] * speed_ref[...]
+
+    def alone(p, row, lap):
+        part_ref[p, rows(row), :] = 2.0 * now_ref[p, rows(row), :] - next_ref[p, rows(row), :] + lap
+
+    sweep_own_alone(own, weights, alone)
+    copy.wait()
+    part_ref[...] = part_ref[...] + inject_ref[HALF : HALF + DEPTH, 0]
+
+    def store(j, row, lam, base, speed):
+        for n, value in enumerate((lam, base, speed, lam * speed)):
+            out_ref[n * HALF + j, rows(row), :] = value
+
+    def one(upper):
+        side = (now_side, next_side, speed_side)
+        adjoint_side(got_a, upper, now_ref, speed_ref, inject_ref, side, buf, weights, store)
+        for p in side_planes(upper):
+            for row in range(0, NX, CHUNK):
+                part_ref[p, rows(row), :] = part_ref[p, rows(row), :] + side_terms(buf, upper, p, row)
+
+    by_parity(par, one)
+
+
+def by_parity(par, one):
+    @pl.when(par == 0)
+    def _():
+        one(True)
+
+    @pl.when(par == 1)
+    def _():
+        one(False)
+
+
+def adjoint_first_kernel(
+    now_ref, speed_ref, inject_hbm, side_ref, part_ref, got_b, order_ref,
+    first_ref, second_ref, lam_ref, speed_ext, q3_ref,
+    buf, now_side, next_side, speed_side, inject_ref, sems,
+):
+    par = parity()
+    (copy,) = fetch((inject_hbm.at[:, 0:2],), (inject_ref,), sems)
+    zero_pads(buf)
     zero_pads(q3_ref)
     weights = band()
+    own = slice(HALF, HALF + DEPTH)
     inner = slice(PAD, PAD + NX)
     speed_ext[own] = speed_ref[...]
-    buf4[2 * HALF : 2 * HALF + DEPTH, inner, :] = now_ref[...] * speed_ext[own]
-
-    def halo(lower, upper):
-        for ref, at, close, far_at in ((lower, 0, 3, 0), (upper, HALF, 0, WIDE - HALF)):
-            ext_at = ext_of_halo(at)
-            for n, (held, to) in enumerate(((now_halo, at), (next_halo, at), (speed_ext, ext_at))):
-                held[to : to + HALF] = ref[HALF * n : HALF * n + HALF].astype(f32)
-                held[to + close] = held[to + close] + ref[4 * HALF + n].astype(f32)
-            buf4[far_at : far_at + HALF, inner, :] = ref[3 * HALF : 4 * HALF].astype(f32)
-            buf4[ext_at + HALF : ext_at + 2 * HALF, inner, :] = (
-                now_halo[at : at + HALF] * speed_ext[ext_at : ext_at + HALF]
-            )
-
-    by_side(par, got_a, got_b, halo)
     copy.wait()
 
-    def halo_lam3(h, row, lap):
-        e = ext_of_halo(h)
-        now = now_halo[h, rows(row), :]
-        lam = 2.0 * now - next_halo[h, rows(row), :] + lap + inject_ref[e, 0, rows(row), :]
-        lam_ref[e, rows(row), :] = lam
-        lam_ref[EXT + DEPTH + h, rows(row), :] = 2.0 * lam - now + inject_ref[e, 1, rows(row), :]
-        q3_ref[e, padded(row), :] = lam * speed_ext[e, rows(row), :]
-
-    sweep_halo(buf4, weights, halo_lam3)
-
-    def own_lam3(p, row, lap):
-        lam = 2.0 * now_ref[p, rows(row), :] - next_ref[p, rows(row), :] + lap
-        lam = lam + inject_ref[p + HALF, 0, rows(row), :]
-        lam_ref[p + HALF, rows(row), :] = lam
-        q3_ref[p + HALF, padded(row), :] = lam * speed_ext[p + HALF, rows(row), :]
-
-    sweep_own(buf4, 2 * HALF, weights, own_lam3)
+    def one(upper_a):
+        ext_a, halo_a = (HALF + DEPTH, HALF) if upper_a else (0, 0)
+        lam_ref[ext_a : ext_a + HALF] = side_ref[0:HALF]
+        lam_ref[EXT + DEPTH + halo_a : EXT + DEPTH + halo_a + HALF] = side_ref[HALF : 2 * HALF]
+        speed_ext[ext_a : ext_a + HALF] = side_ref[2 * HALF : 3 * HALF]
+        q3_ref[ext_a : ext_a + HALF, inner, :] = side_ref[3 * HALF : 4 * HALF]
+        upper = not upper_a
+        ext_b, halo_b = (HALF + DEPTH, HALF) if upper else (0, 0)
+
+        def store(j, row, lam, base, speed):
+            lam_ref[ext_b + j, rows(row), :] = lam
+            lam_ref[EXT + DEPTH + halo_b + j, rows(row), :] = base
+            speed_ext[ext_b + j, rows(row), :] = speed
+            q3_ref[ext_b + j, padded(row), :] = lam * speed
+
+        side = (now_side, next_side, speed_side)
+        adjoint_side(got_b, upper, now_ref, speed_ref, inject_ref, side, buf, weights, store)
+        for p in range(DEPTH):
+            for row in range(0, NX, CHUNK):
+                lam = part_ref[p, rows(row), :]
+                if p in side_planes(upper):
+                    lam = lam + side_terms(buf, upper, p, row)
+                lam_ref[p + HALF, rows(row), :] = lam
+                q3_ref[p + HALF, padded(row), :] = lam * speed_ref[p, rows(row), :]
+
+    by_parity(par, one)
 
     def own_lam2(p, row, lap):
         lam = 2.0 * lam_ref[p + HALF, rows(row), :] - now_ref[p, rows(row), :] + lap
@@ -329,48 +420,72 @@
     return local, row_ref[0] // NY, lax.rem(row_ref[0], NY)
 
 
+def forward_own_kernel(mine_ref, order_ref, own_ref, part_ref, mark_ref):
+    mark_ref[...] = jnp.zeros(mark_ref.shape, f32)
+    zero_pads(own_ref)
+    own_ref[:, PAD : PAD + NX, :] = mine_ref[HALF : HALF + DEPTH].astype(f32)
+
+    def alone(p, row, lap):
+        part_ref[p, rows(row), :] = lap
+
+    sweep_own_alone(own_ref, band(), alone)
+
+
 def forward_first_kernel(
-    depth_ref, row_ref, wave_ref, mine_a, mine_b, got_a, got_b, speed_ext,
+    depth_ref, row_ref, wave_ref, mine_a, mine_b, own_ref, part_ref, got_a, got_b, speed_ext,
     first_ref, second_ref, u1_ref, u2_ref, base_ref, lap0_ref, lap1_ref,
-    buf0, prev_ext,
+    below, above, prev_own,
 ):
     par = parity()
-    zero_pads(buf0)
+    zero_pads(below)
+    zero_pads(above)
     zero_pads(u1_ref)
     weights = band()
     inner = slice(PAD, PAD + NX)
-    prev_ext[pl.ds(HALF + HALF * (1 - par), HALF)] = mine_a[0:HALF].astype(f32)
-    prev_ext[pl.ds(HALF + HALF * par, HALF)] = mine_b[0:HALF].astype(f32)
-    buf0[2 * HALF : 2 * HALF + DEPTH, inner, :] = mine_a[HALF : HALF + DEPTH].astype(f32)
+    prev_own[pl.ds(HALF * (1 - par), HALF)] = mine_a[0:HALF].astype(f32)
+    prev_own[pl.ds(HALF * par, HALF)] = mine_b[0:HALF].astype(f32)
 
     def halo(lower, upper):
-        for ref, at, wide_at in ((lower, 0, 0), (upper, HALF + DEPTH, 2 * HALF + DEPTH)):
-            prev_ext[at : at + HALF] = ref[0:HALF].astype(f32)
-            buf0[wide_at : wide_at + DEPTH, inner, :] = ref[HALF : HALF + DEPTH].astype(f32)
+        for ref, buf, is_upper in ((lower, below, False), (upper, above, True)):
+            near_at, far_at = (HALF, 2 * HALF) if is_upper else (2 * HALF, HALF)
+            fill_side(
+                buf,
+                is_upper,
+                lambda j, ref=ref, at=near_at: ref[at + j].astype(f32),
+                lambda j, ref=ref, at=far_at: ref[at + j].astype(f32),
+                lambda p: own_ref[p, inner, :],
+            )
+            first, at = (HALF + DEPTH, HALF) if is_upper else (0, 0)
+
+            def body(j, row, lap, ref=ref, buf=buf, first=first, at=at):
+                now = buf[HALF + j, padded(row), :]
+                value = 2.0 * now - ref[j, rows(row), :].astype(f32) + speed_ext[first + j, rows(row), :] * lap
+                u1_ref[first + j, padded(row), :] = value
+                base_ref[at + j, rows(row), :] = 2.0 * value - now
+
+            group_laps(buf, HALF, weights, body)
 
     by_side(par, got_a, got_b, halo)
-
-    def step(e, row, lap):
-        now = buf0[e + HALF, padded(row), :]
-        value = 2.0 * now - prev_ext[e, rows(row), :] + speed_ext[e, rows(row), :] * lap
-        u1_ref[e, padded(row), :] = value
-        return now
-
-    sweep_halo(buf0, weights, lambda h, row, lap: step(ext_of_halo(h), row, lap))
-
-    def own_u1(p, row, lap):
-        step(p + HALF, row, lap)
-        lap0_ref[p, rows(row), :] = lap
-
-    sweep_own(buf0, 2 * HALF, weights, own_u1)
+    for p in range(DEPTH):
+        upper = p >= HALF
+        for row in range(0, NX, CHUNK):
+            lap = part_ref[p, rows(row), :] + side_terms(above if upper else below, upper, p, row)
+            lap0_ref[p, rows(row), :] = lap
+            value = 2.0 * own_ref[p, padded(row), :] - prev_own[p, rows(row), :]
+            u1_ref[p + HALF, padded(row), :] = value + speed_ext[p + HALF, rows(row), :] * lap
     local, across, along_y = source_place(depth_ref, row_ref)
+    outside = ((local >= 0) & (local < HALF)) | ((local >= HALF + DEPTH) & (local < EXT))
 
     @pl.when((local >= 0) & (local < EXT))
     def _():
         add_cell(u1_ref, local, across + PAD, along_y, wave_ref[0, 0])
 
+    @pl.when(outside)
+    def _():
+        add_cell(base_ref, jnp.where(local < HALF, local, local - DEPTH), across, along_y, 2.0 * wave_ref[0, 0])
+
     def own_u2(p, row, lap):
-        value = 2.0 * u1_ref[p + HALF, padded(row), :] - buf0[p + 2 * HALF, padded(row), :]
+        value = 2.0 * u1_ref[p + HALF, padded(row), :] - own_ref[p, padded(row), :]
         u2_ref[p, rows(row), :] = value + speed_ext[p + HALF, rows(row), :] * lap
         lap1_ref[p, rows(row), :] = lap
 
@@ -381,14 +496,11 @@
         add_cell(u2_ref, local - HALF, across, along_y, wave_ref[0, 1])
 
     send_second(par, u1_ref, u2_ref, speed_ext, False, first_ref, second_ref)
-    for h in range(2 * HALF):
-        e = ext_of_halo(h)
-        base_ref[h] = 2.0 * u1_ref[e, inner, :] - buf0[e + HALF, inner, :]
 
 
 def middle_kernel(
-    depth_ref, row_ref, wave_ref, inject_hbm, got_a, got_b, lam_ref, q3_ref, speed_ext, u1_ref, base_ref, lap0_ref, lap1_ref,
-    late_ref, u2_ref, grad_ref, lam2_halo, buf2,
+    depth_ref, row_ref, wave_ref, inject_hbm, got_a, got_b, lam_ref, q3_ref, speed_ext, u1_ref, u2_own, base_ref, lap0_ref, lap1_ref,
+    late_ref, u2_ref, grad_ref, lam2_halo, buf2, own_ref, part_ref,
     inject_ref, sems,
 ):
     par = parity()
@@ -435,9 +547,17 @@
     def _():
         add_cell(u2_ref, jnp.where(local < HALF, local, local - DEPTH), across, along_y, wave_ref[0, 1])
 
+    zero_pads(own_ref)
+    own_ref[:, inner, :] = u2_own[...]
+
+    def u2_alone(p, row, lap):
+        part_ref[p, rows(row), :] = lap
+
+    sweep_own_alone(own_ref, weights, u2_alone)
+
 
 def adjoint_last_kernel(
-    inject_hbm, late_ref, lam_ref, lam2_halo, buf2, speed_ext, order_hbm, early_ref, buf1, inject_ref, sems
+    inject_hbm, late_ref, lam_ref, lam2_halo, buf2, speed_ext, order_ref, early_ref, buf1, inject_ref, sems
 ):
     (copy,) = fetch((inject_hbm.at[:, 2:4],), (inject_ref,), sems)
     zero_pads(buf1)
@@ -461,35 +581,42 @@
 
 
 def forward_second_kernel(
-    depth_ref, row_ref, wave_ref, got_a, got_b, u1_ref, u2_ref, u2_halo_ref, speed_ext, lam3_ref, lam4_ref, grad_ref,
-    keep_ref, send_ref, buf2, buf3, total,
+    depth_ref, row_ref, wave_ref, got_a, got_b, u1_ref, own_ref, part_ref, u2_halo_ref, speed_ext, lam_ref, lam4_ref,
+    grad_ref, keep_ref, send_ref, below, above, buf3, total,
 ):
     par = parity()
-    zero_pads(buf2)
+    zero_pads(below)
+    zero_pads(above)
     zero_pads(buf3)
     weights = band()
     inner = slice(PAD, PAD + NX)
 
     def halo(lower, upper):
-        for ref, at, far_at in ((lower, 0, 0), (upper, HALF, WIDE - HALF)):
-            ext_at = ext_of_halo(at)
-            buf2[ext_at + HALF : ext_at + 2 * HALF, inner, :] = u2_halo_ref[at : at + HALF] + ref[0:HALF].astype(f32)
-            buf2[far_at : far_at + HALF, inner, :] = ref[HALF : 2 * HALF].astype(f32)
+        for ref, buf, is_upper in ((lower, below, False), (upper, above, True)):
+            first, at = (HALF + DEPTH, HALF) if is_upper else (0, 0)
+            fill_side(
+                buf,
+                is_upper,
+                lambda j, ref=ref, at=at: u2_halo_ref[at + j] + ref[j].astype(f32),
+                lambda j, ref=ref: ref[HALF + j].astype(f32),
+                lambda p: own_ref[p, inner, :],
+            )
+
+            def body(j, row, lap, buf=buf, first=first):
+                value = 2.0 * buf[HALF + j, padded(row), :] - u1_ref[first + j, padded(row), :]
+                buf3[first + j, padded(row), :] = value + speed_ext[first + j, rows(row), :] * lap
+
+            group_laps(buf, HALF, weights, body)
 
     by_side(par, got_a, got_b, halo)
-    buf2[2 * HALF : 2 * HALF + DEPTH, inner, :] = u2_ref[...]
-
-    def step(e, row, lap):
-        value = 2.0 * buf2[e + HALF, padded(row), :] - u1_ref[e, padded(row), :]
-        buf3[e, padded(row), :] = value + speed_ext[e, rows(row), :] * lap
-
-    sweep_halo(buf2, weights, lambda h, row, lap: step(ext_of_halo(h), row, lap))
-
-    def own_u3(p, row, lap):
-        step(p + HALF, row, lap)
-        total[p, rows(row), :] = grad_ref[p, rows(row), :] + lap * lam3_ref[p + HALF, rows(row), :]
-
-    sweep_own(buf2, 2 * HALF, weights, own_u3)
+    for p in range(DEPTH):
+        upper = p >= HALF
+        e = p + HALF
+        for row in range(0, NX, CHUNK):
+            lap = part_ref[p, rows(row), :] + side_terms(above if upper else below, upper, p, row)
+            value = 2.0 * own_ref[p, padded(row), :] - u1_ref[e, padded(row), :]
+            buf3[e, padded(row), :] = value + speed_ext[e, rows(row), :] * lap
+            total[p, rows(row), :] = grad_ref[p, rows(row), :] + lap * lam_ref[e, rows(row), :]
     local, across, along_y = source_place(depth_ref, row_ref)
 
     @pl.when((local >= 0) & (local < EXT))
@@ -534,10 +661,10 @@
     (outgoing,) = call(
         gather_kernel, "gather", [HB] * 2, [((64, 32, NY), bf16)],
         [
-            pltpu.VMEM((64 * 32, NY), f32), pltpu.VMEM((1, 64), jnp.int32), pltpu.VMEM((64, 4096), bf16),
-            pltpu.SemaphoreType.DMA((5,)),
+            pltpu.VMEM((4, 64 * 8, NY), f32), pltpu.VMEM((1, 64), jnp.int32), pltpu.VMEM((64, 4096), bf16),
+            pltpu.VMEM((4, 64, 8, NY), bf16), pltpu.SemaphoreType.DMA((5,)), pltpu.SemaphoreType.DMA((4,)),
         ],
-        in_hbm(parked_slot[0], parked[0]),
+        in_hbm(parked_slot[0], parked[0]), out=HB,
     )
     incoming = lax.all_to_all(outgoing, "dom", split_axis=0, concat_axis=0, tiled=True)
     send_a, send_b = call(
@@ -553,48 +680,60 @@
             pltpu.VMEM((2, steps * NY, count), bf16), pltpu.VMEM((EXT, steps, NX, NY), f32),
             pltpu.SemaphoreType.DMA((EXT // 2 + 1,)),
         ],
-        (rec_depth.reshape(1, count), rec_row.reshape(1, count), residuals[0]), us=4,
+        (rec_depth.reshape(1, count), rec_row.reshape(1, count), residuals[0]), us=4, out=HB,
     )
     fields = pltpu.VMEM((EXT, 2, NX, NY), f32)
-    send_a, send_b, lam23, speed_ext, q3 = call(
-        adjoint_first_kernel, "adjoint_first", [VM] * 3 + [HB] + [VM] * 2,
-        [planes(8)] * 2 + [((EXT + 2 * DEPTH, NX, NY), f32), ext, wide],
-        [buffer(WIDE), pltpu.VMEM(*slab), pltpu.VMEM(*slab), fields, pltpu.SemaphoreType.DMA((1,))],
-        (lam4, lam5, speed_sq) + in_hbm(inject) + (got_a, got_b),
-    )
-    back_a, back_b = swap(send_a, send_b)
-
+    trio = ((3 * HALF, ROWS, NY), f32)
+    four = pltpu.VMEM((HALF, NX, NY), f32)
+    own_wide = ((DEPTH, ROWS, NY), f32)
     mine_a, mine_b = call(
         forward_pack_kernel, "forward_pack", [SM, VM, HB], [planes(12)] * 2, [],
         (holder_list.reshape(64), incoming) + in_hbm(order),
     )
+    side, part, order = call(
+        adjoint_side_kernel, "adjoint_side", [VM] * 3 + [HB, VM], [((4 * HALF, NX, NY), f32), slab, mark],
+        [buffer(DEPTH), pltpu.VMEM(*trio), four, four, four, fields, pltpu.SemaphoreType.DMA((1,))],
+        (lam4, lam5, speed_sq) + in_hbm(inject) + (got_a,),
+    )
+    own0, lap0_part, order = call(
+        forward_own_kernel, "forward_own", [VM, VM], [own_wide, slab, mark], [], (mine_a, order),
+    )
+    send_a, send_b, lam23, speed_ext, q3 = call(
+        adjoint_first_kernel, "adjoint_first", [VM] * 2 + [HB] + [VM] * 4,
+        [planes(8)] * 2 + [((EXT + 2 * DEPTH, NX, NY), f32), ext, wide],
+        [pltpu.VMEM(*trio), four, four, four, fields, pltpu.SemaphoreType.DMA((1,))],
+        (lam4, speed_sq) + in_hbm(inject) + (side, part, got_b, order),
+    )
+    back_a, back_b = swap(send_a, send_b)
+
     got_a, got_b = swap(mine_a, mine_b)
     send_a, send_b, u1, u2, base_u, lap0, lap1 = call(
-        forward_first_kernel, "forward_first", [SM] * 3 + [VM] * 5,
+        forward_first_kernel, "forward_first", [SM] * 3 + [VM] * 7,
         [planes(8)] * 2 + [wide, slab, slab, slab, slab],
-        [buffer(WIDE), pltpu.VMEM(*ext)],
-        (src_depth, src_row, wavelet, mine_a, mine_b, got_a, got_b, speed_ext),
+        [pltpu.VMEM(*trio), pltpu.VMEM(*trio), pltpu.VMEM(*slab)],
+        (src_depth, src_row, wavelet, mine_a, mine_b, own0, lap0_part, got_a, got_b, speed_ext),
     )
     got_a, got_b = swap(send_a, send_b)
-    late, u2_halo, grad, lam2_halo, q2 = call(
-        middle_kernel, "middle", [SM] * 3 + [HB] + [VM] * 9, [slab] * 4 + [((WIDE, ROWS, NY), f32)],
+    late, u2_halo, grad, lam2_halo, q2, own2, lap2_part = call(
+        middle_kernel, "middle", [SM] * 3 + [HB] + [VM] * 10,
+        [slab] * 4 + [((WIDE, ROWS, NY), f32), own_wide, slab],
         [pltpu.VMEM(*slab), pltpu.SemaphoreType.DMA((1,))],
         (src_depth, src_row, wavelet) + in_hbm(inject)
-        + (back_a, back_b, lam23, q3, speed_ext, u1, base_u, lap0, lap1),
+        + (back_a, back_b, lam23, q3, speed_ext, u1, u2, base_u, lap0, lap1),
     )
     quarter = ((2, DEPTH, NX // 4, NY), f32)
     keep, send = call(
-        forward_second_kernel, "forward_second", [SM] * 3 + [VM] * 9, [quarter] * 2,
-        [buffer(WIDE), buffer(EXT), pltpu.VMEM(*slab)],
-        (src_depth, src_row, wavelet, got_a, got_b, u1, u2, u2_halo, speed_ext, lam23, lam4, grad),
+        forward_second_kernel, "forward_second", [SM] * 3 + [VM] * 10, [quarter] * 2,
+        [pltpu.VMEM(*trio), pltpu.VMEM(*trio), buffer(EXT), pltpu.VMEM(*slab)],
+        (src_depth, src_row, wavelet, got_a, got_b, u1, own2, lap2_part, u2_halo, speed_ext, lam23, lam4, grad),
     )
     got = lax.ppermute(send, "shot", [(0, 1), (1, 0), (2, 3), (3, 2)])
     part = keep[1] + got[1]
     other = lax.ppermute(part, "shot", [(0, 2), (2, 0), (1, 3), (3, 1)])
     (early,) = call(
-        adjoint_last_kernel, "adjoint_last", [HB] + [VM] * 5 + [HB], [slab],
+        adjoint_last_kernel, "adjoint_last", [HB] + [VM] * 6, [slab],
         [buffer(EXT), fields, pltpu.SemaphoreType.DMA((1,))],
-        in_hbm(inject) + (late, lam23, lam2_halo, q2, speed_ext) + in_hbm(part),
+        in_hbm(inject) + (late, lam23, lam2_halo, q2, speed_ext, part),
     )
     gradient = keep[0] + got[0] + other
     return (gradient, late[None], early[None])

time: 85.7 us -> 83 us (0.968)
  starting transfers between devices: 40.8 us -> 38.5 us
    ppermute x4, starting transfers between devices: 4.17 us -> 2.18 us  [swap(): return (lax.ppermute(a, 'dom', even), far)]
    pallas_call x9 -> x11, Pallas kernels: 33.1 us -> 32.4 us  [call(): pl.pallas_call(kernel, name=name, out_shape=[pltpu.HBM(*o) if out is HB e...]
  transfers between devices with their start and end apart: 11 -> 11, of which waited for: 5 -> 5; matrix products, arithmetic and copies ran while one was open for 0% -> 0% of each run, Pallas kernels for 31% -> 33%
where the time goes in v6:
time: 83 us; the launch traced here: 82.5 us
  starting transfers between devices  38.5 us (46%)
  Pallas kernels  32.4 us (39%)
  waiting for transfers between devices  8.69 us (10%)
  between operations  2.23 us (3%)
    pallas_call x11, Pallas kernels, call(): pl.pallas_call(kernel, name=name, out_shape=[pltpu.HBM(*o) if out is HB e...  32.4 us
    ppermute x4, starting transfers between devices, swap(): far = lax.ppermute(b, 'dom', odd)  20.8 us
    all_to_all x1, starting transfers between devices, per_device(): lax.all_to_all(outgoing, 'dom', split_axis=0, concat_axis=0, tiled=True)  13.2 us
    ppermute x4, waiting for transfers between devices, swap(): far = lax.ppermute(b, 'dom', odd)  6.56 us
    ppermute x1, starting transfers between devices, per_device(): other = lax.ppermute(part, 'shot', [(0, 2), (2, 0), (1, 3), (3, 1)])  2.21 us
    ppermute x4, starting transfers between devices, swap(): return (lax.ppermute(a, 'dom', even), far)  2.18 us
  transfers between devices with their start and end apart: 11, of which 5 were waited for; matrix products, arithmetic and copies ran while one was open for 0% of the time, Pallas kernels for 33%

profile of v6, /device:TPU:2, one launch (start us, length us, event | category | flops | bytes accessed | tf_op | source)
XLA Modules:
  0.0 82.5 jit_solution(7025217206516836200)
XLA Ops:
  0.6 2.4 %gather.1 = bf16[64,32,128]{2,1,0:T(8,128)(2,1)} custom-call(s32[1,64]{1,0:T(1,128)} %bitcast.29, bf16[64,4096]{1,0:T(8,128)(2,1)} %bitcast.28), custom_call_target="tpu_custom_call" | custom-call | flops 2000000000 | bytes 7200000 | tf_op jit(solution)/shard_map/gather/pallas_call | solution.py:43
  3.1 13.2 %all-to-all-start = ((bf16[64,32,128]{2,1,0:T(8,128)(2,1)}), bf16[64,32,128]{2,1,0:T(8,128)(2,1)S(1)}, u32[]{:S(2)}, u32[]{:S(2)}) async-start(bf16[64,32,128]{2,1,0:T(8,128)(2,1)} %gather.1), calls=%async_computation | async-start | bytes 1048576 | tf_op jit(solution)/shard_map/all_to_all | solution.py:669
  16.3 0.0 copy-start.5
  16.3 0.0 copy-start.6
  16.3 0.0 copy-start.7
  16.4 1.5 %adjoint_pack.1 = (bf16[19,128,128]{2,1,0:T(8,128)(2,1)S(1)}, bf16[19,128,128]{2,1,0:T(8,128)(2,1)S(1)}) custom-call(f32[8,128,128]{2,1,0:T(8,128)} %bitcast.16, f32[8,128,128]{2,1,0:T(8,128)} %bitcast.21, f32[8,128,128]{2,1,0:T(8,128)} %speed_ref.3), custom_call_target="tpu_custom_call" | custom-call | flops 2000000000 | bytes 7200000 | tf_op jit(solution)/shard_map/adjoint_pack/pallas_call | solution.py:43
  17.9 1.6 %collective-permute-start = (bf16[19,128,128]{2,1,0:T(8,128)(2,1)S(1)}, bf16[19,128,128]{2,1,0:T(8,128)(2,1)S(1)}, u32[]{:S(2)}, u32[]{:S(2)}) collective-permute-start(bf16[19,128,128]{2,1,0:T(8,128)(2,1)S(1)} %get-tuple-element.40), channel_id=1, source_target_pairs={{0,1},{1,0},{2,3},{3,2},{4,5},{5,4},{6,7},{7,6},{8,9},{9,8},{10,11... | collective-permute-start | bytes 1867784 | tf_op jit(solution)/shard_map/ppermute | solution.py:650
  19.5 6.1 %collective-permute-start.3 = (bf16[19,128,128]{2,1,0:T(8,128)(2,1)S(1)}, bf16[19,128,128]{2,1,0:T(8,128)(2,1)S(1)}, u32[]{:S(2)}, u32[]{:S(2)}) collective-permute-start(bf16[19,128,128]{2,1,0:T(8,128)(2,1)S(1)} %get-tuple-element.46), channel_id=1, source_target_pairs={{1,2},{2,1},{3,4},{4,3},{5,6},{6,5},{7,8},{8,7},{9,10},{10,9},{11,... | collective-permute-start | bytes 1867784 | tf_op jit(solution)/shard_map/ppermute | solution.py:649
  25.5 0.0 copy-done.5
  25.5 0.0 copy-done.6
  25.5 0.0 copy-done.7
  25.6 0.0 copy-start.8
  25.6 7.2 %inject.1 = (f32[16,4,128,128]{3,2,1,0:T(8,128)}, f32[8,128]{1,0:T(8,128)}) custom-call(s32[1,1024]{1,0:T(1,128)S(1)} %bitcast.24, s32[1,1024]{1,0:T(1,128)S(1)} %bitcast.25, f32[4,1024]{1,0:T(4,128)S(1)} %bitcast.23), custom_call_target="tpu_custom_call" | custom-call | flops 4000000000 | bytes 14400000 | tf_op jit(solution)/shard_map/inject/pallas_call | solution.py:43
  34.1 0.0 all-to-all-done.pieces_ref
  34.1 0.0 copy-done.8
  34.1 0.0 copy-start
  34.1 0.0 copy-start.1
  34.1 0.0 copy-start.4
  34.1 0.7 forward_pack.1
  34.8 5.3 %collective-permute-start.2 = (bf16[12,128,128]{2,1,0:T(8,128)(2,1)S(1)}, bf16[12,128,128]{2,1,0:T(8,128)(2,1)S(1)}, u32[]{:S(2)}, u32[]{:S(2)}) collective-permute-start(bf16[12,128,128]{2,1,0:T(8,128)(2,1)S(1)} %get-tuple-element.38.mine_b), channel_id=1, source_target_pairs={{1,2},{2,1},{3,4},{4,3},{5,6},{6,5},{7,8},{8,7},{9,10},{10,9},{11,... | collective-permute-start | bytes 1179656 | tf_op jit(solution)/shard_map/ppermute | solution.py:649
  40.1 0.1 collective-permute-start.1
  40.2 0.0 collective-permute-done.got_a
  40.3 0.0 copy-done
  40.3 0.0 copy-done.1
  40.3 2.2 %adjoint_side.1 = (f32[16,128,128]{2,1,0:T(8,128)S(1)}, f32[8,128,128]{2,1,0:T(8,128)S(1)}, f32[8,128]{1,0:T(8,128)S(1)}) custom-call(f32[8,128,128]{2,1,0:T(8,128)S(1)} %bitcast.17, f32[8,128,128]{2,1,0:T(8,128)S(1)} %bitcast.22, f32[8,128,128]{2,1,0:T(8,128)S(1)} %copy-done.1, f32[16,4,128,128]{3,2,1,0:T(8,128)} %get-tuple-element.39.inject_hbm, ...), custom_call_target="tpu_custom_call" | custom-call | flops 2000000000 | bytes 7200000 | tf_op jit(solution)/shard_map/adjoint_side/pallas_call | solution.py:43
  42.5 0.7 forward_own.1
  43.2 3.5 %collective-permute-done.3.got_b = bf16[19,128,128]{2,1,0:T(8,128)(2,1)S(1)} collective-permute-done((bf16[19,128,128]{2,1,0:T(8,128)(2,1)S(1)}, bf16[19,128,128]{2,1,0:T(8,128)(2,1)S(1)}, u32[]{:S(2)}, u32[]{:S(2)}) %collective-permute-start.3) | collective-permute-done | bytes 622624 | tf_op jit(solution)/shard_map/ppermute | solution.py:649
  46.7 3.4 %adjoint_first.1 = (bf16[8,128,128]{2,1,0:T(8,128)(2,1)S(1)}, bf16[8,128,128]{2,1,0:T(8,128)(2,1)S(1)}, f32[32,128,128]{2,1,0:T(8,128)S(1)}, f32[16,128,128]{2,1,0:T(8,128)S(1)}, f32[16,144,128]{2,1,0:T(8,128)S(1)}) custom-call(f32[8,128,128]{2,1,0:T(8,128)S(1)} %bitcast.18, f32[8,128,128]{2,1,0:T(8,128)S(1)} %copy-done.1, ...), custom_call_target="tpu_custom_call" | custom-call | flops 2000000000 | bytes 7200000 | tf_op jit(solution)/shard_map/adjoint_first/pallas_call | solution.py:43
  50.2 0.1 collective-permute-start.6
  50.3 3.2 %collective-permute-start.7 = (bf16[8,128,128]{2,1,0:T(8,128)(2,1)S(1)}, bf16[8,128,128]{2,1,0:T(8,128)(2,1)S(1)}, u32[]{:S(2)}, u32[]{:S(2)}) collective-permute-start(bf16[8,128,128]{2,1,0:T(8,128)(2,1)S(1)} %get-tuple-element.53), channel_id=1, source_target_pairs={{1,2},{2,1},{3,4},{4,3},{5,6},{6,5},{7,8},{8,7},{9,10},{10,9},{11,... | collective-permute-start | bytes 786440 | tf_op jit(solution)/shard_map/ppermute | solution.py:649
  53.5 0.6 collective-permute-done.2.got_b
  54.1 0.0 collective-permute-done.1.got_a
  54.1 2.8 %forward_first.1 = (bf16[8,128,128]{2,1,0:T(8,128)(2,1)S(1)}, bf16[8,128,128]{2,1,0:T(8,128)(2,1)S(1)}, f32[16,144,128]{2,1,0:T(8,128)S(1)}, f32[8,128,128]{2,1,...) custom-call(s32[1]{0:T(128)S(6)} %copy.15.depth_ref, ...), custom_call_target="tpu_custom_call" | custom-call | flops 2000000000 | bytes 7200000 | tf_op jit(solution)/shard_map/forward_first/pallas_call | solution.py:43
  56.8 0.4 collective-permute-start.4
  57.3 6.2 %collective-permute-start.5 = (bf16[8,128,128]{2,1,0:T(8,128)(2,1)S(1)}, bf16[8,128,128]{2,1,0:T(8,128)(2,1)S(1)}, u32[]{:S(2)}, u32[]{:S(2)}) collective-permute-start(bf16[8,128,128]{2,1,0:T(8,128)(2,1)S(1)} %get-tuple-element.50), channel_id=1, source_target_pairs={{1,2},{2,1},{3,4},{4,3},{5,6},{6,5},{7,8},{8,7},{9,10},{10,9},{11,... | collective-permute-start | bytes 786440 | tf_op jit(solution)/shard_map/ppermute | solution.py:649
  63.4 0.0 collective-permute-done.6.got_a
  63.4 0.0 collective-permute-done.7.got_b
  63.5 4.5 %middle.1 = (f32[8,128,128]{2,1,0:T(8,128)}, f32[8,128,128]{2,1,0:T(8,128)S(1)}, f32[8,128,128]{2,1,0:T(8,128)S(1)}, f32[8,128,128]{2,1,0:T(8,128)S(1)}, f32[24,...) custom-call(s32[1]{0:T(128)S(6)} %copy.15.depth_ref, s32[1]{0:T(128)S(6)} %copy.16.row_ref, ...), custom_call_target="tpu_custom_call" | custom-call | flops 2000000000 | bytes 7200000 | tf_op jit(solution)/shard_map/middle/pallas_call | solution.py:43
  68.0 0.0 collective-permute-done.4.got_a
  68.0 2.5 %collective-permute-done.5.got_b = bf16[8,128,128]{2,1,0:T(8,128)(2,1)S(1)} collective-permute-done((bf16[8,128,128]{2,1,0:T(8,128)(2,1)S(1)}, bf16[8,128,128]{2,1,0:T(8,128)(2,1)S(1)}, u32[]{:S(2)}, u32[]{:S(2)}) %collective-permute-start.5) | collective-permute-done | bytes 262176 | tf_op jit(solution)/shard_map/ppermute | solution.py:649
  70.5 2.6 %forward_second.1 = (f32[2,8,32,128]{3,2,1,0:T(8,128)S(1)}, f32[2,8,32,128]{3,2,1,0:T(8,128)S(1)}) custom-call(s32[1]{0:T(128)S(6)} %copy.15.depth_ref, s32[1]{0:T(128)S(6)} %copy.16.row_ref, f32[1,3]{1,0:T(1,128)S(1)} %copy-done.3, bf16[8,128,128]{2,1,0:T(8,128)(2,1)S(1)} %collective-permute-done.4.got_a, ...), custom_call_target="tpu_custom_call" | custom-call | flops 2000000000 | bytes 7200000 | tf_op jit(solution)/shard_map/forward_second/pallas_call | solution.py:43
  73.1 0.1 collective-permute-start.8
  73.2 1.5 %collective-permute-done.8 = f32[2,8,32,128]{3,2,1,0:T(8,128)S(1)} collective-permute-done((f32[2,8,32,128]{3,2,1,0:T(8,128)S(1)}, f32[2,8,32,128]{3,2,1,0:T(8,128)S(1)}, u32[]{:S(2)}, u32[]{:S(2)}) %collective-permute-start.8) | collective-permute-done | bytes 262176 | tf_op jit(solution)/shard_map/ppermute | solution.py:730
  74.7 2.2 %collective-permute-start.9 = (f32[8,32,128]{2,1,0:T(8,128)S(1)}, f32[8,32,128]{2,1,0:T(8,128)S(1)}, u32[]{:S(2)}, u32[]{:S(2)}) collective-permute-start(f32[8,32,128]{2,1,0:T(8,128)S(1)} %fusion.order_ref), channel_id=1, source_target_pairs={{0,128},{128,0},{64,192},{192,64},{1,129},{129,1},{65,193},{193,65... | collective-permute-start | bytes 393224 | tf_op jit(solution)/shard_map/ppermute | solution.py:732
  76.9 0.0 copy-done.2
  76.9 4.3 %adjoint_last.1 = f32[8,128,128]{2,1,0:T(8,128)} custom-call(f32[16,4,128,128]{3,2,1,0:T(8,128)} %get-tuple-element.39.inject_hbm, f32[8,128,128]{2,1,0:T(8,128)S(1)} %copy-done.2, f32[32,128,128]{2,1,0:T(8,128)S(1)} %get-tuple-element.54.lam_ref, f32[8,128,128]{2,1,0:T(8,128)S(1)} %get-tuple-element.67.lam2_halo, ...), custom_call_target="tpu_custom_call" | custom-call | flops 2000000000 | bytes 7200000 | tf_op jit(solution)/shard_map/adjoint_last/pallas_call | solution.py:43
  81.2 0.6 collective-permute-done.9
  81.8 0.7 fusion.2
  (5 shorter events, 0.0 us)
Async XLA Ops:
  3.1 31.0 %all-to-all-start = ((bf16[64,32,128]{2,1,0:T(8,128)(2,1)}), bf16[64,32,128]{2,1,0:T(8,128)(2,1)S(1)}, u32[]{:S(2)}, u32[]{:S(2)}) async-start(bf16[64,32,128]{2,1,0:T(8,128)(2,1)} %gather.1), calls=%async_computation | async-start | bytes 1048576 | tf_op jit(solution)/shard_map/all_to_all | solution.py:669
  16.3 9.2 %copy-start.5 = (f32[1,4,1024]{2,1,0:T(4,128)S(1)}, f32[1,4,1024]{2,1,0:T(4,128)}, u32[]{:S(2)}) copy-start(f32[1,4,1024]{2,1,0:T(4,128)} %param.23) | copy-start | bytes 49156
  16.3 9.2 %copy-start.6 = (s32[1024]{0:T(1024)S(1)}, s32[1024]{0:T(1024)}, u32[]{:S(2)}) copy-start(s32[1024]{0:T(1024)} %param.21) | copy-start | bytes 12292
  16.3 9.2 %copy-start.7 = (s32[1024]{0:T(1024)S(1)}, s32[1024]{0:T(1024)}, u32[]{:S(2)}) copy-start(s32[1024]{0:T(1024)} %param.22) | copy-start | bytes 12292
  17.9 22.3 %collective-permute-start = (bf16[19,128,128]{2,1,0:T(8,128)(2,1)S(1)}, bf16[19,128,128]{2,1,0:T(8,128)(2,1)S(1)}, u32[]{:S(2)}, u32[]{:S(2)}) collective-permute-start(bf16[19,128,128]{2,1,0:T(8,128)(2,1)S(1)} %get-tuple-element.40), channel_id=1, source_target_pairs={{0,1},{1,0},{2,3},{3,2},{4,5},{5,4},{6,7},{7,6},{8,9},{9,8},{10,11... | collective-permute-start | bytes 1867784 | tf_op jit(solution)/shard_map/ppermute | solution.py:650
  19.5 27.3 %collective-permute-start.3 = (bf16[19,128,128]{2,1,0:T(8,128)(2,1)S(1)}, bf16[19,128,128]{2,1,0:T(8,128)(2,1)S(1)}, u32[]{:S(2)}, u32[]{:S(2)}) collective-permute-start(bf16[19,128,128]{2,1,0:T(8,128)(2,1)S(1)} %get-tuple-element.46), channel_id=1, source_target_pairs={{1,2},{2,1},{3,4},{4,3},{5,6},{6,5},{7,8},{8,7},{9,10},{10,9},{11,... | collective-permute-start | bytes 1867784 | tf_op jit(solution)/shard_map/ppermute | solution.py:649
  25.6 8.5 %copy-start.8 = (s32[1,1,64]{2,1,0:T(1,128)S(1)}, s32[1,1,64]{2,1,0:T(1,128)}, u32[]{:S(2)}) copy-start(s32[1,1,64]{2,1,0:T(1,128)} %param.14) | copy-start | bytes 772
  34.1 6.2 %copy-start = (f32[1,8,128,128]{3,2,1,0:T(8,128)S(1)}, f32[1,8,128,128]{3,2,1,0:T(8,128)}, u32[]{:S(2)}) copy-start(f32[1,8,128,128]{3,2,1,0:T(8,128)} %param.17) | copy-start | bytes 1572868
  34.1 6.2 %copy-start.1 = (f32[8,128,128]{2,1,0:T(8,128)S(1)}, f32[8,128,128]{2,1,0:T(8,128)}, u32[]{:S(2)}) copy-start(f32[8,128,128]{2,1,0:T(8,128)} %speed_ref.3) | copy-start | bytes 1572868
  34.1 6.2 %copy-start.4 = (f32[1,8,128,128]{3,2,1,0:T(8,128)S(1)}, f32[1,8,128,128]{3,2,1,0:T(8,128)}, u32[]{:S(2)}) copy-start(f32[1,8,128,128]{3,2,1,0:T(8,128)} %param.16) | copy-start | bytes 1572868
  34.8 19.3 %collective-permute-start.2 = (bf16[12,128,128]{2,1,0:T(8,128)(2,1)S(1)}, bf16[12,128,128]{2,1,0:T(8,128)(2,1)S(1)}, u32[]{:S(2)}, u32[]{:S(2)}) collective-permute-start(bf16[12,128,128]{2,1,0:T(8,128)(2,1)S(1)} %get-tuple-element.38.mine_b), channel_id=1, source_target_pairs={{1,2},{2,1},{3,4},{4,3},{5,6},{6,5},{7,8},{8,7},{9,10},{10,9},{11,... | collective-permute-start | bytes 1179656 | tf_op jit(solution)/shard_map/ppermute | solution.py:649
  40.1 13.9 %collective-permute-start.1 = (bf16[12,128,128]{2,1,0:T(8,128)(2,1)S(1)}, bf16[12,128,128]{2,1,0:T(8,128)(2,1)S(1)}, u32[]{:S(2)}, u32[]{:S(2)}) collective-permute-start(bf16[12,128,128]{2,1,0:T(8,128)(2,1)S(1)} %get-tuple-element.37.mine_ref.mine_a), channel_id=1, source_target_pairs={{0,1},{1,0},{2,3},{3,2},{4,5},{5,4},{6,7},{7,6},{8,9},{9,8},{10,11... | collective-permute-start | bytes 1179656 | tf_op jit(solution)/shard_map/ppermute | solution.py:650
  46.7 7.3 %copy-start.3 = (f32[1,3]{1,0:T(1,128)S(1)}, f32[1,3]{1,0:T(1,128)}, u32[]{:S(2)}) copy-start(f32[1,3]{1,0:T(1,128)} %wave_ref.5) | copy-start | bytes 40
  50.2 13.3 %collective-permute-start.6 = (bf16[8,128,128]{2,1,0:T(8,128)(2,1)S(1)}, bf16[8,128,128]{2,1,0:T(8,128)(2,1)S(1)}, u32[]{:S(2)}, u32[]{:S(2)}) collective-permute-start(bf16[8,128,128]{2,1,0:T(8,128)(2,1)S(1)} %get-tuple-element.52), channel_id=1, source_target_pairs={{0,1},{1,0},{2,3},{3,2},{4,5},{5,4},{6,7},{7,6},{8,9},{9,8},{10,11... | collective-permute-start | bytes 786440 | tf_op jit(solution)/shard_map/ppermute | solution.py:650
  50.3 13.2 %collective-permute-start.7 = (bf16[8,128,128]{2,1,0:T(8,128)(2,1)S(1)}, bf16[8,128,128]{2,1,0:T(8,128)(2,1)S(1)}, u32[]{:S(2)}, u32[]{:S(2)}) collective-permute-start(bf16[8,128,128]{2,1,0:T(8,128)(2,1)S(1)} %get-tuple-element.53), channel_id=1, source_target_pairs={{1,2},{2,1},{3,4},{4,3},{5,6},{6,5},{7,8},{8,7},{9,10},{10,9},{11,... | collective-permute-start | bytes 786440 | tf_op jit(solution)/shard_map/ppermute | solution.py:649
  56.8 11.1 %collective-permute-start.4 = (bf16[8,128,128]{2,1,0:T(8,128)(2,1)S(1)}, bf16[8,128,128]{2,1,0:T(8,128)(2,1)S(1)}, u32[]{:S(2)}, u32[]{:S(2)}) collective-permute-start(bf16[8,128,128]{2,1,0:T(8,128)(2,1)S(1)} %get-tuple-element.49), channel_id=1, source_target_pairs={{0,1},{1,0},{2,3},{3,2},{4,5},{5,4},{6,7},{7,6},{8,9},{9,8},{10,11... | collective-permute-start | bytes 786440 | tf_op jit(solution)/shard_map/ppermute | solution.py:650
  57.3 13.2 %collective-permute-start.5 = (bf16[8,128,128]{2,1,0:T(8,128)(2,1)S(1)}, bf16[8,128,128]{2,1,0:T(8,128)(2,1)S(1)}, u32[]{:S(2)}, u32[]{:S(2)}) collective-permute-start(bf16[8,128,128]{2,1,0:T(8,128)(2,1)S(1)} %get-tuple-element.50), channel_id=1, source_target_pairs={{1,2},{2,1},{3,4},{4,3},{5,6},{6,5},{7,8},{8,7},{9,10},{10,9},{11,... | collective-permute-start | bytes 786440 | tf_op jit(solution)/shard_map/ppermute | solution.py:649
  70.5 6.5 %copy-start.2 = (f32[8,128,128]{2,1,0:T(8,128)S(1)}, f32[8,128,128]{2,1,0:T(8,128)}, u32[]{:S(2)}) copy-start(f32[8,128,128]{2,1,0:T(8,128)} %get-tuple-element.66.late_ref) | copy-start | bytes 1572868
  73.1 1.6 %collective-permute-start.8 = (f32[2,8,32,128]{3,2,1,0:T(8,128)S(1)}, f32[2,8,32,128]{3,2,1,0:T(8,128)S(1)}, u32[]{:S(2)}, u32[]{:S(2)}) collective-permute-start(f32[2,8,32,128]{3,2,1,0:T(8,128)S(1)} %get-tuple-element.65), channel_id=1, source_target_pairs={{0,64},{64,0},{128,192},{192,128},{1,65},{65,1},{129,193},{193,129... | collective-permute-start | bytes 786440 | tf_op jit(solution)/shard_map/ppermute | solution.py:730
  74.7 7.1 %collective-permute-start.9 = (f32[8,32,128]{2,1,0:T(8,128)S(1)}, f32[8,32,128]{2,1,0:T(8,128)S(1)}, u32[]{:S(2)}, u32[]{:S(2)}) collective-permute-start(f32[8,32,128]{2,1,0:T(8,128)S(1)} %fusion.order_ref), channel_id=1, source_target_pairs={{0,128},{128,0},{64,192},{192,64},{1,129},{129,1},{65,193},{193,65... | collective-permute-start | bytes 393224 | tf_op jit(solution)/shard_map/ppermute | solution.py:732

commit v7 on v6

--- a/solution.py
+++ b/solution.py
@@ -308,8 +308,8 @@
 
 
 def adjoint_side_kernel(
-    now_ref, next_ref, speed_ref, inject_hbm, got_a, out_ref, part_ref, mark_ref,
-    own, buf, now_side, next_side, speed_side, inject_ref, sems,
+    now_ref, next_ref, speed_ref, inject_hbm, got_a, out_ref, part_ref, inject_ref, mark_ref,
+    own, buf, now_side, next_side, speed_side, sems,
 ):
     par = parity()
     (copy,) = fetch((inject_hbm.at[:, 0:2],), (inject_ref,), sems)
@@ -351,19 +351,17 @@
 
 
 def adjoint_first_kernel(
-    now_ref, speed_ref, inject_hbm, side_ref, part_ref, got_b, order_ref,
+    now_ref, speed_ref, inject_ref, side_ref, part_ref, got_b, order_ref,
     first_ref, second_ref, lam_ref, speed_ext, q3_ref,
-    buf, now_side, next_side, speed_side, inject_ref, sems,
+    buf, now_side, next_side, speed_side,
 ):
     par = parity()
-    (copy,) = fetch((inject_hbm.at[:, 0:2],), (inject_ref,), sems)
     zero_pads(buf)
     zero_pads(q3_ref)
     weights = band()
     own = slice(HALF, HALF + DEPTH)
     inner = slice(PAD, PAD + NX)
     speed_ext[own] = speed_ref[...]
-    copy.wait()
 
     def one(upper_a):
         ext_a, halo_a = (HALF + DEPTH, HALF) if upper_a else (0, 0)
@@ -499,7 +497,7 @@
 
 
 def middle_kernel(
-    depth_ref, row_ref, wave_ref, inject_hbm, got_a, got_b, lam_ref, q3_ref, speed_ext, u1_ref, u2_own, base_ref, lap0_ref, lap1_ref,
+    depth_ref, row_ref, wave_ref, inject_hbm, got_b, got_a, lam_ref, q3_ref, speed_ext, u1_ref, u2_own, base_ref, lap0_ref, lap1_ref,
     late_ref, u2_ref, grad_ref, lam2_halo, buf2, own_ref, part_ref,
     inject_ref, sems,
 ):
@@ -581,7 +579,7 @@
 
 
 def forward_second_kernel(
-    depth_ref, row_ref, wave_ref, got_a, got_b, u1_ref, own_ref, part_ref, u2_halo_ref, speed_ext, lam_ref, lam4_ref,
+    depth_ref, row_ref, wave_ref, got_b, got_a, u1_ref, own_ref, part_ref, u2_halo_ref, speed_ext, lam_ref, lam4_ref,
     grad_ref, keep_ref, send_ref, below, above, buf3, total,
 ):
     par = parity()
@@ -690,19 +688,19 @@
         forward_pack_kernel, "forward_pack", [SM, VM, HB], [planes(12)] * 2, [],
         (holder_list.reshape(64), incoming) + in_hbm(order),
     )
-    side, part, order = call(
-        adjoint_side_kernel, "adjoint_side", [VM] * 3 + [HB, VM], [((4 * HALF, NX, NY), f32), slab, mark],
-        [buffer(DEPTH), pltpu.VMEM(*trio), four, four, four, fields, pltpu.SemaphoreType.DMA((1,))],
+    side, part, inject01, order = call(
+        adjoint_side_kernel, "adjoint_side", [VM] * 3 + [HB, VM], [((4 * HALF, NX, NY), f32), slab, ((EXT, 2, NX, NY), f32), mark],
+        [buffer(DEPTH), pltpu.VMEM(*trio), four, four, four, pltpu.SemaphoreType.DMA((1,))],
         (lam4, lam5, speed_sq) + in_hbm(inject) + (got_a,),
     )
     own0, lap0_part, order = call(
         forward_own_kernel, "forward_own", [VM, VM], [own_wide, slab, mark], [], (mine_a, order),
     )
     send_a, send_b, lam23, speed_ext, q3 = call(
-        adjoint_first_kernel, "adjoint_first", [VM] * 2 + [HB] + [VM] * 4,
+        adjoint_first_kernel, "adjoint_first", [VM] * 7,
         [planes(8)] * 2 + [((EXT + 2 * DEPTH, NX, NY), f32), ext, wide],
-        [pltpu.VMEM(*trio), four, four, four, fields, pltpu.SemaphoreType.DMA((1,))],
-        (lam4, speed_sq) + in_hbm(inject) + (side, part, got_b, order),
+        [pltpu.VMEM(*trio), four, four, four],
+        (lam4, speed_sq, inject01, side, part, got_b, order),
     )
     back_a, back_b = swap(send_a, send_b)
 
@@ -719,13 +717,13 @@
         [slab] * 4 + [((WIDE, ROWS, NY), f32), own_wide, slab],
         [pltpu.VMEM(*slab), pltpu.SemaphoreType.DMA((1,))],
         (src_depth, src_row, wavelet) + in_hbm(inject)
-        + (back_a, back_b, lam23, q3, speed_ext, u1, u2, base_u, lap0, lap1),
+        + (back_b, back_a, lam23, q3, speed_ext, u1, u2, base_u, lap0, lap1),
     )
     quarter = ((2, DEPTH, NX // 4, NY), f32)
     keep, send = call(
         forward_second_kernel, "forward_second", [SM] * 3 + [VM] * 10, [quarter] * 2,
         [pltpu.VMEM(*trio), pltpu.VMEM(*trio), buffer(EXT), pltpu.VMEM(*slab)],
-        (src_depth, src_row, wavelet, got_a, got_b, u1, own2, lap2_part, u2_halo, speed_ext, lam23, lam4, grad),
+        (src_depth, src_row, wavelet, got_b, got_a, u1, own2, lap2_part, u2_halo, speed_ext, lam23, lam4, grad),
     )
     got = lax.ppermute(send, "shot", [(0, 1), (1, 0), (2, 3), (3, 2)])
     part = keep[1] + got[1]

time: 83 us -> 82.7 us (level)
  waiting for transfers between devices: 8.69 us -> 11.8 us
  starting transfers between devices: 38.5 us -> 36.6 us
  Pallas kernels: 32.4 us -> 30.9 us
    ppermute x4, waiting for transfers between devices: 6.56 us -> 9.66 us  [swap(): far = lax.ppermute(b, 'dom', odd)]
    ppermute x4, starting transfers between devices: 20.8 us -> 19.2 us  [swap(): far = lax.ppermute(b, 'dom', odd)]
    pallas_call x11, Pallas kernels: 32.4 us -> 30.9 us  [call(): pl.pallas_call(kernel, name=name, out_shape=[pltpu.HBM(*o) if out is HB e...]
  transfers between devices with their start and end apart: 11 -> 11, of which waited for: 5 -> 5; matrix products, arithmetic and copies ran while one was open for 0% -> 0% of each run, Pallas kernels for 33% -> 31%
where the time goes in v7:
time: 82.7 us; the launch traced here: 82.2 us
  starting transfers between devices  36.6 us (44%)
  Pallas kernels  30.9 us (37%)
  waiting for transfers between devices  11.8 us (14%)
  between operations  2.23 us (3%)
    pallas_call x11, Pallas kernels, call(): pl.pallas_call(kernel, name=name, out_shape=[pltpu.HBM(*o) if out is HB e...  30.9 us
    ppermute x4, starting transfers between devices, swap(): far = lax.ppermute(b, 'dom', odd)  19.2 us
    all_to_all x1, starting transfers between devices, per_device(): lax.all_to_all(outgoing, 'dom', split_axis=0, concat_axis=0, tiled=True)  13.2 us
    ppermute x4, waiting for transfers between devices, swap(): far = lax.ppermute(b, 'dom', odd)  9.66 us
    ppermute x1, starting transfers between devices, per_device(): other = lax.ppermute(part, 'shot', [(0, 2), (2, 0), (1, 3), (3, 1)])  2.21 us
    ppermute x4, starting transfers between devices, swap(): return (lax.ppermute(a, 'dom', even), far)  1.83 us
  transfers between devices with their start and end apart: 11, of which 5 were waited for; matrix products, arithmetic and copies ran while one was open for 0% of the time, Pallas kernels for 31%

profile of v7, /device:TPU:2, one launch (start us, length us, event | category | flops | bytes accessed | tf_op | source)
XLA Modules:
  0.0 82.2 jit_solution(3382919080729278400)
XLA Ops:
  0.6 2.4 %gather.1 = bf16[64,32,128]{2,1,0:T(8,128)(2,1)} custom-call(s32[1,64]{1,0:T(1,128)} %bitcast.29, bf16[64,4096]{1,0:T(8,128)(2,1)} %bitcast.28), custom_call_target="tpu_custom_call" | custom-call | flops 2000000000 | bytes 7200000 | tf_op jit(solution)/shard_map/gather/pallas_call | solution.py:43
  3.1 13.2 %all-to-all-start = ((bf16[64,32,128]{2,1,0:T(8,128)(2,1)}), bf16[64,32,128]{2,1,0:T(8,128)(2,1)S(1)}, u32[]{:S(2)}, u32[]{:S(2)}) async-start(bf16[64,32,128]{2,1,0:T(8,128)(2,1)} %gather.1), calls=%async_computation | async-start | bytes 1048576 | tf_op jit(solution)/shard_map/all_to_all | solution.py:667
  16.3 0.0 copy-start.5
  16.3 0.0 copy-start.6
  16.3 0.0 copy-start.7
  16.4 1.5 %adjoint_pack.1 = (bf16[19,128,128]{2,1,0:T(8,128)(2,1)S(1)}, bf16[19,128,128]{2,1,0:T(8,128)(2,1)S(1)}) custom-call(f32[8,128,128]{2,1,0:T(8,128)} %bitcast.16, f32[8,128,128]{2,1,0:T(8,128)} %bitcast.21, f32[8,128,128]{2,1,0:T(8,128)} %speed_ref.3), custom_call_target="tpu_custom_call" | custom-call | flops 2000000000 | bytes 7200000 | tf_op jit(solution)/shard_map/adjoint_pack/pallas_call | solution.py:43
  17.9 1.6 %collective-permute-start = (bf16[19,128,128]{2,1,0:T(8,128)(2,1)S(1)}, bf16[19,128,128]{2,1,0:T(8,128)(2,1)S(1)}, u32[]{:S(2)}, u32[]{:S(2)}) collective-permute-start(bf16[19,128,128]{2,1,0:T(8,128)(2,1)S(1)} %get-tuple-element.41), channel_id=1, source_target_pairs={{0,1},{1,0},{2,3},{3,2},{4,5},{5,4},{6,7},{7,6},{8,9},{9,8},{10,11... | collective-permute-start | bytes 1867784 | tf_op jit(solution)/shard_map/ppermute | solution.py:648
  19.5 6.1 %collective-permute-start.3 = (bf16[19,128,128]{2,1,0:T(8,128)(2,1)S(1)}, bf16[19,128,128]{2,1,0:T(8,128)(2,1)S(1)}, u32[]{:S(2)}, u32[]{:S(2)}) collective-permute-start(bf16[19,128,128]{2,1,0:T(8,128)(2,1)S(1)} %get-tuple-element.48), channel_id=1, source_target_pairs={{1,2},{2,1},{3,4},{4,3},{5,6},{6,5},{7,8},{8,7},{9,10},{10,9},{11,... | collective-permute-start | bytes 1867784 | tf_op jit(solution)/shard_map/ppermute | solution.py:647
  25.5 0.0 copy-done.5
  25.5 0.0 copy-done.6
  25.5 0.0 copy-done.7
  25.6 0.0 copy-start.8
  25.6 7.2 %inject.1 = (f32[16,4,128,128]{3,2,1,0:T(8,128)}, f32[8,128]{1,0:T(8,128)}) custom-call(s32[1,1024]{1,0:T(1,128)S(1)} %bitcast.24, s32[1,1024]{1,0:T(1,128)S(1)} %bitcast.25, f32[4,1024]{1,0:T(4,128)S(1)} %bitcast.23), custom_call_target="tpu_custom_call" | custom-call | flops 4000000000 | bytes 14400000 | tf_op jit(solution)/shard_map/inject/pallas_call | solution.py:43
  34.1 0.0 all-to-all-done.pieces_ref
  34.1 0.0 copy-done.8
  34.1 0.0 copy-start
  34.1 0.0 copy-start.3
  34.1 0.0 copy-start.4
  34.1 0.7 forward_pack.1
  34.8 5.3 %collective-permute-start.2 = (bf16[12,128,128]{2,1,0:T(8,128)(2,1)S(1)}, bf16[12,128,128]{2,1,0:T(8,128)(2,1)S(1)}, u32[]{:S(2)}, u32[]{:S(2)}) collective-permute-start(bf16[12,128,128]{2,1,0:T(8,128)(2,1)S(1)} %get-tuple-element.39.mine_b), channel_id=1, source_target_pairs={{1,2},{2,1},{3,4},{4,3},{5,6},{6,5},{7,8},{8,7},{9,10},{10,9},{11,... | collective-permute-start | bytes 1179656 | tf_op jit(solution)/shard_map/ppermute | solution.py:647
  40.1 0.1 collective-permute-start.1
  40.2 0.0 collective-permute-done.got_a
  40.3 0.0 copy-done
  40.3 0.0 copy-done.3
  40.3 0.0 copy-done.4
  40.3 2.2 %adjoint_side.1 = (f32[16,128,128]{2,1,0:T(8,128)S(1)}, f32[8,128,128]{2,1,0:T(8,128)S(1)}, f32[16,2,128,128]{3,2,1,0:T(8,128)S(1)}, f32[8,128]{1,0:T(8,128)S(1)}) custom-call(f32[8,128,128]{2,1,0:T(8,128)S(1)} %bitcast.17, f32[8,128,128]{2,1,0:T(8,128)S(1)} %bitcast.22, f32[8,128,128]{2,1,0:T(8,128)S(1)} %copy-done.4, ...), custom_call_target="tpu_custom_call" | custom-call | flops 2000000000 | bytes 7200000 | tf_op jit(solution)/shard_map/adjoint_side/pallas_call | solution.py:43
  42.5 0.7 forward_own.1
  43.3 3.5 %collective-permute-done.3.got_b = bf16[19,128,128]{2,1,0:T(8,128)(2,1)S(1)} collective-permute-done((bf16[19,128,128]{2,1,0:T(8,128)(2,1)S(1)}, bf16[19,128,128]{2,1,0:T(8,128)(2,1)S(1)}, u32[]{:S(2)}, u32[]{:S(2)}) %collective-permute-start.3) | collective-permute-done | bytes 622624 | tf_op jit(solution)/shard_map/ppermute | solution.py:647
  46.7 1.9 %adjoint_first.1 = (bf16[8,128,128]{2,1,0:T(8,128)(2,1)S(1)}, bf16[8,128,128]{2,1,0:T(8,128)(2,1)S(1)}, f32[32,128,128]{2,1,0:T(8,128)S(1)}, f32[16,128,128]{2,1,0:T(8,128)S(1)}, f32[16,144,128]{2,1,0:T(8,128)S(1)}) custom-call(f32[8,128,128]{2,1,0:T(8,128)S(1)} %bitcast.18, f32[8,128,128]{2,1,0:T(8,128)S(1)} %copy-done.4, ...), custom_call_target="tpu_custom_call" | custom-call | flops 2000000000 | bytes 7200000 | tf_op jit(solution)/shard_map/adjoint_first/pallas_call | solution.py:43
  48.6 2.9 %collective-permute-start.6 = (bf16[8,128,128]{2,1,0:T(8,128)(2,1)S(1)}, bf16[8,128,128]{2,1,0:T(8,128)(2,1)S(1)}, u32[]{:S(2)}, u32[]{:S(2)}) collective-permute-start(bf16[8,128,128]{2,1,0:T(8,128)(2,1)S(1)} %get-tuple-element.54), channel_id=1, source_target_pairs={{1,2},{2,1},{3,4},{4,3},{5,6},{6,5},{7,8},{8,7},{9,10},{10,9},{11,... | collective-permute-start | bytes 786440 | tf_op jit(solution)/shard_map/ppermute | solution.py:647
  51.5 0.1 collective-permute-start.7
  51.6 2.4 %collective-permute-done.2.got_b = bf16[12,128,128]{2,1,0:T(8,128)(2,1)S(1)} collective-permute-done((bf16[12,128,128]{2,1,0:T(8,128)(2,1)S(1)}, bf16[12,128,128]{2,1,0:T(8,128)(2,1)S(1)}, u32[]{:S(2)}, u32[]{:S(2)}) %collective-permute-start.2) | collective-permute-done | bytes 393248 | tf_op jit(solution)/shard_map/ppermute | solution.py:647
  54.1 0.0 collective-permute-done.1.got_a
  54.1 2.8 %forward_first.1 = (bf16[8,128,128]{2,1,0:T(8,128)(2,1)S(1)}, bf16[8,128,128]{2,1,0:T(8,128)(2,1)S(1)}, f32[16,144,128]{2,1,0:T(8,128)S(1)}, f32[8,128,128]{2,1,...) custom-call(s32[1]{0:T(128)S(6)} %copy.15.depth_ref, ...), custom_call_target="tpu_custom_call" | custom-call | flops 2000000000 | bytes 7200000 | tf_op jit(solution)/shard_map/forward_first/pallas_call | solution.py:43
  56.8 4.9 %collective-permute-start.4 = (bf16[8,128,128]{2,1,0:T(8,128)(2,1)S(1)}, bf16[8,128,128]{2,1,0:T(8,128)(2,1)S(1)}, u32[]{:S(2)}, u32[]{:S(2)}) collective-permute-start(bf16[8,128,128]{2,1,0:T(8,128)(2,1)S(1)} %get-tuple-element.51), channel_id=1, source_target_pairs={{1,2},{2,1},{3,4},{4,3},{5,6},{6,5},{7,8},{8,7},{9,10},{10,9},{11,... | collective-permute-start | bytes 786440 | tf_op jit(solution)/shard_map/ppermute | solution.py:647
  61.8 0.1 collective-permute-start.5
  61.9 0.0 collective-permute-done.6.got_b
  61.9 0.0 collective-permute-done.7.got_a
  61.9 4.5 %middle.1 = (f32[8,128,128]{2,1,0:T(8,128)}, f32[8,128,128]{2,1,0:T(8,128)S(1)}, f32[8,128,128]{2,1,0:T(8,128)S(1)}, f32[8,128,128]{2,1,0:T(8,128)S(1)}, f32[24,...) custom-call(s32[1]{0:T(128)S(6)} %copy.15.depth_ref, s32[1]{0:T(128)S(6)} %copy.16.row_ref, ...), custom_call_target="tpu_custom_call" | custom-call | flops 2000000000 | bytes 7200000 | tf_op jit(solution)/shard_map/middle/pallas_call | solution.py:43
  66.4 3.8 %collective-permute-done.4.got_b = bf16[8,128,128]{2,1,0:T(8,128)(2,1)S(1)} collective-permute-done((bf16[8,128,128]{2,1,0:T(8,128)(2,1)S(1)}, bf16[8,128,128]{2,1,0:T(8,128)(2,1)S(1)}, u32[]{:S(2)}, u32[]{:S(2)}) %collective-permute-start.4) | collective-permute-done | bytes 262176 | tf_op jit(solution)/shard_map/ppermute | solution.py:647
  70.2 0.0 collective-permute-done.5.got_a
  70.2 2.6 %forward_second.1 = (f32[2,8,32,128]{3,2,1,0:T(8,128)S(1)}, f32[2,8,32,128]{3,2,1,0:T(8,128)S(1)}) custom-call(s32[1]{0:T(128)S(6)} %copy.15.depth_ref, s32[1]{0:T(128)S(6)} %copy.16.row_ref, f32[1,3]{1,0:T(1,128)S(1)} %copy-done.2, bf16[8,128,128]{2,1,0:T(8,128)(2,1)S(1)} %collective-permute-done.4.got_b, ...), custom_call_target="tpu_custom_call" | custom-call | flops 2000000000 | bytes 7200000 | tf_op jit(solution)/shard_map/forward_second/pallas_call | solution.py:43
  72.8 0.1 collective-permute-start.8
  72.9 1.5 %collective-permute-done.8 = f32[2,8,32,128]{3,2,1,0:T(8,128)S(1)} collective-permute-done((f32[2,8,32,128]{3,2,1,0:T(8,128)S(1)}, f32[2,8,32,128]{3,2,1,0:T(8,128)S(1)}, u32[]{:S(2)}, u32[]{:S(2)}) %collective-permute-start.8) | collective-permute-done | bytes 262176 | tf_op jit(solution)/shard_map/ppermute | solution.py:728
  74.4 2.2 %collective-permute-start.9 = (f32[8,32,128]{2,1,0:T(8,128)S(1)}, f32[8,32,128]{2,1,0:T(8,128)S(1)}, u32[]{:S(2)}, u32[]{:S(2)}) collective-permute-start(f32[8,32,128]{2,1,0:T(8,128)S(1)} %fusion.order_ref), channel_id=1, source_target_pairs={{0,128},{128,0},{64,192},{192,64},{1,129},{129,1},{65,193},{193,65... | collective-permute-start | bytes 393224 | tf_op jit(solution)/shard_map/ppermute | solution.py:730
  76.6 4.3 %adjoint_last.1 = f32[8,128,128]{2,1,0:T(8,128)} custom-call(f32[16,4,128,128]{3,2,1,0:T(8,128)} %get-tuple-element.40.inject_hbm, f32[8,128,128]{2,1,0:T(8,128)S(1)} %copy-done.1, f32[32,128,128]{2,1,0:T(8,128)S(1)} %get-tuple-element.56.lam_ref, f32[8,128,128]{2,1,0:T(8,128)S(1)} %get-tuple-element.69.lam2_halo, ...), custom_call_target="tpu_custom_call" | custom-call | flops 2000000000 | bytes 7200000 | tf_op jit(solution)/shard_map/adjoint_last/pallas_call | solution.py:43
  81.0 0.6 collective-permute-done.9
  81.6 0.7 fusion.2
  (5 shorter events, 0.0 us)
Async XLA Ops:
  3.1 31.0 %all-to-all-start = ((bf16[64,32,128]{2,1,0:T(8,128)(2,1)}), bf16[64,32,128]{2,1,0:T(8,128)(2,1)S(1)}, u32[]{:S(2)}, u32[]{:S(2)}) async-start(bf16[64,32,128]{2,1,0:T(8,128)(2,1)} %gather.1), calls=%async_computation | async-start | bytes 1048576 | tf_op jit(solution)/shard_map/all_to_all | solution.py:667
  16.3 9.2 %copy-start.5 = (f32[1,4,1024]{2,1,0:T(4,128)S(1)}, f32[1,4,1024]{2,1,0:T(4,128)}, u32[]{:S(2)}) copy-start(f32[1,4,1024]{2,1,0:T(4,128)} %param.23) | copy-start | bytes 49156
  16.3 9.2 %copy-start.6 = (s32[1024]{0:T(1024)S(1)}, s32[1024]{0:T(1024)}, u32[]{:S(2)}) copy-start(s32[1024]{0:T(1024)} %param.21) | copy-start | bytes 12292
  16.3 9.2 %copy-start.7 = (s32[1024]{0:T(1024)S(1)}, s32[1024]{0:T(1024)}, u32[]{:S(2)}) copy-start(s32[1024]{0:T(1024)} %param.22) | copy-start | bytes 12292
  17.9 22.3 %collective-permute-start = (bf16[19,128,128]{2,1,0:T(8,128)(2,1)S(1)}, bf16[19,128,128]{2,1,0:T(8,128)(2,1)S(1)}, u32[]{:S(2)}, u32[]{:S(2)}) collective-permute-start(bf16[19,128,128]{2,1,0:T(8,128)(2,1)S(1)} %get-tuple-element.41), channel_id=1, source_target_pairs={{0,1},{1,0},{2,3},{3,2},{4,5},{5,4},{6,7},{7,6},{8,9},{9,8},{10,11... | collective-permute-start | bytes 1867784 | tf_op jit(solution)/shard_map/ppermute | solution.py:648
  19.5 27.3 %collective-permute-start.3 = (bf16[19,128,128]{2,1,0:T(8,128)(2,1)S(1)}, bf16[19,128,128]{2,1,0:T(8,128)(2,1)S(1)}, u32[]{:S(2)}, u32[]{:S(2)}) collective-permute-start(bf16[19,128,128]{2,1,0:T(8,128)(2,1)S(1)} %get-tuple-element.48), channel_id=1, source_target_pairs={{1,2},{2,1},{3,4},{4,3},{5,6},{6,5},{7,8},{8,7},{9,10},{10,9},{11,... | collective-permute-start | bytes 1867784 | tf_op jit(solution)/shard_map/ppermute | solution.py:647
  25.6 8.5 %copy-start.8 = (s32[1,1,64]{2,1,0:T(1,128)S(1)}, s32[1,1,64]{2,1,0:T(1,128)}, u32[]{:S(2)}) copy-start(s32[1,1,64]{2,1,0:T(1,128)} %param.14) | copy-start | bytes 772
  34.1 6.2 %copy-start = (f32[1,8,128,128]{3,2,1,0:T(8,128)S(1)}, f32[1,8,128,128]{3,2,1,0:T(8,128)}, u32[]{:S(2)}) copy-start(f32[1,8,128,128]{3,2,1,0:T(8,128)} %param.17) | copy-start | bytes 1572868
  34.1 6.2 %copy-start.3 = (f32[1,8,128,128]{3,2,1,0:T(8,128)S(1)}, f32[1,8,128,128]{3,2,1,0:T(8,128)}, u32[]{:S(2)}) copy-start(f32[1,8,128,128]{3,2,1,0:T(8,128)} %param.16) | copy-start | bytes 1572868
  34.1 6.2 %copy-start.4 = (f32[8,128,128]{2,1,0:T(8,128)S(1)}, f32[8,128,128]{2,1,0:T(8,128)}, u32[]{:S(2)}) copy-start(f32[8,128,128]{2,1,0:T(8,128)} %speed_ref.3) | copy-start | bytes 1572868
  34.8 19.3 %collective-permute-start.2 = (bf16[12,128,128]{2,1,0:T(8,128)(2,1)S(1)}, bf16[12,128,128]{2,1,0:T(8,128)(2,1)S(1)}, u32[]{:S(2)}, u32[]{:S(2)}) collective-permute-start(bf16[12,128,128]{2,1,0:T(8,128)(2,1)S(1)} %get-tuple-element.39.mine_b), channel_id=1, source_target_pairs={{1,2},{2,1},{3,4},{4,3},{5,6},{6,5},{7,8},{8,7},{9,10},{10,9},{11,... | collective-permute-start | bytes 1179656 | tf_op jit(solution)/shard_map/ppermute | solution.py:647
  40.1 13.9 %collective-permute-start.1 = (bf16[12,128,128]{2,1,0:T(8,128)(2,1)S(1)}, bf16[12,128,128]{2,1,0:T(8,128)(2,1)S(1)}, u32[]{:S(2)}, u32[]{:S(2)}) collective-permute-start(bf16[12,128,128]{2,1,0:T(8,128)(2,1)S(1)} %get-tuple-element.38.mine_ref.mine_a), channel_id=1, source_target_pairs={{0,1},{1,0},{2,3},{3,2},{4,5},{5,4},{6,7},{7,6},{8,9},{9,8},{10,11... | collective-permute-start | bytes 1179656 | tf_op jit(solution)/shard_map/ppermute | solution.py:648
  46.7 7.3 %copy-start.2 = (f32[1,3]{1,0:T(1,128)S(1)}, f32[1,3]{1,0:T(1,128)}, u32[]{:S(2)}) copy-start(f32[1,3]{1,0:T(1,128)} %wave_ref.5) | copy-start | bytes 40
  48.6 13.3 %collective-permute-start.6 = (bf16[8,128,128]{2,1,0:T(8,128)(2,1)S(1)}, bf16[8,128,128]{2,1,0:T(8,128)(2,1)S(1)}, u32[]{:S(2)}, u32[]{:S(2)}) collective-permute-start(bf16[8,128,128]{2,1,0:T(8,128)(2,1)S(1)} %get-tuple-element.54), channel_id=1, source_target_pairs={{1,2},{2,1},{3,4},{4,3},{5,6},{6,5},{7,8},{8,7},{9,10},{10,9},{11,... | collective-permute-start | bytes 786440 | tf_op jit(solution)/shard_map/ppermute | solution.py:647
  51.5 10.4 %collective-permute-start.7 = (bf16[8,128,128]{2,1,0:T(8,128)(2,1)S(1)}, bf16[8,128,128]{2,1,0:T(8,128)(2,1)S(1)}, u32[]{:S(2)}, u32[]{:S(2)}) collective-permute-start(bf16[8,128,128]{2,1,0:T(8,128)(2,1)S(1)} %get-tuple-element.55), channel_id=1, source_target_pairs={{0,1},{1,0},{2,3},{3,2},{4,5},{5,4},{6,7},{7,6},{8,9},{9,8},{10,11... | collective-permute-start | bytes 786440 | tf_op jit(solution)/shard_map/ppermute | solution.py:648
  56.8 13.3 %collective-permute-start.4 = (bf16[8,128,128]{2,1,0:T(8,128)(2,1)S(1)}, bf16[8,128,128]{2,1,0:T(8,128)(2,1)S(1)}, u32[]{:S(2)}, u32[]{:S(2)}) collective-permute-start(bf16[8,128,128]{2,1,0:T(8,128)(2,1)S(1)} %get-tuple-element.51), channel_id=1, source_target_pairs={{1,2},{2,1},{3,4},{4,3},{5,6},{6,5},{7,8},{8,7},{9,10},{10,9},{11,... | collective-permute-start | bytes 786440 | tf_op jit(solution)/shard_map/ppermute | solution.py:647
  61.8 8.4 %collective-permute-start.5 = (bf16[8,128,128]{2,1,0:T(8,128)(2,1)S(1)}, bf16[8,128,128]{2,1,0:T(8,128)(2,1)S(1)}, u32[]{:S(2)}, u32[]{:S(2)}) collective-permute-start(bf16[8,128,128]{2,1,0:T(8,128)(2,1)S(1)} %get-tuple-element.52), channel_id=1, source_target_pairs={{0,1},{1,0},{2,3},{3,2},{4,5},{5,4},{6,7},{7,6},{8,9},{9,8},{10,11... | collective-permute-start | bytes 786440 | tf_op jit(solution)/shard_map/ppermute | solution.py:648
  70.2 6.5 %copy-start.1 = (f32[8,128,128]{2,1,0:T(8,128)S(1)}, f32[8,128,128]{2,1,0:T(8,128)}, u32[]{:S(2)}) copy-start(f32[8,128,128]{2,1,0:T(8,128)} %get-tuple-element.68.late_ref) | copy-start | bytes 1572868
  72.8 1.6 %collective-permute-start.8 = (f32[2,8,32,128]{3,2,1,0:T(8,128)S(1)}, f32[2,8,32,128]{3,2,1,0:T(8,128)S(1)}, u32[]{:S(2)}, u32[]{:S(2)}) collective-permute-start(f32[2,8,32,128]{3,2,1,0:T(8,128)S(1)} %get-tuple-element.67), channel_id=1, source_target_pairs={{0,64},{64,0},{128,192},{192,128},{1,65},{65,1},{129,193},{193,129... | collective-permute-start | bytes 786440 | tf_op jit(solution)/shard_map/ppermute | solution.py:728
  74.4 7.1 %collective-permute-start.9 = (f32[8,32,128]{2,1,0:T(8,128)S(1)}, f32[8,32,128]{2,1,0:T(8,128)S(1)}, u32[]{:S(2)}, u32[]{:S(2)}) collective-permute-start(f32[8,32,128]{2,1,0:T(8,128)S(1)} %fusion.order_ref), channel_id=1, source_target_pairs={{0,128},{128,0},{64,192},{192,64},{1,129},{129,1},{65,193},{193,65... | collective-permute-start | bytes 393224 | tf_op jit(solution)/shard_map/ppermute | solution.py:730

commit v8 on v7

--- a/solution.py
+++ b/solution.py
@@ -312,7 +312,7 @@
     own, buf, now_side, next_side, speed_side, sems,
 ):
     par = parity()
-    (copy,) = fetch((inject_hbm.at[:, 0:2],), (inject_ref,), sems)
+    (copy,) = fetch((inject_hbm.at[:, 0:3],), (inject_ref,), sems)
     mark_ref[...] = jnp.zeros(mark_ref.shape, f32)
     zero_pads(own)
     zero_pads(buf)
@@ -352,11 +352,12 @@
 
 def adjoint_first_kernel(
     now_ref, speed_ref, inject_ref, side_ref, part_ref, got_b, order_ref,
-    first_ref, second_ref, lam_ref, speed_ext, q3_ref,
-    buf, now_side, next_side, speed_side,
+    first_ref, second_ref, lam_ref, speed_ext, part1_ref,
+    buf, q3_ref, q2_own, now_side, next_side, speed_side,
 ):
     par = parity()
     zero_pads(buf)
+    zero_pads(q2_own)
     zero_pads(q3_ref)
     weights = band()
     own = slice(HALF, HALF + DEPTH)
@@ -392,9 +393,22 @@
 
     def own_lam2(p, row, lap):
         lam = 2.0 * lam_ref[p + HALF, rows(row), :] - now_ref[p, rows(row), :] + lap
-        lam_ref[EXT + p, rows(row), :] = lam + inject_ref[p + HALF, 1, rows(row), :]
+        lam = lam + inject_ref[p + HALF, 1, rows(row), :]
+        lam_ref[EXT + p, rows(row), :] = lam
+        q2_own[p, padded(row), :] = lam * speed_ref[p, rows(row), :]
 
     sweep_own(q3_ref, HALF, weights, own_lam2)
+
+    def halo_lam2(h, row, lap):
+        lam_ref[EXT + DEPTH + h, rows(row), :] = lam_ref[EXT + DEPTH + h, rows(row), :] + lap
+
+    sweep_halo_alone(q3_ref, weights, halo_lam2)
+
+    def own_lam1(p, row, lap):
+        lam = 2.0 * lam_ref[EXT + p, rows(row), :] - lam_ref[p + HALF, rows(row), :] + lap
+        part1_ref[p, rows(row), :] = lam + inject_ref[p + HALF, 2, rows(row), :]
+
+    sweep_own_alone(q2_own, weights, own_lam1)
     send_second(par, q3_ref, lam_ref.at[EXT : EXT + DEPTH], speed_ext, True, first_ref, second_ref)
 
 
@@ -430,7 +444,7 @@
 
 
 def forward_first_kernel(
-    depth_ref, row_ref, wave_ref, mine_a, mine_b, own_ref, part_ref, got_a, got_b, speed_ext,
+    depth_ref, row_ref, wave_ref, mine_a, mine_b, own_ref, part_ref, got_a, got_b, speed_ext, adjoint_a, adjoint_b,
     first_ref, second_ref, u1_ref, u2_ref, base_ref, lap0_ref, lap1_ref,
     below, above, prev_own,
 ):
@@ -494,74 +508,59 @@
         add_cell(u2_ref, local - HALF, across, along_y, wave_ref[0, 1])
 
     send_second(par, u1_ref, u2_ref, speed_ext, False, first_ref, second_ref)
+    first_ref[2 * HALF : 4 * HALF] = adjoint_a[...]
+    second_ref[2 * HALF : 4 * HALF] = adjoint_b[...]
 
 
 def middle_kernel(
-    depth_ref, row_ref, wave_ref, inject_hbm, got_b, got_a, lam_ref, q3_ref, speed_ext, u1_ref, u2_own, base_ref, lap0_ref, lap1_ref,
-    late_ref, u2_ref, grad_ref, lam2_halo, buf2, own_ref, part_ref,
-    inject_ref, sems,
+    depth_ref, row_ref, wave_ref, inject_hbm, speed_ext, u1_ref, u2_own, base_ref,
+    u2_ref, own_ref, part_ref, inject_ref,
+    sems,
+):
+    (copy,) = fetch((inject_hbm.at[:, 2:4],), (inject_ref,), sems)
+    weights = band()
+
+    def halo_u2(h, row, lap):
+        e = ext_of_halo(h)
+        u2_ref[h, rows(row), :] = base_ref[h, rows(row), :] + speed_ext[e, rows(row), :] * lap
+
+    sweep_halo_alone(u1_ref, weights, halo_u2)
+    local, across, along_y = source_place(depth_ref, row_ref)
+
+    @pl.when(((local >= 0) & (local < HALF)) | ((local >= HALF + DEPTH) & (local < EXT)))
+    def _():
+        add_cell(u2_ref, jnp.where(local < HALF, local, local - DEPTH), across, along_y, wave_ref[0, 1])
+
+    zero_pads(own_ref)
+    own_ref[:, PAD : PAD + NX, :] = u2_own[...]
+
+    def u2_alone(p, row, lap):
+        part_ref[p, rows(row), :] = lap
+
+    sweep_own_alone(own_ref, weights, u2_alone)
+    copy.wait()
+
+
+def adjoint_last_kernel(
+    inject_ref, late_ref, lam_ref, lam2_halo, got_b, got_a, speed_ext, order_ref, early_ref, buf2, buf1
 ):
     par = parity()
-    (copy,) = fetch((inject_hbm.at[HALF : HALF + DEPTH, 2],), (inject_ref,), sems)
     zero_pads(buf2)
+    zero_pads(buf1)
     weights = band()
     inner = slice(PAD, PAD + NX)
-
-    def alone(h, row, lap):
-        lam2_halo[h, rows(row), :] = lam_ref[EXT + DEPTH + h, rows(row), :] + lap
-
-    sweep_halo_alone(q3_ref, weights, alone)
-    copy.wait()
+    buf1[HALF : HALF + DEPTH, inner, :] = late_ref[...] * speed_ext[HALF : HALF + DEPTH]
+    buf2[2 * HALF : 2 * HALF + DEPTH, inner, :] = lam_ref[EXT : EXT + DEPTH] * speed_ext[HALF : HALF + DEPTH]
 
     def halo(lower, upper):
         for ref, at, far_at in ((lower, 0, 0), (upper, HALF, WIDE - HALF)):
             ext_at = ext_of_halo(at)
-            value = lam2_halo[at : at + HALF] + ref[0:HALF].astype(f32)
-            lam2_halo[at : at + HALF] = value
-            buf2[ext_at + HALF : ext_at + 2 * HALF, inner, :] = value * speed_ext[ext_at : ext_at + HALF]
-            buf2[far_at : far_at + HALF, inner, :] = ref[HALF : 2 * HALF].astype(f32)
+            buf2[ext_at + HALF : ext_at + 2 * HALF, inner, :] = (
+                lam2_halo[at : at + HALF] * speed_ext[ext_at : ext_at + HALF]
+            )
+            buf2[far_at : far_at + HALF, inner, :] = ref[3 * HALF : 4 * HALF].astype(f32)
 
     by_side(par, got_a, got_b, halo)
-    buf2[2 * HALF : 2 * HALF + DEPTH, inner, :] = lam_ref[EXT : EXT + DEPTH] * speed_ext[HALF : HALF + DEPTH]
-
-    def own_lam1(p, row, lap):
-        lam = 2.0 * lam_ref[EXT + p, rows(row), :] - lam_ref[p + HALF, rows(row), :] + lap
-        lam = lam + inject_ref[p, rows(row), :]
-        late_ref[p, rows(row), :] = lam
-        grad_ref[p, rows(row), :] = (
-            lam * lap0_ref[p, rows(row), :] + lam_ref[EXT + p, rows(row), :] * lap1_ref[p, rows(row), :]
-        )
-
-    sweep_own(buf2, 2 * HALF, weights, own_lam1)
-
-    def halo_u2(h, row, lap):
-        e = ext_of_halo(h)
-        u2_ref[h, rows(row), :] = base_ref[h, rows(row), :] + speed_ext[e, rows(row), :] * lap
-
-    sweep_halo_alone(u1_ref, weights, halo_u2)
-    local, across, along_y = source_place(depth_ref, row_ref)
-
-    @pl.when(((local >= 0) & (local < HALF)) | ((local >= HALF + DEPTH) & (local < EXT)))
-    def _():
-        add_cell(u2_ref, jnp.where(local < HALF, local, local - DEPTH), across, along_y, wave_ref[0, 1])
-
-    zero_pads(own_ref)
-    own_ref[:, inner, :] = u2_own[...]
-
-    def u2_alone(p, row, lap):
-        part_ref[p, rows(row), :] = lap
-
-    sweep_own_alone(own_ref, weights, u2_alone)
-
-
-def adjoint_last_kernel(
-    inject_hbm, late_ref, lam_ref, lam2_halo, buf2, speed_ext, order_ref, early_ref, buf1, inject_ref, sems
-):
-    (copy,) = fetch((inject_hbm.at[:, 2:4],), (inject_ref,), sems)
-    zero_pads(buf1)
-    weights = band()
-    buf1[HALF : HALF + DEPTH, PAD : PAD + NX, :] = late_ref[...] * speed_ext[HALF : HALF + DEPTH]
-    copy.wait()
 
     def halo_lam1(h, row, lap):
         e = ext_of_halo(h)
@@ -580,7 +579,9 @@
 
 def forward_second_kernel(
     depth_ref, row_ref, wave_ref, got_b, got_a, u1_ref, own_ref, part_ref, u2_halo_ref, speed_ext, lam_ref, lam4_ref,
-    grad_ref, keep_ref, send_ref, below, above, buf3, total,
+    part1_ref, lap0_ref, lap1_ref,
+    keep_ref, send_ref, late_ref, lam2_halo,
+    below, above, buf3, total, q2_halo,
 ):
     par = parity()
     zero_pads(below)
@@ -600,6 +601,10 @@
                 lambda p: own_ref[p, inner, :],
             )
 
+            value = lam_ref[EXT + DEPTH + at : EXT + DEPTH + at + HALF] + ref[2 * HALF : 3 * HALF].astype(f32)
+            lam2_halo[at : at + HALF] = value
+            q2_halo[at : at + HALF] = value * speed_ext[first : first + HALF]
+
             def body(j, row, lap, buf=buf, first=first):
                 value = 2.0 * buf[HALF + j, padded(row), :] - u1_ref[first + j, padded(row), :]
                 buf3[first + j, padded(row), :] = value + speed_ext[first + j, rows(row), :] * lap
@@ -614,7 +619,17 @@
             lap = part_ref[p, rows(row), :] + side_terms(above if upper else below, upper, p, row)
             value = 2.0 * own_ref[p, padded(row), :] - u1_ref[e, padded(row), :]
             buf3[e, padded(row), :] = value + speed_ext[e, rows(row), :] * lap
-            total[p, rows(row), :] = grad_ref[p, rows(row), :] + lap * lam_ref[e, rows(row), :]
+            lam1 = part1_ref[p, rows(row), :]
+            for k in range(1, HALF + 1):
+                q = p + k - HALF if upper else p - k + HALF
+                if (q >= HALF) if upper else (q < HALF):
+                    lam1 = lam1 + stencil_coef[k] * q2_halo[q, rows(row), :]
+            late_ref[p, rows(row), :] = lam1
+            total[p, rows(row), :] = (
+                lam1 * lap0_ref[p, rows(row), :]
+                + lam_ref[EXT + p, rows(row), :] * lap1_ref[p, rows(row), :]
+                + lap * lam_ref[e, rows(row), :]
+            )
     local, across, along_y = source_place(depth_ref, row_ref)
 
     @pl.when((local >= 0) & (local < EXT))
@@ -680,7 +695,6 @@
         ],
         (rec_depth.reshape(1, count), rec_row.reshape(1, count), residuals[0]), us=4, out=HB,
     )
-    fields = pltpu.VMEM((EXT, 2, NX, NY), f32)
     trio = ((3 * HALF, ROWS, NY), f32)
     four = pltpu.VMEM((HALF, NX, NY), f32)
     own_wide = ((DEPTH, ROWS, NY), f32)
@@ -689,49 +703,48 @@
         (holder_list.reshape(64), incoming) + in_hbm(order),
     )
     side, part, inject01, order = call(
-        adjoint_side_kernel, "adjoint_side", [VM] * 3 + [HB, VM], [((4 * HALF, NX, NY), f32), slab, ((EXT, 2, NX, NY), f32), mark],
+        adjoint_side_kernel, "adjoint_side", [VM] * 3 + [HB, VM], [((4 * HALF, NX, NY), f32), slab, ((EXT, 3, NX, NY), f32), mark],
         [buffer(DEPTH), pltpu.VMEM(*trio), four, four, four, pltpu.SemaphoreType.DMA((1,))],
         (lam4, lam5, speed_sq) + in_hbm(inject) + (got_a,),
     )
     own0, lap0_part, order = call(
         forward_own_kernel, "forward_own", [VM, VM], [own_wide, slab, mark], [], (mine_a, order),
     )
-    send_a, send_b, lam23, speed_ext, q3 = call(
+    adjoint_a, adjoint_b, lam23, speed_ext, part1 = call(
         adjoint_first_kernel, "adjoint_first", [VM] * 7,
-        [planes(8)] * 2 + [((EXT + 2 * DEPTH, NX, NY), f32), ext, wide],
-        [pltpu.VMEM(*trio), four, four, four],
+        [planes(8)] * 2 + [((EXT + 2 * DEPTH, NX, NY), f32), ext, slab],
+        [pltpu.VMEM(*trio), buffer(EXT), buffer(DEPTH), four, four, four],
         (lam4, speed_sq, inject01, side, part, got_b, order),
     )
-    back_a, back_b = swap(send_a, send_b)
-
     got_a, got_b = swap(mine_a, mine_b)
     send_a, send_b, u1, u2, base_u, lap0, lap1 = call(
-        forward_first_kernel, "forward_first", [SM] * 3 + [VM] * 7,
-        [planes(8)] * 2 + [wide, slab, slab, slab, slab],
+        forward_first_kernel, "forward_first", [SM] * 3 + [VM] * 9,
+        [planes(16)] * 2 + [wide, slab, slab, slab, slab],
         [pltpu.VMEM(*trio), pltpu.VMEM(*trio), pltpu.VMEM(*slab)],
-        (src_depth, src_row, wavelet, mine_a, mine_b, own0, lap0_part, got_a, got_b, speed_ext),
+        (src_depth, src_row, wavelet, mine_a, mine_b, own0, lap0_part, got_a, got_b, speed_ext, adjoint_a, adjoint_b),
     )
     got_a, got_b = swap(send_a, send_b)
-    late, u2_halo, grad, lam2_halo, q2, own2, lap2_part = call(
-        middle_kernel, "middle", [SM] * 3 + [HB] + [VM] * 10,
-        [slab] * 4 + [((WIDE, ROWS, NY), f32), own_wide, slab],
-        [pltpu.VMEM(*slab), pltpu.SemaphoreType.DMA((1,))],
-        (src_depth, src_row, wavelet) + in_hbm(inject)
-        + (back_b, back_a, lam23, q3, speed_ext, u1, u2, base_u, lap0, lap1),
+    u2_halo, own2, lap2_part, inject23 = call(
+        middle_kernel, "middle", [SM] * 3 + [HB] + [VM] * 4, [slab, own_wide, slab, ((EXT, 2, NX, NY), f32)],
+        [pltpu.SemaphoreType.DMA((1,))],
+        (src_depth, src_row, wavelet) + in_hbm(inject) + (speed_ext, u1, u2, base_u),
     )
     quarter = ((2, DEPTH, NX // 4, NY), f32)
-    keep, send = call(
-        forward_second_kernel, "forward_second", [SM] * 3 + [VM] * 10, [quarter] * 2,
-        [pltpu.VMEM(*trio), pltpu.VMEM(*trio), buffer(EXT), pltpu.VMEM(*slab)],
-        (src_depth, src_row, wavelet, got_b, got_a, u1, own2, lap2_part, u2_halo, speed_ext, lam23, lam4, grad),
+    keep, send, late, lam2_halo = call(
+        forward_second_kernel, "forward_second", [SM] * 3 + [VM] * 12, [quarter] * 2 + [slab] * 2,
+        [pltpu.VMEM(*trio), pltpu.VMEM(*trio), buffer(EXT), pltpu.VMEM(*slab), pltpu.VMEM(*slab)],
+        (
+            src_depth, src_row, wavelet, got_b, got_a, u1, own2, lap2_part, u2_halo, speed_ext, lam23, lam4,
+            part1, lap0, lap1,
+        ),
     )
     got = lax.ppermute(send, "shot", [(0, 1), (1, 0), (2, 3), (3, 2)])
     part = keep[1] + got[1]
     other = lax.ppermute(part, "shot", [(0, 2), (2, 0), (1, 3), (3, 1)])
     (early,) = call(
-        adjoint_last_kernel, "adjoint_last", [HB] + [VM] * 6, [slab],
-        [buffer(EXT), fields, pltpu.SemaphoreType.DMA((1,))],
-        in_hbm(inject) + (late, lam23, lam2_halo, q2, speed_ext, part),
+        adjoint_last_kernel, "adjoint_last", [VM] * 8, [slab],
+        [buffer(WIDE), buffer(EXT)],
+        (inject23, late, lam23, lam2_halo, got_b, got_a, speed_ext, part),
     )
     gradient = keep[0] + got[0] + other
     return (gradient, late[None], early[None])

time: 82.7 us -> 89 us (1.076)
  waiting for transfers between devices: 11.8 us -> 22.2 us
  starting transfers between devices: 36.6 us -> 33 us
  Pallas kernels: 30.9 us -> 29.5 us
  local copies, waits for them, and re-layouts: 0.05 us -> 1.09 us
    ppermute x4 -> x3, waiting for transfers between devices: 9.66 us -> 19.6 us  [swap(): far = lax.ppermute(b, 'dom', odd)]
    ppermute x4 -> x3, starting transfers between devices: 19.2 us -> 15.4 us  [swap(): far = lax.ppermute(b, 'dom', odd)]
    pallas_call x11, Pallas kernels: 30.9 us -> 29.5 us  [call(): pl.pallas_call(kernel, name=name, out_shape=[pltpu.HBM(*o) if out is HB e...]
    unnamed x18, local copies, waits for them, and re-layouts: 0.05 us -> 1.09 us
    ppermute x4 -> x3, starting transfers between devices: 1.83 us -> 2.12 us  [swap(): return (lax.ppermute(a, 'dom', even), far)]
  transfers between devices with their start and end apart: 11 -> 9, of which waited for: 5 -> 5; matrix products, arithmetic and copies ran while one was open for 0% -> 0% of each run, Pallas kernels for 31% -> 23%
where the time goes in v8:
time: 89 us; the launch traced here: 88.6 us
  starting transfers between devices  33 us (37%)
  Pallas kernels  29.5 us (33%)
  waiting for transfers between devices  22.2 us (25%)
  between operations  2.18 us (2%)
  local copies, waits for them, and re-layouts  1.09 us (1%)
    pallas_call x11, Pallas kernels, call(): pl.pallas_call(kernel, name=name, out_shape=[pltpu.HBM(*o) if out is HB e...  29.5 us
    ppermute x3, waiting for transfers between devices, swap(): far = lax.ppermute(b, 'dom', odd)  19.6 us
    ppermute x3, starting transfers between devices, swap(): far = lax.ppermute(b, 'dom', odd)  15.4 us
    all_to_all x1, starting transfers between devices, per_device(): lax.all_to_all(outgoing, 'dom', split_axis=0, concat_axis=0, tiled=True)  13.2 us
    ppermute x1, starting transfers between devices, per_device(): other = lax.ppermute(part, 'shot', [(0, 2), (2, 0), (1, 3), (3, 1)])  2.2 us
    ppermute x3, starting transfers between devices, swap(): return (lax.ppermute(a, 'dom', even), far)  2.12 us
  transfers between devices with their start and end apart: 9, of which 5 were waited for; matrix products, arithmetic and copies ran while one was open for 0% of the time, Pallas kernels for 23%

profile of v8, /device:TPU:2, one launch (start us, length us, event | category | flops | bytes accessed | tf_op | source)
XLA Modules:
  0.0 88.6 jit_solution(1876406706446332389)
XLA Ops:
  0.6 2.4 %gather.1 = bf16[64,32,128]{2,1,0:T(8,128)(2,1)} custom-call(s32[1,64]{1,0:T(1,128)} %bitcast.29, bf16[64,4096]{1,0:T(8,128)(2,1)} %bitcast.28), custom_call_target="tpu_custom_call" | custom-call | flops 2000000000 | bytes 7200000 | tf_op jit(solution)/shard_map/gather/pallas_call | solution.py:43
  3.1 13.2 %all-to-all-start = ((bf16[64,32,128]{2,1,0:T(8,128)(2,1)}), bf16[64,32,128]{2,1,0:T(8,128)(2,1)S(1)}, u32[]{:S(2)}, u32[]{:S(2)}) async-start(bf16[64,32,128]{2,1,0:T(8,128)(2,1)} %gather.1), calls=%async_computation | async-start | bytes 1048576 | tf_op jit(solution)/shard_map/all_to_all | solution.py:682
  16.3 0.0 copy-start.5
  16.3 0.0 copy-start.6
  16.3 0.0 copy-start.7
  16.4 1.5 %adjoint_pack.1 = (bf16[19,128,128]{2,1,0:T(8,128)(2,1)S(1)}, bf16[19,128,128]{2,1,0:T(8,128)(2,1)S(1)}) custom-call(f32[8,128,128]{2,1,0:T(8,128)} %bitcast.16, f32[8,128,128]{2,1,0:T(8,128)} %bitcast.21, f32[8,128,128]{2,1,0:T(8,128)} %speed_ref.3), custom_call_target="tpu_custom_call" | custom-call | flops 2000000000 | bytes 7200000 | tf_op jit(solution)/shard_map/adjoint_pack/pallas_call | solution.py:43
  17.9 1.6 %collective-permute-start = (bf16[19,128,128]{2,1,0:T(8,128)(2,1)S(1)}, bf16[19,128,128]{2,1,0:T(8,128)(2,1)S(1)}, u32[]{:S(2)}, u32[]{:S(2)}) collective-permute-start(bf16[19,128,128]{2,1,0:T(8,128)(2,1)S(1)} %get-tuple-element.40), channel_id=1, source_target_pairs={{0,1},{1,0},{2,3},{3,2},{4,5},{5,4},{6,7},{7,6},{8,9},{9,8},{10,11... | collective-permute-start | bytes 1867784 | tf_op jit(solution)/shard_map/ppermute | solution.py:663
  19.5 6.1 %collective-permute-start.3 = (bf16[19,128,128]{2,1,0:T(8,128)(2,1)S(1)}, bf16[19,128,128]{2,1,0:T(8,128)(2,1)S(1)}, u32[]{:S(2)}, u32[]{:S(2)}) collective-permute-start(bf16[19,128,128]{2,1,0:T(8,128)(2,1)S(1)} %get-tuple-element.47), channel_id=1, source_target_pairs={{1,2},{2,1},{3,4},{4,3},{5,6},{6,5},{7,8},{8,7},{9,10},{10,9},{11,... | collective-permute-start | bytes 1867784 | tf_op jit(solution)/shard_map/ppermute | solution.py:662
  25.5 0.0 copy-done.5
  25.5 0.0 copy-done.6
  25.5 0.0 copy-done.7
  25.6 0.0 copy-start.8
  25.6 7.2 %inject.1 = (f32[16,4,128,128]{3,2,1,0:T(8,128)}, f32[8,128]{1,0:T(8,128)}) custom-call(s32[1,1024]{1,0:T(1,128)S(1)} %bitcast.24, s32[1,1024]{1,0:T(1,128)S(1)} %bitcast.25, f32[4,1024]{1,0:T(4,128)S(1)} %bitcast.23), custom_call_target="tpu_custom_call" | custom-call | flops 4000000000 | bytes 14400000 | tf_op jit(solution)/shard_map/inject/pallas_call | solution.py:43
  34.1 0.0 all-to-all-done.pieces_ref
  34.1 0.0 copy-done.8
  34.1 0.0 copy-start
  34.1 0.0 copy-start.3
  34.1 0.0 copy-start.4
  34.1 0.7 forward_pack.1
  34.8 0.5 collective-permute-start.1
  35.3 6.0 %collective-permute-start.2 = (bf16[12,128,128]{2,1,0:T(8,128)(2,1)S(1)}, bf16[12,128,128]{2,1,0:T(8,128)(2,1)S(1)}, u32[]{:S(2)}, u32[]{:S(2)}) collective-permute-start(bf16[12,128,128]{2,1,0:T(8,128)(2,1)S(1)} %get-tuple-element.38.mine_b), channel_id=1, source_target_pairs={{1,2},{2,1},{3,4},{4,3},{5,6},{6,5},{7,8},{8,7},{9,10},{10,9},{11,... | collective-permute-start | bytes 1179656 | tf_op jit(solution)/shard_map/ppermute | solution.py:662
  41.3 0.0 collective-permute-done.got_a
  41.3 0.0 copy-done
  41.3 0.0 copy-done.3
  41.3 0.0 copy-done.4
  41.3 2.5 %adjoint_side.1 = (f32[16,128,128]{2,1,0:T(8,128)S(1)}, f32[8,128,128]{2,1,0:T(8,128)S(1)}, f32[16,3,128,128]{3,2,1,0:T(8,128)S(1)}, f32[8,128]{1,0:T(8,128)S(1)}) custom-call(f32[8,128,128]{2,1,0:T(8,128)S(1)} %bitcast.17, f32[8,128,128]{2,1,0:T(8,128)S(1)} %bitcast.22, f32[8,128,128]{2,1,0:T(8,128)S(1)} %copy-done.4, ...), custom_call_target="tpu_custom_call" | custom-call | flops 2000000000 | bytes 7200000 | tf_op jit(solution)/shard_map/adjoint_side/pallas_call | solution.py:43
  43.9 0.7 forward_own.1
  44.6 2.1 %collective-permute-done.3.got_b = bf16[19,128,128]{2,1,0:T(8,128)(2,1)S(1)} collective-permute-done((bf16[19,128,128]{2,1,0:T(8,128)(2,1)S(1)}, bf16[19,128,128]{2,1,0:T(8,128)(2,1)S(1)}, u32[]{:S(2)}, u32[]{:S(2)}) %collective-permute-start.3) | collective-permute-done | bytes 622624 | tf_op jit(solution)/shard_map/ppermute | solution.py:662
  46.7 0.0 copy-start.2
  46.7 3.1 %adjoint_first.1 = (bf16[8,128,128]{2,1,0:T(8,128)(2,1)S(1)}, bf16[8,128,128]{2,1,0:T(8,128)(2,1)S(1)}, f32[32,128,128]{2,1,0:T(8,128)S(1)}, f32[16,128,128]{2,1,0:T(8,128)S(1)}, f32[8,128,128]{2,1,0:T(8,128)S(1)}) custom-call(f32[8,128,128]{2,1,0:T(8,128)S(1)} %bitcast.18, f32[8,128,128]{2,1,0:T(8,128)S(1)} %copy-done.4, ...), custom_call_target="tpu_custom_call" | custom-call | flops 2000000000 | bytes 7200000 | tf_op jit(solution)/shard_map/adjoint_first/pallas_call | solution.py:43
  49.9 0.0 collective-permute-done.1.got_a
  49.9 4.2 %collective-permute-done.2.got_b = bf16[12,128,128]{2,1,0:T(8,128)(2,1)S(1)} collective-permute-done((bf16[12,128,128]{2,1,0:T(8,128)(2,1)S(1)}, bf16[12,128,128]{2,1,0:T(8,128)(2,1)S(1)}, u32[]{:S(2)}, u32[]{:S(2)}) %collective-permute-start.2) | collective-permute-done | bytes 393248 | tf_op jit(solution)/shard_map/ppermute | solution.py:662
  54.1 0.0 copy-done.2
  54.1 3.0 %forward_first.1 = (bf16[16,128,128]{2,1,0:T(8,128)(2,1)S(1)}, bf16[16,128,128]{2,1,0:T(8,128)(2,1)S(1)}, f32[16,144,128]{2,1,0:T(8,128)S(1)}, f32[8,128,128]{2,...) custom-call(s32[1]{0:T(128)S(6)} %copy.15.depth_ref, ...), custom_call_target="tpu_custom_call" | custom-call | flops 2000000000 | bytes 7200000 | tf_op jit(solution)/shard_map/forward_first/pallas_call | solution.py:43
  57.0 3.4 %collective-permute-start.4 = (bf16[16,128,128]{2,1,0:T(8,128)(2,1)S(1)}, bf16[16,128,128]{2,1,0:T(8,128)(2,1)S(1)}, u32[]{:S(2)}, u32[]{:S(2)}) collective-permute-start(bf16[16,128,128]{2,1,0:T(8,128)(2,1)S(1)} %get-tuple-element.52), channel_id=1, source_target_pairs={{1,2},{2,1},{3,4},{4,3},{5,6},{6,5},{7,8},{8,7},{9,10},{10,9},{11,... | collective-permute-start | bytes 1572872 | tf_op jit(solution)/shard_map/ppermute | solution.py:662
  60.4 0.1 collective-permute-start.5
  60.5 2.2 %middle.1 = (f32[8,128,128]{2,1,0:T(8,128)S(1)}, f32[8,144,128]{2,1,0:T(8,128)S(1)}, f32[8,128,128]{2,1,0:T(8,128)S(1)}, f32[16,2,128,128]{3,2,1,0:T(8,128)S(1)}) custom-call(s32[1]{0:T(128)S(6)} %copy.15.depth_ref, s32[1]{0:T(128)S(6)} %copy.16.row_ref, f32[1,3]{1,0:T(1,128)S(1)} %copy-done.2, f32[16,4,128,128]{3,2,1,0:T(8,128)} %get-tuple-element.39.inject_hbm, ...), custom_call_target="tpu_custom_call" | custom-call | flops 2000000000 | bytes 7200000 | tf_op jit(solution)/shard_map/middle/pallas_call | solution.py:43
  62.7 13.3 %collective-permute-done.4.got_b = bf16[16,128,128]{2,1,0:T(8,128)(2,1)S(1)} collective-permute-done((bf16[16,128,128]{2,1,0:T(8,128)(2,1)S(1)}, bf16[16,128,128]{2,1,0:T(8,128)(2,1)S(1)}, u32[]{:S(2)}, u32[]{:S(2)}) %collective-permute-start.4) | collective-permute-done | bytes 524320 | tf_op jit(solution)/shard_map/ppermute | solution.py:662
  76.0 0.0 collective-permute-done.5.got_a
  76.0 3.2 %forward_second.1 = (f32[2,8,32,128]{3,2,1,0:T(8,128)S(1)}, f32[2,8,32,128]{3,2,1,0:T(8,128)S(1)}, f32[8,128,128]{2,1,0:T(8,128)}, f32[8,128,128]{2,1,0:T(8,128)S(1)}) custom-call(s32[1]{0:T(128)S(6)} %copy.15.depth_ref, s32[1]{0:T(128)S(6)} %copy.16.row_ref, f32[1,3]{1,0:T(1,128)S(1)} %copy-done.2, bf16[16,128,128]{2,1,0:T(8,128)(2,1)S(1)} %collective-permute-done.4.got_b, ...), custom_call_target="tpu_custom_call" | custom-call | flops 2000000000 | bytes 7200000 | tf_op jit(solution)/shard_map/forward_second/pallas_call | solution.py:43
  79.3 0.0 collective-permute-start.6
  79.3 1.5 %collective-permute-done.6 = f32[2,8,32,128]{3,2,1,0:T(8,128)S(1)} collective-permute-done((f32[2,8,32,128]{3,2,1,0:T(8,128)S(1)}, f32[2,8,32,128]{3,2,1,0:T(8,128)S(1)}, u32[]{:S(2)}, u32[]{:S(2)}) %collective-permute-start.6) | collective-permute-done | bytes 262176 | tf_op jit(solution)/shard_map/ppermute | solution.py:741
  80.8 2.2 %collective-permute-start.7 = (f32[8,32,128]{2,1,0:T(8,128)S(1)}, f32[8,32,128]{2,1,0:T(8,128)S(1)}, u32[]{:S(2)}, u32[]{:S(2)}) collective-permute-start(f32[8,32,128]{2,1,0:T(8,128)S(1)} %fusion.order_ref), channel_id=1, source_target_pairs={{0,128},{128,0},{64,192},{192,64},{1,129},{129,1},{65,193},{193,65... | collective-permute-start | bytes 393224 | tf_op jit(solution)/shard_map/ppermute | solution.py:743
  83.0 0.0 copy-start.1
  83.0 1.0 %copy-done.1 = f32[8,128,128]{2,1,0:T(8,128)S(1)} copy-done((f32[8,128,128]{2,1,0:T(8,128)S(1)}, f32[8,128,128]{2,1,0:T(8,128)}, u32[]{:S(2)}) %copy-start.1) | copy-done | bytes 524312
  84.1 2.8 %adjoint_last.1 = f32[8,128,128]{2,1,0:T(8,128)} custom-call(f32[16,2,128,128]{3,2,1,0:T(8,128)S(1)} %get-tuple-element.67.inject_ref, f32[8,128,128]{2,1,0:T(8,128)S(1)} %copy-done.1, f32[32,128,128]{2,1,0:T(8,128)S(1)} %get-tuple-element.60.lam_ref, f32[8,128,128]{2,1,0:T(8,128)S(1)} %get-tuple-element.68.lam2_halo, ...), custom_call_target="tpu_custom_call" | custom-call | flops 2000000000 | bytes 7200000 | tf_op jit(solution)/shard_map/adjoint_last/pallas_call | solution.py:43
  86.9 1.0 %collective-permute-done.7 = f32[8,32,128]{2,1,0:T(8,128)S(1)} collective-permute-done((f32[8,32,128]{2,1,0:T(8,128)S(1)}, f32[8,32,128]{2,1,0:T(8,128)S(1)}, u32[]{:S(2)}, u32[]{:S(2)}) %collective-permute-start.7) | collective-permute-done | bytes 131104 | tf_op jit(solution)/shard_map/ppermute | solution.py:743
  87.9 0.7 fusion.2
  (1 shorter events, 0.0 us)
Async XLA Ops:
  3.1 31.0 %all-to-all-start = ((bf16[64,32,128]{2,1,0:T(8,128)(2,1)}), bf16[64,32,128]{2,1,0:T(8,128)(2,1)S(1)}, u32[]{:S(2)}, u32[]{:S(2)}) async-start(bf16[64,32,128]{2,1,0:T(8,128)(2,1)} %gather.1), calls=%async_computation | async-start | bytes 1048576 | tf_op jit(solution)/shard_map/all_to_all | solution.py:682
  16.3 9.2 %copy-start.5 = (f32[1,4,1024]{2,1,0:T(4,128)S(1)}, f32[1,4,1024]{2,1,0:T(4,128)}, u32[]{:S(2)}) copy-start(f32[1,4,1024]{2,1,0:T(4,128)} %param.23) | copy-start | bytes 49156
  16.3 9.2 %copy-start.6 = (s32[1024]{0:T(1024)S(1)}, s32[1024]{0:T(1024)}, u32[]{:S(2)}) copy-start(s32[1024]{0:T(1024)} %param.21) | copy-start | bytes 12292
  16.3 9.2 %copy-start.7 = (s32[1024]{0:T(1024)S(1)}, s32[1024]{0:T(1024)}, u32[]{:S(2)}) copy-start(s32[1024]{0:T(1024)} %param.22) | copy-start | bytes 12292
  17.9 23.4 %collective-permute-start = (bf16[19,128,128]{2,1,0:T(8,128)(2,1)S(1)}, bf16[19,128,128]{2,1,0:T(8,128)(2,1)S(1)}, u32[]{:S(2)}, u32[]{:S(2)}) collective-permute-start(bf16[19,128,128]{2,1,0:T(8,128)(2,1)S(1)} %get-tuple-element.40), channel_id=1, source_target_pairs={{0,1},{1,0},{2,3},{3,2},{4,5},{5,4},{6,7},{7,6},{8,9},{9,8},{10,11... | collective-permute-start | bytes 1867784 | tf_op jit(solution)/shard_map/ppermute | solution.py:663
  19.5 27.3 %collective-permute-start.3 = (bf16[19,128,128]{2,1,0:T(8,128)(2,1)S(1)}, bf16[19,128,128]{2,1,0:T(8,128)(2,1)S(1)}, u32[]{:S(2)}, u32[]{:S(2)}) collective-permute-start(bf16[19,128,128]{2,1,0:T(8,128)(2,1)S(1)} %get-tuple-element.47), channel_id=1, source_target_pairs={{1,2},{2,1},{3,4},{4,3},{5,6},{6,5},{7,8},{8,7},{9,10},{10,9},{11,... | collective-permute-start | bytes 1867784 | tf_op jit(solution)/shard_map/ppermute | solution.py:662
  25.6 8.5 %copy-start.8 = (s32[1,1,64]{2,1,0:T(1,128)S(1)}, s32[1,1,64]{2,1,0:T(1,128)}, u32[]{:S(2)}) copy-start(s32[1,1,64]{2,1,0:T(1,128)} %param.14) | copy-start | bytes 772
  34.1 7.2 %copy-start = (f32[1,8,128,128]{3,2,1,0:T(8,128)S(1)}, f32[1,8,128,128]{3,2,1,0:T(8,128)}, u32[]{:S(2)}) copy-start(f32[1,8,128,128]{3,2,1,0:T(8,128)} %param.17) | copy-start | bytes 1572868
  34.1 7.2 %copy-start.3 = (f32[1,8,128,128]{3,2,1,0:T(8,128)S(1)}, f32[1,8,128,128]{3,2,1,0:T(8,128)}, u32[]{:S(2)}) copy-start(f32[1,8,128,128]{3,2,1,0:T(8,128)} %param.16) | copy-start | bytes 1572868
  34.1 7.2 %copy-start.4 = (f32[8,128,128]{2,1,0:T(8,128)S(1)}, f32[8,128,128]{2,1,0:T(8,128)}, u32[]{:S(2)}) copy-start(f32[8,128,128]{2,1,0:T(8,128)} %speed_ref.3) | copy-start | bytes 1572868
  34.8 15.1 %collective-permute-start.1 = (bf16[12,128,128]{2,1,0:T(8,128)(2,1)S(1)}, bf16[12,128,128]{2,1,0:T(8,128)(2,1)S(1)}, u32[]{:S(2)}, u32[]{:S(2)}) collective-permute-start(bf16[12,128,128]{2,1,0:T(8,128)(2,1)S(1)} %get-tuple-element.37.mine_ref.mine_a), channel_id=1, source_target_pairs={{0,1},{1,0},{2,3},{3,2},{4,5},{5,4},{6,7},{7,6},{8,9},{9,8},{10,11... | collective-permute-start | bytes 1179656 | tf_op jit(solution)/shard_map/ppermute | solution.py:663
  35.3 18.8 %collective-permute-start.2 = (bf16[12,128,128]{2,1,0:T(8,128)(2,1)S(1)}, bf16[12,128,128]{2,1,0:T(8,128)(2,1)S(1)}, u32[]{:S(2)}, u32[]{:S(2)}) collective-permute-start(bf16[12,128,128]{2,1,0:T(8,128)(2,1)S(1)} %get-tuple-element.38.mine_b), channel_id=1, source_target_pairs={{1,2},{2,1},{3,4},{4,3},{5,6},{6,5},{7,8},{8,7},{9,10},{10,9},{11,... | collective-permute-start | bytes 1179656 | tf_op jit(solution)/shard_map/ppermute | solution.py:662
  46.7 7.3 %copy-start.2 = (f32[1,3]{1,0:T(1,128)S(1)}, f32[1,3]{1,0:T(1,128)}, u32[]{:S(2)}) copy-start(f32[1,3]{1,0:T(1,128)} %wave_ref.5) | copy-start | bytes 40
  57.0 19.0 %collective-permute-start.4 = (bf16[16,128,128]{2,1,0:T(8,128)(2,1)S(1)}, bf16[16,128,128]{2,1,0:T(8,128)(2,1)S(1)}, u32[]{:S(2)}, u32[]{:S(2)}) collective-permute-start(bf16[16,128,128]{2,1,0:T(8,128)(2,1)S(1)} %get-tuple-element.52), channel_id=1, source_target_pairs={{1,2},{2,1},{3,4},{4,3},{5,6},{6,5},{7,8},{8,7},{9,10},{10,9},{11,... | collective-permute-start | bytes 1572872 | tf_op jit(solution)/shard_map/ppermute | solution.py:662
  60.4 15.6 %collective-permute-start.5 = (bf16[16,128,128]{2,1,0:T(8,128)(2,1)S(1)}, bf16[16,128,128]{2,1,0:T(8,128)(2,1)S(1)}, u32[]{:S(2)}, u32[]{:S(2)}) collective-permute-start(bf16[16,128,128]{2,1,0:T(8,128)(2,1)S(1)} %get-tuple-element.53), channel_id=1, source_target_pairs={{0,1},{1,0},{2,3},{3,2},{4,5},{5,4},{6,7},{7,6},{8,9},{9,8},{10,11... | collective-permute-start | bytes 1572872 | tf_op jit(solution)/shard_map/ppermute | solution.py:663
  79.3 1.5 %collective-permute-start.6 = (f32[2,8,32,128]{3,2,1,0:T(8,128)S(1)}, f32[2,8,32,128]{3,2,1,0:T(8,128)S(1)}, u32[]{:S(2)}, u32[]{:S(2)}) collective-permute-start(f32[2,8,32,128]{3,2,1,0:T(8,128)S(1)} %get-tuple-element.65), channel_id=1, source_target_pairs={{0,64},{64,0},{128,192},{192,128},{1,65},{65,1},{129,193},{193,129... | collective-permute-start | bytes 786440 | tf_op jit(solution)/shard_map/ppermute | solution.py:741
  80.8 7.1 %collective-permute-start.7 = (f32[8,32,128]{2,1,0:T(8,128)S(1)}, f32[8,32,128]{2,1,0:T(8,128)S(1)}, u32[]{:S(2)}, u32[]{:S(2)}) collective-permute-start(f32[8,32,128]{2,1,0:T(8,128)S(1)} %fusion.order_ref), channel_id=1, source_target_pairs={{0,128},{128,0},{64,192},{192,64},{1,129},{129,1},{65,193},{193,65... | collective-permute-start | bytes 393224 | tf_op jit(solution)/shard_map/ppermute | solution.py:743
  83.0 1.0 %copy-start.1 = (f32[8,128,128]{2,1,0:T(8,128)S(1)}, f32[8,128,128]{2,1,0:T(8,128)}, u32[]{:S(2)}) copy-start(f32[8,128,128]{2,1,0:T(8,128)} %get-tuple-element.66.late_ref) | copy-start | bytes 1572868

commit v9 on v7

--- a/solution.py
+++ b/solution.py
@@ -207,10 +207,8 @@
         store.wait()
 
 
-def adjoint_pack_kernel(now_hbm, next_hbm, speed_hbm, first_ref, second_ref, now_ref, next_ref, speed_ref, sems):
+def adjoint_pack_kernel(now_ref, next_ref, speed_ref, first_ref, second_ref):
     fields = (now_ref, next_ref, speed_ref)
-    for copy in fetch((now_hbm, next_hbm, speed_hbm), fields, sems):
-        copy.wait()
     par = parity()
     for out_ref, near in ((first_ref, HALF * (1 - par)), (second_ref, HALF * par)):
         far = HALF - near
@@ -666,8 +664,7 @@
     )
     incoming = lax.all_to_all(outgoing, "dom", split_axis=0, concat_axis=0, tiled=True)
     send_a, send_b = call(
-        adjoint_pack_kernel, "adjoint_pack", [HB] * 3, [planes(19)] * 2,
-        [pltpu.VMEM(*slab)] * 3 + [pltpu.SemaphoreType.DMA((3,))], in_hbm(lam4, lam5, speed_sq),
+        adjoint_pack_kernel, "adjoint_pack", [VM] * 3, [planes(19)] * 2, [], (lam4, lam5, speed_sq),
     )
     got_a, got_b = swap(send_a, send_b)
     count = rec_depth.shape[0]

time: 82.7 us -> 82.8 us (level)
  Pallas kernels: 30.9 us -> 29.6 us
  starting transfers between devices: 36.6 us -> 37.7 us
    pallas_call x11, Pallas kernels: 30.9 us -> 29.6 us  [call(): pl.pallas_call(kernel, name=name, out_shape=[pltpu.HBM(*o) if out is HB e...]
    ppermute x4, starting transfers between devices: 19.2 us -> 20.3 us  [swap(): far = lax.ppermute(b, 'dom', odd)]
  transfers between devices with their start and end apart: 11 -> 11, of which waited for: 5 -> 6; matrix products, arithmetic and copies ran while one was open for 0% -> 0% of each run, Pallas kernels for 31% -> 30%
where the time goes in v9:
time: 82.8 us; the launch traced here: 82.4 us
  starting transfers between devices  37.7 us (46%)
  Pallas kernels  29.6 us (36%)
  waiting for transfers between devices  12.1 us (15%)
  between operations  2.23 us (3%)
    pallas_call x11, Pallas kernels, call(): pl.pallas_call(kernel, name=name, out_shape=[pltpu.HBM(*o) if out is HB e...  29.6 us
    ppermute x4, starting transfers between devices, swap(): far = lax.ppermute(b, 'dom', odd)  20.3 us
    all_to_all x1, starting transfers between devices, per_device(): lax.all_to_all(outgoing, 'dom', split_axis=0, concat_axis=0, tiled=True)  13.2 us
    ppermute x4, waiting for transfers between devices, swap(): far = lax.ppermute(b, 'dom', odd)  9.52 us
    ppermute x1, starting transfers between devices, per_device(): other = lax.ppermute(part, 'shot', [(0, 2), (2, 0), (1, 3), (3, 1)])  2.2 us
    ppermute x4, starting transfers between devices, swap(): return (lax.ppermute(a, 'dom', even), far)  1.83 us
  transfers between devices with their start and end apart: 11, of which 6 were waited for; matrix products, arithmetic and copies ran while one was open for 0% of the time, Pallas kernels for 30%

profile of v9, /device:TPU:2, one launch (start us, length us, event | category | flops | bytes accessed | tf_op | source)
XLA Modules:
  0.0 82.4 jit_solution(2636014129695348409)
XLA Ops:
  0.6 0.0 copy-start
  0.6 0.0 copy-start.3
  0.7 0.0 copy-start.5
  0.7 2.6 %gather.1 = bf16[64,32,128]{2,1,0:T(8,128)(2,1)} custom-call(s32[1,64]{1,0:T(1,128)} %bitcast.29, bf16[64,4096]{1,0:T(8,128)(2,1)} %bitcast.28), custom_call_target="tpu_custom_call" | custom-call | flops 2000000000 | bytes 7200000 | tf_op jit(solution)/shard_map/gather/pallas_call | solution.py:43
  3.2 13.2 %all-to-all-start = ((bf16[64,32,128]{2,1,0:T(8,128)(2,1)}), bf16[64,32,128]{2,1,0:T(8,128)(2,1)S(1)}, u32[]{:S(2)}, u32[]{:S(2)}) async-start(bf16[64,32,128]{2,1,0:T(8,128)(2,1)} %gather.1), calls=%async_computation | async-start | bytes 1048576 | tf_op jit(solution)/shard_map/all_to_all | solution.py:665
  16.5 0.0 copy-done
  16.5 0.0 copy-done.3
  16.5 0.0 copy-done.5
  16.5 0.0 copy-start.7
  16.5 0.0 copy-start.8
  16.5 0.0 copy-start.9
  16.5 0.2 adjoint_pack.1
  16.7 1.6 %collective-permute-start = (bf16[19,128,128]{2,1,0:T(8,128)(2,1)S(1)}, bf16[19,128,128]{2,1,0:T(8,128)(2,1)S(1)}, u32[]{:S(2)}, u32[]{:S(2)}) collective-permute-start(bf16[19,128,128]{2,1,0:T(8,128)(2,1)S(1)} %get-tuple-element.41), channel_id=1, source_target_pairs={{0,1},{1,0},{2,3},{3,2},{4,5},{5,4},{6,7},{7,6},{8,9},{9,8},{10,11... | collective-permute-start | bytes 1867784 | tf_op jit(solution)/shard_map/ppermute | solution.py:646
  18.3 6.1 %collective-permute-start.3 = (bf16[19,128,128]{2,1,0:T(8,128)(2,1)S(1)}, bf16[19,128,128]{2,1,0:T(8,128)(2,1)S(1)}, u32[]{:S(2)}, u32[]{:S(2)}) collective-permute-start(bf16[19,128,128]{2,1,0:T(8,128)(2,1)S(1)} %get-tuple-element.48), channel_id=1, source_target_pairs={{1,2},{2,1},{3,4},{4,3},{5,6},{6,5},{7,8},{8,7},{9,10},{10,9},{11,... | collective-permute-start | bytes 1867784 | tf_op jit(solution)/shard_map/ppermute | solution.py:645
  24.3 0.0 copy-done.7
  24.3 0.0 copy-done.8
  24.3 0.0 copy-start.10
  24.4 7.2 %inject.1 = (f32[16,4,128,128]{3,2,1,0:T(8,128)}, f32[8,128]{1,0:T(8,128)}) custom-call(s32[1,1024]{1,0:T(1,128)S(1)} %bitcast.24, s32[1,1024]{1,0:T(1,128)S(1)} %bitcast.25, f32[4,1024]{1,0:T(4,128)S(1)} %bitcast.23), custom_call_target="tpu_custom_call" | custom-call | flops 4000000000 | bytes 14400000 | tf_op jit(solution)/shard_map/inject/pallas_call | solution.py:43
  32.9 0.4 all-to-all-done.pieces_ref
  33.3 0.0 copy-done.10
  33.3 0.7 forward_pack.1
  34.0 6.3 %collective-permute-start.2 = (bf16[12,128,128]{2,1,0:T(8,128)(2,1)S(1)}, bf16[12,128,128]{2,1,0:T(8,128)(2,1)S(1)}, u32[]{:S(2)}, u32[]{:S(2)}) collective-permute-start(bf16[12,128,128]{2,1,0:T(8,128)(2,1)S(1)} %get-tuple-element.39.mine_b), channel_id=1, source_target_pairs={{1,2},{2,1},{3,4},{4,3},{5,6},{6,5},{7,8},{8,7},{9,10},{10,9},{11,... | collective-permute-start | bytes 1179656 | tf_op jit(solution)/shard_map/ppermute | solution.py:645
  40.3 0.1 collective-permute-start.1
  40.4 0.0 collective-permute-done.got_a
  40.4 2.2 %adjoint_side.1 = (f32[16,128,128]{2,1,0:T(8,128)S(1)}, f32[8,128,128]{2,1,0:T(8,128)S(1)}, f32[16,2,128,128]{3,2,1,0:T(8,128)S(1)}, f32[8,128]{1,0:T(8,128)S(1)}) custom-call(f32[8,128,128]{2,1,0:T(8,128)S(1)} %bitcast.17, f32[8,128,128]{2,1,0:T(8,128)S(1)} %bitcast.22, f32[8,128,128]{2,1,0:T(8,128)S(1)} %copy-done.6, ...), custom_call_target="tpu_custom_call" | custom-call | flops 2000000000 | bytes 7200000 | tf_op jit(solution)/shard_map/adjoint_side/pallas_call | solution.py:43
  42.7 0.7 forward_own.1
  43.4 3.5 %collective-permute-done.3.got_b = bf16[19,128,128]{2,1,0:T(8,128)(2,1)S(1)} collective-permute-done((bf16[19,128,128]{2,1,0:T(8,128)(2,1)S(1)}, bf16[19,128,128]{2,1,0:T(8,128)(2,1)S(1)}, u32[]{:S(2)}, u32[]{:S(2)}) %collective-permute-start.3) | collective-permute-done | bytes 622624 | tf_op jit(solution)/shard_map/ppermute | solution.py:645
  46.9 1.9 %adjoint_first.1 = (bf16[8,128,128]{2,1,0:T(8,128)(2,1)S(1)}, bf16[8,128,128]{2,1,0:T(8,128)(2,1)S(1)}, f32[32,128,128]{2,1,0:T(8,128)S(1)}, f32[16,128,128]{2,1,0:T(8,128)S(1)}, f32[16,144,128]{2,1,0:T(8,128)S(1)}) custom-call(f32[8,128,128]{2,1,0:T(8,128)S(1)} %bitcast.18, f32[8,128,128]{2,1,0:T(8,128)S(1)} %copy-done.6, ...), custom_call_target="tpu_custom_call" | custom-call | flops 2000000000 | bytes 7200000 | tf_op jit(solution)/shard_map/adjoint_first/pallas_call | solution.py:43
  48.8 3.1 %collective-permute-start.6 = (bf16[8,128,128]{2,1,0:T(8,128)(2,1)S(1)}, bf16[8,128,128]{2,1,0:T(8,128)(2,1)S(1)}, u32[]{:S(2)}, u32[]{:S(2)}) collective-permute-start(bf16[8,128,128]{2,1,0:T(8,128)(2,1)S(1)} %get-tuple-element.54), channel_id=1, source_target_pairs={{1,2},{2,1},{3,4},{4,3},{5,6},{6,5},{7,8},{8,7},{9,10},{10,9},{11,... | collective-permute-start | bytes 786440 | tf_op jit(solution)/shard_map/ppermute | solution.py:645
  51.8 0.1 collective-permute-start.7
  51.9 2.3 %collective-permute-done.2.got_b = bf16[12,128,128]{2,1,0:T(8,128)(2,1)S(1)} collective-permute-done((bf16[12,128,128]{2,1,0:T(8,128)(2,1)S(1)}, bf16[12,128,128]{2,1,0:T(8,128)(2,1)S(1)}, u32[]{:S(2)}, u32[]{:S(2)}) %collective-permute-start.2) | collective-permute-done | bytes 393248 | tf_op jit(solution)/shard_map/ppermute | solution.py:645
  54.2 0.0 collective-permute-done.1.got_a
  54.2 0.0 copy-done.2
  54.2 2.8 %forward_first.1 = (bf16[8,128,128]{2,1,0:T(8,128)(2,1)S(1)}, bf16[8,128,128]{2,1,0:T(8,128)(2,1)S(1)}, f32[16,144,128]{2,1,0:T(8,128)S(1)}, f32[8,128,128]{2,1,...) custom-call(s32[1]{0:T(128)S(6)} %copy.15.depth_ref, ...), custom_call_target="tpu_custom_call" | custom-call | flops 2000000000 | bytes 7200000 | tf_op jit(solution)/shard_map/forward_first/pallas_call | solution.py:43
  57.0 4.9 %collective-permute-start.4 = (bf16[8,128,128]{2,1,0:T(8,128)(2,1)S(1)}, bf16[8,128,128]{2,1,0:T(8,128)(2,1)S(1)}, u32[]{:S(2)}, u32[]{:S(2)}) collective-permute-start(bf16[8,128,128]{2,1,0:T(8,128)(2,1)S(1)} %get-tuple-element.51), channel_id=1, source_target_pairs={{1,2},{2,1},{3,4},{4,3},{5,6},{6,5},{7,8},{8,7},{9,10},{10,9},{11,... | collective-permute-start | bytes 786440 | tf_op jit(solution)/shard_map/ppermute | solution.py:645
  61.9 0.1 collective-permute-start.5
  62.0 0.0 collective-permute-done.6.got_b
  62.1 0.0 collective-permute-done.7.got_a
  62.1 4.5 %middle.1 = (f32[8,128,128]{2,1,0:T(8,128)}, f32[8,128,128]{2,1,0:T(8,128)S(1)}, f32[8,128,128]{2,1,0:T(8,128)S(1)}, f32[8,128,128]{2,1,0:T(8,128)S(1)}, f32[24,...) custom-call(s32[1]{0:T(128)S(6)} %copy.15.depth_ref, s32[1]{0:T(128)S(6)} %copy.16.row_ref, ...), custom_call_target="tpu_custom_call" | custom-call | flops 2000000000 | bytes 7200000 | tf_op jit(solution)/shard_map/middle/pallas_call | solution.py:43
  66.6 3.8 %collective-permute-done.4.got_b = bf16[8,128,128]{2,1,0:T(8,128)(2,1)S(1)} collective-permute-done((bf16[8,128,128]{2,1,0:T(8,128)(2,1)S(1)}, bf16[8,128,128]{2,1,0:T(8,128)(2,1)S(1)}, u32[]{:S(2)}, u32[]{:S(2)}) %collective-permute-start.4) | collective-permute-done | bytes 262176 | tf_op jit(solution)/shard_map/ppermute | solution.py:645
  70.3 0.0 collective-permute-done.5.got_a
  70.3 2.6 %forward_second.1 = (f32[2,8,32,128]{3,2,1,0:T(8,128)S(1)}, f32[2,8,32,128]{3,2,1,0:T(8,128)S(1)}) custom-call(s32[1]{0:T(128)S(6)} %copy.15.depth_ref, s32[1]{0:T(128)S(6)} %copy.16.row_ref, f32[1,3]{1,0:T(1,128)S(1)} %copy-done.2, bf16[8,128,128]{2,1,0:T(8,128)(2,1)S(1)} %collective-permute-done.4.got_b, ...), custom_call_target="tpu_custom_call" | custom-call | flops 2000000000 | bytes 7200000 | tf_op jit(solution)/shard_map/forward_second/pallas_call | solution.py:43
  72.9 0.1 collective-permute-start.8
  73.0 1.5 %collective-permute-done.8 = f32[2,8,32,128]{3,2,1,0:T(8,128)S(1)} collective-permute-done((f32[2,8,32,128]{3,2,1,0:T(8,128)S(1)}, f32[2,8,32,128]{3,2,1,0:T(8,128)S(1)}, u32[]{:S(2)}, u32[]{:S(2)}) %collective-permute-start.8) | collective-permute-done | bytes 262176 | tf_op jit(solution)/shard_map/ppermute | solution.py:725
  74.6 2.2 %collective-permute-start.9 = (f32[8,32,128]{2,1,0:T(8,128)S(1)}, f32[8,32,128]{2,1,0:T(8,128)S(1)}, u32[]{:S(2)}, u32[]{:S(2)}) collective-permute-start(f32[8,32,128]{2,1,0:T(8,128)S(1)} %fusion.order_ref), channel_id=1, source_target_pairs={{0,128},{128,0},{64,192},{192,64},{1,129},{129,1},{65,193},{193,65... | collective-permute-start | bytes 393224 | tf_op jit(solution)/shard_map/ppermute | solution.py:727
  76.8 4.3 %adjoint_last.1 = f32[8,128,128]{2,1,0:T(8,128)} custom-call(f32[16,4,128,128]{3,2,1,0:T(8,128)} %get-tuple-element.40.inject_hbm, f32[8,128,128]{2,1,0:T(8,128)S(1)} %copy-done.1, f32[32,128,128]{2,1,0:T(8,128)S(1)} %get-tuple-element.56.lam_ref, f32[8,128,128]{2,1,0:T(8,128)S(1)} %get-tuple-element.69.lam2_halo, ...), custom_call_target="tpu_custom_call" | custom-call | flops 2000000000 | bytes 7200000 | tf_op jit(solution)/shard_map/adjoint_last/pallas_call | solution.py:43
  81.1 0.6 collective-permute-done.9
  81.7 0.7 fusion.2
  (9 shorter events, 0.0 us)
Async XLA Ops:
  0.6 15.8 %copy-start = (f32[1,8,128,128]{3,2,1,0:T(8,128)S(1)}, f32[1,8,128,128]{3,2,1,0:T(8,128)}, u32[]{:S(2)}) copy-start(f32[1,8,128,128]{3,2,1,0:T(8,128)} %param.17) | copy-start | bytes 1572868
  0.6 15.8 %copy-start.3 = (f32[1,8,128,128]{3,2,1,0:T(8,128)S(1)}, f32[1,8,128,128]{3,2,1,0:T(8,128)}, u32[]{:S(2)}) copy-start(f32[1,8,128,128]{3,2,1,0:T(8,128)} %param.16) | copy-start | bytes 1572868
  0.7 15.8 %copy-start.5 = (f32[8,128,128]{2,1,0:T(8,128)S(1)}, f32[8,128,128]{2,1,0:T(8,128)}, u32[]{:S(2)}) copy-start(f32[8,128,128]{2,1,0:T(8,128)} %speed_ref.5) | copy-start | bytes 1572868
  3.2 30.1 %all-to-all-start = ((bf16[64,32,128]{2,1,0:T(8,128)(2,1)}), bf16[64,32,128]{2,1,0:T(8,128)(2,1)S(1)}, u32[]{:S(2)}, u32[]{:S(2)}) async-start(bf16[64,32,128]{2,1,0:T(8,128)(2,1)} %gather.1), calls=%async_computation | async-start | bytes 1048576 | tf_op jit(solution)/shard_map/all_to_all | solution.py:665
  16.5 7.8 %copy-start.7 = (f32[1,4,1024]{2,1,0:T(4,128)S(1)}, f32[1,4,1024]{2,1,0:T(4,128)}, u32[]{:S(2)}) copy-start(f32[1,4,1024]{2,1,0:T(4,128)} %param.23) | copy-start | bytes 49156
  16.5 7.8 %copy-start.8 = (s32[1024]{0:T(1024)S(1)}, s32[1024]{0:T(1024)}, u32[]{:S(2)}) copy-start(s32[1024]{0:T(1024)} %param.21) | copy-start | bytes 12292
  16.5 7.8 %copy-start.9 = (s32[1024]{0:T(1024)S(1)}, s32[1024]{0:T(1024)}, u32[]{:S(2)}) copy-start(s32[1024]{0:T(1024)} %param.22) | copy-start | bytes 12292
  16.7 23.7 %collective-permute-start = (bf16[19,128,128]{2,1,0:T(8,128)(2,1)S(1)}, bf16[19,128,128]{2,1,0:T(8,128)(2,1)S(1)}, u32[]{:S(2)}, u32[]{:S(2)}) collective-permute-start(bf16[19,128,128]{2,1,0:T(8,128)(2,1)S(1)} %get-tuple-element.41), channel_id=1, source_target_pairs={{0,1},{1,0},{2,3},{3,2},{4,5},{5,4},{6,7},{7,6},{8,9},{9,8},{10,11... | collective-permute-start | bytes 1867784 | tf_op jit(solution)/shard_map/ppermute | solution.py:646
  18.3 28.6 %collective-permute-start.3 = (bf16[19,128,128]{2,1,0:T(8,128)(2,1)S(1)}, bf16[19,128,128]{2,1,0:T(8,128)(2,1)S(1)}, u32[]{:S(2)}, u32[]{:S(2)}) collective-permute-start(bf16[19,128,128]{2,1,0:T(8,128)(2,1)S(1)} %get-tuple-element.48), channel_id=1, source_target_pairs={{1,2},{2,1},{3,4},{4,3},{5,6},{6,5},{7,8},{8,7},{9,10},{10,9},{11,... | collective-permute-start | bytes 1867784 | tf_op jit(solution)/shard_map/ppermute | solution.py:645
  24.3 9.0 %copy-start.10 = (s32[1,1,64]{2,1,0:T(1,128)S(1)}, s32[1,1,64]{2,1,0:T(1,128)}, u32[]{:S(2)}) copy-start(s32[1,1,64]{2,1,0:T(1,128)} %param.14) | copy-start | bytes 772
  33.3 7.1 %copy-start.4 = (f32[1,8,128,128]{3,2,1,0:T(8,128)S(1)}, f32[1,8,128,128]{3,2,1,0:T(8,128)}, u32[]{:S(2)}) copy-start(f32[1,8,128,128]{3,2,1,0:T(8,128)} %param.16) | copy-start | bytes 1572868
  33.3 7.1 %copy-start.6 = (f32[8,128,128]{2,1,0:T(8,128)S(1)}, f32[8,128,128]{2,1,0:T(8,128)}, u32[]{:S(2)}) copy-start(f32[8,128,128]{2,1,0:T(8,128)} %speed_ref.5) | copy-start | bytes 1572868
  34.0 20.2 %collective-permute-start.2 = (bf16[12,128,128]{2,1,0:T(8,128)(2,1)S(1)}, bf16[12,128,128]{2,1,0:T(8,128)(2,1)S(1)}, u32[]{:S(2)}, u32[]{:S(2)}) collective-permute-start(bf16[12,128,128]{2,1,0:T(8,128)(2,1)S(1)} %get-tuple-element.39.mine_b), channel_id=1, source_target_pairs={{1,2},{2,1},{3,4},{4,3},{5,6},{6,5},{7,8},{8,7},{9,10},{10,9},{11,... | collective-permute-start | bytes 1179656 | tf_op jit(solution)/shard_map/ppermute | solution.py:645
  40.3 13.9 %collective-permute-start.1 = (bf16[12,128,128]{2,1,0:T(8,128)(2,1)S(1)}, bf16[12,128,128]{2,1,0:T(8,128)(2,1)S(1)}, u32[]{:S(2)}, u32[]{:S(2)}) collective-permute-start(bf16[12,128,128]{2,1,0:T(8,128)(2,1)S(1)} %get-tuple-element.38.mine_ref.mine_a), channel_id=1, source_target_pairs={{0,1},{1,0},{2,3},{3,2},{4,5},{5,4},{6,7},{7,6},{8,9},{9,8},{10,11... | collective-permute-start | bytes 1179656 | tf_op jit(solution)/shard_map/ppermute | solution.py:646
  46.9 7.3 %copy-start.2 = (f32[1,3]{1,0:T(1,128)S(1)}, f32[1,3]{1,0:T(1,128)}, u32[]{:S(2)}) copy-start(f32[1,3]{1,0:T(1,128)} %wave_ref.5) | copy-start | bytes 40
  48.8 13.3 %collective-permute-start.6 = (bf16[8,128,128]{2,1,0:T(8,128)(2,1)S(1)}, bf16[8,128,128]{2,1,0:T(8,128)(2,1)S(1)}, u32[]{:S(2)}, u32[]{:S(2)}) collective-permute-start(bf16[8,128,128]{2,1,0:T(8,128)(2,1)S(1)} %get-tuple-element.54), channel_id=1, source_target_pairs={{1,2},{2,1},{3,4},{4,3},{5,6},{6,5},{7,8},{8,7},{9,10},{10,9},{11,... | collective-permute-start | bytes 786440 | tf_op jit(solution)/shard_map/ppermute | solution.py:645
  51.8 10.2 %collective-permute-start.7 = (bf16[8,128,128]{2,1,0:T(8,128)(2,1)S(1)}, bf16[8,128,128]{2,1,0:T(8,128)(2,1)S(1)}, u32[]{:S(2)}, u32[]{:S(2)}) collective-permute-start(bf16[8,128,128]{2,1,0:T(8,128)(2,1)S(1)} %get-tuple-element.55), channel_id=1, source_target_pairs={{0,1},{1,0},{2,3},{3,2},{4,5},{5,4},{6,7},{7,6},{8,9},{9,8},{10,11... | collective-permute-start | bytes 786440 | tf_op jit(solution)/shard_map/ppermute | solution.py:646
  57.0 13.4 %collective-permute-start.4 = (bf16[8,128,128]{2,1,0:T(8,128)(2,1)S(1)}, bf16[8,128,128]{2,1,0:T(8,128)(2,1)S(1)}, u32[]{:S(2)}, u32[]{:S(2)}) collective-permute-start(bf16[8,128,128]{2,1,0:T(8,128)(2,1)S(1)} %get-tuple-element.51), channel_id=1, source_target_pairs={{1,2},{2,1},{3,4},{4,3},{5,6},{6,5},{7,8},{8,7},{9,10},{10,9},{11,... | collective-permute-start | bytes 786440 | tf_op jit(solution)/shard_map/ppermute | solution.py:645
  61.9 8.4 %collective-permute-start.5 = (bf16[8,128,128]{2,1,0:T(8,128)(2,1)S(1)}, bf16[8,128,128]{2,1,0:T(8,128)(2,1)S(1)}, u32[]{:S(2)}, u32[]{:S(2)}) collective-permute-start(bf16[8,128,128]{2,1,0:T(8,128)(2,1)S(1)} %get-tuple-element.52), channel_id=1, source_target_pairs={{0,1},{1,0},{2,3},{3,2},{4,5},{5,4},{6,7},{7,6},{8,9},{9,8},{10,11... | collective-permute-start | bytes 786440 | tf_op jit(solution)/shard_map/ppermute | solution.py:646
  70.3 6.4 %copy-start.1 = (f32[8,128,128]{2,1,0:T(8,128)S(1)}, f32[8,128,128]{2,1,0:T(8,128)}, u32[]{:S(2)}) copy-start(f32[8,128,128]{2,1,0:T(8,128)} %get-tuple-element.68.late_ref) | copy-start | bytes 1572868
  72.9 1.6 %collective-permute-start.8 = (f32[2,8,32,128]{3,2,1,0:T(8,128)S(1)}, f32[2,8,32,128]{3,2,1,0:T(8,128)S(1)}, u32[]{:S(2)}, u32[]{:S(2)}) collective-permute-start(f32[2,8,32,128]{3,2,1,0:T(8,128)S(1)} %get-tuple-element.67), channel_id=1, source_target_pairs={{0,64},{64,0},{128,192},{192,128},{1,65},{65,1},{129,193},{193,129... | collective-permute-start | bytes 786440 | tf_op jit(solution)/shard_map/ppermute | solution.py:725
  74.6 7.1 %collective-permute-start.9 = (f32[8,32,128]{2,1,0:T(8,128)S(1)}, f32[8,32,128]{2,1,0:T(8,128)S(1)}, u32[]{:S(2)}, u32[]{:S(2)}) collective-permute-start(f32[8,32,128]{2,1,0:T(8,128)S(1)} %fusion.order_ref), channel_id=1, source_target_pairs={{0,128},{128,0},{64,192},{192,64},{1,129},{129,1},{65,193},{193,65... | collective-permute-start | bytes 393224 | tf_op jit(solution)/shard_map/ppermute | solution.py:727
